TPU v7x, 256 devices: a whole 4x4x8 slice. The times are simulated.
256 devices in a mesh: rep: 32 (over z, x_hi, core), exp: 8 (over x_lo, y).
Axes of the slice: x: 4 (x_hi: 2, x_lo: 2; x = x_hi * 2 + x_lo), y: 4, z: 8, core: 2. Of those that a mesh axis runs over, the one named last changes fastest.
Arguments:
- residual: bfloat16 [3, 512, 4096], P(None, ('rep', 'exp')), may hold values from -6 to 6
- queries: bfloat16 [3, 512, 4096], P(None, ('rep', 'exp')), may hold values from -30 to 30
- key_cache: bfloat16 [512, 1024, 256], P(('rep', 'exp')), may hold values from -6 to 6
- value_cache: bfloat16 [512, 1024, 256], P(('rep', 'exp')), may hold values from -6 to 6
- new_keys: bfloat16 [3, 512, 256], P(None, ('rep', 'exp')), may hold values from -6 to 6
- new_values: bfloat16 [3, 512, 256], P(None, ('rep', 'exp')), may hold values from -6 to 6
- cache_len: int32 [512], P(('rep', 'exp')), may hold values from 128 to 1024, as said below
- norm_gain: bfloat16 [4096], replicated, may hold values from 0.099609375 to 1.8984375
- expert_ids: int32 [3, 512, 8], P(None, ('rep', 'exp')), may hold values from 0 to 63, all different within a row; in each aligned block of 16 rows (0 to 15, 16 to 31, ..., all dimensions but the last counted through in order) at most 4 rows name the same one
- gate_scores: int32 [3, 512, 8], P(None, ('rep', 'exp')), may hold values from 1 to 1000
- gate_weight: bfloat16 [64, 1536, 4096], P('rep', 'exp'), may hold values from -0.09375 to 0.09375
- up_weight: bfloat16 [64, 1536, 4096], P('rep', 'exp'), may hold values from -0.09375 to 0.09375
- down_weight: bfloat16 [64, 1536, 4096], P('rep', 'exp'), may hold values from -0.15625 to 0.15625
Outputs:
- mixed: bfloat16 [3, 512, 4096], P(None, ('rep', 'exp'))
Inputs may be any that keep to these rules, and one draw needn't show every extreme that they name: `expert_ids`: within each step and each aligned block of 16 sequences (the sequences of one index of rep), no expert is named more than 4 times, and that count is reached; a token names different experts. `cache_len`: some sequence holds all 1024 cached tokens.
All inputs are finite; a program needn't handle non-finite values.
Results may differ from a plain program's by a relative error of at most 0.013.
Values may be sent and summed in bfloat16 or wider, within the bound.
No kernel may reach another device: no remote copies, remote signals or barrier semaphores. Data moves between devices by JAX's collectives and lax.ppermute only.
A program may use at most 128 MiB of HBM per device.

v0:
```python
import math

import jax
import jax.numpy as jnp
from jax import lax
from jax.sharding import PartitionSpec as P

D = 4096
HD = 128
QH = 32
KVH = 2
TOPK = 8
EXP_REP = 2
CAPE = 4
STEPS = 3
CACHE = 1024


def attend_rows(decode_query_rows, key_cache, value_cache, new_keys, new_values, cache_len, step):
    row_count = decode_query_rows.shape[0]
    group_size = QH // KVH
    scaling = 1.0 / math.sqrt(HD)
    query_heads = decode_query_rows.reshape(row_count, KVH, group_size, HD)
    cached_keys = key_cache.reshape(row_count, CACHE, KVH, HD)
    cached_values = value_cache.reshape(row_count, CACHE, KVH, HD)
    fresh_keys = new_keys[: step + 1].reshape(step + 1, row_count, KVH, HD)
    fresh_values = new_values[: step + 1].reshape(step + 1, row_count, KVH, HD)
    previous_scores = (
        jnp.einsum("sjgd,stjd->sjgt", query_heads, cached_keys, preferred_element_type=jnp.float32)
        * scaling
    )
    new_scores = (
        jnp.einsum("sjgd,tsjd->sjgt", query_heads, fresh_keys, preferred_element_type=jnp.float32)
        * scaling
    )
    position = lax.broadcasted_iota(jnp.int32, (row_count, 1, 1, CACHE), 3)
    previous_scores = jnp.where(position < cache_len[:, None, None, None], previous_scores, -1e30)
    row_max = jnp.maximum(
        jnp.max(previous_scores, axis=-1, keepdims=True),
        jnp.max(new_scores, axis=-1, keepdims=True),
    )
    old_expo = jnp.exp(previous_scores - row_max)
    new_expo = jnp.exp(new_scores - row_max)
    denominator = jnp.sum(old_expo, axis=-1, keepdims=True) + jnp.sum(
        new_expo, axis=-1, keepdims=True
    )
    old_probs = (old_expo / denominator).astype(jnp.bfloat16)
    new_probs = (new_expo / denominator).astype(jnp.bfloat16)
    blended = jnp.einsum(
        "sjgt,stjd->sjgd", old_probs, cached_values, preferred_element_type=jnp.float32
    )
    blended = blended + jnp.einsum(
        "sjgt,tsjd->sjgd", new_probs, fresh_values, preferred_element_type=jnp.float32
    )
    return blended.reshape(row_count, QH * HD)


def norm_rows(hidden, norm_gain):
    mean_square = jnp.mean(hidden * hidden, axis=-1, keepdims=True)
    return (hidden * lax.rsqrt(mean_square + 1e-06) * norm_gain.astype(jnp.float32)).astype(
        jnp.bfloat16
    )


def slot_targets(chosen, experts):
    flat_ids = chosen.reshape(-1)
    matches = (flat_ids[:, None] == lax.broadcasted_iota(jnp.int32, (1, experts), 1)).astype(
        jnp.int32
    )
    ranking = jnp.cumsum(matches, axis=0) - 1
    slot_rank = jnp.sum(matches * ranking, axis=1)
    return (flat_ids * CAPE + slot_rank).reshape(chosen.shape)


def placement_matrix(target, slot_total):
    slot_ids = lax.broadcasted_iota(jnp.int32, (slot_total, 1, 1), 0)
    return jnp.any(target[None, :, :] == slot_ids, axis=2).astype(jnp.bfloat16)


def expert_block(inbound, gate_weight, up_weight, down_weight):
    sources, width, features = inbound.shape
    slotted = inbound.reshape(sources, EXP_REP, CAPE, features)
    gate_act = jnp.einsum(
        "recd,efd->recf", slotted, gate_weight, preferred_element_type=jnp.float32
    )
    up_act = jnp.einsum("recd,efd->recf", slotted, up_weight, preferred_element_type=jnp.float32)
    hidden_activation = (jax.nn.silu(gate_act) * up_act).astype(jnp.bfloat16)
    partial_value = jnp.einsum(
        "recf,efd->recd", hidden_activation, down_weight, preferred_element_type=jnp.float32
    )
    return partial_value.reshape(sources, width, features)


def per_device(
    residual,
    queries,
    key_cache,
    value_cache,
    new_keys,
    new_values,
    cache_len,
    norm_gain,
    expert_ids,
    gate_scores,
    gate_weight,
    up_weight,
    down_weight,
):
    groups = lax.axis_size("rep")
    slot_width = EXP_REP * CAPE
    slot_total = groups * slot_width
    results = []
    for step in range(STEPS):
        attention = attend_rows(
            queries[step], key_cache, value_cache, new_keys, new_values, cache_len, step
        )
        hidden = residual[step].astype(jnp.float32) + attention
        normed = norm_rows(hidden, norm_gain)
        chosen_now, scores_now = (
            lax.all_gather(expert_ids[step], "exp", axis=0, tiled=True),
            lax.all_gather(gate_scores[step], "exp", axis=0, tiled=True),
        )
        unscaled_scores = scores_now.astype(jnp.float32)
        gate_values = unscaled_scores / jnp.sum(unscaled_scores, axis=-1, keepdims=True)
        target = slot_targets(chosen_now, EXP_REP * groups)
        placing = placement_matrix(target, slot_total)
        group_count = target.shape[0]
        group_rows = lax.all_gather(normed, "exp", axis=0, tiled=True)
        outbound = jnp.dot(placing, group_rows, preferred_element_type=jnp.float32).astype(
            jnp.bfloat16
        )
        outbound = outbound.reshape(groups, slot_width, D)
        inbound = lax.all_to_all(outbound, "rep", split_axis=0, concat_axis=0, tiled=True)
        partial_value = expert_block(inbound, gate_weight, up_weight, down_weight).astype(
            jnp.bfloat16
        )
        returned = lax.all_to_all(
            partial_value, "rep", split_axis=0, concat_axis=0, tiled=True
        ).reshape(slot_total, D)
        selected_experts = jnp.take(returned, target.reshape(-1), axis=0).reshape(
            group_count, TOPK, D
        )
        weighted = jnp.einsum("gk,gkd->gd", gate_values, selected_experts.astype(jnp.float32))
        expert_sum = lax.psum_scatter(
            weighted.astype(jnp.bfloat16), "exp", scatter_dimension=0, tiled=True
        ).astype(jnp.float32)
        results.append((hidden + expert_sum).astype(jnp.bfloat16))
    return jnp.stack(results)


def solution(mesh):
    in_specs = (
        P(None, ("rep", "exp"), None),
        P(None, ("rep", "exp"), None),
        P(("rep", "exp"), None, None),
        P(("rep", "exp"), None, None),
        P(None, ("rep", "exp"), None),
        P(None, ("rep", "exp"), None),
        P(("rep", "exp")),
        P(),
        P(None, ("rep", "exp"), None),
        P(None, ("rep", "exp"), None),
        P("rep", "exp", None),
        P("rep", "exp", None),
        P("rep", "exp", None),
    )
    out_specs = P(None, ("rep", "exp"), None)
    return jax.shard_map(
        per_device, mesh=mesh, in_specs=in_specs, out_specs=out_specs, check_vma=False
    )
```

profile of v0, /device:TPU:4, one launch (start us, length us, event | category | flops | bytes accessed | tf_op | source)
XLA Modules:
  0.0 557.4 jit_solution(2346105998204464573)
XLA Ops:
  20.5 2.2 fusion.59
  34.1 28.4 %all-gather.7 = bf16[8,2,4096]{2,1,0:T(2,128)(2,1)S(1)} all-gather(bf16[1,2,4096]{2,1,0:T(2,128)(2,1)S(1)} %get-tuple-element.16), channel_id=1, replica_groups=mesh['rep'=32,'exp'=8] {'exp'}, dimensions={0}, use_global_device_ids=true | all-gather | bytes 147456 | tf_op jit(solution)/shard_map/all_gather | solution.py:128
  63.9 18.5 %all-gather.3 = s32[1,16,8]{2,0,1:T(1,128)S(1)} all-gather(s32[1,2,8]{2,0,1:T(1,128)S(1)} %bitcast.349), channel_id=5, replica_groups=mesh['rep'=32,'exp'=8] {'exp'}, dimensions={1}, use_global_device_ids=true | all-gather | bytes 576 | tf_op jit(solution)/shard_map/all_gather | solution.py:120
  89.1 11.6 %all-to-all-start.2 = ((bf16[32,8,4096]{2,1,0:T(8,128)(2,1)}), bf16[32,8,4096]{2,1,0:T(8,128)(2,1)}, u32[]{:S(2)}, u32[]{:S(2)}) async-start(bf16[32,8,4096]{2,1,0:T(8,128)(2,1)} %fusion.1), calls=%async_computation.2 | async-start | bytes 4194304 | tf_op jit(solution)/shard_map/all_to_all | solution.py:133
  100.8 16.8 %all-gather.1 = s32[1,16,8]{2,0,1:T(1,128)S(1)} all-gather(s32[1,2,8]{2,0,1:T(1,128)S(1)} %bitcast.346), channel_id=3, replica_groups=mesh['rep'=32,'exp'=8] {'exp'}, dimensions={1}, use_global_device_ids=true | all-gather | bytes 576 | tf_op jit(solution)/shard_map/all_gather | solution.py:120
  119.5 29.7 %all-gather.6 = bf16[8,2,4096]{2,1,0:T(2,128)(2,1)S(1)} all-gather(bf16[1,2,4096]{2,1,0:T(2,128)(2,1)S(1)} %get-tuple-element.15), channel_id=1, replica_groups=mesh['rep'=32,'exp'=8] {'exp'}, dimensions={0}, use_global_device_ids=true | all-gather | bytes 147456 | tf_op jit(solution)/shard_map/all_gather | solution.py:128
  153.6 11.7 %all-to-all-start = ((bf16[32,8,4096]{2,1,0:T(8,128)(2,1)}), bf16[32,8,4096]{2,1,0:T(8,128)(2,1)}, u32[]{:S(2)}, u32[]{:S(2)}) async-start(bf16[32,8,4096]{2,1,0:T(8,128)(2,1)} %fusion), calls=%async_computation | async-start | bytes 4194304 | tf_op jit(solution)/shard_map/all_to_all | solution.py:133
  165.2 16.8 %all-gather.5 = s32[1,16,8]{2,0,1:T(1,128)S(1)} all-gather(s32[1,2,8]{2,0,1:T(1,128)S(1)} %bitcast.345), channel_id=7, replica_groups=mesh['rep'=32,'exp'=8] {'exp'}, dimensions={1}, use_global_device_ids=true | all-gather | bytes 576 | tf_op jit(solution)/shard_map/all_gather | solution.py:120
  182.8 29.5 %all-gather.8 = bf16[8,2,4096]{2,1,0:T(2,128)(2,1)S(1)} all-gather(bf16[1,2,4096]{2,1,0:T(2,128)(2,1)S(1)} %get-tuple-element.17), channel_id=1, replica_groups=mesh['rep'=32,'exp'=8] {'exp'}, dimensions={0}, use_global_device_ids=true | all-gather | bytes 147456 | tf_op jit(solution)/shard_map/all_gather | solution.py:128
  215.9 11.2 %all-to-all-start.4 = ((bf16[32,8,4096]{2,1,0:T(8,128)(2,1)}), bf16[32,8,4096]{2,1,0:T(8,128)(2,1)}, u32[]{:S(2)}, u32[]{:S(2)}) async-start(bf16[32,8,4096]{2,1,0:T(8,128)(2,1)} %fusion.2), calls=%async_computation.4 | async-start | bytes 4194304 | tf_op jit(solution)/shard_map/all_to_all | solution.py:133
  227.1 2.9 copy.128
  232.6 5.8 %convolution_convert_fusion.4 = bf16[2,32,4,4096]{3,1,2,0:T(8,128)(2,1)} fusion(bf16[2,192,4096]{2,1,0:T(8,128)(2,1)S(1)} %copy-done, bf16[32,2,4,4096]{3,0,2,1:T(8,128)(2,1)} %bitcast.317, bf16[2,192,4096]{2,1,0:T(8,128)(2,1)} %param.26, f32[32,2,4,192]{3,0,2,1:T(8,128)S(1)} %fusion.21), kind=kOutput, calls=%fused_computation.7 | convolution fusion | flops 806649856 | bytes 10682368 | tf_op jit(solution)/shard_map/recf,efd->recd/dot_general | solution.py:88
  238.3 4.1 copy.129
  242.4 35.0 %all-to-all-done.4 = bf16[32,8,4096]{2,1,0:T(8,128)(2,1)} async-done(((bf16[32,8,4096]{2,1,0:T(8,128)(2,1)}), bf16[32,8,4096]{2,1,0:T(8,128)(2,1)}, u32[]{:S(2)}, u32[]{:S(2)}) %all-to-all-start.4) | async-done | bytes 2097184 | tf_op jit(solution)/shard_map/all_to_all | solution.py:133
  277.4 6.2 %all-to-all-start.3 = ((bf16[32,8,4096]{2,1,0:T(8,128)(2,1)}), bf16[32,8,4096]{2,1,0:T(8,128)(2,1)}, u32[]{:S(2)}, u32[]{:S(2)}) async-start(bf16[32,8,4096]{2,1,0:T(8,128)(2,1)} %copy.129), calls=%async_computation.3 | async-start | bytes 4194304 | tf_op jit(solution)/shard_map/all_to_all | solution.py:137
  283.6 2.9 copy.116
  289.1 5.7 %convolution_convert_fusion.5 = bf16[2,32,4,4096]{3,1,2,0:T(8,128)(2,1)} fusion(bf16[2,192,4096]{2,1,0:T(8,128)(2,1)S(1)} %copy-done, bf16[32,2,4,4096]{3,0,2,1:T(8,128)(2,1)} %bitcast.319, bf16[2,192,4096]{2,1,0:T(8,128)(2,1)} %param.26, f32[32,2,4,192]{3,0,2,1:T(8,128)S(1)} %fusion.18), kind=kOutput, calls=%fused_computation.8 | convolution fusion | flops 806649856 | bytes 10682368 | tf_op jit(solution)/shard_map/recf,efd->recd/dot_general | solution.py:88
  294.8 4.1 copy.117
  298.9 35.0 %all-to-all-done.3 = bf16[32,8,4096]{2,1,0:T(8,128)(2,1)} async-done(((bf16[32,8,4096]{2,1,0:T(8,128)(2,1)}), bf16[32,8,4096]{2,1,0:T(8,128)(2,1)}, u32[]{:S(2)}, u32[]{:S(2)}) %all-to-all-start.3) | async-done | bytes 2097184 | tf_op jit(solution)/shard_map/all_to_all | solution.py:137
  333.9 6.2 %all-to-all-start.1 = ((bf16[32,8,4096]{2,1,0:T(8,128)(2,1)}), bf16[32,8,4096]{2,1,0:T(8,128)(2,1)}, u32[]{:S(2)}, u32[]{:S(2)}) async-start(bf16[32,8,4096]{2,1,0:T(8,128)(2,1)} %copy.117), calls=%async_computation.1 | async-start | bytes 4194304 | tf_op jit(solution)/shard_map/all_to_all | solution.py:137
  340.2 2.9 copy.140
  345.6 5.7 %convolution_convert_fusion.3 = bf16[2,32,4,4096]{3,1,2,0:T(8,128)(2,1)} fusion(bf16[2,192,4096]{2,1,0:T(8,128)(2,1)S(1)} %copy-done, bf16[32,2,4,4096]{3,0,2,1:T(8,128)(2,1)} %bitcast.321, bf16[2,192,4096]{2,1,0:T(8,128)(2,1)} %param.26, f32[32,2,4,192]{3,0,2,1:T(8,128)S(1)} %fusion.24), kind=kOutput, calls=%fused_computation.6 | convolution fusion | flops 806649856 | bytes 10682368 | tf_op jit(solution)/shard_map/recf,efd->recd/dot_general | solution.py:88
  351.3 4.1 copy.141
  355.4 35.0 %all-to-all-done.1 = bf16[32,8,4096]{2,1,0:T(8,128)(2,1)} async-done(((bf16[32,8,4096]{2,1,0:T(8,128)(2,1)}), bf16[32,8,4096]{2,1,0:T(8,128)(2,1)}, u32[]{:S(2)}, u32[]{:S(2)}) %all-to-all-start.1) | async-done | bytes 2097184 | tf_op jit(solution)/shard_map/all_to_all | solution.py:137
  390.5 6.2 %all-to-all-start.5 = ((bf16[32,8,4096]{2,1,0:T(8,128)(2,1)}), bf16[32,8,4096]{2,1,0:T(8,128)(2,1)}, u32[]{:S(2)}, u32[]{:S(2)}) async-start(bf16[32,8,4096]{2,1,0:T(8,128)(2,1)} %copy.141), calls=%async_computation.5 | async-start | bytes 4194304 | tf_op jit(solution)/shard_map/all_to_all | solution.py:137
  396.8 16.8 %all-gather.2 = s32[1,16,8]{2,0,1:T(1,128)S(1)} all-gather(s32[1,2,8]{2,0,1:T(1,128)S(1)} %bitcast.350), channel_id=4, replica_groups=mesh['rep'=32,'exp'=8] {'exp'}, dimensions={1}, use_global_device_ids=true | all-gather | bytes 576 | tf_op jit(solution)/shard_map/all_gather | solution.py:121
  413.7 15.6 %all-gather = s32[1,16,8]{2,0,1:T(1,128)S(1)} all-gather(s32[1,2,8]{2,0,1:T(1,128)S(1)} %bitcast.348), channel_id=2, replica_groups=mesh['rep'=32,'exp'=8] {'exp'}, dimensions={1}, use_global_device_ids=true | all-gather | bytes 576 | tf_op jit(solution)/shard_map/all_gather | solution.py:121
  429.5 16.7 %all-gather.4 = s32[1,16,8]{2,0,1:T(1,128)S(1)} all-gather(s32[1,2,8]{2,0,1:T(1,128)S(1)} %bitcast.347), channel_id=6, replica_groups=mesh['rep'=32,'exp'=8] {'exp'}, dimensions={1}, use_global_device_ids=true | all-gather | bytes 576 | tf_op jit(solution)/shard_map/all_gather | solution.py:121
  446.5 5.1 gather_fusion.1
  454.2 5.1 gather_fusion
  461.8 5.1 gather_fusion.2
  470.8 78.0 %all-reduce.6.cloned.1.call-done = (bf16[16,4096]{1,0:T(8,128)(2,1)}, bf16[16,4096]{1,0:T(8,128)(2,1)}, bf16[16,4096]{1,0:T(8,128)(2,1)}) async-done(((bf16[16,4096]{1,0:T(8,128)(2,1)}, bf16[16,4096]{1,0:T(8,128)(2,1)}, bf16[16,4096]{1,0:T(8,128)(2,1)}), (bf16[16,4096]{1,0:T(8,128)(2,1)}, bf16[16,4096]{1,0:T(8,128)(2,1)}, bf16[16,4096]{1,0:T(8,128)(2,1)})) %all-reduce.6.cloned.1.call-update) | async-done | bytes 393232
  (213 shorter events, 61.9 us)
Async XLA Ops:
  6.5 226.0 %copy-start = (bf16[2,192,4096]{2,1,0:T(8,128)(2,1)S(1)}, bf16[2,192,4096]{2,1,0:T(8,128)(2,1)}, u32[]{:S(2)}) copy-start(bf16[2,192,4096]{2,1,0:T(8,128)(2,1)} %param.27) | copy-start | bytes 9437188
  14.8 3.5 copy-start.13
  14.9 3.3 copy-start.24
  16.6 6.1 %copy-start.19 = (f32[2,2,16]{2,1,0:T(2,128)}, f32[2,2,16]{2,1,0:T(2,128)S(1)}, u32[]{:S(2)}) copy-start(f32[2,2,16]{2,1,0:T(2,128)S(1)} %max.23) | copy-start | bytes 772
  18.3 4.5 copy-start.44
  20.2 3.5 copy-start.11
  20.2 3.5 copy-start.17
  20.5 3.2 copy-start.32
  20.5 3.2 copy-start.15
  20.5 3.9 copy-start.7
  20.5 3.9 copy-start.14
  24.4 9.6 %copy-start.8 = (bf16[3,2,4096]{2,1,0:T(2,128)(2,1)S(1)}, bf16[3,2,4096]{2,1,0:T(2,128)(2,1)}, u32[]{:S(2)}) copy-start(bf16[3,2,4096]{2,1,0:T(2,128)(2,1)} %param.15) | copy-start | bytes 147460
  86.0 3.1 copy-start.35
  89.1 11.7 %copy-start.42 = (s32[1,2,8]{2,1,0:T(2,128)S(1)}, s32[1,2,8]{2,1,0:T(2,128)}, u32[]{:S(2)}) copy-start(s32[1,2,8]{2,1,0:T(2,128)} %get-tuple-element.29) | copy-start | bytes 196
  89.1 64.5 %all-to-all-start.2 = ((bf16[32,8,4096]{2,1,0:T(8,128)(2,1)}), bf16[32,8,4096]{2,1,0:T(8,128)(2,1)}, u32[]{:S(2)}, u32[]{:S(2)}) async-start(bf16[32,8,4096]{2,1,0:T(8,128)(2,1)} %fusion.1), calls=%async_computation.2 | async-start | bytes 4194304 | tf_op jit(solution)/shard_map/all_to_all | solution.py:133
  150.4 3.1 copy-start.37
  153.6 11.7 %copy-start.41 = (s32[1,2,8]{2,1,0:T(2,128)S(1)}, s32[1,2,8]{2,1,0:T(2,128)}, u32[]{:S(2)}) copy-start(s32[1,2,8]{2,1,0:T(2,128)} %get-tuple-element.31) | copy-start | bytes 196
  153.6 62.4 %all-to-all-start = ((bf16[32,8,4096]{2,1,0:T(8,128)(2,1)}), bf16[32,8,4096]{2,1,0:T(8,128)(2,1)}, u32[]{:S(2)}, u32[]{:S(2)}) async-start(bf16[32,8,4096]{2,1,0:T(8,128)(2,1)} %fusion), calls=%async_computation | async-start | bytes 4194304 | tf_op jit(solution)/shard_map/all_to_all | solution.py:133
  215.9 61.5 %all-to-all-start.4 = ((bf16[32,8,4096]{2,1,0:T(8,128)(2,1)}), bf16[32,8,4096]{2,1,0:T(8,128)(2,1)}, u32[]{:S(2)}, u32[]{:S(2)}) async-start(bf16[32,8,4096]{2,1,0:T(8,128)(2,1)} %fusion.2), calls=%async_computation.4 | async-start | bytes 4194304 | tf_op jit(solution)/shard_map/all_to_all | solution.py:133
  227.1 4.3 copy-start.1
  277.4 56.5 %all-to-all-start.3 = ((bf16[32,8,4096]{2,1,0:T(8,128)(2,1)}), bf16[32,8,4096]{2,1,0:T(8,128)(2,1)}, u32[]{:S(2)}, u32[]{:S(2)}) async-start(bf16[32,8,4096]{2,1,0:T(8,128)(2,1)} %copy.129), calls=%async_computation.3 | async-start | bytes 4194304 | tf_op jit(solution)/shard_map/all_to_all | solution.py:137
  283.6 4.3 copy-start.2
  333.9 56.5 %all-to-all-start.1 = ((bf16[32,8,4096]{2,1,0:T(8,128)(2,1)}), bf16[32,8,4096]{2,1,0:T(8,128)(2,1)}, u32[]{:S(2)}, u32[]{:S(2)}) async-start(bf16[32,8,4096]{2,1,0:T(8,128)(2,1)} %copy.117), calls=%async_computation.1 | async-start | bytes 4194304 | tf_op jit(solution)/shard_map/all_to_all | solution.py:137
  340.2 4.2 copy-start.3
  355.4 41.3 %copy-start.43 = (s32[3,2,8]{2,1,0:T(2,128)S(1)}, s32[3,2,8]{2,1,0:T(2,128)}, u32[]{:S(2)}) copy-start(s32[3,2,8]{2,1,0:T(2,128)} %param.24) | copy-start | bytes 580
  355.4 91.0 %copy-start.30 = (s32[128]{0:T(128)S(1)}, s32[128]{0:T(128)}, u32[]{:S(2)}) copy-start(s32[128]{0:T(128)} %copy-done.29) | copy-start | bytes 1540
  355.4 91.0 %copy-start.36 = (s32[128]{0:T(128)S(1)}, s32[128]{0:T(128)}, u32[]{:S(2)}) copy-start(s32[128]{0:T(128)} %copy-done.35) | copy-start | bytes 1540
  355.4 91.0 %copy-start.38 = (s32[128]{0:T(128)S(1)}, s32[128]{0:T(128)}, u32[]{:S(2)}) copy-start(s32[128]{0:T(128)} %copy-done.37) | copy-start | bytes 1540
  355.4 91.1 %copy-start.40 = (s32[128]{0:T(128)S(1)}, s32[128]{0:T(128)}, u32[]{:S(2)}) copy-start(s32[128]{0:T(128)} %copy-done.39) | copy-start | bytes 1540
  390.5 71.3 %all-to-all-start.5 = ((bf16[32,8,4096]{2,1,0:T(8,128)(2,1)}), bf16[32,8,4096]{2,1,0:T(8,128)(2,1)}, u32[]{:S(2)}, u32[]{:S(2)}) async-start(bf16[32,8,4096]{2,1,0:T(8,128)(2,1)} %copy.141), calls=%async_computation.5 | async-start | bytes 4194304 | tf_op jit(solution)/shard_map/all_to_all | solution.py:137
  396.7 152.1 %all-reduce.6.cloned.1.call-start = ((), (), s32[]{:S(2)}) async-start(), calls=%async_computation.6 | async-start | bytes 786432
  466.8 82.0 %copy-start.10 = (f32[2,2,16,128]{3,2,1,0:T(8,128)S(1)}, f32[2,2,16,128]{3,2,1,0:T(8,128)}, u32[]{:S(2)}) copy-start(f32[2,2,16,128]{3,2,1,0:T(8,128)} %copy-done.9) | copy-start | bytes 98308
  (21 other events, 32.6 us)
Sparse Core Ops, SparseCore 0:
  469.5 79.2 all-reduce.5
where the time goes:
time: 559 us; the launch traced here: 557 us
  blocking collectives  189 us (34%)
  waiting for transfers between devices  183 us (33%)
  local copies, waits for them, and re-layouts  60.6 us (11%)
  starting transfers between devices  53.2 us (10%)
  matrix products  43.2 us (8%)
  between operations  14.9 us (3%)
  other arithmetic  13.7 us (2%)
    all_gather x3, blocking collectives, per_device(): group_rows = lax.all_gather(normed, 'exp', axis=0, tiled=True)  87.6 us
    unnamed x2, waiting for transfers between devices  78.1 us
    all_to_all x3, waiting for transfers between devices, per_device(): lax.all_to_all(partial_value, 'rep', split_axis=0, concat_axis=0, tiled=T...  70 us
    all_gather x3, blocking collectives, per_device(): lax.all_gather(expert_ids[step], 'exp', axis=0, tiled=True)  52 us
    all_gather x3, blocking collectives, per_device(): lax.all_gather(gate_scores[step], 'exp', axis=0, tiled=True)  49.1 us
    all_to_all x3, waiting for transfers between devices, per_device(): lax.all_to_all(outbound, 'rep', split_axis=0, concat_axis=0, tiled=True)  35 us
    all_to_all x3, starting transfers between devices, per_device(): lax.all_to_all(outbound, 'rep', split_axis=0, concat_axis=0, tiled=True)  34.4 us
    all_to_all x3, starting transfers between devices, per_device(): lax.all_to_all(partial_value, 'rep', split_axis=0, concat_axis=0, tiled=T...  18.7 us
  transfers between devices with their start and end apart: 7, of which 4 were waited for; matrix products, arithmetic and copies ran while one was open for 12% of the time, Pallas kernels for 0%

commit v1 on v0

v1 whole, which is shorter than its diff:
```python
import math

import numpy as np

import jax
import jax.numpy as jnp
from jax import lax
from jax.sharding import PartitionSpec as P

D = 4096
FF = 1536
HD = 128
QH = 32
KVH = 2
TOPK = 8
CAPE = 4
STEPS = 3
CACHE = 1024
N_EXP = 8
SEQ = 2
UNITS = FF // N_EXP
TOK = N_EXP * STEPS * SEQ
BLK = D // 4
THIRD = UNITS // 3

PARITY = [(e // 4 + e % 4) % 2 for e in range(N_EXP)]
GROUPS = [[e for e in range(N_EXP) if PARITY[e] == side] for side in range(2)]
NEAR = [4, 1, 3]
SAME = [0, 2, 5, 7]


def attend_rows(decode_query_rows, key_cache, value_cache, new_keys, new_values, cache_len, step):
    row_count = decode_query_rows.shape[0]
    group_size = QH // KVH
    scaling = 1.0 / math.sqrt(HD)
    query_heads = decode_query_rows.reshape(row_count, KVH, group_size, HD)
    cached_keys = key_cache.reshape(row_count, CACHE, KVH, HD)
    cached_values = value_cache.reshape(row_count, CACHE, KVH, HD)
    fresh_keys = new_keys[: step + 1].reshape(step + 1, row_count, KVH, HD)
    fresh_values = new_values[: step + 1].reshape(step + 1, row_count, KVH, HD)
    previous_scores = (
        jnp.einsum("sjgd,stjd->sjgt", query_heads, cached_keys, preferred_element_type=jnp.float32)
        * scaling
    )
    new_scores = (
        jnp.einsum("sjgd,tsjd->sjgt", query_heads, fresh_keys, preferred_element_type=jnp.float32)
        * scaling
    )
    position = lax.broadcasted_iota(jnp.int32, (row_count, 1, 1, CACHE), 3)
    previous_scores = jnp.where(position < cache_len[:, None, None, None], previous_scores, -1e30)
    row_max = jnp.maximum(
        jnp.max(previous_scores, axis=-1, keepdims=True),
        jnp.max(new_scores, axis=-1, keepdims=True),
    )
    old_expo = jnp.exp(previous_scores - row_max)
    new_expo = jnp.exp(new_scores - row_max)
    denominator = jnp.sum(old_expo, axis=-1, keepdims=True) + jnp.sum(
        new_expo, axis=-1, keepdims=True
    )
    old_probs = (old_expo / denominator).astype(jnp.bfloat16)
    new_probs = (new_expo / denominator).astype(jnp.bfloat16)
    blended = jnp.einsum(
        "sjgt,stjd->sjgd", old_probs, cached_values, preferred_element_type=jnp.float32
    )
    blended = blended + jnp.einsum(
        "sjgt,tsjd->sjgd", new_probs, fresh_values, preferred_element_type=jnp.float32
    )
    return blended.reshape(row_count, QH * HD)


def norm_rows(hidden, norm_gain):
    mean_square = jnp.mean(hidden * hidden, axis=-1, keepdims=True)
    return (hidden * lax.rsqrt(mean_square + 1e-06) * norm_gain.astype(jnp.float32)).astype(
        jnp.bfloat16
    )


def exchange(array, axis, groups=None):
    return lax.all_to_all(
        array, axis, split_axis=0, concat_axis=0, tiled=True, axis_index_groups=groups
    )


def swap(array, turn):
    if turn == 0:
        return array
    return lax.ppermute(array, "exp", [(e, e ^ turn) for e in range(N_EXP)])


def routing_tables(chosen, scores, side, groups):
    gate_values = scores.astype(jnp.float32)
    gate_values = gate_values / jnp.sum(gate_values, axis=-1, keepdims=True)
    token = np.arange(TOK)
    source, step, seq = token // (STEPS * SEQ), token // SEQ % STEPS, token % SEQ
    order = source * SEQ + seq
    earlier = (step[:, None] == step[None, :]) & (order[None, :] < order[:, None])
    experts = 2 * lax.broadcasted_iota(jnp.int32, (1, 1, groups), 2) + side
    hits = (chosen[:, :, None] == experts).astype(jnp.float32)
    named = jnp.sum(hits, axis=1)
    weights = jnp.sum(hits * gate_values[:, :, None], axis=1)
    rank = jnp.dot(jnp.asarray(earlier, jnp.float32), named, preferred_element_type=jnp.float32)
    places = np.arange(STEPS * CAPE)
    rank = jnp.where(named > 0, rank, -1.0)
    wanted = np.where(
        step[:, None] == places[None, :] // CAPE, places[None, :] % CAPE, -2
    ).astype(np.float32)
    table = (rank[:, :, None] == wanted[:, None, :]).astype(jnp.float32)
    combine = (table * weights[:, :, None]).reshape(TOK, groups * STEPS * CAPE)
    return table.astype(jnp.bfloat16).reshape(TOK, groups * STEPS * CAPE), combine


def per_device(
    residual,
    queries,
    key_cache,
    value_cache,
    new_keys,
    new_values,
    cache_len,
    norm_gain,
    expert_ids,
    gate_scores,
    gate_weight,
    up_weight,
    down_weight,
):
    groups = lax.axis_size("rep")
    rows = groups * STEPS * CAPE
    me = lax.axis_index("exp")
    side = (me // 4 + me % 4) % 2

    routing = jnp.concatenate([expert_ids, gate_scores], axis=-1).reshape(1, STEPS * SEQ, 2 * TOPK)
    routing = exchange(jnp.broadcast_to(routing, (N_EXP, STEPS * SEQ, 2 * TOPK)), "exp")
    routing = routing.reshape(TOK, 2 * TOPK)

    units = [
        lax.dynamic_index_in_dim(gate_weight, side, 0, keepdims=False),
        lax.dynamic_index_in_dim(up_weight, side, 0, keepdims=False),
    ]
    borrowed = []
    for turn, near in enumerate(NEAR):
        third = jnp.concatenate(
            [
                lax.dynamic_slice(weight, (1 - side, turn * THIRD, 0), (1, THIRD, D))
                for weight in (gate_weight, up_weight)
            ]
        )
        borrowed.append(swap(third, near))
    down_blocks = []
    for turn in range(N_EXP):
        target = me ^ turn
        block = lax.dynamic_slice(
            down_weight, ((target // 4 + target % 4) % 2, 0, target // 2 * BLK), (1, UNITS, BLK)
        )[0]
        down_blocks.append(swap(block, turn))

    hidden, normed = [], []
    for step in range(STEPS):
        attention = attend_rows(
            queries[step], key_cache, value_cache, new_keys, new_values, cache_len, step
        )
        hidden.append(residual[step].astype(jnp.float32) + attention)
        normed.append(norm_rows(hidden[-1], norm_gain))
    normed = jnp.stack(normed).reshape(STEPS * SEQ, 4, 1, BLK)
    normed = jnp.broadcast_to(normed, (STEPS * SEQ, 4, 2, BLK)).reshape(STEPS * SEQ, N_EXP, BLK)
    normed, borrowed, routing = lax.optimization_barrier((normed, borrowed, routing))
    tokens = exchange(normed.transpose(1, 0, 2), "exp").reshape(TOK, BLK)

    table, combine = routing_tables(routing[:, :TOPK], routing[:, TOPK:], side, groups)

    def to_wire(array):
        return (
            array.reshape(groups, STEPS * CAPE, 2, BLK // 2)
            .transpose(0, 2, 1, 3)
            .reshape(groups, 2 * STEPS * CAPE, BLK // 2)
        )

    def from_wire(array):
        return (
            array.reshape(groups, 2, STEPS * CAPE, BLK // 2).transpose(0, 2, 1, 3).reshape(rows, BLK)
        )

    outbound = lax.dot_general(
        table, tokens, (((0,), (0,)), ((), ())), preferred_element_type=jnp.float32
    ).astype(jnp.bfloat16)
    inbound = from_wire(exchange(to_wire(outbound), "rep"))
    inbound, down_blocks = lax.optimization_barrier((inbound, down_blocks))
    slotted = exchange(
        jnp.broadcast_to(inbound[None], (4, rows, BLK)).reshape(4, rows, BLK), "exp", GROUPS
    )

    def project(which):
        weight = jnp.concatenate([units[which]] + [third[which] for third in borrowed], axis=0)
        total = jnp.zeros((rows, 2 * UNITS), jnp.float32)
        for q in range(4):
            total = total + lax.dot_general(
                slotted[q],
                weight[:, q * BLK : (q + 1) * BLK],
                (((1,), (1,)), ((), ())),
                preferred_element_type=jnp.float32,
            )
        return total

    activation = (jax.nn.silu(project(0)) * project(1)).astype(jnp.bfloat16)
    partial_value = jnp.zeros((rows, BLK), jnp.float32)
    for turn in SAME:
        down = jnp.concatenate(
            [down_blocks[turn]]
            + [
                down_blocks[turn ^ near][i * THIRD : (i + 1) * THIRD]
                for i, near in enumerate(NEAR)
            ],
            axis=0,
        )
        partial_value = partial_value + jnp.dot(
            swap(activation, turn), down, preferred_element_type=jnp.float32
        )
    partial_value = partial_value.astype(jnp.bfloat16)
    returned = from_wire(exchange(to_wire(partial_value), "rep"))
    weighted = jnp.dot(
        combine,
        returned.astype(jnp.float32),
        precision=lax.Precision.HIGHEST,
        preferred_element_type=jnp.float32,
    ).astype(jnp.bfloat16)
    expert_sum = exchange(weighted.reshape(N_EXP, STEPS * SEQ, BLK), "exp").astype(jnp.float32)
    expert_sum = expert_sum.reshape(4, 2, STEPS * SEQ, BLK).sum(axis=1)
    expert_sum = expert_sum.transpose(1, 0, 2).reshape(STEPS, SEQ, D)
    return (jnp.stack(hidden) + expert_sum).astype(jnp.bfloat16)


def solution(mesh):
    in_specs = (
        P(None, ("rep", "exp"), None),
        P(None, ("rep", "exp"), None),
        P(("rep", "exp"), None, None),
        P(("rep", "exp"), None, None),
        P(None, ("rep", "exp"), None),
        P(None, ("rep", "exp"), None),
        P(("rep", "exp")),
        P(),
        P(None, ("rep", "exp"), None),
        P(None, ("rep", "exp"), None),
        P("rep", "exp", None),
        P("rep", "exp", None),
        P("rep", "exp", None),
    )
    out_specs = P(None, ("rep", "exp"), None)
    return jax.shard_map(
        per_device, mesh=mesh, in_specs=in_specs, out_specs=out_specs, check_vma=False
    )
```

time: 559 us -> 255 us (0.46)
  blocking collectives: 189 us -> 11.7 us
  waiting for transfers between devices: 183 us -> 108 us
  local copies, waits for them, and re-layouts: 60.6 us -> 36.1 us
  matrix products: 43.2 us -> 24.9 us
  between operations: 14.9 us -> 1.29 us
    all_gather x9 -> x0, blocking collectives: 189 us -> none  [the longest x3 87.6 us: per_device(): group_rows = lax.all_gather(normed, 'exp', axis=0, tiled=True)]
    unnamed x2 -> x0, waiting for transfers between devices: 78.1 us -> none
    ppermute x0 -> x13, starting transfers between devices: none -> 21.9 us  [swap(): return lax.ppermute(array, 'exp', [(e, e ^ turn) for e in range(N_EXP)])]
    all_to_all x6 -> x5, starting transfers between devices: 53.1 us -> 34.4 us  [exchange(): lax.all_to_all(array, axis, split_axis=0, concat_axis=0, tiled=True, axis...]
    gather x3 -> x0, local copies, waits for them, and re-layouts: 15.2 us -> none  [per_device(): jnp.take(returned, target.reshape(-1), axis=0).reshape(group_count, TOPK, D)]
    ppermute x0 -> x13, waiting for transfers between devices: none -> 15.1 us  [swap(): return lax.ppermute(array, 'exp', [(e, e ^ turn) for e in range(N_EXP)])]
    concatenate x0 -> x6, other arithmetic: none -> 12.8 us  [the longest x2 9.51 us: project(): jnp.concatenate([units[which]] + [third[which] for third in borrowed], ax...]
    all_to_all x6 -> x5, waiting for transfers between devices: 105 us -> 92.5 us  [exchange(): lax.all_to_all(array, axis, split_axis=0, concat_axis=0, tiled=True, axis...]
  transfers between devices with their start and end apart: 7 -> 18, of which waited for: 4 -> 7; matrix products, arithmetic and copies ran while one was open for 12% -> 20% of each run, Pallas kernels for 0% -> 0%
where the time goes in v1:
time: 255 us; the launch traced here: 254 us
  waiting for transfers between devices  108 us (42%)
  starting transfers between devices  56.3 us (22%)
  local copies, waits for them, and re-layouts  36.1 us (14%)
  matrix products  24.9 us (10%)
  other arithmetic  16 us (6%)
  blocking collectives  11.7 us (5%)
    all_to_all x5, waiting for transfers between devices, exchange(): lax.all_to_all(array, axis, split_axis=0, concat_axis=0, tiled=True, axis...  92.5 us
    all_to_all x5, starting transfers between devices, exchange(): lax.all_to_all(array, axis, split_axis=0, concat_axis=0, tiled=True, axis...  34.4 us
    ppermute x13, starting transfers between devices, swap(): return lax.ppermute(array, 'exp', [(e, e ^ turn) for e in range(N_EXP)])  21.9 us
    ppermute x13, waiting for transfers between devices, swap(): return lax.ppermute(array, 'exp', [(e, e ^ turn) for e in range(N_EXP)])  15.1 us
    dot_general x8, matrix products, project(): lax.dot_general(slotted[q], weight[:, q * BLK:(q + 1) * BLK], (((1,), (1,...  14.3 us
    all_to_all x1, blocking collectives, exchange(): lax.all_to_all(array, axis, split_axis=0, concat_axis=0, tiled=True, axis...  11.7 us
    concatenate x2, other arithmetic, project(): jnp.concatenate([units[which]] + [third[which] for third in borrowed], ax...  9.51 us
    slice x4, local copies, waits for them, and re-layouts, per_device(): down_blocks[turn ^ near][i * THIRD:(i + 1) * THIRD]  6.49 us
  transfers between devices with their start and end apart: 18, of which 7 were waited for; matrix products, arithmetic and copies ran while one was open for 20% of the time, Pallas kernels for 0%

profile of v1, /device:TPU:4, one launch (start us, length us, event | category | flops | bytes accessed | tf_op | source)
XLA Modules:
  0.0 253.8 jit_solution(3662006960131098422)
XLA Ops:
  0.0 2.1 constant_dynamic-slice_fusion
  3.2 3.0 %collective-permute-start.2 = (bf16[2,64,4096]{2,1,0:T(8,128)(2,1)}, bf16[2,64,4096]{2,1,0:T(8,128)(2,1)}, u32[]{:S(2)}, u32[]{:S(2)}) collective-permute-start(bf16[2,64,4096]{2,1,0:T(8,128)(2,1)} %pad_maximum_fusion.4), channel_id=1, source_target_pairs={{0,3},{1,2},{2,1},{3,0},{4,7},{5,6},{6,5},{7,4},{8,11},{9,10},{10,... | collective-permute-start | bytes 3145736 | tf_op jit(solution)/shard_map/ppermute | solution.py:87
  10.5 3.4 %all-to-all-start = ((s32[8,6,16]{2,1,0:T(8,128)}), s32[8,6,16]{2,1,0:T(8,128)S(1)}, u32[]{:S(2)}, u32[]{:S(2)}) async-start(s32[8,6,16]{2,1,0:T(8,128)} %broadcast_in_dim.38), calls=%async_computation | async-start | bytes 65536 | tf_op jit(solution)/shard_map/all_to_all | solution.py:79
  14.4 3.6 %dynamic-slice_bitcast_fusion.2 = (bf16[192,1024]{1,0:T(8,128)(2,1)}, bf16[192,1024]{1,0:T(8,128)(2,1)}, bf16[192,1024]{1,0:T(8,128)(2,1)}, bf16[192,1024]{1,0:T...) fusion(bf16[2,192,4096]{2,1,0:T(8,128)(2,1)} %param.27, ...), kind=kLoop, calls=%fused_computation.96 | loop fusion | bytes 6291520 | tf_op jit(solution)/shard_map/squeeze | solution.py:152
  18.0 1.8 collective-permute-start.3
  19.9 2.4 collective-permute-start.4
  27.8 2.1 dynamic-slice_bitcast_fusion
  30.0 4.7 %all-to-all-done = s32[8,6,16]{2,1,0:T(8,128)S(1)} async-done(((s32[8,6,16]{2,1,0:T(8,128)}), s32[8,6,16]{2,1,0:T(8,128)S(1)}, u32[]{:S(2)}, u32[]{:S(2)}) %all-to-all-start) | async-done | bytes 3104 | tf_op jit(solution)/shard_map/all_to_all | solution.py:79
  34.8 2.8 %collective-permute-start.5 = (bf16[192,1024]{1,0:T(8,128)(2,1)}, bf16[192,1024]{1,0:T(8,128)(2,1)}, u32[]{:S(2)}, u32[]{:S(2)}) collective-permute-start(bf16[192,1024]{1,0:T(8,128)(2,1)} %get-tuple-element.44), channel_id=1, source_target_pairs={{0,3},{1,2},{2,1},{3,0},{4,7},{5,6},{6,5},{7,4},{8,11},{9,10},{10,... | collective-permute-start | bytes 1179656 | tf_op jit(solution)/shard_map/ppermute | solution.py:87
  39.6 4.2 %all-to-all-start.1 = ((bf16[8,6,1024]{2,1,0:T(8,128)(2,1)}), bf16[8,6,1024]{2,1,0:T(8,128)(2,1)S(1)}, u32[]{:S(2)}, u32[]{:S(2)}) async-start(bf16[8,6,1024]{2,1,0:T(8,128)(2,1)} %bitcast.3), calls=%async_computation.1 | async-start | bytes 262144 | tf_op jit(solution)/shard_map/all_to_all | solution.py:79
  44.7 14.4 %all-to-all-done.1 = bf16[8,6,1024]{2,1,0:T(8,128)(2,1)S(1)} async-done(((bf16[8,6,1024]{2,1,0:T(8,128)(2,1)}), bf16[8,6,1024]{2,1,0:T(8,128)(2,1)S(1)}, u32[]{:S(2)}, u32[]{:S(2)}) %all-to-all-start.1) | async-done | bytes 98336 | tf_op jit(solution)/shard_map/all_to_all | solution.py:79
  60.4 3.3 %reshape.292 = bf16[32,12,2,512]{3,2,1,0:T(2,128)(2,1)} reshape(bf16[384,1024]{1,0:T(8,128)(2,1)} %convolution_convert_fusion) | data formatting | bytes 1572864 | tf_op jit(solution)/shard_map/reshape | solution.py:173
  66.4 11.6 %all-to-all-start.2 = ((bf16[32,24,512]{2,1,0:T(8,128)(2,1)}), bf16[32,24,512]{2,1,0:T(8,128)(2,1)}, u32[]{:S(2)}, u32[]{:S(2)}) async-start(bf16[32,24,512]{2,1,0:T(8,128)(2,1)} %copy.115), calls=%async_computation.2 | async-start | bytes 1572864 | tf_op jit(solution)/shard_map/all_to_all | solution.py:79
  78.0 2.3 slice_bitcast_fusion.17
  80.4 2.3 collective-permute-start.8
  84.3 2.3 slice_bitcast_fusion.16
  86.6 14.8 %all-to-all-done.2 = bf16[32,24,512]{2,1,0:T(8,128)(2,1)} async-done(((bf16[32,24,512]{2,1,0:T(8,128)(2,1)}), bf16[32,24,512]{2,1,0:T(8,128)(2,1)}, u32[]{:S(2)}, u32[]{:S(2)}) %all-to-all-start.2) | async-done | bytes 786464 | tf_op jit(solution)/shard_map/all_to_all | solution.py:79
  103.8 5.8 %collective-permute-done.9 = bf16[192,1024]{1,0:T(8,128)(2,1)} collective-permute-done((bf16[192,1024]{1,0:T(8,128)(2,1)S(1)}, bf16[192,1024]{1,0:T(8,128)(2,1)}, u32[]{:S(2)}, u32[]{:S(2)}) %collective-permute-start.9) | collective-permute-done | bytes 393248 | tf_op jit(solution)/shard_map/ppermute | solution.py:87
  109.6 2.1 broadcast_in_dim.41
  111.7 4.7 %all-to-all-start.3 = ((bf16[4,384,1024]{2,1,0:T(8,128)(2,1)}), bf16[4,384,1024]{2,1,0:T(8,128)(2,1)}, u32[]{:S(2)}, u32[]{:S(2)}) async-start(bf16[4,384,1024]{2,1,0:T(8,128)(2,1)} %broadcast_in_dim.41), calls=%async_computation.3 | async-start | bytes 6291456 | tf_op jit(solution)/shard_map/all_to_all | solution.py:79
  117.6 4.7 %pad_maximum_fusion = bf16[384,4096]{1,0:T(8,128)(2,1)} fusion(bf16[64,4096]{1,0:T(8,128)(2,1)S(1)} %get-tuple-element.59, bf16[64,4096]{1,0:T(8,128)(2,1)} %get-tuple-element.57, bf16[64,4096]{1,0:T(8,128)(2,1)} %get-tuple-element.55, bf16[192,4096]{1,0:T(8,128)(2,1)S(1)} %get-tuple-element.107), kind=kLoop, calls=%fused_computation | loop fusion | flops 12582912 | bytes 6291456 | tf_op jit(solution)/shard_map/concatenate | solution.py:193
  122.3 4.9 %pad_maximum_fusion.1 = bf16[384,4096]{1,0:T(8,128)(2,1)} fusion(bf16[64,4096]{1,0:T(8,128)(2,1)S(1)} %get-tuple-element.60, bf16[64,4096]{1,0:T(8,128)(2,1)S(1)} %copy-done.5, bf16[64,4096]{1,0:T(8,128)(2,1)S(1)} %copy-done.4, bf16[192,4096]{1,0:T(8,128)(2,1)S(1)} %get-tuple-element.106), kind=kLoop, calls=%fused_computation.1 | loop fusion | flops 12582912 | bytes 6291456 | tf_op jit(solution)/shard_map/concatenate | solution.py:193
  127.2 1.9 fusion.94
  132.6 35.4 %all-to-all-done.3 = bf16[4,384,1024]{2,1,0:T(8,128)(2,1)} async-done(((bf16[4,384,1024]{2,1,0:T(8,128)(2,1)}), bf16[4,384,1024]{2,1,0:T(8,128)(2,1)}, u32[]{:S(2)}, u32[]{:S(2)}) %all-to-all-start.3) | async-done | bytes 3145760 | tf_op jit(solution)/shard_map/all_to_all | solution.py:79
  167.9 2.0 fusion.27
  171.7 1.9 convolution_add_fusion.4
  182.4 2.8 %collective-permute-start.10 = (bf16[384,384]{1,0:T(8,128)(2,1)S(1)}, bf16[384,384]{1,0:T(8,128)(2,1)S(1)}, u32[]{:S(2)}, u32[]{:S(2)}) collective-permute-start(bf16[384,384]{1,0:T(8,128)(2,1)S(1)} %fusion.1), channel_id=1, source_target_pairs={{0,2},{1,3},{2,0},{3,1},{4,6},{5,7},{6,4},{7,5},{8,10},{9,11},{10,... | collective-permute-start | bytes 884744 | tf_op jit(solution)/shard_map/ppermute | solution.py:87
  186.9 1.9 collective-permute-start.12
  189.4 9.3 %collective-permute-done.10 = bf16[384,384]{1,0:T(8,128)(2,1)S(1)} collective-permute-done((bf16[384,384]{1,0:T(8,128)(2,1)S(1)}, bf16[384,384]{1,0:T(8,128)(2,1)S(1)}, u32[]{:S(2)}, u32[]{:S(2)}) %collective-permute-start.10) | collective-permute-done | bytes 294944 | tf_op jit(solution)/shard_map/ppermute | solution.py:87
  205.6 10.5 %all-to-all-start.4 = ((bf16[32,24,512]{2,1,0:T(8,128)(2,1)}), bf16[32,24,512]{2,1,0:T(8,128)(2,1)S(1)}, u32[]{:S(2)}, u32[]{:S(2)}) async-start(bf16[32,24,512]{2,1,0:T(8,128)(2,1)} %copy.119), calls=%async_computation.4 | async-start | bytes 1572864 | tf_op jit(solution)/shard_map/all_to_all | solution.py:79
  216.2 23.2 %all-to-all-done.4 = bf16[32,24,512]{2,1,0:T(8,128)(2,1)S(1)} async-done(((bf16[32,24,512]{2,1,0:T(8,128)(2,1)}), bf16[32,24,512]{2,1,0:T(8,128)(2,1)S(1)}, u32[]{:S(2)}, u32[]{:S(2)}) %all-to-all-start.4) | async-done | bytes 786464 | tf_op jit(solution)/shard_map/all_to_all | solution.py:79
  241.2 11.7 %all_to_all.30 = bf16[8,6,1024]{2,1,0:T(8,128)(2,1)S(1)} all-to-all(bf16[8,6,1024]{2,1,0:T(8,128)(2,1)S(1)} %reshape.300), channel_id=1, replica_groups=mesh['rep'=32,'exp'=8] {'exp'}, dimensions={0} | all-to-all | bytes 196608 | tf_op jit(solution)/shard_map/all_to_all | solution.py:79
  (183 shorter events, 48.9 us)
Async XLA Ops:
  0.0 22.6 %copy-start = (bf16[2,1024,256]{2,1,0:T(8,128)(2,1)S(1)}, bf16[2,1024,256]{2,1,0:T(8,128)(2,1)}, u32[]{:S(2)}) copy-start(bf16[2,1024,256]{2,1,0:T(8,128)(2,1)} %param.17) | copy-start | bytes 3145732
  3.2 31.5 %collective-permute-start.2 = (bf16[2,64,4096]{2,1,0:T(8,128)(2,1)}, bf16[2,64,4096]{2,1,0:T(8,128)(2,1)}, u32[]{:S(2)}, u32[]{:S(2)}) collective-permute-start(bf16[2,64,4096]{2,1,0:T(8,128)(2,1)} %pad_maximum_fusion.4), channel_id=1, source_target_pairs={{0,3},{1,2},{2,1},{3,0},{4,7},{5,6},{6,5},{7,4},{8,11},{9,10},{10,... | collective-permute-start | bytes 3145736 | tf_op jit(solution)/shard_map/ppermute | solution.py:87
  7.3 30.3 %collective-permute-start.1 = (bf16[2,64,4096]{2,1,0:T(8,128)(2,1)}, bf16[2,64,4096]{2,1,0:T(8,128)(2,1)}, u32[]{:S(2)}, u32[]{:S(2)}) collective-permute-start(bf16[2,64,4096]{2,1,0:T(8,128)(2,1)} %pad_maximum_fusion.3), channel_id=1, source_target_pairs={{0,1},{1,0},{2,3},{3,2},{4,5},{5,4},{6,7},{7,6},{8,9},{9,8},{10,11... | collective-permute-start | bytes 3145736 | tf_op jit(solution)/shard_map/ppermute | solution.py:87
  8.6 30.2 %collective-permute-start = (bf16[2,64,4096]{2,1,0:T(8,128)(2,1)}, bf16[2,64,4096]{2,1,0:T(8,128)(2,1)}, u32[]{:S(2)}, u32[]{:S(2)}) collective-permute-start(bf16[2,64,4096]{2,1,0:T(8,128)(2,1)} %pad_maximum_fusion.2), channel_id=1, source_target_pairs={{0,4},{1,5},{2,6},{3,7},{4,0},{5,1},{6,2},{7,3},{8,12},{9,13},{10,... | collective-permute-start | bytes 3145736 | tf_op jit(solution)/shard_map/ppermute | solution.py:87
  10.5 24.3 %all-to-all-start = ((s32[8,6,16]{2,1,0:T(8,128)}), s32[8,6,16]{2,1,0:T(8,128)S(1)}, u32[]{:S(2)}, u32[]{:S(2)}) async-start(s32[8,6,16]{2,1,0:T(8,128)} %broadcast_in_dim.38), calls=%async_computation | async-start | bytes 65536 | tf_op jit(solution)/shard_map/all_to_all | solution.py:79
  18.0 62.3 %collective-permute-start.3 = (bf16[192,1024]{1,0:T(8,128)(2,1)}, bf16[192,1024]{1,0:T(8,128)(2,1)}, u32[]{:S(2)}, u32[]{:S(2)}) collective-permute-start(bf16[192,1024]{1,0:T(8,128)(2,1)} %get-tuple-element.46), channel_id=1, source_target_pairs={{0,1},{1,0},{2,3},{3,2},{4,5},{5,4},{6,7},{7,6},{8,9},{9,8},{10,11... | collective-permute-start | bytes 1179656 | tf_op jit(solution)/shard_map/ppermute | solution.py:87
  19.9 62.9 %collective-permute-start.4 = (bf16[192,1024]{1,0:T(8,128)(2,1)}, bf16[192,1024]{1,0:T(8,128)(2,1)}, u32[]{:S(2)}, u32[]{:S(2)}) collective-permute-start(bf16[192,1024]{1,0:T(8,128)(2,1)} %get-tuple-element.45), channel_id=1, source_target_pairs={{0,2},{1,3},{2,0},{3,1},{4,6},{5,7},{6,4},{7,5},{8,10},{9,11},{10,... | collective-permute-start | bytes 1179656 | tf_op jit(solution)/shard_map/ppermute | solution.py:87
  27.8 16.7 %copy-start.24 = (bf16[48,48]{1,0:T(8,128)(2,1)S(1)}, bf16[48,48]{1,0:T(8,128)(2,1)}, u32[]{:S(2)}) copy-start(bf16[48,48]{1,0:T(8,128)(2,1)} %constant.382) | copy-start | bytes 13828
  27.8 16.8 %copy-start.20 = (f32[48,12]{0,1:T(8,128)S(1)}, f32[48,12]{0,1:T(8,128)}, u32[]{:S(2)}) copy-start(f32[48,12]{0,1:T(8,128)} %constant.275) | copy-start | bytes 6916
  34.8 69.0 %collective-permute-start.5 = (bf16[192,1024]{1,0:T(8,128)(2,1)}, bf16[192,1024]{1,0:T(8,128)(2,1)}, u32[]{:S(2)}, u32[]{:S(2)}) collective-permute-start(bf16[192,1024]{1,0:T(8,128)(2,1)} %get-tuple-element.44), channel_id=1, source_target_pairs={{0,3},{1,2},{2,1},{3,0},{4,7},{5,6},{6,5},{7,4},{8,11},{9,10},{10,... | collective-permute-start | bytes 1179656 | tf_op jit(solution)/shard_map/ppermute | solution.py:87
  37.6 66.2 %collective-permute-start.6 = (bf16[192,1024]{1,0:T(8,128)(2,1)}, bf16[192,1024]{1,0:T(8,128)(2,1)}, u32[]{:S(2)}, u32[]{:S(2)}) collective-permute-start(bf16[192,1024]{1,0:T(8,128)(2,1)} %get-tuple-element.43), channel_id=1, source_target_pairs={{0,4},{1,5},{2,6},{3,7},{4,0},{5,1},{6,2},{7,3},{8,12},{9,13},{10,... | collective-permute-start | bytes 1179656 | tf_op jit(solution)/shard_map/ppermute | solution.py:87
  38.8 65.0 %collective-permute-start.7 = (bf16[192,1024]{1,0:T(8,128)(2,1)}, bf16[192,1024]{1,0:T(8,128)(2,1)}, u32[]{:S(2)}, u32[]{:S(2)}) collective-permute-start(bf16[192,1024]{1,0:T(8,128)(2,1)} %get-tuple-element.42), channel_id=1, source_target_pairs={{0,5},{1,4},{2,7},{3,6},{4,1},{5,0},{6,3},{7,2},{8,13},{9,12},{10,... | collective-permute-start | bytes 1179656 | tf_op jit(solution)/shard_map/ppermute | solution.py:87
  39.6 19.5 %all-to-all-start.1 = ((bf16[8,6,1024]{2,1,0:T(8,128)(2,1)}), bf16[8,6,1024]{2,1,0:T(8,128)(2,1)S(1)}, u32[]{:S(2)}, u32[]{:S(2)}) async-start(bf16[8,6,1024]{2,1,0:T(8,128)(2,1)} %bitcast.3), calls=%async_computation.1 | async-start | bytes 262144 | tf_op jit(solution)/shard_map/all_to_all | solution.py:79
  63.6 19.1 %copy-start.7 = (bf16[192,1024]{1,0:T(8,128)(2,1)S(1)}, bf16[192,1024]{1,0:T(8,128)(2,1)}, u32[]{:S(2)}) copy-start(bf16[192,1024]{1,0:T(8,128)(2,1)} %get-tuple-element.41) | copy-start | bytes 1179652
  66.4 35.0 %all-to-all-start.2 = ((bf16[32,24,512]{2,1,0:T(8,128)(2,1)}), bf16[32,24,512]{2,1,0:T(8,128)(2,1)}, u32[]{:S(2)}, u32[]{:S(2)}) async-start(bf16[32,24,512]{2,1,0:T(8,128)(2,1)} %copy.115), calls=%async_computation.2 | async-start | bytes 1572864 | tf_op jit(solution)/shard_map/all_to_all | solution.py:79
  80.4 23.4 %collective-permute-start.8 = (bf16[192,1024]{1,0:T(8,128)(2,1)}, bf16[192,1024]{1,0:T(8,128)(2,1)}, u32[]{:S(2)}, u32[]{:S(2)}) collective-permute-start(bf16[192,1024]{1,0:T(8,128)(2,1)} %get-tuple-element.48), channel_id=1, source_target_pairs={{0,6},{1,7},{2,4},{3,5},{4,2},{5,3},{6,0},{7,1},{8,14},{9,15},{10,... | collective-permute-start | bytes 1179656 | tf_op jit(solution)/shard_map/ppermute | solution.py:87
  82.7 26.9 %collective-permute-start.9 = (bf16[192,1024]{1,0:T(8,128)(2,1)S(1)}, bf16[192,1024]{1,0:T(8,128)(2,1)}, u32[]{:S(2)}, u32[]{:S(2)}) collective-permute-start(bf16[192,1024]{1,0:T(8,128)(2,1)S(1)} %copy-done.7), channel_id=1, source_target_pairs={{0,7},{1,6},{2,5},{3,4},{4,3},{5,2},{6,1},{7,0},{8,15},{9,14},{10,... | collective-permute-start | bytes 1179656 | tf_op jit(solution)/shard_map/ppermute | solution.py:87
  111.7 56.3 %all-to-all-start.3 = ((bf16[4,384,1024]{2,1,0:T(8,128)(2,1)}), bf16[4,384,1024]{2,1,0:T(8,128)(2,1)}, u32[]{:S(2)}, u32[]{:S(2)}) async-start(bf16[4,384,1024]{2,1,0:T(8,128)(2,1)} %broadcast_in_dim.41), calls=%async_computation.3 | async-start | bytes 6291456 | tf_op jit(solution)/shard_map/all_to_all | solution.py:79
  127.1 42.8 %copy-start.2 = (bf16[384,4096]{1,0:T(8,128)(2,1)S(1)}, bf16[384,4096]{1,0:T(8,128)(2,1)}, u32[]{:S(2)}) copy-start(bf16[384,4096]{1,0:T(8,128)(2,1)} %pad_maximum_fusion) | copy-start | bytes 9437188
  182.3 16.3 %copy-start.12 = (bf16[64,1024]{1,0:T(8,128)(2,1)S(1)}, bf16[64,1024]{1,0:T(8,128)(2,1)}, u32[]{:S(2)}) copy-start(bf16[64,1024]{1,0:T(8,128)(2,1)} %get-tuple-element.62) | copy-start | bytes 393220
  182.3 16.3 %copy-start.14 = (bf16[64,1024]{1,0:T(8,128)(2,1)S(1)}, bf16[64,1024]{1,0:T(8,128)(2,1)}, u32[]{:S(2)}) copy-start(bf16[64,1024]{1,0:T(8,128)(2,1)} %get-tuple-element.66) | copy-start | bytes 393220
  182.3 16.3 %copy-start.16 = (bf16[64,1024]{1,0:T(8,128)(2,1)S(1)}, bf16[64,1024]{1,0:T(8,128)(2,1)}, u32[]{:S(2)}) copy-start(bf16[64,1024]{1,0:T(8,128)(2,1)} %get-tuple-element.70) | copy-start | bytes 393220
  182.4 16.3 %collective-permute-start.10 = (bf16[384,384]{1,0:T(8,128)(2,1)S(1)}, bf16[384,384]{1,0:T(8,128)(2,1)S(1)}, u32[]{:S(2)}, u32[]{:S(2)}) collective-permute-start(bf16[384,384]{1,0:T(8,128)(2,1)S(1)} %fusion.1), channel_id=1, source_target_pairs={{0,2},{1,3},{2,0},{3,1},{4,6},{5,7},{6,4},{7,5},{8,10},{9,11},{10,... | collective-permute-start | bytes 884744 | tf_op jit(solution)/shard_map/ppermute | solution.py:87
  186.2 14.1 %collective-permute-start.11 = (bf16[384,384]{1,0:T(8,128)(2,1)S(1)}, bf16[384,384]{1,0:T(8,128)(2,1)S(1)}, u32[]{:S(2)}, u32[]{:S(2)}) collective-permute-start(bf16[384,384]{1,0:T(8,128)(2,1)S(1)} %fusion.1), channel_id=1, source_target_pairs={{0,5},{1,4},{2,7},{3,6},{4,1},{5,0},{6,3},{7,2},{8,13},{9,12},{10,... | collective-permute-start | bytes 884744 | tf_op jit(solution)/shard_map/ppermute | solution.py:87
  186.9 14.9 %collective-permute-start.12 = (bf16[384,384]{1,0:T(8,128)(2,1)S(1)}, bf16[384,384]{1,0:T(8,128)(2,1)S(1)}, u32[]{:S(2)}, u32[]{:S(2)}) collective-permute-start(bf16[384,384]{1,0:T(8,128)(2,1)S(1)} %fusion.1), channel_id=1, source_target_pairs={{0,7},{1,6},{2,5},{3,4},{4,3},{5,2},{6,1},{7,0},{8,15},{9,14},{10,... | collective-permute-start | bytes 884744 | tf_op jit(solution)/shard_map/ppermute | solution.py:87
  203.4 12.6 %copy-start.18 = (f32[48,32]{0,1:T(8,128)S(1)}, f32[48,32]{0,1:T(8,128)}, u32[]{:S(2)}) copy-start(f32[48,32]{0,1:T(8,128)} %get-tuple-element.34) | copy-start | bytes 18436
  203.4 12.6 %copy-start.21 = (f32[48,12]{0,1:T(8,128)S(1)}, f32[48,12]{0,1:T(8,128)}, u32[]{:S(2)}) copy-start(f32[48,12]{0,1:T(8,128)} %constant.275) | copy-start | bytes 6916
  205.6 33.8 %all-to-all-start.4 = ((bf16[32,24,512]{2,1,0:T(8,128)(2,1)}), bf16[32,24,512]{2,1,0:T(8,128)(2,1)S(1)}, u32[]{:S(2)}, u32[]{:S(2)}) async-start(bf16[32,24,512]{2,1,0:T(8,128)(2,1)} %copy.119), calls=%async_computation.4 | async-start | bytes 1572864 | tf_op jit(solution)/shard_map/all_to_all | solution.py:79
  216.2 36.9 %copy-start.9 = (f32[1,2,4096]{2,1,0:T(2,128)S(1)}, f32[1,2,4096]{2,1,0:T(2,128)}, u32[]{:S(2)}) copy-start(f32[1,2,4096]{2,1,0:T(2,128)} %get-tuple-element.36) | copy-start | bytes 98308
  216.2 36.9 %copy-start.10 = (f32[1,2,4096]{2,1,0:T(2,128)S(1)}, f32[1,2,4096]{2,1,0:T(2,128)}, u32[]{:S(2)}) copy-start(f32[1,2,4096]{2,1,0:T(2,128)} %get-tuple-element.74) | copy-start | bytes 98308
  216.2 36.9 %copy-start.11 = (f32[1,2,4096]{2,1,0:T(2,128)S(1)}, f32[1,2,4096]{2,1,0:T(2,128)}, u32[]{:S(2)}) copy-start(f32[1,2,4096]{2,1,0:T(2,128)} %get-tuple-element.76) | copy-start | bytes 98308
  239.4 14.4 %copy-start.1 = (bf16[2,1024,256]{2,1,0:T(8,128)(2,1)S(1)}, bf16[2,1024,256]{2,1,0:T(8,128)(2,1)}, u32[]{:S(2)}) copy-start(bf16[2,1024,256]{2,1,0:T(8,128)(2,1)} %param.17) | copy-start | bytes 3145732
  (19 other events, 133.0 us)

commit v2 on v0

v2 whole, which is shorter than its diff:
```python
import math

import numpy as np

import jax
import jax.numpy as jnp
from jax import lax
from jax.experimental import pallas as pl
from jax.experimental.pallas import tpu as pltpu
from jax.sharding import PartitionSpec as P

D = 4096
FF = 1536
HD = 128
QH = 32
KVH = 2
TOPK = 8
CAPE = 4
STEPS = 3
CACHE = 1024
N_EXP = 8
SEQ = 2
UNITS = FF // N_EXP
BLK = D // 4
HALF = BLK // 2
LOCAL = STEPS * SEQ
KEYS = N_EXP * 2 * LOCAL
PLACES = STEPS * CAPE
WIRE = 2 * PLACES


def attend_rows(decode_query_rows, key_cache, value_cache, new_keys, new_values, cache_len, step):
    row_count = decode_query_rows.shape[0]
    group_size = QH // KVH
    scaling = 1.0 / math.sqrt(HD)
    query_heads = decode_query_rows.reshape(row_count, KVH, group_size, HD)
    cached_keys = key_cache.reshape(row_count, CACHE, KVH, HD)
    cached_values = value_cache.reshape(row_count, CACHE, KVH, HD)
    fresh_keys = new_keys[: step + 1].reshape(step + 1, row_count, KVH, HD)
    fresh_values = new_values[: step + 1].reshape(step + 1, row_count, KVH, HD)
    previous_scores = (
        jnp.einsum("sjgd,stjd->sjgt", query_heads, cached_keys, preferred_element_type=jnp.float32)
        * scaling
    )
    new_scores = (
        jnp.einsum("sjgd,tsjd->sjgt", query_heads, fresh_keys, preferred_element_type=jnp.float32)
        * scaling
    )
    position = lax.broadcasted_iota(jnp.int32, (row_count, 1, 1, CACHE), 3)
    previous_scores = jnp.where(position < cache_len[:, None, None, None], previous_scores, -1e30)
    row_max = jnp.maximum(
        jnp.max(previous_scores, axis=-1, keepdims=True),
        jnp.max(new_scores, axis=-1, keepdims=True),
    )
    old_expo = jnp.exp(previous_scores - row_max)
    new_expo = jnp.exp(new_scores - row_max)
    denominator = jnp.sum(old_expo, axis=-1, keepdims=True) + jnp.sum(
        new_expo, axis=-1, keepdims=True
    )
    old_probs = (old_expo / denominator).astype(jnp.bfloat16)
    new_probs = (new_expo / denominator).astype(jnp.bfloat16)
    blended = jnp.einsum(
        "sjgt,stjd->sjgd", old_probs, cached_values, preferred_element_type=jnp.float32
    )
    blended = blended + jnp.einsum(
        "sjgt,tsjd->sjgd", new_probs, fresh_values, preferred_element_type=jnp.float32
    )
    return blended.reshape(row_count, QH * HD)


def norm_rows(hidden, norm_gain):
    mean_square = jnp.mean(hidden * hidden, axis=-1, keepdims=True)
    return (hidden * lax.rsqrt(mean_square + 1e-06) * norm_gain.astype(jnp.float32)).astype(
        jnp.bfloat16
    )


def exchange(array, axis):
    return lax.all_to_all(array, axis, split_axis=0, concat_axis=0, tiled=True)


def shift(array, step):
    pairs = [(e, e // 4 * 4 + (e + step) % 4) for e in range(N_EXP)]
    return lax.ppermute(array, "exp", pairs)


def across(array):
    return lax.ppermute(array, "exp", [(e, e ^ 4) for e in range(N_EXP)])


def ring(block):
    half = block.shape[0] // 2
    below, above = shift(block, 1), shift(block, -1)
    return block, below, above, shift(below[:half], 1), shift(above[half:], -1)


def routing_tables(chosen, scores, side, groups):
    gate_values = scores.astype(jnp.float32)
    gate_values = gate_values / jnp.sum(gate_values, axis=-1, keepdims=True)
    key = np.arange(KEYS)
    source, half, step, seq = (
        key // (2 * LOCAL),
        key // LOCAL % 2,
        key % LOCAL // SEQ,
        key % SEQ,
    )
    order = source * SEQ + seq
    earlier = (
        (step[:, None] == step[None, :])
        & (half[:, None] == half[None, :])
        & (order[None, :] < order[:, None])
    )
    experts = 2 * lax.broadcasted_iota(jnp.int32, (1, 1, groups), 2) + side
    hits = (chosen[:, :, None] == experts).astype(jnp.float32)
    named = jnp.sum(hits, axis=1)
    weights = jnp.sum(hits * gate_values[:, :, None], axis=1)
    rank = jnp.dot(jnp.asarray(earlier, jnp.float32), named, preferred_element_type=jnp.float32)
    rank = jnp.where(named > 0, rank, -1.0)
    place = np.arange(WIRE)
    wanted = np.where(
        (half[:, None] == place[None, :] // PLACES)
        & (step[:, None] == place[None, :] % PLACES // CAPE),
        place[None, :] % CAPE,
        -2,
    ).astype(np.float32)
    table = (rank[:, :, None] == wanted[:, None, :]).astype(jnp.float32)
    combine = (table * weights[:, :, None]).reshape(KEYS, groups * WIRE)
    return table.astype(jnp.bfloat16).reshape(KEYS, groups * WIRE), combine


def contract_last(left, right):
    return lax.dot_general(
        left, right, (((1,), (1,)), ((), ())), preferred_element_type=jnp.float32
    )


def expand_kernel(
    where,
    own_rows,
    below_rows,
    above_rows,
    far_low,
    far_high,
    own_gate,
    own_up,
    lent_gate,
    lent_up,
    out,
    gate_total,
    up_total,
):
    turn = pl.program_id(0)
    gate_block = jnp.concatenate([own_gate[0], lent_gate[...]], axis=0)
    up_block = jnp.concatenate([own_up[0], lent_up[...]], axis=0)

    @pl.when(turn == 0)
    def _():
        gate_total[...] = contract_last(own_rows[...], gate_block)
        up_total[...] = contract_last(own_rows[...], up_block)

    @pl.when(turn == 1)
    def _():
        gate_total[...] += contract_last(below_rows[...], gate_block)
        up_total[...] += contract_last(below_rows[...], up_block)

    @pl.when(turn == 2)
    def _():
        gate_total[...] += contract_last(above_rows[...], gate_block)
        up_total[...] += contract_last(above_rows[...], up_block)

    @pl.when(turn == 3)
    def _():
        half = far_low.shape[0]
        for start, rows in ((0, far_low), (half, far_high)):
            span = pl.ds(start, half)
            gate = gate_total[span, :] + contract_last(rows[...], gate_block)
            up = up_total[span, :] + contract_last(rows[...], up_block)
            out[span, :] = (gate / (1.0 + jnp.exp(-gate)) * up).astype(jnp.bfloat16)


def expand(where, rows, gate_weight, up_weight, lent_gate, lent_up):
    count = rows[0].shape[0]

    def column(turn, where):
        return (where[1] + jnp.where(turn == 1, 3, jnp.where(turn == 2, 1, turn - turn // 3))) % 4

    def whole(shape):
        return pl.BlockSpec(shape, lambda turn, where: (0, 0))

    own = pl.BlockSpec((1, UNITS, BLK), lambda turn, where: (where[0], 0, column(turn, where)))
    lent = pl.BlockSpec((UNITS, BLK), lambda turn, where: (0, column(turn, where)))
    return pl.pallas_call(
        expand_kernel,
        out_shape=jax.ShapeDtypeStruct((count, 2 * UNITS), jnp.bfloat16),
        grid_spec=pltpu.PrefetchScalarGridSpec(
            num_scalar_prefetch=1,
            grid=(4,),
            in_specs=[whole(array.shape) for array in rows] + [own, own, lent, lent],
            out_specs=whole((count, 2 * UNITS)),
            scratch_shapes=[
                pltpu.VMEM((count, 2 * UNITS), jnp.float32),
                pltpu.VMEM((count, 2 * UNITS), jnp.float32),
            ],
        ),
        compiler_params=pltpu.CompilerParams(
            dimension_semantics=("arbitrary",), vmem_limit_bytes=32 << 20
        ),
        cost_estimate=pl.CostEstimate(
            flops=8 * count * UNITS * D,
            bytes_accessed=2 * count * D + 8 * UNITS * D + 4 * count * UNITS,
            transcendentals=2 * count * UNITS,
        ),
        name="expand",
    )(where, *rows, gate_weight, up_weight, lent_gate, lent_up)


def contract_kernel(own, below, above, far_low, far_high, w_own, w_below, w_above, w_far, out):
    half = far_low.shape[0]
    for start, far in ((0, far_low), (half, far_high)):
        span = pl.ds(start, half)
        total = jnp.dot(own[span, :], w_own[...], preferred_element_type=jnp.float32)
        total += jnp.dot(below[span, :], w_below[...], preferred_element_type=jnp.float32)
        total += jnp.dot(above[span, :], w_above[...], preferred_element_type=jnp.float32)
        total += jnp.dot(far[...], w_far[...], preferred_element_type=jnp.float32)
        out[span, :] = total.astype(jnp.bfloat16)


def contract(acts, weights):
    count = acts[0].shape[0]
    return pl.pallas_call(
        contract_kernel,
        out_shape=jax.ShapeDtypeStruct((count, BLK), jnp.bfloat16),
        compiler_params=pltpu.CompilerParams(vmem_limit_bytes=32 << 20),
        cost_estimate=pl.CostEstimate(
            flops=2 * count * FF * BLK,
            bytes_accessed=2 * (count * FF + FF * BLK + count * BLK),
            transcendentals=0,
        ),
        name="contract",
    )(*acts, *weights)


def per_device(
    residual,
    queries,
    key_cache,
    value_cache,
    new_keys,
    new_values,
    cache_len,
    norm_gain,
    expert_ids,
    gate_scores,
    gate_weight,
    up_weight,
    down_weight,
):
    groups = lax.axis_size("rep")
    rows = groups * PLACES
    me = lax.axis_index("exp")
    side, place = me // 4, me % 4

    routing = jnp.concatenate([expert_ids, gate_scores], axis=-1).reshape(1, LOCAL, 2 * TOPK)
    routing = exchange(jnp.broadcast_to(routing, (N_EXP, LOCAL, 2 * TOPK)), "exp")
    routing = jnp.broadcast_to(routing[:, None], (N_EXP, 2, LOCAL, 2 * TOPK))
    routing = routing.reshape(KEYS, 2 * TOPK)

    lent_down, lent_gate, lent_up = [
        across(lax.dynamic_index_in_dim(weight, 1 - side, 0, keepdims=False))
        for weight in (down_weight, gate_weight, up_weight)
    ]

    hidden, normed = [], []
    for step in range(STEPS):
        attention = attend_rows(
            queries[step], key_cache, value_cache, new_keys, new_values, cache_len, step
        )
        hidden.append(residual[step].astype(jnp.float32) + attention)
        normed.append(norm_rows(hidden[-1], norm_gain))
    normed = jnp.stack(normed).reshape(LOCAL, 4, 2, HALF).transpose(1, 2, 0, 3)
    normed = jnp.broadcast_to(
        normed.reshape(1, 4, 2 * LOCAL, HALF), (2, 4, 2 * LOCAL, HALF)
    ).reshape(N_EXP, 2 * LOCAL, HALF)
    tokens = exchange(normed, "exp").reshape(KEYS, HALF)
    table, combine = routing_tables(routing[:, :TOPK], routing[:, TOPK:], side, groups)
    outbound = lax.dot_general(
        table, tokens, (((0,), (0,)), ((), ())), preferred_element_type=jnp.float32
    ).astype(jnp.bfloat16)

    outbound, lent_down = lax.optimization_barrier((outbound, lent_down))

    def quarter(step):
        start = (place + step) % 4 * BLK
        kept = lax.dynamic_slice(down_weight, (side, 0, start), (1, UNITS, BLK))[0]
        return jnp.concatenate([kept, lax.dynamic_slice(lent_down, (0, start), (UNITS, BLK))])

    down = [quarter(0)] + [shift(quarter(step), step) for step in (1, -1, 2)]

    inbound = exchange(outbound.reshape(groups, WIRE, HALF), "rep")
    inbound, down, lent_gate = lax.optimization_barrier((inbound, down, lent_gate))
    slotted = inbound.reshape(groups, 2, PLACES, HALF).transpose(0, 2, 1, 3).reshape(rows, BLK)
    where = jnp.stack([side, place])
    activation = expand(where, ring(slotted), gate_weight, up_weight, lent_gate, lent_up)
    partial_value = contract(ring(activation), down)
    partial_value = partial_value.reshape(groups, PLACES, 2, HALF).transpose(0, 2, 1, 3)
    returned = exchange(partial_value.reshape(groups, WIRE, HALF), "rep")
    weighted = jnp.dot(
        combine,
        returned.reshape(groups * WIRE, HALF).astype(jnp.float32),
        precision=lax.Precision.HIGHEST,
        preferred_element_type=jnp.float32,
    ).astype(jnp.bfloat16)
    expert_sum = exchange(weighted.reshape(N_EXP, 2 * LOCAL, HALF), "exp").astype(jnp.float32)
    expert_sum = expert_sum.reshape(2, 4, 2, LOCAL, HALF).sum(axis=0)
    expert_sum = expert_sum.transpose(2, 0, 1, 3).reshape(STEPS, SEQ, D)
    return (jnp.stack(hidden) + expert_sum).astype(jnp.bfloat16)


def solution(mesh):
    in_specs = (
        P(None, ("rep", "exp"), None),
        P(None, ("rep", "exp"), None),
        P(("rep", "exp"), None, None),
        P(("rep", "exp"), None, None),
        P(None, ("rep", "exp"), None),
        P(None, ("rep", "exp"), None),
        P(("rep", "exp")),
        P(),
        P(None, ("rep", "exp"), None),
        P(None, ("rep", "exp"), None),
        P("rep", "exp", None),
        P("rep", "exp", None),
        P("rep", "exp", None),
    )
    out_specs = P(None, ("rep", "exp"), None)
    return jax.shard_map(
        per_device, mesh=mesh, in_specs=in_specs, out_specs=out_specs, check_vma=False
    )
```

time: 559 us -> 244 us (0.44)
  blocking collectives: 189 us -> 42.3 us
  waiting for transfers between devices: 183 us -> 123 us
  local copies, waits for them, and re-layouts: 60.6 us -> 17.1 us
  matrix products: 43.2 us -> 7.83 us
  between operations: 14.9 us -> 0.74 us
  starting transfers between devices: 53.2 us -> 40.1 us
  other arithmetic: 13.7 us -> 3.15 us
  Pallas kernels: 0 us -> 8.48 us
    all_gather x9 -> x0, blocking collectives: 189 us -> none  [the longest x3 87.6 us: per_device(): group_rows = lax.all_gather(normed, 'exp', axis=0, tiled=True)]
    unnamed x2 -> x0, waiting for transfers between devices: 78.1 us -> none
    ppermute x0 -> x14, waiting for transfers between devices: none -> 67.8 us  [the longest x11 67.8 us: shift(): return lax.ppermute(array, 'exp', pairs)]
    all_to_all x6 -> x3, waiting for transfers between devices: 105 us -> 55.6 us  [exchange(): return lax.all_to_all(array, axis, split_axis=0, concat_axis=0, tiled=True)]
    all_to_all x0 -> x2, blocking collectives: none -> 42.3 us  [exchange(): return lax.all_to_all(array, axis, split_axis=0, concat_axis=0, tiled=True)]
    all_to_all x6 -> x3, starting transfers between devices: 53.1 us -> 22.4 us  [exchange(): return lax.all_to_all(array, axis, split_axis=0, concat_axis=0, tiled=True)]
    dot_general x12 -> x3, matrix products: 32.1 us -> 1.91 us  [the longest x1 1.26 us: per_device(): lax.dot_general(table, tokens, (((0,), (0,)), ((), ())), preferred_elemen...]
    ppermute x0 -> x14, starting transfers between devices: none -> 17.7 us  [the longest x11 14.1 us: shift(): return lax.ppermute(array, 'exp', pairs)]
  transfers between devices with their start and end apart: 7 -> 17, of which waited for: 4 -> 8; matrix products, arithmetic and copies ran while one was open for 12% -> 9% of each run, Pallas kernels for 0% -> 0%
where the time goes in v2:
time: 244 us; the launch traced here: 243 us
  waiting for transfers between devices  123 us (50%)
  blocking collectives  42.3 us (17%)
  starting transfers between devices  40.1 us (16%)
  local copies, waits for them, and re-layouts  17.1 us (7%)
  Pallas kernels  8.48 us (3%)
  matrix products  7.83 us (3%)
  other arithmetic  3.15 us (1%)
    ppermute x11, waiting for transfers between devices, shift(): return lax.ppermute(array, 'exp', pairs)  67.8 us
    all_to_all x3, waiting for transfers between devices, exchange(): return lax.all_to_all(array, axis, split_axis=0, concat_axis=0, tiled=True)  55.6 us
    all_to_all x2, blocking collectives, exchange(): return lax.all_to_all(array, axis, split_axis=0, concat_axis=0, tiled=True)  42.3 us
    all_to_all x3, starting transfers between devices, exchange(): return lax.all_to_all(array, axis, split_axis=0, concat_axis=0, tiled=True)  22.4 us
    ppermute x11, starting transfers between devices, shift(): return lax.ppermute(array, 'exp', pairs)  14.1 us
    pallas_call x1, Pallas kernels, expand(): pl.pallas_call(expand_kernel, out_shape=jax.ShapeDtypeStruct((count, 2 *...  6.7 us
    squeeze x3, local copies, waits for them, and re-layouts, per_device(): lax.dynamic_index_in_dim(weight, 1 - side, 0, keepdims=False)  5.4 us
  transfers between devices with their start and end apart: 17, of which 8 were waited for; matrix products, arithmetic and copies ran while one was open for 9% of the time, Pallas kernels for 0%

profile of v2, /device:TPU:4, one launch (start us, length us, event | category | flops | bytes accessed | tf_op | source)
XLA Modules:
  0.0 243.1 jit_solution(15057452321460232241)
XLA Ops:
  1.5 5.1 %all-to-all-start = ((s32[8,6,16]{2,1,0:T(8,128)}), s32[8,6,16]{2,1,0:T(8,128)S(1)}, u32[]{:S(2)}, u32[]{:S(2)}) async-start(s32[8,6,16]{2,1,0:T(8,128)} %broadcast_in_dim.36), calls=%async_computation | async-start | bytes 65536 | tf_op jit(solution)/shard_map/all_to_all | solution.py:79
  6.6 2.9 %dynamic-slice_bitcast_fusion.2 = bf16[192,4096]{1,0:T(8,128)(2,1)} fusion(bf16[2,192,4096]{2,1,0:T(8,128)(2,1)} %param.27, s32[]{:T(128)S(6)} %select_n.75), kind=kLoop, calls=%fused_computation.2 | loop fusion | bytes 3145732 | tf_op jit(solution)/shard_map/jit(dynamic_index_in_dim)/squeeze | solution.py:269
  9.5 2.1 collective-permute-start
  11.6 1.3 dynamic-slice_bitcast_fusion.1
  16.3 1.5 fusion.4
  18.4 1.6 multiply_reduce_fusion.2
  21.3 5.7 %all-to-all-start.1 = ((bf16[8,12,512]{2,1,0:T(8,128)(2,1)}), bf16[8,12,512]{2,1,0:T(8,128)(2,1)S(1)}, u32[]{:S(2)}, u32[]{:S(2)}) async-start(bf16[8,12,512]{2,1,0:T(8,128)(2,1)} %bitcast.7), calls=%async_computation.1 | async-start | bytes 262144 | tf_op jit(solution)/shard_map/all_to_all | solution.py:79
  27.5 55.6 %all-to-all-done.1 = bf16[8,12,512]{2,1,0:T(8,128)(2,1)S(1)} async-done(((bf16[8,12,512]{2,1,0:T(8,128)(2,1)}), bf16[8,12,512]{2,1,0:T(8,128)(2,1)S(1)}, u32[]{:S(2)}, u32[]{:S(2)}) %all-to-all-start.1) | async-done | bytes 98336 | tf_op jit(solution)/shard_map/all_to_all | solution.py:79
  83.2 1.3 convolution_convert_fusion
  84.5 11.6 %all-to-all-start.2 = ((bf16[32,24,512]{2,1,0:T(8,128)(2,1)}), bf16[32,24,512]{2,1,0:T(8,128)(2,1)}, u32[]{:S(2)}, u32[]{:S(2)}) async-start(bf16[32,24,512]{2,1,0:T(8,128)(2,1)} %bitcast.9), calls=%async_computation.2 | async-start | bytes 1572864 | tf_op jit(solution)/shard_map/all_to_all | solution.py:79
  96.1 1.5 dynamic-slice_bitcast_fusion.3
  97.6 1.5 constant_dynamic-slice_fusion
  99.9 2.8 %collective-permute-start.2 = (bf16[384,1024]{1,0:T(8,128)(2,1)S(1)}, bf16[384,1024]{1,0:T(8,128)(2,1)S(1)}, u32[]{:S(2)}, u32[]{:S(2)}) collective-permute-start(bf16[384,1024]{1,0:T(8,128)(2,1)S(1)} %pad_maximum_fusion.2), channel_id=1, source_target_pairs={{0,3},{1,0},{2,1},{3,2},{4,7},{5,4},{6,5},{7,6},{8,11},{9,8},{10,9... | collective-permute-start | bytes 2359304 | tf_op jit(solution)/shard_map/ppermute | solution.py:84
  102.8 1.3 dynamic-slice_bitcast_fusion
  104.1 1.5 collective-permute-start.9
  105.6 31.3 %collective-permute-done.1.w_below = bf16[384,1024]{1,0:T(8,128)(2,1)S(1)} collective-permute-done((bf16[384,1024]{1,0:T(8,128)(2,1)S(1)}, bf16[384,1024]{1,0:T(8,128)(2,1)S(1)}, u32[]{:S(2)}, u32[]{:S(2)}) %collective-permute-start.1) | collective-permute-done | bytes 786464 | tf_op jit(solution)/shard_map/ppermute | solution.py:84
  137.8 0.9 copy-done.7
  139.7 1.5 copy.130
  142.1 2.3 collective-permute-start.6
  144.4 16.0 %collective-permute-done.6.above_rows = bf16[384,1024]{1,0:T(8,128)(2,1)S(1)} collective-permute-done((bf16[384,1024]{1,0:T(8,128)(2,1)S(1)}, bf16[384,1024]{1,0:T(8,128)(2,1)S(1)}, u32[]{:S(2)}, u32[]{:S(2)}) %collective-permute-start.6) | collective-permute-done | bytes 786464 | tf_op jit(solution)/shard_map/ppermute | solution.py:84
  160.4 4.0 %collective-permute-start.8 = (bf16[192,1024]{1,0:T(8,128)(2,1)S(1)}, bf16[192,1024]{1,0:T(8,128)(2,1)S(1)}, u32[]{:S(2)}, u32[]{:S(2)}) collective-permute-start(bf16[192,1024]{1,0:T(8,128)(2,1)S(1)} %slice.67), channel_id=1, source_target_pairs={{0,3},{1,0},{2,1},{3,2},{4,7},{5,4},{6,5},{7,6},{8,11},{9,8},{10,9... | collective-permute-start | bytes 1179656 | tf_op jit(solution)/shard_map/ppermute | solution.py:84
  164.6 6.4 %collective-permute-done.8.far_high = bf16[192,1024]{1,0:T(8,128)(2,1)S(1)} collective-permute-done((bf16[192,1024]{1,0:T(8,128)(2,1)S(1)}, bf16[192,1024]{1,0:T(8,128)(2,1)S(1)}, u32[]{:S(2)}, u32[]{:S(2)}) %collective-permute-start.8) | collective-permute-done | bytes 393248 | tf_op jit(solution)/shard_map/ppermute | solution.py:84
  171.0 3.5 %collective-permute-done.7.far_low = bf16[192,1024]{1,0:T(8,128)(2,1)S(1)} collective-permute-done((bf16[192,1024]{1,0:T(8,128)(2,1)S(1)}, bf16[192,1024]{1,0:T(8,128)(2,1)S(1)}, u32[]{:S(2)}, u32[]{:S(2)}) %collective-permute-start.7) | collective-permute-done | bytes 393248 | tf_op jit(solution)/shard_map/ppermute | solution.py:84
  174.5 6.7 %expand.1.own = bf16[384,384]{1,0:T(8,128)(2,1)S(1)} custom-call(s32[2]{0:T(128)S(1)} %pad_add_fusion.1.where, bf16[384,1024]{1,0:T(8,128)(2,1)S(1)} %bitcast.132, bf16[384,1024]{1,0:T(8,128)(2,1)S(1)} %collective-permute-done.5.below_rows, bf16[384,1024]{1,0:T(8,128)(2,1)S(1)} %collective-permute-done.6.above_rows, ...), custom_call_target="tpu_custom_call" | custom-call | flops 2415919104 | bytes 9732096 | tf_op jit(solution)/shard_map/expand/pallas_call | solution.py:192
  181.5 1.8 collective-permute-start.10
  183.3 6.2 %collective-permute-done.11.above = bf16[384,384]{1,0:T(8,128)(2,1)S(1)} collective-permute-done((bf16[384,384]{1,0:T(8,128)(2,1)S(1)}, bf16[384,384]{1,0:T(8,128)(2,1)S(1)}, u32[]{:S(2)}, u32[]{:S(2)}) %collective-permute-start.11) | collective-permute-done | bytes 294944 | tf_op jit(solution)/shard_map/ppermute | solution.py:84
  189.7 2.1 collective-permute-start.12
  191.8 3.0 %collective-permute-done.13.far_high = bf16[192,384]{1,0:T(8,128)(2,1)S(1)} collective-permute-done((bf16[192,384]{1,0:T(8,128)(2,1)S(1)}, bf16[192,384]{1,0:T(8,128)(2,1)S(1)}, u32[]{:S(2)}, u32[]{:S(2)}) %collective-permute-start.13) | collective-permute-done | bytes 147488 | tf_op jit(solution)/shard_map/ppermute | solution.py:84
  194.8 1.3 collective-permute-done.12.far_low
  196.1 1.8 contract.1
  199.2 32.9 %all_to_all.25 = bf16[32,24,512]{2,1,0:T(8,128)(2,1)S(1)} all-to-all(bf16[32,24,512]{2,1,0:T(8,128)(2,1)S(1)} %copy.133), channel_id=1, replica_groups=mesh['rep'=32,'exp'=8] {'rep'}, dimensions={0} | all-to-all | bytes 1572864 | tf_op jit(solution)/shard_map/all_to_all | solution.py:79
  232.6 9.4 %all_to_all.26 = bf16[8,12,512]{2,1,0:T(8,128)(2,1)S(1)} all-to-all(bf16[8,12,512]{2,1,0:T(8,128)(2,1)S(1)} %reshape.277), channel_id=1, replica_groups=mesh['rep'=32,'exp'=8] {'exp'}, dimensions={0} | all-to-all | bytes 196608 | tf_op jit(solution)/shard_map/all_to_all | solution.py:79
  (146 shorter events, 14.0 us)
Async XLA Ops:
  0.0 13.4 %copy-start = (bf16[2,1024,256]{2,1,0:T(8,128)(2,1)S(1)}, bf16[2,1024,256]{2,1,0:T(8,128)(2,1)}, u32[]{:S(2)}) copy-start(bf16[2,1024,256]{2,1,0:T(8,128)(2,1)} %param.17) | copy-start | bytes 3145732
  1.5 19.1 %all-to-all-start = ((s32[8,6,16]{2,1,0:T(8,128)}), s32[8,6,16]{2,1,0:T(8,128)S(1)}, u32[]{:S(2)}, u32[]{:S(2)}) async-start(s32[8,6,16]{2,1,0:T(8,128)} %broadcast_in_dim.36), calls=%async_computation | async-start | bytes 65536 | tf_op jit(solution)/shard_map/all_to_all | solution.py:79
  6.6 5.0 %copy-start.1 = (bf16[2,192,4096]{2,1,0:T(8,128)(2,1)S(1)}, bf16[2,192,4096]{2,1,0:T(8,128)(2,1)}, u32[]{:S(2)}) copy-start(bf16[2,192,4096]{2,1,0:T(8,128)(2,1)} %own_gate.1) | copy-start | bytes 9437188
  9.5 3.5 %slice-start = ((bf16[3,2,256]{2,1,0:T(2,128)(2,1)}), bf16[1,2,256]{2,1,0:T(2,128)(2,1)S(1)}, s32[]{:S(2)}) async-start(bf16[3,2,256]{2,1,0:T(2,128)(2,1)} %param.19), calls=%async_computation.5 | async-start | bytes 2048 | tf_op jit(solution)/shard_map/slice | solution.py:39
  9.5 3.5 %slice-start.1 = ((bf16[3,2,256]{2,1,0:T(2,128)(2,1)}), bf16[2,2,256]{2,1,0:T(2,128)(2,1)S(1)}, s32[]{:S(2)}) async-start(bf16[3,2,256]{2,1,0:T(2,128)(2,1)} %param.19), calls=%async_computation.6 | async-start | bytes 4096 | tf_op jit(solution)/shard_map/slice | solution.py:39
  9.5 3.6 %slice-start.2 = ((bf16[3,2,256]{2,1,0:T(2,128)(2,1)}), bf16[2,2,256]{2,1,0:T(2,128)(2,1)S(1)}, s32[]{:S(2)}) async-start(bf16[3,2,256]{2,1,0:T(2,128)(2,1)} %param.20), calls=%async_computation.7 | async-start | bytes 4096 | tf_op jit(solution)/shard_map/slice | solution.py:40
  9.5 3.6 %copy-start.18 = (s32[2]{0:T(128)S(1)}, s32[2]{0:T(128)}, u32[]{:S(2)}) copy-start(s32[2]{0:T(128)} %param.21) | copy-start | bytes 28
  9.5 3.6 %copy-start.17 = (bf16[4096]{0:T(1024)(128)(2,1)S(1)}, bf16[4096]{0:T(1024)(128)(2,1)}, u32[]{:S(2)}) copy-start(bf16[4096]{0:T(1024)(128)(2,1)} %param.22) | copy-start | bytes 24580
  9.5 3.6 %copy-start.13 = (bf16[3,2,4096]{2,1,0:T(2,128)(2,1)S(1)}, bf16[3,2,4096]{2,1,0:T(2,128)(2,1)}, u32[]{:S(2)}) copy-start(bf16[3,2,4096]{2,1,0:T(2,128)(2,1)} %param.16) | copy-start | bytes 147460
  9.5 74.9 %collective-permute-start = (bf16[192,4096]{1,0:T(8,128)(2,1)}, bf16[192,4096]{1,0:T(8,128)(2,1)}, u32[]{:S(2)}, u32[]{:S(2)}) collective-permute-start(bf16[192,4096]{1,0:T(8,128)(2,1)} %dynamic-slice_bitcast_fusion.2), channel_id=1, source_target_pairs={{0,4},{1,5},{2,6},{3,7},{4,0},{5,1},{6,2},{7,3},{8,12},{9,13},{10,... | collective-permute-start | bytes 4718600 | tf_op jit(solution)/shard_map/ppermute | solution.py:88
  12.9 92.7 %collective-permute-start.4 = (bf16[192,4096]{1,0:T(8,128)(2,1)}, bf16[192,4096]{1,0:T(8,128)(2,1)S(1)}, u32[]{:S(2)}, u32[]{:S(2)}) collective-permute-start(bf16[192,4096]{1,0:T(8,128)(2,1)} %dynamic-slice_bitcast_fusion.1), channel_id=1, source_target_pairs={{0,4},{1,5},{2,6},{3,7},{4,0},{5,1},{6,2},{7,3},{8,12},{9,13},{10,... | collective-permute-start | bytes 4718600 | tf_op jit(solution)/shard_map/ppermute | solution.py:88
  18.4 8.9 %copy-start.14 = (bf16[96,96]{1,0:T(8,128)(2,1)S(1)}, bf16[96,96]{1,0:T(8,128)(2,1)}, u32[]{:S(2)}) copy-start(bf16[96,96]{1,0:T(8,128)(2,1)} %constant.164) | copy-start | bytes 55300
  20.1 7.4 %copy-start.12 = (f32[96,24]{0,1:T(8,128)S(1)}, f32[96,24]{0,1:T(8,128)}, u32[]{:S(2)}) copy-start(f32[96,24]{0,1:T(8,128)} %constant.105) | copy-start | bytes 27652
  21.3 61.9 %all-to-all-start.1 = ((bf16[8,12,512]{2,1,0:T(8,128)(2,1)}), bf16[8,12,512]{2,1,0:T(8,128)(2,1)S(1)}, u32[]{:S(2)}, u32[]{:S(2)}) async-start(bf16[8,12,512]{2,1,0:T(8,128)(2,1)} %bitcast.7), calls=%async_computation.1 | async-start | bytes 262144 | tf_op jit(solution)/shard_map/all_to_all | solution.py:79
  84.5 55.2 %all-to-all-start.2 = ((bf16[32,24,512]{2,1,0:T(8,128)(2,1)}), bf16[32,24,512]{2,1,0:T(8,128)(2,1)}, u32[]{:S(2)}, u32[]{:S(2)}) async-start(bf16[32,24,512]{2,1,0:T(8,128)(2,1)} %bitcast.9), calls=%async_computation.2 | async-start | bytes 1572864 | tf_op jit(solution)/shard_map/all_to_all | solution.py:79
  99.2 37.7 %collective-permute-start.1 = (bf16[384,1024]{1,0:T(8,128)(2,1)S(1)}, bf16[384,1024]{1,0:T(8,128)(2,1)S(1)}, u32[]{:S(2)}, u32[]{:S(2)}) collective-permute-start(bf16[384,1024]{1,0:T(8,128)(2,1)S(1)} %pad_maximum_fusion.1), channel_id=1, source_target_pairs={{0,1},{1,2},{2,3},{3,0},{4,5},{5,6},{6,7},{7,4},{8,9},{9,10},{10,1... | collective-permute-start | bytes 2359304 | tf_op jit(solution)/shard_map/ppermute | solution.py:84
  99.9 38.0 %collective-permute-start.2 = (bf16[384,1024]{1,0:T(8,128)(2,1)S(1)}, bf16[384,1024]{1,0:T(8,128)(2,1)S(1)}, u32[]{:S(2)}, u32[]{:S(2)}) collective-permute-start(bf16[384,1024]{1,0:T(8,128)(2,1)S(1)} %pad_maximum_fusion.2), channel_id=1, source_target_pairs={{0,3},{1,0},{2,1},{3,2},{4,7},{5,4},{6,5},{7,6},{8,11},{9,8},{10,9... | collective-permute-start | bytes 2359304 | tf_op jit(solution)/shard_map/ppermute | solution.py:84
  102.7 36.0 %collective-permute-start.3 = (bf16[384,1024]{1,0:T(8,128)(2,1)S(1)}, bf16[384,1024]{1,0:T(8,128)(2,1)S(1)}, u32[]{:S(2)}, u32[]{:S(2)}) collective-permute-start(bf16[384,1024]{1,0:T(8,128)(2,1)S(1)} %pad_maximum_fusion.3), channel_id=1, source_target_pairs={{0,2},{1,3},{2,0},{3,1},{4,6},{5,7},{6,4},{7,5},{8,10},{9,11},{10,... | collective-permute-start | bytes 2359304 | tf_op jit(solution)/shard_map/ppermute | solution.py:84
  104.1 60.5 %collective-permute-start.9 = (bf16[192,4096]{1,0:T(8,128)(2,1)}, bf16[192,4096]{1,0:T(8,128)(2,1)}, u32[]{:S(2)}, u32[]{:S(2)}) collective-permute-start(bf16[192,4096]{1,0:T(8,128)(2,1)} %dynamic-slice_bitcast_fusion), channel_id=1, source_target_pairs={{0,4},{1,5},{2,6},{3,7},{4,0},{5,1},{6,2},{7,3},{8,12},{9,13},{10,... | collective-permute-start | bytes 4718600 | tf_op jit(solution)/shard_map/ppermute | solution.py:88
  139.7 34.9 %copy-start.4 = (bf16[2,192,4096]{2,1,0:T(8,128)(2,1)S(1)}, bf16[2,192,4096]{2,1,0:T(8,128)(2,1)}, u32[]{:S(2)}) copy-start(bf16[2,192,4096]{2,1,0:T(8,128)(2,1)} %own_up.1) | copy-start | bytes 9437188
  142.0 32.5 %copy-start.2 = (bf16[2,192,4096]{2,1,0:T(8,128)(2,1)S(1)}, bf16[2,192,4096]{2,1,0:T(8,128)(2,1)}, u32[]{:S(2)}) copy-start(bf16[2,192,4096]{2,1,0:T(8,128)(2,1)} %own_gate.1) | copy-start | bytes 9437188
  142.1 18.2 %collective-permute-start.6 = (bf16[384,1024]{1,0:T(8,128)(2,1)S(1)}, bf16[384,1024]{1,0:T(8,128)(2,1)S(1)}, u32[]{:S(2)}, u32[]{:S(2)}) collective-permute-start(bf16[384,1024]{1,0:T(8,128)(2,1)S(1)} %bitcast.130), channel_id=1, source_target_pairs={{0,3},{1,0},{2,1},{3,2},{4,7},{5,4},{6,5},{7,6},{8,11},{9,8},{10,9... | collective-permute-start | bytes 2359304 | tf_op jit(solution)/shard_map/ppermute | solution.py:84
  144.4 19.9 %collective-permute-start.5 = (bf16[384,1024]{1,0:T(8,128)(2,1)S(1)}, bf16[384,1024]{1,0:T(8,128)(2,1)S(1)}, u32[]{:S(2)}, u32[]{:S(2)}) collective-permute-start(bf16[384,1024]{1,0:T(8,128)(2,1)S(1)} %bitcast.131), channel_id=1, source_target_pairs={{0,1},{1,2},{2,3},{3,0},{4,5},{5,6},{6,7},{7,4},{8,9},{9,10},{10,1... | collective-permute-start | bytes 2359304 | tf_op jit(solution)/shard_map/ppermute | solution.py:84
  160.4 10.6 %collective-permute-start.8 = (bf16[192,1024]{1,0:T(8,128)(2,1)S(1)}, bf16[192,1024]{1,0:T(8,128)(2,1)S(1)}, u32[]{:S(2)}, u32[]{:S(2)}) collective-permute-start(bf16[192,1024]{1,0:T(8,128)(2,1)S(1)} %slice.67), channel_id=1, source_target_pairs={{0,3},{1,0},{2,1},{3,2},{4,7},{5,4},{6,5},{7,6},{8,11},{9,8},{10,9... | collective-permute-start | bytes 1179656 | tf_op jit(solution)/shard_map/ppermute | solution.py:84
  164.4 10.1 %collective-permute-start.7 = (bf16[192,1024]{1,0:T(8,128)(2,1)S(1)}, bf16[192,1024]{1,0:T(8,128)(2,1)S(1)}, u32[]{:S(2)}, u32[]{:S(2)}) collective-permute-start(bf16[192,1024]{1,0:T(8,128)(2,1)S(1)} %slice.66), channel_id=1, source_target_pairs={{0,1},{1,2},{2,3},{3,0},{4,5},{5,6},{6,7},{7,4},{8,9},{9,10},{10,1... | collective-permute-start | bytes 1179656 | tf_op jit(solution)/shard_map/ppermute | solution.py:84
  164.6 31.5 %copy-start.6 = (bf16[384,1024]{1,0:T(8,128)(2,1)S(1)}, bf16[384,1024]{1,0:T(8,128)(2,1)}, u32[]{:S(2)}) copy-start(bf16[384,1024]{1,0:T(8,128)(2,1)} %copy-done.5) | copy-start | bytes 2359300
  164.6 31.5 %copy-start.8 = (bf16[384,1024]{1,0:T(8,128)(2,1)S(1)}, bf16[384,1024]{1,0:T(8,128)(2,1)}, u32[]{:S(2)}) copy-start(bf16[384,1024]{1,0:T(8,128)(2,1)} %copy-done.7) | copy-start | bytes 2359300
  164.6 31.5 %copy-start.10 = (bf16[384,1024]{1,0:T(8,128)(2,1)S(1)}, bf16[384,1024]{1,0:T(8,128)(2,1)}, u32[]{:S(2)}) copy-start(bf16[384,1024]{1,0:T(8,128)(2,1)} %copy-done.9) | copy-start | bytes 2359300
  181.2 8.3 %collective-permute-start.11 = (bf16[384,384]{1,0:T(8,128)(2,1)S(1)}, bf16[384,384]{1,0:T(8,128)(2,1)S(1)}, u32[]{:S(2)}, u32[]{:S(2)}) collective-permute-start(bf16[384,384]{1,0:T(8,128)(2,1)S(1)} %expand.1.own), channel_id=1, source_target_pairs={{0,3},{1,0},{2,1},{3,2},{4,7},{5,4},{6,5},{7,6},{8,11},{9,8},{10,9... | collective-permute-start | bytes 884744 | tf_op jit(solution)/shard_map/ppermute | solution.py:84
  181.5 8.2 %collective-permute-start.10 = (bf16[384,384]{1,0:T(8,128)(2,1)S(1)}, bf16[384,384]{1,0:T(8,128)(2,1)S(1)}, u32[]{:S(2)}, u32[]{:S(2)}) collective-permute-start(bf16[384,384]{1,0:T(8,128)(2,1)S(1)} %expand.1.own), channel_id=1, source_target_pairs={{0,1},{1,2},{2,3},{3,0},{4,5},{5,6},{6,7},{7,4},{8,9},{9,10},{10,1... | collective-permute-start | bytes 884744 | tf_op jit(solution)/shard_map/ppermute | solution.py:84
  189.6 5.2 %collective-permute-start.13 = (bf16[192,384]{1,0:T(8,128)(2,1)S(1)}, bf16[192,384]{1,0:T(8,128)(2,1)S(1)}, u32[]{:S(2)}, u32[]{:S(2)}) collective-permute-start(bf16[192,384]{1,0:T(8,128)(2,1)S(1)} %slice.69), channel_id=1, source_target_pairs={{0,3},{1,0},{2,1},{3,2},{4,7},{5,4},{6,5},{7,6},{8,11},{9,8},{10,9... | collective-permute-start | bytes 442376 | tf_op jit(solution)/shard_map/ppermute | solution.py:84
  189.7 6.4 %collective-permute-start.12 = (bf16[192,384]{1,0:T(8,128)(2,1)S(1)}, bf16[192,384]{1,0:T(8,128)(2,1)S(1)}, u32[]{:S(2)}, u32[]{:S(2)}) collective-permute-start(bf16[192,384]{1,0:T(8,128)(2,1)S(1)} %slice.68), channel_id=1, source_target_pairs={{0,1},{1,2},{2,3},{3,0},{4,5},{5,6},{6,7},{7,4},{8,9},{9,10},{10,1... | collective-permute-start | bytes 442376 | tf_op jit(solution)/shard_map/ppermute | solution.py:84
  (8 other events, 15.5 us)

commit v3 on v2

--- a/solution.py
+++ b/solution.py
@@ -134,23 +134,21 @@
     )
 
 
-def expand_kernel(
+def expand_near_kernel(
     where,
     own_rows,
     below_rows,
     above_rows,
-    far_low,
-    far_high,
     own_gate,
     own_up,
-    lent_gate,
+    lent_gate_low,
+    lent_gate_high,
     lent_up,
-    out,
     gate_total,
     up_total,
 ):
     turn = pl.program_id(0)
-    gate_block = jnp.concatenate([own_gate[0], lent_gate[...]], axis=0)
+    gate_block = jnp.concatenate([own_gate[0], lent_gate_low[...], lent_gate_high[...]], axis=0)
     up_block = jnp.concatenate([own_up[0], lent_up[...]], axis=0)
 
     @pl.when(turn == 0)
@@ -168,64 +166,94 @@
         gate_total[...] += contract_last(above_rows[...], gate_block)
         up_total[...] += contract_last(above_rows[...], up_block)
 
-    @pl.when(turn == 3)
-    def _():
-        half = far_low.shape[0]
-        for start, rows in ((0, far_low), (half, far_high)):
-            span = pl.ds(start, half)
-            gate = gate_total[span, :] + contract_last(rows[...], gate_block)
-            up = up_total[span, :] + contract_last(rows[...], up_block)
-            out[span, :] = (gate / (1.0 + jnp.exp(-gate)) * up).astype(jnp.bfloat16)
-
-
-def expand(where, rows, gate_weight, up_weight, lent_gate, lent_up):
+
+def expand_far_kernel(
+    where,
+    far_low,
+    far_high,
+    gate_total,
+    up_total,
+    own_gate,
+    own_up,
+    lent_gate_low,
+    lent_gate_high,
+    lent_up,
+    out,
+):
+    gate_block = jnp.concatenate([own_gate[0], lent_gate_low[...], lent_gate_high[...]], axis=0)
+    up_block = jnp.concatenate([own_up[0], lent_up[...]], axis=0)
+    half = far_low.shape[0]
+    for start, rows in ((0, far_low), (half, far_high)):
+        span = pl.ds(start, half)
+        gate = gate_total[span, :] + contract_last(rows[...], gate_block)
+        up = up_total[span, :] + contract_last(rows[...], up_block)
+        out[span, :] = (gate / (1.0 + jnp.exp(-gate)) * up).astype(jnp.bfloat16)
+
+
+def expand(where, rows, weights):
     count = rows[0].shape[0]
 
-    def column(turn, where):
-        return (where[1] + jnp.where(turn == 1, 3, jnp.where(turn == 2, 1, turn - turn // 3))) % 4
+    def near_column(turn, where):
+        return (where[1] + jnp.where(turn == 1, 3, jnp.where(turn == 2, 1, 0))) % 4
+
+    def far_column(turn, where):
+        return (where[1] + 2) % 4
 
     def whole(shape):
         return pl.BlockSpec(shape, lambda turn, where: (0, 0))
 
-    own = pl.BlockSpec((1, UNITS, BLK), lambda turn, where: (where[0], 0, column(turn, where)))
-    lent = pl.BlockSpec((UNITS, BLK), lambda turn, where: (0, column(turn, where)))
-    return pl.pallas_call(
-        expand_kernel,
-        out_shape=jax.ShapeDtypeStruct((count, 2 * UNITS), jnp.bfloat16),
-        grid_spec=pltpu.PrefetchScalarGridSpec(
-            num_scalar_prefetch=1,
-            grid=(4,),
-            in_specs=[whole(array.shape) for array in rows] + [own, own, lent, lent],
-            out_specs=whole((count, 2 * UNITS)),
-            scratch_shapes=[
-                pltpu.VMEM((count, 2 * UNITS), jnp.float32),
-                pltpu.VMEM((count, 2 * UNITS), jnp.float32),
-            ],
-        ),
-        compiler_params=pltpu.CompilerParams(
-            dimension_semantics=("arbitrary",), vmem_limit_bytes=32 << 20
-        ),
-        cost_estimate=pl.CostEstimate(
-            flops=8 * count * UNITS * D,
-            bytes_accessed=2 * count * D + 8 * UNITS * D + 4 * count * UNITS,
-            transcendentals=2 * count * UNITS,
-        ),
-        name="expand",
-    )(where, *rows, gate_weight, up_weight, lent_gate, lent_up)
-
-
-def contract_kernel(own, below, above, far_low, far_high, w_own, w_below, w_above, w_far, out):
+    def call(kernel, name, steps, column, inputs, out_shape):
+        own = pl.BlockSpec((1, UNITS, BLK), lambda turn, where: (where[0], 0, column(turn, where)))
+        lent = pl.BlockSpec((UNITS, BLK), lambda turn, where: (0, column(turn, where)))
+        part = pl.BlockSpec((UNITS // 2, BLK), lambda turn, where: (0, column(turn, where)))
+        outs = jax.tree.leaves(out_shape)
+        out_specs = jax.tree.unflatten(
+            jax.tree.structure(out_shape), [whole(leaf.shape) for leaf in outs]
+        )
+        return pl.pallas_call(
+            kernel,
+            out_shape=out_shape,
+            grid_spec=pltpu.PrefetchScalarGridSpec(
+                num_scalar_prefetch=1,
+                grid=(steps,),
+                in_specs=[whole(array.shape) for array in inputs] + [own, own, part, part, lent],
+                out_specs=out_specs,
+            ),
+            compiler_params=pltpu.CompilerParams(
+                dimension_semantics=("arbitrary",), vmem_limit_bytes=32 << 20
+            ),
+            cost_estimate=pl.CostEstimate(
+                flops=8 * count * UNITS * BLK * steps,
+                bytes_accessed=steps * BLK * (2 * count + 8 * UNITS) + 16 * count * UNITS,
+                transcendentals=0,
+            ),
+            name=name,
+        )(where, *inputs, *weights)
+
+    total = jax.ShapeDtypeStruct((count, 2 * UNITS), jnp.float32)
+    totals = call(expand_near_kernel, "expand_near", 3, near_column, rows[:3], (total, total))
+    out = jax.ShapeDtypeStruct((count, 2 * UNITS), jnp.bfloat16)
+    return call(
+        expand_far_kernel, "expand_far", 1, far_column, (*rows[3:], *totals), out
+    )
+
+
+def contract_kernel(own, below, above, far_low, far_high, w_own, w_below, w_above, w_far, lent, out):
     half = far_low.shape[0]
+    blocks = [
+        jnp.concatenate([kept[0], lent[turn * UNITS : (turn + 1) * UNITS]], axis=0)
+        for turn, kept in enumerate((w_own, w_below, w_above, w_far))
+    ]
     for start, far in ((0, far_low), (half, far_high)):
         span = pl.ds(start, half)
-        total = jnp.dot(own[span, :], w_own[...], preferred_element_type=jnp.float32)
-        total += jnp.dot(below[span, :], w_below[...], preferred_element_type=jnp.float32)
-        total += jnp.dot(above[span, :], w_above[...], preferred_element_type=jnp.float32)
-        total += jnp.dot(far[...], w_far[...], preferred_element_type=jnp.float32)
+        total = jnp.dot(own[span, :], blocks[0], preferred_element_type=jnp.float32)
+        total += jnp.dot(below[span, :], blocks[1], preferred_element_type=jnp.float32)
+        total += jnp.dot(above[span, :], blocks[2], preferred_element_type=jnp.float32)
+        total += jnp.dot(far[...], blocks[3], preferred_element_type=jnp.float32)
         out[span, :] = total.astype(jnp.bfloat16)
 
 
-def contract(acts, weights):
+def contract(acts, kept, lent):
     count = acts[0].shape[0]
     return pl.pallas_call(
         contract_kernel,
@@ -237,7 +265,7 @@
             transcendentals=0,
         ),
         name="contract",
-    )(*acts, *weights)
+    )(*acts, *kept, lent)
 
 
 def per_device(
@@ -265,10 +293,8 @@
     routing = jnp.broadcast_to(routing[:, None], (N_EXP, 2, LOCAL, 2 * TOPK))
     routing = routing.reshape(KEYS, 2 * TOPK)
 
-    lent_down, lent_gate, lent_up = [
-        across(lax.dynamic_index_in_dim(weight, 1 - side, 0, keepdims=False))
-        for weight in (down_weight, gate_weight, up_weight)
-    ]
+    half = UNITS // 2
+    lent_gate_low = across(lax.dynamic_slice(gate_weight, (1 - side, 0, 0), (1, half, D))[0])
 
     hidden, normed = [], []
     for step in range(STEPS):
@@ -281,27 +307,37 @@
     normed = jnp.broadcast_to(
         normed.reshape(1, 4, 2 * LOCAL, HALF), (2, 4, 2 * LOCAL, HALF)
     ).reshape(N_EXP, 2 * LOCAL, HALF)
+    normed, lent_gate_low = lax.optimization_barrier((normed, lent_gate_low))
     tokens = exchange(normed, "exp").reshape(KEYS, HALF)
     table, combine = routing_tables(routing[:, :TOPK], routing[:, TOPK:], side, groups)
     outbound = lax.dot_general(
         table, tokens, (((0,), (0,)), ((), ())), preferred_element_type=jnp.float32
     ).astype(jnp.bfloat16)
 
-    outbound, lent_down = lax.optimization_barrier((outbound, lent_down))
+    outbound, gate_late, up_late, down_late = lax.optimization_barrier(
+        (outbound, gate_weight, up_weight, down_weight)
+    )
+    inbound = exchange(outbound.reshape(groups, WIRE, HALF), "rep")
 
     def quarter(step):
         start = (place + step) % 4 * BLK
-        kept = lax.dynamic_slice(down_weight, (side, 0, start), (1, UNITS, BLK))[0]
-        return jnp.concatenate([kept, lax.dynamic_slice(lent_down, (0, start), (UNITS, BLK))])
-
-    down = [quarter(0)] + [shift(quarter(step), step) for step in (1, -1, 2)]
-
-    inbound = exchange(outbound.reshape(groups, WIRE, HALF), "rep")
-    inbound, down, lent_gate = lax.optimization_barrier((inbound, down, lent_gate))
+        return jnp.concatenate(
+            [
+                lax.dynamic_slice(down_late, (expert, 0, start), (1, UNITS, BLK))
+                for expert in (side, 1 - side)
+            ]
+        )
+
+    kept = [quarter(0)] + [shift(quarter(step), step) for step in (1, -1, 2)]
+    lent_gate_high = across(lax.dynamic_slice(gate_late, (1 - side, half, 0), (1, half, D))[0])
+    lent_up = across(lax.dynamic_index_in_dim(up_late, 1 - side, 0, keepdims=False))
+    inbound, kept, lent_gate_high = lax.optimization_barrier((inbound, kept, lent_gate_high))
+    lent_down = across(jnp.concatenate([block[1] for block in kept]))
     slotted = inbound.reshape(groups, 2, PLACES, HALF).transpose(0, 2, 1, 3).reshape(rows, BLK)
     where = jnp.stack([side, place])
-    activation = expand(where, ring(slotted), gate_weight, up_weight, lent_gate, lent_up)
-    partial_value = contract(ring(activation), down)
+    weights = (gate_weight, up_weight, lent_gate_low, lent_gate_high, lent_up)
+    activation = expand(where, ring(slotted), weights)
+    partial_value = contract(ring(activation), kept, lent_down)
     partial_value = partial_value.reshape(groups, PLACES, 2, HALF).transpose(0, 2, 1, 3)
     returned = exchange(partial_value.reshape(groups, WIRE, HALF), "rep")
     weighted = jnp.dot(

time: 244 us -> 199 us (0.82)
  waiting for transfers between devices: 123 us -> 69.7 us
  starting transfers between devices: 40.1 us -> 44.1 us
    all_to_all x3, waiting for transfers between devices: 55.6 us -> 6.53 us  [exchange(): return lax.all_to_all(array, axis, split_axis=0, concat_axis=0, tiled=True)]
    ppermute x11, waiting for transfers between devices: 67.8 us -> 51 us  [shift(): return lax.ppermute(array, 'exp', pairs)]
    ppermute x3 -> x4, waiting for transfers between devices: 0.01 us -> 12.2 us  [across(): return lax.ppermute(array, 'exp', [(e, e ^ 4) for e in range(N_EXP)])]
    squeeze x4 -> x7, local copies, waits for them, and re-layouts: 6.92 us -> 3.73 us  [the longest x1 1.25 us: per_device(): lax.dynamic_index_in_dim(up_late, 1 - side, 0, keepdims=False)]
    ppermute x11, starting transfers between devices: 14.1 us -> 16.9 us  [shift(): return lax.ppermute(array, 'exp', pairs)]
    ppermute x3 -> x4, starting transfers between devices: 3.6 us -> 5.17 us  [across(): return lax.ppermute(array, 'exp', [(e, e ^ 4) for e in range(N_EXP)])]
    pallas_call x1 -> x2, Pallas kernels: 6.7 us -> 6.23 us  [call(): pl.pallas_call(kernel, out_shape=out_shape, grid_spec=pltpu.PrefetchScala...]
  transfers between devices with their start and end apart: 17 -> 18, of which waited for: 8 -> 7; matrix products, arithmetic and copies ran while one was open for 9% -> 11% of each run, Pallas kernels for 0% -> 3%
where the time goes in v3:
time: 199 us; the launch traced here: 198 us
  waiting for transfers between devices  69.7 us (35%)
  starting transfers between devices  44.1 us (22%)
  blocking collectives  43.1 us (22%)
  local copies, waits for them, and re-layouts  18.3 us (9%)
  matrix products  9.04 us (5%)
  Pallas kernels  8.01 us (4%)
  other arithmetic  5.45 us (3%)
    ppermute x11, waiting for transfers between devices, shift(): return lax.ppermute(array, 'exp', pairs)  51 us
    all_to_all x2, blocking collectives, exchange(): return lax.all_to_all(array, axis, split_axis=0, concat_axis=0, tiled=True)  43.1 us
    all_to_all x3, starting transfers between devices, exchange(): return lax.all_to_all(array, axis, split_axis=0, concat_axis=0, tiled=True)  22 us
    ppermute x11, starting transfers between devices, shift(): return lax.ppermute(array, 'exp', pairs)  16.9 us
    ppermute x4, waiting for transfers between devices, across(): return lax.ppermute(array, 'exp', [(e, e ^ 4) for e in range(N_EXP)])  12.2 us
    all_to_all x3, waiting for transfers between devices, exchange(): return lax.all_to_all(array, axis, split_axis=0, concat_axis=0, tiled=True)  6.53 us
    pallas_call x2, Pallas kernels, call(): pl.pallas_call(kernel, out_shape=out_shape, grid_spec=pltpu.PrefetchScala...  6.23 us
    ppermute x4, starting transfers between devices, across(): return lax.ppermute(array, 'exp', [(e, e ^ 4) for e in range(N_EXP)])  5.17 us
  transfers between devices with their start and end apart: 18, of which 7 were waited for; matrix products, arithmetic and copies ran while one was open for 11% of the time, Pallas kernels for 3%

profile of v3, /device:TPU:4, one launch (start us, length us, event | category | flops | bytes accessed | tf_op | source)
XLA Modules:
  0.0 198.4 jit_solution(17572451835226422926)
XLA Ops:
  1.5 5.1 %all-to-all-start = ((s32[8,6,16]{2,1,0:T(8,128)}), s32[8,6,16]{2,1,0:T(8,128)S(1)}, u32[]{:S(2)}, u32[]{:S(2)}) async-start(s32[8,6,16]{2,1,0:T(8,128)} %broadcast_in_dim.36), calls=%async_computation | async-start | bytes 65536 | tf_op jit(solution)/shard_map/all_to_all | solution.py:79
  6.6 1.2 dynamic-slice_bitcast_fusion.2
  7.8 2.1 %collective-permute-start = (bf16[96,4096]{1,0:T(8,128)(2,1)S(1)}, bf16[96,4096]{1,0:T(8,128)(2,1)S(1)}, u32[]{:S(2)}, u32[]{:S(2)}) collective-permute-start(bf16[96,4096]{1,0:T(8,128)(2,1)S(1)} %dynamic-slice_bitcast_fusion.2), channel_id=1, source_target_pairs={{0,4},{1,5},{2,6},{3,7},{4,0},{5,1},{6,2},{7,3},{8,12},{9,13},{10,... | collective-permute-start | bytes 2359304 | tf_op jit(solution)/shard_map/ppermute | solution.py:88
  15.9 1.6 multiply_reduce_fusion.2
  18.5 1.5 fusion.4
  21.0 1.5 fusion.6
  24.2 2.9 %collective-permute-done.lent_gate_low = bf16[96,4096]{1,0:T(8,128)(2,1)S(1)} collective-permute-done((bf16[96,4096]{1,0:T(8,128)(2,1)S(1)}, bf16[96,4096]{1,0:T(8,128)(2,1)S(1)}, u32[]{:S(2)}, u32[]{:S(2)}) %collective-permute-start) | collective-permute-done | bytes 786464 | tf_op jit(solution)/shard_map/ppermute | solution.py:88
  27.8 5.2 %all-to-all-start.1 = ((bf16[8,12,512]{2,1,0:T(8,128)(2,1)}), bf16[8,12,512]{2,1,0:T(8,128)(2,1)S(1)}, u32[]{:S(2)}, u32[]{:S(2)}) async-start(bf16[8,12,512]{2,1,0:T(8,128)(2,1)} %bitcast.7), calls=%async_computation.1 | async-start | bytes 262144 | tf_op jit(solution)/shard_map/all_to_all | solution.py:79
  33.1 6.5 %all-to-all-done.1 = bf16[8,12,512]{2,1,0:T(8,128)(2,1)S(1)} async-done(((bf16[8,12,512]{2,1,0:T(8,128)(2,1)}), bf16[8,12,512]{2,1,0:T(8,128)(2,1)S(1)}, u32[]{:S(2)}, u32[]{:S(2)}) %all-to-all-start.1) | async-done | bytes 98336 | tf_op jit(solution)/shard_map/all_to_all | solution.py:79
  39.6 1.3 convolution_convert_fusion
  40.9 11.6 %all-to-all-start.2 = ((bf16[32,24,512]{2,1,0:T(8,128)(2,1)}), bf16[32,24,512]{2,1,0:T(8,128)(2,1)}, u32[]{:S(2)}, u32[]{:S(2)}) async-start(bf16[32,24,512]{2,1,0:T(8,128)(2,1)} %bitcast.9), calls=%async_computation.2 | async-start | bytes 1572864 | tf_op jit(solution)/shard_map/all_to_all | solution.py:79
  52.5 2.2 %constant_dynamic-slice_fusion.1 = (bf16[1,192,1024]{2,1,0:T(8,128)(2,1)S(1)}, bf16[1,192,1024]{2,1,0:T(8,128)(2,1)S(1)}, bf16[1,192,1024]{2,1,0:T(8,128)(2,1)S(...) fusion(bf16[2,192,4096]{2,1,0:T(8,128)(2,1)} %param.27, ...), kind=kLoop, calls=%fused_computation.100 | loop fusion | bytes 6291480 | tf_op jit(solution)/shard_map/dynamic_slice | solution.py:326
  55.5 2.8 %collective-permute-start.2 = (bf16[2,192,1024]{2,1,0:T(8,128)(2,1)S(1)}, bf16[2,192,1024]{2,1,0:T(8,128)(2,1)S(1)}, u32[]{:S(2)}, u32[]{:S(2)}) collective-permute-start(bf16[2,192,1024]{2,1,0:T(8,128)(2,1)S(1)} %pad_maximum_fusion.3), channel_id=1, source_target_pairs={{0,3},{1,0},{2,1},{3,2},{4,7},{5,4},{6,5},{7,6},{8,11},{9,8},{10,9... | collective-permute-start | bytes 2359304 | tf_op jit(solution)/shard_map/ppermute | solution.py:84
  58.4 1.2 dynamic-slice_bitcast_fusion.1
  60.4 1.3 dynamic-slice_bitcast_fusion
  61.7 1.3 collective-permute-start.9
  63.1 29.4 %collective-permute-done.1.w_below = bf16[2,192,1024]{2,1,0:T(8,128)(2,1)S(1)} collective-permute-done((bf16[2,192,1024]{2,1,0:T(8,128)(2,1)S(1)}, bf16[2,192,1024]{2,1,0:T(8,128)(2,1)S(1)}, u32[]{:S(2)}, u32[]{:S(2)}) %collective-permute-start.1) | collective-permute-done | bytes 786464 | tf_op jit(solution)/shard_map/ppermute | solution.py:84
  96.1 1.5 copy.130
  98.7 3.2 %collective-permute-start.7 = (bf16[384,1024]{1,0:T(8,128)(2,1)S(1)}, bf16[384,1024]{1,0:T(8,128)(2,1)S(1)}, u32[]{:S(2)}, u32[]{:S(2)}) collective-permute-start(bf16[384,1024]{1,0:T(8,128)(2,1)S(1)} %bitcast.131), channel_id=1, source_target_pairs={{0,3},{1,0},{2,1},{3,2},{4,7},{5,4},{6,5},{7,6},{8,11},{9,8},{10,9... | collective-permute-start | bytes 2359304 | tf_op jit(solution)/shard_map/ppermute | solution.py:84
  102.2 0.9 collective-permute-start.14
  103.2 14.4 %collective-permute-done.5.below_rows = bf16[384,1024]{1,0:T(8,128)(2,1)S(1)} collective-permute-done((bf16[384,1024]{1,0:T(8,128)(2,1)S(1)}, bf16[384,1024]{1,0:T(8,128)(2,1)S(1)}, u32[]{:S(2)}, u32[]{:S(2)}) %collective-permute-start.5) | collective-permute-done | bytes 786464 | tf_op jit(solution)/shard_map/ppermute | solution.py:84
  117.8 3.3 %collective-permute-start.8 = (bf16[192,1024]{1,0:T(8,128)(2,1)S(1)}, bf16[192,1024]{1,0:T(8,128)(2,1)S(1)}, u32[]{:S(2)}, u32[]{:S(2)}) collective-permute-start(bf16[192,1024]{1,0:T(8,128)(2,1)S(1)} %slice.83), channel_id=1, source_target_pairs={{0,3},{1,0},{2,1},{3,2},{4,7},{5,4},{6,5},{7,6},{8,11},{9,8},{10,9... | collective-permute-start | bytes 1179656 | tf_op jit(solution)/shard_map/ppermute | solution.py:84
  121.1 4.5 %expand_near.1 = (f32[384,384]{1,0:T(8,128)S(1)}, f32[384,384]{1,0:T(8,128)S(1)}) custom-call(s32[2]{0:T(128)S(1)} %pad_add_fusion.1.where, bf16[384,1024]{1,0:T(8,128)(2,1)S(1)} %bitcast.132, bf16[384,1024]{1,0:T(8,128)(2,1)S(1)} %collective-permute-done.5.below_rows, bf16[384,1024]{1,0:T(8,128)(2,1)S(1)} %collective-permute-done.7.above_rows, ...), custom_call_target="tpu_custom_call" | custom-call | flops 1811939328 | bytes 8257536 | tf_op jit(solution)/shard_map/expand_near/pallas_call | solution.py:213
  125.6 1.7 collective-permute-done.6.far_low
  127.3 1.8 expand_far.1.own
  129.9 2.5 %collective-permute-start.11 = (bf16[384,384]{1,0:T(8,128)(2,1)S(1)}, bf16[384,384]{1,0:T(8,128)(2,1)S(1)}, u32[]{:S(2)}, u32[]{:S(2)}) collective-permute-start(bf16[384,384]{1,0:T(8,128)(2,1)S(1)} %expand_far.1.own), channel_id=1, source_target_pairs={{0,3},{1,0},{2,1},{3,2},{4,7},{5,4},{6,5},{7,6},{8,11},{9,8},{10,9... | collective-permute-start | bytes 884744 | tf_op jit(solution)/shard_map/ppermute | solution.py:84
  132.4 5.4 %collective-permute-done.10.below = bf16[384,384]{1,0:T(8,128)(2,1)S(1)} collective-permute-done((bf16[384,384]{1,0:T(8,128)(2,1)S(1)}, bf16[384,384]{1,0:T(8,128)(2,1)S(1)}, u32[]{:S(2)}, u32[]{:S(2)}) %collective-permute-start.10) | collective-permute-done | bytes 294944 | tf_op jit(solution)/shard_map/ppermute | solution.py:84
  138.0 3.4 %collective-permute-start.13 = (bf16[192,384]{1,0:T(8,128)(2,1)S(1)}, bf16[192,384]{1,0:T(8,128)(2,1)S(1)}, u32[]{:S(2)}, u32[]{:S(2)}) collective-permute-start(bf16[192,384]{1,0:T(8,128)(2,1)S(1)} %slice.85), channel_id=1, source_target_pairs={{0,3},{1,0},{2,1},{3,2},{4,7},{5,4},{6,5},{7,6},{8,11},{9,8},{10,9... | collective-permute-start | bytes 442376 | tf_op jit(solution)/shard_map/ppermute | solution.py:84
  141.3 9.3 %collective-permute-done.14.lent = bf16[768,1024]{1,0:T(8,128)(2,1)S(1)} collective-permute-done((bf16[768,1024]{1,0:T(8,128)(2,1)S(1)}, bf16[768,1024]{1,0:T(8,128)(2,1)S(1)}, u32[]{:S(2)}, u32[]{:S(2)}) %collective-permute-start.14) | collective-permute-done | bytes 1572896 | tf_op jit(solution)/shard_map/ppermute | solution.py:88
  150.6 1.8 contract.1
  153.7 32.4 %all_to_all.25 = bf16[32,24,512]{2,1,0:T(8,128)(2,1)S(1)} all-to-all(bf16[32,24,512]{2,1,0:T(8,128)(2,1)S(1)} %copy.133), channel_id=1, replica_groups=mesh['rep'=32,'exp'=8] {'rep'}, dimensions={0} | all-to-all | bytes 1572864 | tf_op jit(solution)/shard_map/all_to_all | solution.py:79
  186.6 10.7 %all_to_all.26 = bf16[8,12,512]{2,1,0:T(8,128)(2,1)S(1)} all-to-all(bf16[8,12,512]{2,1,0:T(8,128)(2,1)S(1)} %reshape.277), channel_id=1, replica_groups=mesh['rep'=32,'exp'=8] {'exp'}, dimensions={0} | all-to-all | bytes 196608 | tf_op jit(solution)/shard_map/all_to_all | solution.py:79
  (148 shorter events, 22.0 us)
Async XLA Ops:
  0.0 15.2 %copy-start = (bf16[2,1024,256]{2,1,0:T(8,128)(2,1)S(1)}, bf16[2,1024,256]{2,1,0:T(8,128)(2,1)}, u32[]{:S(2)}) copy-start(bf16[2,1024,256]{2,1,0:T(8,128)(2,1)} %param.17) | copy-start | bytes 3145732
  0.0 17.6 %copy-start.17 = (bf16[4096]{0:T(1024)(128)(2,1)S(1)}, bf16[4096]{0:T(1024)(128)(2,1)}, u32[]{:S(2)}) copy-start(bf16[4096]{0:T(1024)(128)(2,1)} %param.22) | copy-start | bytes 24580
  1.5 22.1 %all-to-all-start = ((s32[8,6,16]{2,1,0:T(8,128)}), s32[8,6,16]{2,1,0:T(8,128)S(1)}, u32[]{:S(2)}, u32[]{:S(2)}) async-start(s32[8,6,16]{2,1,0:T(8,128)} %broadcast_in_dim.36), calls=%async_computation | async-start | bytes 65536 | tf_op jit(solution)/shard_map/all_to_all | solution.py:79
  7.8 19.3 %collective-permute-start = (bf16[96,4096]{1,0:T(8,128)(2,1)S(1)}, bf16[96,4096]{1,0:T(8,128)(2,1)S(1)}, u32[]{:S(2)}, u32[]{:S(2)}) collective-permute-start(bf16[96,4096]{1,0:T(8,128)(2,1)S(1)} %dynamic-slice_bitcast_fusion.2), channel_id=1, source_target_pairs={{0,4},{1,5},{2,6},{3,7},{4,0},{5,1},{6,2},{7,3},{8,12},{9,13},{10,... | collective-permute-start | bytes 2359304 | tf_op jit(solution)/shard_map/ppermute | solution.py:88
  18.3 4.3 %slice-start.1 = ((bf16[3,2,256]{2,1,0:T(2,128)(2,1)}), bf16[2,2,256]{2,1,0:T(2,128)(2,1)S(1)}, s32[]{:S(2)}) async-start(bf16[3,2,256]{2,1,0:T(2,128)(2,1)} %param.20), calls=%async_computation.6 | async-start | bytes 4096 | tf_op jit(solution)/shard_map/slice | solution.py:40
  18.5 4.7 %copy-start.14 = (bf16[3,2,4096]{2,1,0:T(2,128)(2,1)S(1)}, bf16[3,2,4096]{2,1,0:T(2,128)(2,1)}, u32[]{:S(2)}) copy-start(bf16[3,2,4096]{2,1,0:T(2,128)(2,1)} %param.15) | copy-start | bytes 147460
  20.1 13.0 %copy-start.15 = (f32[96,24]{0,1:T(8,128)S(1)}, f32[96,24]{0,1:T(8,128)}, u32[]{:S(2)}) copy-start(f32[96,24]{0,1:T(8,128)} %constant.103) | copy-start | bytes 27652
  27.1 27.6 %copy-start.4 = (bf16[96,4096]{1,0:T(8,128)(2,1)}, bf16[96,4096]{1,0:T(8,128)(2,1)S(1)}, u32[]{:S(2)}) copy-start(bf16[96,4096]{1,0:T(8,128)(2,1)S(1)} %collective-permute-done.lent_gate_low) | copy-start | bytes 2359300
  27.8 11.8 %all-to-all-start.1 = ((bf16[8,12,512]{2,1,0:T(8,128)(2,1)}), bf16[8,12,512]{2,1,0:T(8,128)(2,1)S(1)}, u32[]{:S(2)}, u32[]{:S(2)}) async-start(bf16[8,12,512]{2,1,0:T(8,128)(2,1)} %bitcast.7), calls=%async_computation.1 | async-start | bytes 262144 | tf_op jit(solution)/shard_map/all_to_all | solution.py:79
  40.9 55.2 %all-to-all-start.2 = ((bf16[32,24,512]{2,1,0:T(8,128)(2,1)}), bf16[32,24,512]{2,1,0:T(8,128)(2,1)}, u32[]{:S(2)}, u32[]{:S(2)}) async-start(bf16[32,24,512]{2,1,0:T(8,128)(2,1)} %bitcast.9), calls=%async_computation.2 | async-start | bytes 1572864 | tf_op jit(solution)/shard_map/all_to_all | solution.py:79
  54.7 5.7 %copy-start.2 = (bf16[2,192,4096]{2,1,0:T(8,128)(2,1)S(1)}, bf16[2,192,4096]{2,1,0:T(8,128)(2,1)}, u32[]{:S(2)}) copy-start(bf16[2,192,4096]{2,1,0:T(8,128)(2,1)} %own_up.3) | copy-start | bytes 9437188
  54.8 37.7 %collective-permute-start.1 = (bf16[2,192,1024]{2,1,0:T(8,128)(2,1)S(1)}, bf16[2,192,1024]{2,1,0:T(8,128)(2,1)S(1)}, u32[]{:S(2)}, u32[]{:S(2)}) collective-permute-start(bf16[2,192,1024]{2,1,0:T(8,128)(2,1)S(1)} %pad_maximum_fusion.2), channel_id=1, source_target_pairs={{0,1},{1,2},{2,3},{3,0},{4,5},{5,6},{6,7},{7,4},{8,9},{9,10},{10,1... | collective-permute-start | bytes 2359304 | tf_op jit(solution)/shard_map/ppermute | solution.py:84
  55.5 37.1 %collective-permute-start.2 = (bf16[2,192,1024]{2,1,0:T(8,128)(2,1)S(1)}, bf16[2,192,1024]{2,1,0:T(8,128)(2,1)S(1)}, u32[]{:S(2)}, u32[]{:S(2)}) collective-permute-start(bf16[2,192,1024]{2,1,0:T(8,128)(2,1)S(1)} %pad_maximum_fusion.3), channel_id=1, source_target_pairs={{0,3},{1,0},{2,1},{3,2},{4,7},{5,4},{6,5},{7,6},{8,11},{9,8},{10,9... | collective-permute-start | bytes 2359304 | tf_op jit(solution)/shard_map/ppermute | solution.py:84
  58.3 35.1 %collective-permute-start.3 = (bf16[2,192,1024]{2,1,0:T(8,128)(2,1)S(1)}, bf16[2,192,1024]{2,1,0:T(8,128)(2,1)S(1)}, u32[]{:S(2)}, u32[]{:S(2)}) collective-permute-start(bf16[2,192,1024]{2,1,0:T(8,128)(2,1)S(1)} %pad_maximum_fusion.4), channel_id=1, source_target_pairs={{0,2},{1,3},{2,0},{3,1},{4,6},{5,7},{6,4},{7,5},{8,10},{9,11},{10,... | collective-permute-start | bytes 2359304 | tf_op jit(solution)/shard_map/ppermute | solution.py:84
  59.6 35.6 %collective-permute-start.4 = (bf16[96,4096]{1,0:T(8,128)(2,1)S(1)}, bf16[96,4096]{1,0:T(8,128)(2,1)S(1)}, u32[]{:S(2)}, u32[]{:S(2)}) collective-permute-start(bf16[96,4096]{1,0:T(8,128)(2,1)S(1)} %dynamic-slice_bitcast_fusion.1), channel_id=1, source_target_pairs={{0,4},{1,5},{2,6},{3,7},{4,0},{5,1},{6,2},{7,3},{8,12},{9,13},{10,... | collective-permute-start | bytes 2359304 | tf_op jit(solution)/shard_map/ppermute | solution.py:88
  61.7 59.5 %collective-permute-start.9 = (bf16[192,4096]{1,0:T(8,128)(2,1)}, bf16[192,4096]{1,0:T(8,128)(2,1)S(1)}, u32[]{:S(2)}, u32[]{:S(2)}) collective-permute-start(bf16[192,4096]{1,0:T(8,128)(2,1)} %dynamic-slice_bitcast_fusion), channel_id=1, source_target_pairs={{0,4},{1,5},{2,6},{3,7},{4,0},{5,1},{6,2},{7,3},{8,12},{9,13},{10,... | collective-permute-start | bytes 4718600 | tf_op jit(solution)/shard_map/ppermute | solution.py:88
  96.1 5.8 %copy-start.13 = (bf16[2,192,1024]{2,1,0:T(8,128)(2,1)S(1)}, bf16[2,192,1024]{2,1,0:T(8,128)(2,1)}, u32[]{:S(2)}) copy-start(bf16[2,192,1024]{2,1,0:T(8,128)(2,1)} %copy-done.12) | copy-start | bytes 2359300
  96.1 5.8 %copy-start.11 = (bf16[2,192,1024]{2,1,0:T(8,128)(2,1)S(1)}, bf16[2,192,1024]{2,1,0:T(8,128)(2,1)}, u32[]{:S(2)}) copy-start(bf16[2,192,1024]{2,1,0:T(8,128)(2,1)} %copy-done.10) | copy-start | bytes 2359300
  96.1 5.9 %copy-start.9 = (bf16[2,192,1024]{2,1,0:T(8,128)(2,1)S(1)}, bf16[2,192,1024]{2,1,0:T(8,128)(2,1)}, u32[]{:S(2)}) copy-start(bf16[2,192,1024]{2,1,0:T(8,128)(2,1)} %copy-done.8) | copy-start | bytes 2359300
  98.6 19.0 %collective-permute-start.5 = (bf16[384,1024]{1,0:T(8,128)(2,1)S(1)}, bf16[384,1024]{1,0:T(8,128)(2,1)S(1)}, u32[]{:S(2)}, u32[]{:S(2)}) collective-permute-start(bf16[384,1024]{1,0:T(8,128)(2,1)S(1)} %bitcast.130), channel_id=1, source_target_pairs={{0,1},{1,2},{2,3},{3,0},{4,5},{5,6},{6,7},{7,4},{8,9},{9,10},{10,1... | collective-permute-start | bytes 2359304 | tf_op jit(solution)/shard_map/ppermute | solution.py:84
  98.7 19.0 %collective-permute-start.7 = (bf16[384,1024]{1,0:T(8,128)(2,1)S(1)}, bf16[384,1024]{1,0:T(8,128)(2,1)S(1)}, u32[]{:S(2)}, u32[]{:S(2)}) collective-permute-start(bf16[384,1024]{1,0:T(8,128)(2,1)S(1)} %bitcast.131), channel_id=1, source_target_pairs={{0,3},{1,0},{2,1},{3,2},{4,7},{5,4},{6,5},{7,6},{8,11},{9,8},{10,9... | collective-permute-start | bytes 2359304 | tf_op jit(solution)/shard_map/ppermute | solution.py:84
  101.9 19.2 %copy-start.7 = (bf16[96,4096]{1,0:T(8,128)(2,1)S(1)}, bf16[96,4096]{1,0:T(8,128)(2,1)}, u32[]{:S(2)}) copy-start(bf16[96,4096]{1,0:T(8,128)(2,1)} %copy-done.6) | copy-start | bytes 2359300
  101.9 19.2 %copy-start.5 = (bf16[96,4096]{1,0:T(8,128)(2,1)S(1)}, bf16[96,4096]{1,0:T(8,128)(2,1)}, u32[]{:S(2)}) copy-start(bf16[96,4096]{1,0:T(8,128)(2,1)} %copy-done.4) | copy-start | bytes 2359300
  102.0 19.1 %copy-start.1 = (bf16[2,192,4096]{2,1,0:T(8,128)(2,1)S(1)}, bf16[2,192,4096]{2,1,0:T(8,128)(2,1)}, u32[]{:S(2)}) copy-start(bf16[2,192,4096]{2,1,0:T(8,128)(2,1)} %own_gate.3) | copy-start | bytes 9437188
  102.0 19.1 %copy-start.3 = (bf16[2,192,4096]{2,1,0:T(8,128)(2,1)S(1)}, bf16[2,192,4096]{2,1,0:T(8,128)(2,1)}, u32[]{:S(2)}) copy-start(bf16[2,192,4096]{2,1,0:T(8,128)(2,1)} %own_up.3) | copy-start | bytes 9437188
  102.2 48.4 %collective-permute-start.14 = (bf16[768,1024]{1,0:T(8,128)(2,1)S(1)}, bf16[768,1024]{1,0:T(8,128)(2,1)S(1)}, u32[]{:S(2)}, u32[]{:S(2)}) collective-permute-start(bf16[768,1024]{1,0:T(8,128)(2,1)S(1)} %pad_maximum_fusion), channel_id=1, source_target_pairs={{0,4},{1,5},{2,6},{3,7},{4,0},{5,1},{6,2},{7,3},{8,12},{9,13},{10,... | collective-permute-start | bytes 4718600 | tf_op jit(solution)/shard_map/ppermute | solution.py:88
  117.6 9.7 %collective-permute-start.6 = (bf16[192,1024]{1,0:T(8,128)(2,1)S(1)}, bf16[192,1024]{1,0:T(8,128)(2,1)S(1)}, u32[]{:S(2)}, u32[]{:S(2)}) collective-permute-start(bf16[192,1024]{1,0:T(8,128)(2,1)S(1)} %slice.82), channel_id=1, source_target_pairs={{0,1},{1,2},{2,3},{3,0},{4,5},{5,6},{6,7},{7,4},{8,9},{9,10},{10,1... | collective-permute-start | bytes 1179656 | tf_op jit(solution)/shard_map/ppermute | solution.py:84
  117.8 9.5 %collective-permute-start.8 = (bf16[192,1024]{1,0:T(8,128)(2,1)S(1)}, bf16[192,1024]{1,0:T(8,128)(2,1)S(1)}, u32[]{:S(2)}, u32[]{:S(2)}) collective-permute-start(bf16[192,1024]{1,0:T(8,128)(2,1)S(1)} %slice.83), channel_id=1, source_target_pairs={{0,3},{1,0},{2,1},{3,2},{4,7},{5,4},{6,5},{7,6},{8,11},{9,8},{10,9... | collective-permute-start | bytes 1179656 | tf_op jit(solution)/shard_map/ppermute | solution.py:84
  129.0 8.8 %collective-permute-start.10 = (bf16[384,384]{1,0:T(8,128)(2,1)S(1)}, bf16[384,384]{1,0:T(8,128)(2,1)S(1)}, u32[]{:S(2)}, u32[]{:S(2)}) collective-permute-start(bf16[384,384]{1,0:T(8,128)(2,1)S(1)} %expand_far.1.own), channel_id=1, source_target_pairs={{0,1},{1,2},{2,3},{3,0},{4,5},{5,6},{6,7},{7,4},{8,9},{9,10},{10,1... | collective-permute-start | bytes 884744 | tf_op jit(solution)/shard_map/ppermute | solution.py:84
  129.9 8.0 %collective-permute-start.11 = (bf16[384,384]{1,0:T(8,128)(2,1)S(1)}, bf16[384,384]{1,0:T(8,128)(2,1)S(1)}, u32[]{:S(2)}, u32[]{:S(2)}) collective-permute-start(bf16[384,384]{1,0:T(8,128)(2,1)S(1)} %expand_far.1.own), channel_id=1, source_target_pairs={{0,3},{1,0},{2,1},{3,2},{4,7},{5,4},{6,5},{7,6},{8,11},{9,8},{10,9... | collective-permute-start | bytes 884744 | tf_op jit(solution)/shard_map/ppermute | solution.py:84
  137.8 12.8 %collective-permute-start.12 = (bf16[192,384]{1,0:T(8,128)(2,1)S(1)}, bf16[192,384]{1,0:T(8,128)(2,1)S(1)}, u32[]{:S(2)}, u32[]{:S(2)}) collective-permute-start(bf16[192,384]{1,0:T(8,128)(2,1)S(1)} %slice.84), channel_id=1, source_target_pairs={{0,1},{1,2},{2,3},{3,0},{4,5},{5,6},{6,7},{7,4},{8,9},{9,10},{10,1... | collective-permute-start | bytes 442376 | tf_op jit(solution)/shard_map/ppermute | solution.py:84
  138.0 12.7 %collective-permute-start.13 = (bf16[192,384]{1,0:T(8,128)(2,1)S(1)}, bf16[192,384]{1,0:T(8,128)(2,1)S(1)}, u32[]{:S(2)}, u32[]{:S(2)}) collective-permute-start(bf16[192,384]{1,0:T(8,128)(2,1)S(1)} %slice.85), channel_id=1, source_target_pairs={{0,3},{1,0},{2,1},{3,2},{4,7},{5,4},{6,5},{7,6},{8,11},{9,8},{10,9... | collective-permute-start | bytes 442376 | tf_op jit(solution)/shard_map/ppermute | solution.py:84
  (6 other events, 10.6 us)

commit v4 on v3

--- a/solution.py
+++ b/solution.py
@@ -307,17 +307,10 @@
     normed = jnp.broadcast_to(
         normed.reshape(1, 4, 2 * LOCAL, HALF), (2, 4, 2 * LOCAL, HALF)
     ).reshape(N_EXP, 2 * LOCAL, HALF)
-    normed, lent_gate_low = lax.optimization_barrier((normed, lent_gate_low))
+    normed, lent_gate_low, gate_late, down_late = lax.optimization_barrier(
+        (normed, lent_gate_low, gate_weight, down_weight)
+    )
     tokens = exchange(normed, "exp").reshape(KEYS, HALF)
-    table, combine = routing_tables(routing[:, :TOPK], routing[:, TOPK:], side, groups)
-    outbound = lax.dot_general(
-        table, tokens, (((0,), (0,)), ((), ())), preferred_element_type=jnp.float32
-    ).astype(jnp.bfloat16)
-
-    outbound, gate_late, up_late, down_late = lax.optimization_barrier(
-        (outbound, gate_weight, up_weight, down_weight)
-    )
-    inbound = exchange(outbound.reshape(groups, WIRE, HALF), "rep")
 
     def quarter(step):
         start = (place + step) % 4 * BLK
@@ -330,6 +323,14 @@
 
     kept = [quarter(0)] + [shift(quarter(step), step) for step in (1, -1, 2)]
     lent_gate_high = across(lax.dynamic_slice(gate_late, (1 - side, half, 0), (1, half, D))[0])
+
+    table, combine = routing_tables(routing[:, :TOPK], routing[:, TOPK:], side, groups)
+    outbound = lax.dot_general(
+        table, tokens, (((0,), (0,)), ((), ())), preferred_element_type=jnp.float32
+    ).astype(jnp.bfloat16)
+
+    outbound, up_late = lax.optimization_barrier((outbound, up_weight))
+    inbound = exchange(outbound.reshape(groups, WIRE, HALF), "rep")
     lent_up = across(lax.dynamic_index_in_dim(up_late, 1 - side, 0, keepdims=False))
     inbound, kept, lent_gate_high = lax.optimization_barrier((inbound, kept, lent_gate_high))
     lent_down = across(jnp.concatenate([block[1] for block in kept]))

time: 199 us -> 200 us (level)
  waiting for transfers between devices: 69.7 us -> 65.2 us
  other arithmetic: 5.45 us -> 8.46 us
    all_to_all x3, waiting for transfers between devices: 6.53 us -> 3.25 us  [exchange(): return lax.all_to_all(array, axis, split_axis=0, concat_axis=0, tiled=True)]
    unnamed x45 -> x59, local copies, waits for them, and re-layouts: 4.6 us -> 4.68 us
  transfers between devices with their start and end apart: 18 -> 18, of which waited for: 7 -> 7; matrix products, arithmetic and copies ran while one was open for 11% -> 14% of each run, Pallas kernels for 3% -> 3%
where the time goes in v4:
time: 200 us; the launch traced here: 199 us
  waiting for transfers between devices  65.2 us (33%)
  starting transfers between devices  44.1 us (22%)
  blocking collectives  42.6 us (21%)
  local copies, waits for them, and re-layouts  20.2 us (10%)
  matrix products  9.99 us (5%)
  other arithmetic  8.46 us (4%)
  Pallas kernels  8.01 us (4%)
    ppermute x11, waiting for transfers between devices, shift(): return lax.ppermute(array, 'exp', pairs)  50.9 us
    all_to_all x2, blocking collectives, exchange(): return lax.all_to_all(array, axis, split_axis=0, concat_axis=0, tiled=True)  42.6 us
    all_to_all x3, starting transfers between devices, exchange(): return lax.all_to_all(array, axis, split_axis=0, concat_axis=0, tiled=True)  22 us
    ppermute x11, starting transfers between devices, shift(): return lax.ppermute(array, 'exp', pairs)  16.9 us
    ppermute x4, waiting for transfers between devices, across(): return lax.ppermute(array, 'exp', [(e, e ^ 4) for e in range(N_EXP)])  11 us
    pallas_call x2, Pallas kernels, call(): pl.pallas_call(kernel, out_shape=out_shape, grid_spec=pltpu.PrefetchScala...  6.23 us
    ppermute x4, starting transfers between devices, across(): return lax.ppermute(array, 'exp', [(e, e ^ 4) for e in range(N_EXP)])  5.17 us
    dot_general x3, matrix products, attend_rows(): jnp.einsum('sjgt,stjd->sjgd', old_probs, cached_values, preferred_element...  4.71 us
  transfers between devices with their start and end apart: 18, of which 7 were waited for; matrix products, arithmetic and copies ran while one was open for 14% of the time, Pallas kernels for 3%

profile of v4, /device:TPU:4, one launch (start us, length us, event | category | flops | bytes accessed | tf_op | source)
XLA Modules:
  0.0 199.3 jit_solution(9165546697598889546)
XLA Ops:
  1.5 5.1 %all-to-all-start = ((s32[8,6,16]{2,1,0:T(8,128)}), s32[8,6,16]{2,1,0:T(8,128)S(1)}, u32[]{:S(2)}, u32[]{:S(2)}) async-start(s32[8,6,16]{2,1,0:T(8,128)} %broadcast_in_dim.36), calls=%async_computation | async-start | bytes 65536 | tf_op jit(solution)/shard_map/all_to_all | solution.py:79
  6.6 1.2 dynamic-slice_bitcast_fusion.2
  7.8 2.1 %collective-permute-start = (bf16[96,4096]{1,0:T(8,128)(2,1)S(1)}, bf16[96,4096]{1,0:T(8,128)(2,1)S(1)}, u32[]{:S(2)}, u32[]{:S(2)}) collective-permute-start(bf16[96,4096]{1,0:T(8,128)(2,1)S(1)} %dynamic-slice_bitcast_fusion.2), channel_id=1, source_target_pairs={{0,4},{1,5},{2,6},{3,7},{4,0},{5,1},{6,2},{7,3},{8,12},{9,13},{10,... | collective-permute-start | bytes 2359304 | tf_op jit(solution)/shard_map/ppermute | solution.py:88
  15.9 1.6 multiply_reduce_fusion.2
  18.5 1.5 fusion.4
  21.0 1.5 fusion.6
  26.1 1.0 collective-permute-done.lent_gate_low
  27.8 5.2 %all-to-all-start.1 = ((bf16[8,12,512]{2,1,0:T(8,128)(2,1)}), bf16[8,12,512]{2,1,0:T(8,128)(2,1)S(1)}, u32[]{:S(2)}, u32[]{:S(2)}) async-start(bf16[8,12,512]{2,1,0:T(8,128)(2,1)} %bitcast.7), calls=%async_computation.1 | async-start | bytes 262144 | tf_op jit(solution)/shard_map/all_to_all | solution.py:79
  33.0 3.3 %constant_dynamic-slice_fusion.1 = (bf16[1,192,1024]{2,1,0:T(8,128)(2,1)S(1)}, bf16[1,192,1024]{2,1,0:T(8,128)(2,1)S(1)}, bf16[1,192,1024]{2,1,0:T(8,128)(2,1)},...) fusion(bf16[2,192,4096]{2,1,0:T(8,128)(2,1)} %param.27, ...), kind=kLoop, calls=%fused_computation.100 | loop fusion | bytes 6291480 | tf_op jit(solution)/shard_map/dynamic_slice | solution.py:319
  36.4 3.2 %all-to-all-done.1 = bf16[8,12,512]{2,1,0:T(8,128)(2,1)S(1)} async-done(((bf16[8,12,512]{2,1,0:T(8,128)(2,1)}), bf16[8,12,512]{2,1,0:T(8,128)(2,1)S(1)}, u32[]{:S(2)}, u32[]{:S(2)}) %all-to-all-start.1) | async-done | bytes 98336 | tf_op jit(solution)/shard_map/all_to_all | solution.py:79
  40.3 2.2 %convolution_convert_fusion = bf16[768,512]{1,0:T(8,128)(2,1)} fusion(bf16[96,768]{0,1:T(8,128)(2,1)} %bitcast.136, bf16[96,512]{1,0:T(8,128)(2,1)} %reshape.271), kind=kOutput, calls=%fused_computation.2 | convolution fusion | flops 75890688 | bytes 1032192 | tf_op jit(solution)/shard_map/dot_general | solution.py:328
  42.5 11.6 %all-to-all-start.2 = ((bf16[32,24,512]{2,1,0:T(8,128)(2,1)}), bf16[32,24,512]{2,1,0:T(8,128)(2,1)}, u32[]{:S(2)}, u32[]{:S(2)}) async-start(bf16[32,24,512]{2,1,0:T(8,128)(2,1)} %bitcast.9), calls=%async_computation.2 | async-start | bytes 1572864 | tf_op jit(solution)/shard_map/all_to_all | solution.py:79
  54.1 1.2 pad_maximum_fusion.2
  56.0 2.8 %collective-permute-start.2 = (bf16[2,192,1024]{2,1,0:T(8,128)(2,1)S(1)}, bf16[2,192,1024]{2,1,0:T(8,128)(2,1)S(1)}, u32[]{:S(2)}, u32[]{:S(2)}) collective-permute-start(bf16[2,192,1024]{2,1,0:T(8,128)(2,1)S(1)} %pad_maximum_fusion.3), channel_id=1, source_target_pairs={{0,3},{1,0},{2,1},{3,2},{4,7},{5,4},{6,5},{7,6},{8,11},{9,8},{10,9... | collective-permute-start | bytes 2359304 | tf_op jit(solution)/shard_map/ppermute | solution.py:84
  59.0 1.2 dynamic-slice_bitcast_fusion.1
  61.0 1.3 dynamic-slice_bitcast_fusion
  62.3 1.3 collective-permute-start.9
  63.7 29.4 %collective-permute-done.1.w_below = bf16[2,192,1024]{2,1,0:T(8,128)(2,1)S(1)} collective-permute-done((bf16[2,192,1024]{2,1,0:T(8,128)(2,1)S(1)}, bf16[2,192,1024]{2,1,0:T(8,128)(2,1)S(1)}, u32[]{:S(2)}, u32[]{:S(2)}) %collective-permute-start.1) | collective-permute-done | bytes 786464 | tf_op jit(solution)/shard_map/ppermute | solution.py:84
  96.7 1.5 copy.130
  99.2 3.2 %collective-permute-start.7 = (bf16[384,1024]{1,0:T(8,128)(2,1)S(1)}, bf16[384,1024]{1,0:T(8,128)(2,1)S(1)}, u32[]{:S(2)}, u32[]{:S(2)}) collective-permute-start(bf16[384,1024]{1,0:T(8,128)(2,1)S(1)} %bitcast.131), channel_id=1, source_target_pairs={{0,3},{1,0},{2,1},{3,2},{4,7},{5,4},{6,5},{7,6},{8,11},{9,8},{10,9... | collective-permute-start | bytes 2359304 | tf_op jit(solution)/shard_map/ppermute | solution.py:84
  103.7 14.4 %collective-permute-done.5.below_rows = bf16[384,1024]{1,0:T(8,128)(2,1)S(1)} collective-permute-done((bf16[384,1024]{1,0:T(8,128)(2,1)S(1)}, bf16[384,1024]{1,0:T(8,128)(2,1)S(1)}, u32[]{:S(2)}, u32[]{:S(2)}) %collective-permute-start.5) | collective-permute-done | bytes 786464 | tf_op jit(solution)/shard_map/ppermute | solution.py:84
  118.3 3.3 %collective-permute-start.8 = (bf16[192,1024]{1,0:T(8,128)(2,1)S(1)}, bf16[192,1024]{1,0:T(8,128)(2,1)S(1)}, u32[]{:S(2)}, u32[]{:S(2)}) collective-permute-start(bf16[192,1024]{1,0:T(8,128)(2,1)S(1)} %slice.83), channel_id=1, source_target_pairs={{0,3},{1,0},{2,1},{3,2},{4,7},{5,4},{6,5},{7,6},{8,11},{9,8},{10,9... | collective-permute-start | bytes 1179656 | tf_op jit(solution)/shard_map/ppermute | solution.py:84
  121.7 4.5 %expand_near.1 = (f32[384,384]{1,0:T(8,128)S(1)}, f32[384,384]{1,0:T(8,128)S(1)}) custom-call(s32[2]{0:T(128)S(1)} %pad_add_fusion.1.where, bf16[384,1024]{1,0:T(8,128)(2,1)S(1)} %bitcast.132, bf16[384,1024]{1,0:T(8,128)(2,1)S(1)} %collective-permute-done.5.below_rows, bf16[384,1024]{1,0:T(8,128)(2,1)S(1)} %collective-permute-done.7.above_rows, ...), custom_call_target="tpu_custom_call" | custom-call | flops 1811939328 | bytes 8257536 | tf_op jit(solution)/shard_map/expand_near/pallas_call | solution.py:213
  126.2 1.6 collective-permute-done.6.far_low
  127.8 1.8 expand_far.1.own
  130.4 2.5 %collective-permute-start.11 = (bf16[384,384]{1,0:T(8,128)(2,1)S(1)}, bf16[384,384]{1,0:T(8,128)(2,1)S(1)}, u32[]{:S(2)}, u32[]{:S(2)}) collective-permute-start(bf16[384,384]{1,0:T(8,128)(2,1)S(1)} %expand_far.1.own), channel_id=1, source_target_pairs={{0,3},{1,0},{2,1},{3,2},{4,7},{5,4},{6,5},{7,6},{8,11},{9,8},{10,9... | collective-permute-start | bytes 884744 | tf_op jit(solution)/shard_map/ppermute | solution.py:84
  132.9 5.4 %collective-permute-done.10.below = bf16[384,384]{1,0:T(8,128)(2,1)S(1)} collective-permute-done((bf16[384,384]{1,0:T(8,128)(2,1)S(1)}, bf16[384,384]{1,0:T(8,128)(2,1)S(1)}, u32[]{:S(2)}, u32[]{:S(2)}) %collective-permute-start.10) | collective-permute-done | bytes 294944 | tf_op jit(solution)/shard_map/ppermute | solution.py:84
  138.5 3.4 %collective-permute-start.13 = (bf16[192,384]{1,0:T(8,128)(2,1)S(1)}, bf16[192,384]{1,0:T(8,128)(2,1)S(1)}, u32[]{:S(2)}, u32[]{:S(2)}) collective-permute-start(bf16[192,384]{1,0:T(8,128)(2,1)S(1)} %slice.85), channel_id=1, source_target_pairs={{0,3},{1,0},{2,1},{3,2},{4,7},{5,4},{6,5},{7,6},{8,11},{9,8},{10,9... | collective-permute-start | bytes 442376 | tf_op jit(solution)/shard_map/ppermute | solution.py:84
  141.9 10.0 %collective-permute-done.14.lent = bf16[768,1024]{1,0:T(8,128)(2,1)S(1)} collective-permute-done((bf16[768,1024]{1,0:T(8,128)(2,1)S(1)}, bf16[768,1024]{1,0:T(8,128)(2,1)S(1)}, u32[]{:S(2)}, u32[]{:S(2)}) %collective-permute-start.14) | collective-permute-done | bytes 1572896 | tf_op jit(solution)/shard_map/ppermute | solution.py:88
  151.9 1.8 contract.1
  155.0 31.8 %all_to_all.25 = bf16[32,24,512]{2,1,0:T(8,128)(2,1)S(1)} all-to-all(bf16[32,24,512]{2,1,0:T(8,128)(2,1)S(1)} %copy.133), channel_id=1, replica_groups=mesh['rep'=32,'exp'=8] {'rep'}, dimensions={0} | all-to-all | bytes 1572864 | tf_op jit(solution)/shard_map/all_to_all | solution.py:79
  187.4 10.9 %all_to_all.26 = bf16[8,12,512]{2,1,0:T(8,128)(2,1)S(1)} all-to-all(bf16[8,12,512]{2,1,0:T(8,128)(2,1)S(1)} %reshape.277), channel_id=1, replica_groups=mesh['rep'=32,'exp'=8] {'exp'}, dimensions={0} | all-to-all | bytes 196608 | tf_op jit(solution)/shard_map/all_to_all | solution.py:79
  (162 shorter events, 25.5 us)
Async XLA Ops:
  0.0 15.2 %copy-start = (bf16[2,1024,256]{2,1,0:T(8,128)(2,1)S(1)}, bf16[2,1024,256]{2,1,0:T(8,128)(2,1)}, u32[]{:S(2)}) copy-start(bf16[2,1024,256]{2,1,0:T(8,128)(2,1)} %param.17) | copy-start | bytes 3145732
  0.0 17.6 %copy-start.24 = (bf16[4096]{0:T(1024)(128)(2,1)S(1)}, bf16[4096]{0:T(1024)(128)(2,1)}, u32[]{:S(2)}) copy-start(bf16[4096]{0:T(1024)(128)(2,1)} %param.22) | copy-start | bytes 24580
  1.5 22.7 %all-to-all-start = ((s32[8,6,16]{2,1,0:T(8,128)}), s32[8,6,16]{2,1,0:T(8,128)S(1)}, u32[]{:S(2)}, u32[]{:S(2)}) async-start(s32[8,6,16]{2,1,0:T(8,128)} %broadcast_in_dim.36), calls=%async_computation | async-start | bytes 65536 | tf_op jit(solution)/shard_map/all_to_all | solution.py:79
  7.8 19.3 %collective-permute-start = (bf16[96,4096]{1,0:T(8,128)(2,1)S(1)}, bf16[96,4096]{1,0:T(8,128)(2,1)S(1)}, u32[]{:S(2)}, u32[]{:S(2)}) collective-permute-start(bf16[96,4096]{1,0:T(8,128)(2,1)S(1)} %dynamic-slice_bitcast_fusion.2), channel_id=1, source_target_pairs={{0,4},{1,5},{2,6},{3,7},{4,0},{5,1},{6,2},{7,3},{8,12},{9,13},{10,... | collective-permute-start | bytes 2359304 | tf_op jit(solution)/shard_map/ppermute | solution.py:88
  27.1 9.3 %copy-start.4 = (bf16[96,4096]{1,0:T(8,128)(2,1)}, bf16[96,4096]{1,0:T(8,128)(2,1)S(1)}, u32[]{:S(2)}) copy-start(bf16[96,4096]{1,0:T(8,128)(2,1)S(1)} %collective-permute-done.lent_gate_low) | copy-start | bytes 2359300
  27.8 11.8 %all-to-all-start.1 = ((bf16[8,12,512]{2,1,0:T(8,128)(2,1)}), bf16[8,12,512]{2,1,0:T(8,128)(2,1)S(1)}, u32[]{:S(2)}, u32[]{:S(2)}) async-start(bf16[8,12,512]{2,1,0:T(8,128)(2,1)} %bitcast.7), calls=%async_computation.1 | async-start | bytes 262144 | tf_op jit(solution)/shard_map/all_to_all | solution.py:79
  39.6 16.3 %copy-start.14 = (bf16[1,192,1024]{2,1,0:T(8,128)(2,1)S(1)}, bf16[1,192,1024]{2,1,0:T(8,128)(2,1)}, u32[]{:S(2)}) copy-start(bf16[1,192,1024]{2,1,0:T(8,128)(2,1)} %get-tuple-element.43) | copy-start | bytes 1179652
  39.6 16.3 %copy-start.15 = (bf16[1,192,1024]{2,1,0:T(8,128)(2,1)S(1)}, bf16[1,192,1024]{2,1,0:T(8,128)(2,1)}, u32[]{:S(2)}) copy-start(bf16[1,192,1024]{2,1,0:T(8,128)(2,1)} %get-tuple-element.44) | copy-start | bytes 1179652
  42.5 54.2 %all-to-all-start.2 = ((bf16[32,24,512]{2,1,0:T(8,128)(2,1)}), bf16[32,24,512]{2,1,0:T(8,128)(2,1)}, u32[]{:S(2)}, u32[]{:S(2)}) async-start(bf16[32,24,512]{2,1,0:T(8,128)(2,1)} %bitcast.9), calls=%async_computation.2 | async-start | bytes 1572864 | tf_op jit(solution)/shard_map/all_to_all | solution.py:79
  55.3 37.7 %collective-permute-start.1 = (bf16[2,192,1024]{2,1,0:T(8,128)(2,1)S(1)}, bf16[2,192,1024]{2,1,0:T(8,128)(2,1)S(1)}, u32[]{:S(2)}, u32[]{:S(2)}) collective-permute-start(bf16[2,192,1024]{2,1,0:T(8,128)(2,1)S(1)} %pad_maximum_fusion.2), channel_id=1, source_target_pairs={{0,1},{1,2},{2,3},{3,0},{4,5},{5,6},{6,7},{7,4},{8,9},{9,10},{10,1... | collective-permute-start | bytes 2359304 | tf_op jit(solution)/shard_map/ppermute | solution.py:84
  56.0 37.1 %collective-permute-start.2 = (bf16[2,192,1024]{2,1,0:T(8,128)(2,1)S(1)}, bf16[2,192,1024]{2,1,0:T(8,128)(2,1)S(1)}, u32[]{:S(2)}, u32[]{:S(2)}) collective-permute-start(bf16[2,192,1024]{2,1,0:T(8,128)(2,1)S(1)} %pad_maximum_fusion.3), channel_id=1, source_target_pairs={{0,3},{1,0},{2,1},{3,2},{4,7},{5,4},{6,5},{7,6},{8,11},{9,8},{10,9... | collective-permute-start | bytes 2359304 | tf_op jit(solution)/shard_map/ppermute | solution.py:84
  58.9 35.1 %collective-permute-start.3 = (bf16[2,192,1024]{2,1,0:T(8,128)(2,1)S(1)}, bf16[2,192,1024]{2,1,0:T(8,128)(2,1)S(1)}, u32[]{:S(2)}, u32[]{:S(2)}) collective-permute-start(bf16[2,192,1024]{2,1,0:T(8,128)(2,1)S(1)} %pad_maximum_fusion.4), channel_id=1, source_target_pairs={{0,2},{1,3},{2,0},{3,1},{4,6},{5,7},{6,4},{7,5},{8,10},{9,11},{10,... | collective-permute-start | bytes 2359304 | tf_op jit(solution)/shard_map/ppermute | solution.py:84
  60.2 35.6 %collective-permute-start.4 = (bf16[96,4096]{1,0:T(8,128)(2,1)S(1)}, bf16[96,4096]{1,0:T(8,128)(2,1)S(1)}, u32[]{:S(2)}, u32[]{:S(2)}) collective-permute-start(bf16[96,4096]{1,0:T(8,128)(2,1)S(1)} %dynamic-slice_bitcast_fusion.1), channel_id=1, source_target_pairs={{0,4},{1,5},{2,6},{3,7},{4,0},{5,1},{6,2},{7,3},{8,12},{9,13},{10,... | collective-permute-start | bytes 2359304 | tf_op jit(solution)/shard_map/ppermute | solution.py:88
  62.3 59.4 %collective-permute-start.9 = (bf16[192,4096]{1,0:T(8,128)(2,1)}, bf16[192,4096]{1,0:T(8,128)(2,1)S(1)}, u32[]{:S(2)}, u32[]{:S(2)}) collective-permute-start(bf16[192,4096]{1,0:T(8,128)(2,1)} %dynamic-slice_bitcast_fusion), channel_id=1, source_target_pairs={{0,4},{1,5},{2,6},{3,7},{4,0},{5,1},{6,2},{7,3},{8,12},{9,13},{10,... | collective-permute-start | bytes 4718600 | tf_op jit(solution)/shard_map/ppermute | solution.py:88
  99.1 19.0 %collective-permute-start.5 = (bf16[384,1024]{1,0:T(8,128)(2,1)S(1)}, bf16[384,1024]{1,0:T(8,128)(2,1)S(1)}, u32[]{:S(2)}, u32[]{:S(2)}) collective-permute-start(bf16[384,1024]{1,0:T(8,128)(2,1)S(1)} %bitcast.130), channel_id=1, source_target_pairs={{0,1},{1,2},{2,3},{3,0},{4,5},{5,6},{6,7},{7,4},{8,9},{9,10},{10,1... | collective-permute-start | bytes 2359304 | tf_op jit(solution)/shard_map/ppermute | solution.py:84
  99.2 19.0 %collective-permute-start.7 = (bf16[384,1024]{1,0:T(8,128)(2,1)S(1)}, bf16[384,1024]{1,0:T(8,128)(2,1)S(1)}, u32[]{:S(2)}, u32[]{:S(2)}) collective-permute-start(bf16[384,1024]{1,0:T(8,128)(2,1)S(1)} %bitcast.131), channel_id=1, source_target_pairs={{0,3},{1,0},{2,1},{3,2},{4,7},{5,4},{6,5},{7,6},{8,11},{9,8},{10,9... | collective-permute-start | bytes 2359304 | tf_op jit(solution)/shard_map/ppermute | solution.py:84
  102.5 19.2 %copy-start.7 = (bf16[96,4096]{1,0:T(8,128)(2,1)S(1)}, bf16[96,4096]{1,0:T(8,128)(2,1)}, u32[]{:S(2)}) copy-start(bf16[96,4096]{1,0:T(8,128)(2,1)} %copy-done.6) | copy-start | bytes 2359300
  102.5 19.2 %copy-start.5 = (bf16[96,4096]{1,0:T(8,128)(2,1)S(1)}, bf16[96,4096]{1,0:T(8,128)(2,1)}, u32[]{:S(2)}) copy-start(bf16[96,4096]{1,0:T(8,128)(2,1)} %copy-done.4) | copy-start | bytes 2359300
  102.5 19.1 %copy-start.1 = (bf16[2,192,4096]{2,1,0:T(8,128)(2,1)S(1)}, bf16[2,192,4096]{2,1,0:T(8,128)(2,1)}, u32[]{:S(2)}) copy-start(bf16[2,192,4096]{2,1,0:T(8,128)(2,1)} %own_gate.3) | copy-start | bytes 9437188
  102.6 19.1 %copy-start.3 = (bf16[2,192,4096]{2,1,0:T(8,128)(2,1)S(1)}, bf16[2,192,4096]{2,1,0:T(8,128)(2,1)}, u32[]{:S(2)}) copy-start(bf16[2,192,4096]{2,1,0:T(8,128)(2,1)} %own_up.3) | copy-start | bytes 9437188
  102.8 49.1 %collective-permute-start.14 = (bf16[768,1024]{1,0:T(8,128)(2,1)S(1)}, bf16[768,1024]{1,0:T(8,128)(2,1)S(1)}, u32[]{:S(2)}, u32[]{:S(2)}) collective-permute-start(bf16[768,1024]{1,0:T(8,128)(2,1)S(1)} %pad_maximum_fusion), channel_id=1, source_target_pairs={{0,4},{1,5},{2,6},{3,7},{4,0},{5,1},{6,2},{7,3},{8,12},{9,13},{10,... | collective-permute-start | bytes 4718600 | tf_op jit(solution)/shard_map/ppermute | solution.py:88
  118.2 9.7 %collective-permute-start.6 = (bf16[192,1024]{1,0:T(8,128)(2,1)S(1)}, bf16[192,1024]{1,0:T(8,128)(2,1)S(1)}, u32[]{:S(2)}, u32[]{:S(2)}) collective-permute-start(bf16[192,1024]{1,0:T(8,128)(2,1)S(1)} %slice.82), channel_id=1, source_target_pairs={{0,1},{1,2},{2,3},{3,0},{4,5},{5,6},{6,7},{7,4},{8,9},{9,10},{10,1... | collective-permute-start | bytes 1179656 | tf_op jit(solution)/shard_map/ppermute | solution.py:84
  118.3 9.5 %collective-permute-start.8 = (bf16[192,1024]{1,0:T(8,128)(2,1)S(1)}, bf16[192,1024]{1,0:T(8,128)(2,1)S(1)}, u32[]{:S(2)}, u32[]{:S(2)}) collective-permute-start(bf16[192,1024]{1,0:T(8,128)(2,1)S(1)} %slice.83), channel_id=1, source_target_pairs={{0,3},{1,0},{2,1},{3,2},{4,7},{5,4},{6,5},{7,6},{8,11},{9,8},{10,9... | collective-permute-start | bytes 1179656 | tf_op jit(solution)/shard_map/ppermute | solution.py:84
  129.6 8.8 %collective-permute-start.10 = (bf16[384,384]{1,0:T(8,128)(2,1)S(1)}, bf16[384,384]{1,0:T(8,128)(2,1)S(1)}, u32[]{:S(2)}, u32[]{:S(2)}) collective-permute-start(bf16[384,384]{1,0:T(8,128)(2,1)S(1)} %expand_far.1.own), channel_id=1, source_target_pairs={{0,1},{1,2},{2,3},{3,0},{4,5},{5,6},{6,7},{7,4},{8,9},{9,10},{10,1... | collective-permute-start | bytes 884744 | tf_op jit(solution)/shard_map/ppermute | solution.py:84
  130.4 8.0 %collective-permute-start.11 = (bf16[384,384]{1,0:T(8,128)(2,1)S(1)}, bf16[384,384]{1,0:T(8,128)(2,1)S(1)}, u32[]{:S(2)}, u32[]{:S(2)}) collective-permute-start(bf16[384,384]{1,0:T(8,128)(2,1)S(1)} %expand_far.1.own), channel_id=1, source_target_pairs={{0,3},{1,0},{2,1},{3,2},{4,7},{5,4},{6,5},{7,6},{8,11},{9,8},{10,9... | collective-permute-start | bytes 884744 | tf_op jit(solution)/shard_map/ppermute | solution.py:84
  138.4 13.5 %collective-permute-start.12 = (bf16[192,384]{1,0:T(8,128)(2,1)S(1)}, bf16[192,384]{1,0:T(8,128)(2,1)S(1)}, u32[]{:S(2)}, u32[]{:S(2)}) collective-permute-start(bf16[192,384]{1,0:T(8,128)(2,1)S(1)} %slice.84), channel_id=1, source_target_pairs={{0,1},{1,2},{2,3},{3,0},{4,5},{5,6},{6,7},{7,4},{8,9},{9,10},{10,1... | collective-permute-start | bytes 442376 | tf_op jit(solution)/shard_map/ppermute | solution.py:84
  138.5 13.4 %collective-permute-start.13 = (bf16[192,384]{1,0:T(8,128)(2,1)S(1)}, bf16[192,384]{1,0:T(8,128)(2,1)S(1)}, u32[]{:S(2)}, u32[]{:S(2)}) collective-permute-start(bf16[192,384]{1,0:T(8,128)(2,1)S(1)} %slice.85), channel_id=1, source_target_pairs={{0,3},{1,0},{2,1},{3,2},{4,7},{5,4},{6,5},{7,6},{8,11},{9,8},{10,9... | collective-permute-start | bytes 442376 | tf_op jit(solution)/shard_map/ppermute | solution.py:84
  153.7 33.1 %copy-start.20 = (f32[96,32]{0,1:T(8,128)S(1)}, f32[96,32]{0,1:T(8,128)}, u32[]{:S(2)}) copy-start(f32[96,32]{0,1:T(8,128)} %get-tuple-element.33) | copy-start | bytes 36868
  153.7 33.1 %copy-start.22 = (f32[96,24]{0,1:T(8,128)S(1)}, f32[96,24]{0,1:T(8,128)}, u32[]{:S(2)}) copy-start(f32[96,24]{0,1:T(8,128)} %constant.103) | copy-start | bytes 27652
  154.6 44.1 %copy-start.17 = (f32[1,2,4096]{2,1,0:T(2,128)S(1)}, f32[1,2,4096]{2,1,0:T(2,128)}, u32[]{:S(2)}) copy-start(f32[1,2,4096]{2,1,0:T(2,128)} %get-tuple-element.36) | copy-start | bytes 98308
  154.6 44.1 %copy-start.18 = (f32[1,2,4096]{2,1,0:T(2,128)S(1)}, f32[1,2,4096]{2,1,0:T(2,128)}, u32[]{:S(2)}) copy-start(f32[1,2,4096]{2,1,0:T(2,128)} %get-tuple-element.50) | copy-start | bytes 98308
  154.6 44.1 %copy-start.19 = (f32[1,2,4096]{2,1,0:T(2,128)S(1)}, f32[1,2,4096]{2,1,0:T(2,128)}, u32[]{:S(2)}) copy-start(f32[1,2,4096]{2,1,0:T(2,128)} %get-tuple-element.52) | copy-start | bytes 98308
  (13 other events, 48.7 us)

commit v5 on v3

--- a/solution.py
+++ b/solution.py
@@ -29,49 +29,102 @@
 WIRE = 2 * PLACES
 
 
-def attend_rows(decode_query_rows, key_cache, value_cache, new_keys, new_values, cache_len, step):
-    row_count = decode_query_rows.shape[0]
-    group_size = QH // KVH
-    scaling = 1.0 / math.sqrt(HD)
-    query_heads = decode_query_rows.reshape(row_count, KVH, group_size, HD)
-    cached_keys = key_cache.reshape(row_count, CACHE, KVH, HD)
-    cached_values = value_cache.reshape(row_count, CACHE, KVH, HD)
-    fresh_keys = new_keys[: step + 1].reshape(step + 1, row_count, KVH, HD)
-    fresh_values = new_values[: step + 1].reshape(step + 1, row_count, KVH, HD)
-    previous_scores = (
-        jnp.einsum("sjgd,stjd->sjgt", query_heads, cached_keys, preferred_element_type=jnp.float32)
-        * scaling
-    )
-    new_scores = (
-        jnp.einsum("sjgd,tsjd->sjgt", query_heads, fresh_keys, preferred_element_type=jnp.float32)
-        * scaling
-    )
-    position = lax.broadcasted_iota(jnp.int32, (row_count, 1, 1, CACHE), 3)
-    previous_scores = jnp.where(position < cache_len[:, None, None, None], previous_scores, -1e30)
-    row_max = jnp.maximum(
-        jnp.max(previous_scores, axis=-1, keepdims=True),
-        jnp.max(new_scores, axis=-1, keepdims=True),
-    )
-    old_expo = jnp.exp(previous_scores - row_max)
-    new_expo = jnp.exp(new_scores - row_max)
-    denominator = jnp.sum(old_expo, axis=-1, keepdims=True) + jnp.sum(
-        new_expo, axis=-1, keepdims=True
-    )
-    old_probs = (old_expo / denominator).astype(jnp.bfloat16)
-    new_probs = (new_expo / denominator).astype(jnp.bfloat16)
-    blended = jnp.einsum(
-        "sjgt,stjd->sjgd", old_probs, cached_values, preferred_element_type=jnp.float32
-    )
-    blended = blended + jnp.einsum(
-        "sjgt,tsjd->sjgd", new_probs, fresh_values, preferred_element_type=jnp.float32
-    )
-    return blended.reshape(row_count, QH * HD)
-
-
-def norm_rows(hidden, norm_gain):
-    mean_square = jnp.mean(hidden * hidden, axis=-1, keepdims=True)
-    return (hidden * lax.rsqrt(mean_square + 1e-06) * norm_gain.astype(jnp.float32)).astype(
-        jnp.bfloat16
+def attend_kernel(lengths, query, keys, values, fresh_keys, fresh_values, residual, gain, hidden, normed):
+    seq = pl.program_id(0)
+    group = QH // KVH
+    count = STEPS * group
+    length = lengths[seq]
+    old_valid = lax.broadcasted_iota(jnp.int32, (count, CACHE), 1) < length
+    step_of = lax.broadcasted_iota(jnp.int32, (count, 8), 0) // group
+    new_valid = lax.broadcasted_iota(jnp.int32, (count, 8), 1) <= step_of
+    for head in range(KVH):
+        rows = slice(head * group, (head + 1) * group)
+        lanes = slice(head * HD, (head + 1) * HD)
+        heads = jnp.concatenate([query[step * SEQ + seq, rows] for step in range(STEPS)], axis=0)
+        old = contract_last(heads, keys[0, :, lanes]) * (1.0 / math.sqrt(HD))
+        new = contract_last(heads, fresh_keys[0, :, lanes]) * (1.0 / math.sqrt(HD))
+        old = jnp.where(old_valid, old, -1e30)
+        new = jnp.where(new_valid, new, -1e30)
+        row_max = jnp.maximum(
+            jnp.max(old, axis=-1, keepdims=True), jnp.max(new, axis=-1, keepdims=True)
+        )
+        old = jnp.exp(old - row_max)
+        new = jnp.exp(new - row_max)
+        total = jnp.sum(old, axis=-1, keepdims=True) + jnp.sum(new, axis=-1, keepdims=True)
+        blended = jnp.dot(
+            (old / total).astype(jnp.bfloat16),
+            values[0, :, lanes],
+            preferred_element_type=jnp.float32,
+        ) + jnp.dot(
+            (new / total).astype(jnp.bfloat16),
+            fresh_values[0, :, lanes],
+            preferred_element_type=jnp.float32,
+        )
+        for step in range(STEPS):
+            token = step * SEQ + seq
+            hidden[token, rows] = (
+                residual[token, rows].astype(jnp.float32)
+                + blended[step * group : (step + 1) * group]
+            )
+    for step in range(STEPS):
+        token = step * SEQ + seq
+        value = hidden[token]
+        mean_square = jnp.sum(value * value) / D
+        scale = lax.rsqrt(jnp.full((QH, HD), mean_square + 1e-06, jnp.float32))
+        normed[token] = (value * scale * gain[...].astype(jnp.float32)).astype(jnp.bfloat16)
+
+
+def attend(cache_len, queries, key_cache, value_cache, new_keys, new_values, residual, norm_gain):
+    def fresh(array):
+        return jnp.pad(array.transpose(1, 0, 2), ((0, 0), (0, 8 - STEPS), (0, 0)))
+
+    def whole(shape):
+        return pl.BlockSpec(shape, lambda seq, lengths: (0,) * len(shape))
+
+    def one(shape):
+        return pl.BlockSpec((1, *shape[1:]), lambda seq, lengths: (seq, 0, 0))
+
+    tokens = (LOCAL, QH, HD)
+    cache = (SEQ, CACHE, KVH * HD)
+    extra = (SEQ, 8, KVH * HD)
+    return pl.pallas_call(
+        attend_kernel,
+        out_shape=(
+            jax.ShapeDtypeStruct(tokens, jnp.float32),
+            jax.ShapeDtypeStruct(tokens, jnp.bfloat16),
+        ),
+        grid_spec=pltpu.PrefetchScalarGridSpec(
+            num_scalar_prefetch=1,
+            grid=(SEQ,),
+            in_specs=[
+                whole(tokens),
+                one(cache),
+                one(cache),
+                one(extra),
+                one(extra),
+                whole(tokens),
+                whole((QH, HD)),
+            ],
+            out_specs=(whole(tokens), whole(tokens)),
+        ),
+        compiler_params=pltpu.CompilerParams(
+            dimension_semantics=("arbitrary",), vmem_limit_bytes=24 << 20
+        ),
+        cost_estimate=pl.CostEstimate(
+            flops=4 * LOCAL * QH * HD * CACHE,
+            bytes_accessed=4 * SEQ * CACHE * KVH * HD + 10 * LOCAL * D,
+            transcendentals=LOCAL * QH * CACHE,
+        ),
+        name="attend",
+    )(
+        cache_len,
+        queries.reshape(tokens),
+        key_cache,
+        value_cache,
+        fresh(new_keys),
+        fresh(new_values),
+        residual.reshape(tokens),
+        norm_gain.reshape(QH, HD),
     )
 
 
@@ -205,7 +258,10 @@
     def call(kernel, name, steps, column, inputs, out_shape):
         own = pl.BlockSpec((1, UNITS, BLK), lambda turn, where: (where[0], 0, column(turn, where)))
         lent = pl.BlockSpec((UNITS, BLK), lambda turn, where: (0, column(turn, where)))
-        part = pl.BlockSpec((UNITS // 2, BLK), lambda turn, where: (0, column(turn, where)))
+        parts = [
+            pl.BlockSpec((array.shape[0], BLK), lambda turn, where: (0, column(turn, where)))
+            for array in weights[2:4]
+        ]
         outs = jax.tree.leaves(out_shape)
         out_specs = jax.tree.unflatten(
             jax.tree.structure(out_shape), [whole(leaf.shape) for leaf in outs]
@@ -216,7 +272,7 @@
             grid_spec=pltpu.PrefetchScalarGridSpec(
                 num_scalar_prefetch=1,
                 grid=(steps,),
-                in_specs=[whole(array.shape) for array in inputs] + [own, own, part, part, lent],
+                in_specs=[whole(array.shape) for array in inputs] + [own, own, *parts, lent],
                 out_specs=out_specs,
             ),
             compiler_params=pltpu.CompilerParams(
@@ -293,21 +349,28 @@
     routing = jnp.broadcast_to(routing[:, None], (N_EXP, 2, LOCAL, 2 * TOPK))
     routing = routing.reshape(KEYS, 2 * TOPK)
 
-    half = UNITS // 2
-    lent_gate_low = across(lax.dynamic_slice(gate_weight, (1 - side, 0, 0), (1, half, D))[0])
-
-    hidden, normed = [], []
-    for step in range(STEPS):
-        attention = attend_rows(
-            queries[step], key_cache, value_cache, new_keys, new_values, cache_len, step
+    early = 2 * UNITS // 3
+    lent_gate_low = across(lax.dynamic_slice(gate_weight, (1 - side, 0, 0), (1, early, D))[0])
+
+    def quarter(weight, step):
+        start = (place + step) % 4 * BLK
+        return jnp.concatenate(
+            [
+                lax.dynamic_slice(weight, (expert, 0, start), (1, UNITS, BLK))
+                for expert in (side, 1 - side)
+            ]
         )
-        hidden.append(residual[step].astype(jnp.float32) + attention)
-        normed.append(norm_rows(hidden[-1], norm_gain))
-    normed = jnp.stack(normed).reshape(LOCAL, 4, 2, HALF).transpose(1, 2, 0, 3)
+
+    kept_near = [shift(quarter(down_weight, step), step) for step in (1, -1)]
+
+    hidden, normed = attend(
+        cache_len, queries, key_cache, value_cache, new_keys, new_values, residual, norm_gain
+    )
+    normed = normed.reshape(LOCAL, 4, 2, HALF).transpose(1, 2, 0, 3)
     normed = jnp.broadcast_to(
         normed.reshape(1, 4, 2 * LOCAL, HALF), (2, 4, 2 * LOCAL, HALF)
     ).reshape(N_EXP, 2 * LOCAL, HALF)
-    normed, lent_gate_low = lax.optimization_barrier((normed, lent_gate_low))
+    normed, lent_gate_low, kept_near = lax.optimization_barrier((normed, lent_gate_low, kept_near))
     tokens = exchange(normed, "exp").reshape(KEYS, HALF)
     table, combine = routing_tables(routing[:, :TOPK], routing[:, TOPK:], side, groups)
     outbound = lax.dot_general(
@@ -318,20 +381,15 @@
         (outbound, gate_weight, up_weight, down_weight)
     )
     inbound = exchange(outbound.reshape(groups, WIRE, HALF), "rep")
-
-    def quarter(step):
-        start = (place + step) % 4 * BLK
-        return jnp.concatenate(
-            [
-                lax.dynamic_slice(down_late, (expert, 0, start), (1, UNITS, BLK))
-                for expert in (side, 1 - side)
-            ]
-        )
-
-    kept = [quarter(0)] + [shift(quarter(step), step) for step in (1, -1, 2)]
-    lent_gate_high = across(lax.dynamic_slice(gate_late, (1 - side, half, 0), (1, half, D))[0])
+    kept_far = shift(quarter(down_late, 2), 2)
+    lent_gate_high = across(
+        lax.dynamic_slice(gate_late, (1 - side, early, 0), (1, UNITS - early, D))[0]
+    )
     lent_up = across(lax.dynamic_index_in_dim(up_late, 1 - side, 0, keepdims=False))
-    inbound, kept, lent_gate_high = lax.optimization_barrier((inbound, kept, lent_gate_high))
+    inbound, kept_far, lent_gate_high = lax.optimization_barrier(
+        (inbound, kept_far, lent_gate_high)
+    )
+    kept = [quarter(down_late, 0), *kept_near, kept_far]
     lent_down = across(jnp.concatenate([block[1] for block in kept]))
     slotted = inbound.reshape(groups, 2, PLACES, HALF).transpose(0, 2, 1, 3).reshape(rows, BLK)
     where = jnp.stack([side, place])
@@ -349,7 +407,7 @@
     expert_sum = exchange(weighted.reshape(N_EXP, 2 * LOCAL, HALF), "exp").astype(jnp.float32)
     expert_sum = expert_sum.reshape(2, 4, 2, LOCAL, HALF).sum(axis=0)
     expert_sum = expert_sum.transpose(2, 0, 1, 3).reshape(STEPS, SEQ, D)
-    return (jnp.stack(hidden) + expert_sum).astype(jnp.bfloat16)
+    return (hidden.reshape(STEPS, SEQ, D) + expert_sum).astype(jnp.bfloat16)
 
 
 def solution(mesh):

time: 199 us -> 200 us (level)
  blocking collectives: 43.1 us -> 31.6 us
  waiting for transfers between devices: 69.7 us -> 79.1 us
  matrix products: 9.04 us -> 2.01 us
  Pallas kernels: 8.01 us -> 13.8 us
  starting transfers between devices: 44.1 us -> 48.7 us
    ppermute x4, waiting for transfers between devices: 12.2 us -> 34.1 us  [across(): return lax.ppermute(array, 'exp', [(e, e ^ 4) for e in range(N_EXP)])]
    ppermute x11, waiting for transfers between devices: 51 us -> 32 us  [shift(): return lax.ppermute(array, 'exp', pairs)]
    all_to_all x2 -> x1, blocking collectives: 43.1 us -> 31.6 us  [exchange(): return lax.all_to_all(array, axis, split_axis=0, concat_axis=0, tiled=True)]
    dot_general x11 -> x0, matrix products: 7.12 us -> none  [the longest x3 4.71 us: attend_rows(): jnp.einsum('sjgt,stjd->sjgd', old_probs, cached_values, preferred_element...]
    all_to_all x3 -> x4, waiting for transfers between devices: 6.53 us -> 13.1 us  [exchange(): return lax.all_to_all(array, axis, split_axis=0, concat_axis=0, tiled=True)]
    all_to_all x3 -> x4, starting transfers between devices: 22 us -> 25.5 us  [exchange(): return lax.all_to_all(array, axis, split_axis=0, concat_axis=0, tiled=True)]
    pallas_call x0 -> x1, Pallas kernels: none -> 2.83 us  [attend(): pl.pallas_call(attend_kernel, out_shape=(jax.ShapeDtypeStruct(tokens, jnp...]
    dynamic_slice x1 -> x2, local copies, waits for them, and re-layouts: 2.16 us -> 4.12 us  [quarter(): lax.dynamic_slice(weight, (expert, 0, start), (1, UNITS, BLK))]
  transfers between devices with their start and end apart: 18 -> 19, of which waited for: 7 -> 9; matrix products, arithmetic and copies ran while one was open for 11% -> 8% of each run, Pallas kernels for 3% -> 5%
where the time goes in v5:
time: 200 us; the launch traced here: 199 us
  waiting for transfers between devices  79.1 us (40%)
  starting transfers between devices  48.7 us (24%)
  blocking collectives  31.6 us (16%)
  local copies, waits for them, and re-layouts  19.6 us (10%)
  Pallas kernels  13.8 us (7%)
  other arithmetic  3.99 us (2%)
  matrix products  2.01 us (1%)
    ppermute x4, waiting for transfers between devices, across(): return lax.ppermute(array, 'exp', [(e, e ^ 4) for e in range(N_EXP)])  34.1 us
    ppermute x11, waiting for transfers between devices, shift(): return lax.ppermute(array, 'exp', pairs)  32 us
    all_to_all x1, blocking collectives, exchange(): return lax.all_to_all(array, axis, split_axis=0, concat_axis=0, tiled=True)  31.6 us
    all_to_all x4, starting transfers between devices, exchange(): return lax.all_to_all(array, axis, split_axis=0, concat_axis=0, tiled=True)  25.5 us
    ppermute x11, starting transfers between devices, shift(): return lax.ppermute(array, 'exp', pairs)  17.8 us
    all_to_all x4, waiting for transfers between devices, exchange(): return lax.all_to_all(array, axis, split_axis=0, concat_axis=0, tiled=True)  13.1 us
    pallas_call x2, Pallas kernels, call(): pl.pallas_call(kernel, out_shape=out_shape, grid_spec=pltpu.PrefetchScala...  8.04 us
    ppermute x4, starting transfers between devices, across(): return lax.ppermute(array, 'exp', [(e, e ^ 4) for e in range(N_EXP)])  5.4 us
  transfers between devices with their start and end apart: 19, of which 9 were waited for; matrix products, arithmetic and copies ran while one was open for 8% of the time, Pallas kernels for 5%

profile of v5, /device:TPU:4, one launch (start us, length us, event | category | flops | bytes accessed | tf_op | source)
XLA Modules:
  0.0 199.4 jit_solution(5276436686753839154)
XLA Ops:
  1.4 5.1 %all-to-all-start = ((s32[8,6,16]{2,1,0:T(8,128)}), s32[8,6,16]{2,1,0:T(8,128)S(1)}, u32[]{:S(2)}, u32[]{:S(2)}) async-start(s32[8,6,16]{2,1,0:T(8,128)} %broadcast_in_dim.15), calls=%async_computation | async-start | bytes 65536 | tf_op jit(solution)/shard_map/all_to_all | solution.py:132
  6.5 2.3 %dynamic-slice_bitcast_fusion.1 = bf16[128,4096]{1,0:T(8,128)(2,1)} fusion(bf16[2,192,4096]{2,1,0:T(8,128)(2,1)} %own_gate.3, s32[]{:T(128)S(6)} %select_n.66), kind=kLoop, calls=%fused_computation.6 | loop fusion | bytes 2097156 | tf_op jit(solution)/shard_map/squeeze | solution.py:353
  8.8 2.0 %collective-permute-start = (bf16[128,4096]{1,0:T(8,128)(2,1)}, bf16[128,4096]{1,0:T(8,128)(2,1)S(1)}, u32[]{:S(2)}, u32[]{:S(2)}) collective-permute-start(bf16[128,4096]{1,0:T(8,128)(2,1)} %dynamic-slice_bitcast_fusion.1), channel_id=1, source_target_pairs={{0,4},{1,5},{2,6},{3,7},{4,0},{5,1},{6,2},{7,3},{8,12},{9,13},{10,... | collective-permute-start | bytes 3145736 | tf_op jit(solution)/shard_map/ppermute | solution.py:141
  10.9 1.5 constant_dynamic-slice_fusion.5
  13.4 1.5 collective-permute-start.1
  15.8 1.8 collective-permute-start.2
  19.0 1.2 copy-done.14
  20.3 2.8 %attend.1 = (f32[6,32,128]{2,1,0:T(8,128)S(1)}, bf16[6,32,128]{2,1,0:T(8,128)(2,1)S(1)}) custom-call(s32[2]{0:T(128)S(1)} %copy-done.16, bf16[6,32,128]{2,1,0:T(8,128)(2,1)S(1)} %reshape.83.query, bf16[2,1024,256]{2,1,0:T(8,128)(2,1)S(1)} %copy-done.13, bf16[2,1024,256]{2,1,0:T(8,128)(2,1)S(1)} %copy-done.14, bf16[2,8,256]{2,1,0:T(8,128)(2,1)S(1)} %pad.7.fresh_keys, ...), custom_call_target="tpu_custom_call" | custom-call | flops 100663296 | bytes 2342912 | tf_op jit(solution)/shard_map/attend/pallas_call | solution.py:90
  23.7 9.6 %collective-permute-done.1.w_below = bf16[2,192,1024]{2,1,0:T(8,128)(2,1)S(1)} collective-permute-done((bf16[2,192,1024]{2,1,0:T(8,128)(2,1)}, bf16[2,192,1024]{2,1,0:T(8,128)(2,1)S(1)}, u32[]{:S(2)}, u32[]{:S(2)}) %collective-permute-start.1) | collective-permute-done | bytes 786464 | tf_op jit(solution)/shard_map/ppermute | solution.py:137
  34.9 4.9 %all-to-all-start.1 = ((bf16[8,12,512]{2,1,0:T(8,128)(2,1)}), bf16[8,12,512]{2,1,0:T(8,128)(2,1)S(1)}, u32[]{:S(2)}, u32[]{:S(2)}) async-start(bf16[8,12,512]{2,1,0:T(8,128)(2,1)} %bitcast.8), calls=%async_computation.1 | async-start | bytes 262144 | tf_op jit(solution)/shard_map/all_to_all | solution.py:132
  39.8 6.5 %all-to-all-done.1 = bf16[8,12,512]{2,1,0:T(8,128)(2,1)S(1)} async-done(((bf16[8,12,512]{2,1,0:T(8,128)(2,1)}), bf16[8,12,512]{2,1,0:T(8,128)(2,1)S(1)}, u32[]{:S(2)}, u32[]{:S(2)}) %all-to-all-start.1) | async-done | bytes 98336 | tf_op jit(solution)/shard_map/all_to_all | solution.py:132
  46.4 1.3 convolution_convert_fusion
  47.7 11.9 %all-to-all-start.2 = ((bf16[32,24,512]{2,1,0:T(8,128)(2,1)}), bf16[32,24,512]{2,1,0:T(8,128)(2,1)}, u32[]{:S(2)}, u32[]{:S(2)}) async-start(bf16[32,24,512]{2,1,0:T(8,128)(2,1)} %bitcast.54), calls=%async_computation.2 | async-start | bytes 1572864 | tf_op jit(solution)/shard_map/all_to_all | solution.py:132
  59.7 2.6 %constant_dynamic-slice_fusion.1 = (bf16[1,192,1024]{2,1,0:T(8,128)(2,1)}, bf16[1,192,1024]{2,1,0:T(8,128)(2,1)}, bf16[1,192,1024]{2,1,0:T(8,128)(2,1)S(1)}, bf16[1,192,1024]{2,1,0:T(8,128)(2,1)S(1)}) fusion(bf16[2,192,4096]{2,1,0:T(8,128)(2,1)} %param.27, s32[]{:T(128)S(6)} %select_n.67, s32[]{:T(128)S(6)} %select_n.75, s32[]{:T(128)S(6)} %select_n.66, ...), kind=kLoop, calls=%fused_computation.34 | loop fusion | bytes 3145744 | tf_op jit(solution)/shard_map/dynamic_slice | solution.py:359
  64.4 1.3 dynamic-slice_bitcast_fusion
  67.8 16.1 %collective-permute-done.4.lent_gate_high = bf16[64,4096]{1,0:T(8,128)(2,1)S(1)} collective-permute-done((bf16[64,4096]{1,0:T(8,128)(2,1)S(1)}, bf16[64,4096]{1,0:T(8,128)(2,1)S(1)}, u32[]{:S(2)}, u32[]{:S(2)}) %collective-permute-start.4) | collective-permute-done | bytes 524320 | tf_op jit(solution)/shard_map/ppermute | solution.py:141
  84.8 1.5 copy.76
  88.2 2.3 %collective-permute-start.7 = (bf16[384,1024]{1,0:T(8,128)(2,1)S(1)}, bf16[384,1024]{1,0:T(8,128)(2,1)S(1)}, u32[]{:S(2)}, u32[]{:S(2)}) collective-permute-start(bf16[384,1024]{1,0:T(8,128)(2,1)S(1)} %bitcast.50), channel_id=1, source_target_pairs={{0,3},{1,0},{2,1},{3,2},{4,7},{5,4},{6,5},{7,6},{8,11},{9,8},{10,9... | collective-permute-start | bytes 2359304 | tf_op jit(solution)/shard_map/ppermute | solution.py:137
  91.7 1.3 collective-permute-start.14
  93.0 14.8 %collective-permute-done.5.below_rows = bf16[384,1024]{1,0:T(8,128)(2,1)S(1)} collective-permute-done((bf16[384,1024]{1,0:T(8,128)(2,1)S(1)}, bf16[384,1024]{1,0:T(8,128)(2,1)S(1)}, u32[]{:S(2)}, u32[]{:S(2)}) %collective-permute-start.5) | collective-permute-done | bytes 786464 | tf_op jit(solution)/shard_map/ppermute | solution.py:137
  108.0 3.5 %collective-permute-start.8 = (bf16[192,1024]{1,0:T(8,128)(2,1)S(1)}, bf16[192,1024]{1,0:T(8,128)(2,1)S(1)}, u32[]{:S(2)}, u32[]{:S(2)}) collective-permute-start(bf16[192,1024]{1,0:T(8,128)(2,1)S(1)} %slice.39), channel_id=1, source_target_pairs={{0,3},{1,0},{2,1},{3,2},{4,7},{5,4},{6,5},{7,6},{8,11},{9,8},{10,9... | collective-permute-start | bytes 1179656 | tf_op jit(solution)/shard_map/ppermute | solution.py:137
  111.5 6.2 %collective-permute-done.9.lent_up = bf16[192,4096]{1,0:T(8,128)(2,1)} collective-permute-done((bf16[192,4096]{1,0:T(8,128)(2,1)}, bf16[192,4096]{1,0:T(8,128)(2,1)}, u32[]{:S(2)}, u32[]{:S(2)}) %collective-permute-start.9) | collective-permute-done | bytes 1572896 | tf_op jit(solution)/shard_map/ppermute | solution.py:141
  117.7 5.2 %expand_near.1 = (f32[384,384]{1,0:T(8,128)S(1)}, f32[384,384]{1,0:T(8,128)S(1)}) custom-call(s32[2]{0:T(128)S(1)} %pad_add_fusion.1.where, bf16[384,1024]{1,0:T(8,128)(2,1)S(1)} %bitcast.51, bf16[384,1024]{1,0:T(8,128)(2,1)S(1)} %collective-permute-done.5.below_rows, bf16[384,1024]{1,0:T(8,128)(2,1)S(1)} %collective-permute-done.7.above_rows, ...), custom_call_target="tpu_custom_call" | custom-call | flops 1811939328 | bytes 8257536 | tf_op jit(solution)/shard_map/expand_near/pallas_call | solution.py:269
  123.0 2.8 %expand_far.1.own = bf16[384,384]{1,0:T(8,128)(2,1)S(1)} custom-call(s32[2]{0:T(128)S(1)} %pad_add_fusion.1.where, bf16[192,1024]{1,0:T(8,128)(2,1)S(1)} %collective-permute-done.6.far_low, bf16[192,1024]{1,0:T(8,128)(2,1)S(1)} %collective-permute-done.8.far_high, f32[384,384]{1,0:T(8,128)S(1)} %get-tuple-element.30.gate_total, ...), custom_call_target="tpu_custom_call" | custom-call | flops 603979776 | bytes 3538944 | tf_op jit(solution)/shard_map/expand_far/pallas_call | solution.py:269
  126.8 2.3 %collective-permute-start.11 = (bf16[384,384]{1,0:T(8,128)(2,1)S(1)}, bf16[384,384]{1,0:T(8,128)(2,1)S(1)}, u32[]{:S(2)}, u32[]{:S(2)}) collective-permute-start(bf16[384,384]{1,0:T(8,128)(2,1)S(1)} %expand_far.1.own), channel_id=1, source_target_pairs={{0,3},{1,0},{2,1},{3,2},{4,7},{5,4},{6,5},{7,6},{8,11},{9,8},{10,9... | collective-permute-start | bytes 884744 | tf_op jit(solution)/shard_map/ppermute | solution.py:137
  129.1 6.6 %collective-permute-done.10.below = bf16[384,384]{1,0:T(8,128)(2,1)S(1)} collective-permute-done((bf16[384,384]{1,0:T(8,128)(2,1)S(1)}, bf16[384,384]{1,0:T(8,128)(2,1)S(1)}, u32[]{:S(2)}, u32[]{:S(2)}) %collective-permute-start.10) | collective-permute-done | bytes 294944 | tf_op jit(solution)/shard_map/ppermute | solution.py:137
  135.9 3.3 %collective-permute-start.13 = (bf16[192,384]{1,0:T(8,128)(2,1)S(1)}, bf16[192,384]{1,0:T(8,128)(2,1)S(1)}, u32[]{:S(2)}, u32[]{:S(2)}) collective-permute-start(bf16[192,384]{1,0:T(8,128)(2,1)S(1)} %slice.41), channel_id=1, source_target_pairs={{0,3},{1,0},{2,1},{3,2},{4,7},{5,4},{6,5},{7,6},{8,11},{9,8},{10,9... | collective-permute-start | bytes 442376 | tf_op jit(solution)/shard_map/ppermute | solution.py:137
  139.3 11.8 %collective-permute-done.14.lent = bf16[768,1024]{1,0:T(8,128)(2,1)S(1)} collective-permute-done((bf16[768,1024]{1,0:T(8,128)(2,1)S(1)}, bf16[768,1024]{1,0:T(8,128)(2,1)S(1)}, u32[]{:S(2)}, u32[]{:S(2)}) %collective-permute-start.14) | collective-permute-done | bytes 1572896 | tf_op jit(solution)/shard_map/ppermute | solution.py:141
  151.1 2.9 %contract.1 = bf16[384,1024]{1,0:T(8,128)(2,1)S(1)} custom-call(bf16[384,384]{1,0:T(8,128)(2,1)S(1)} %expand_far.1.own, bf16[384,384]{1,0:T(8,128)(2,1)S(1)} %collective-permute-done.10.below, bf16[384,384]{1,0:T(8,128)(2,1)S(1)} %collective-permute-done.11.above, bf16[192,384]{1,0:T(8,128)(2,1)S(1)} %collective-permute-done.12.far_low, ...), custom_call_target="tpu_custom_call" | custom-call | flops 1207959552 | bytes 5111808 | tf_op jit(solution)/shard_map/contract/pallas_call | solution.py:314
  155.3 31.6 %all_to_all.25 = bf16[32,24,512]{2,1,0:T(8,128)(2,1)S(1)} all-to-all(bf16[32,24,512]{2,1,0:T(8,128)(2,1)S(1)} %copy.79), channel_id=1, replica_groups=mesh['rep'=32,'exp'=8] {'rep'}, dimensions={0} | all-to-all | bytes 1572864 | tf_op jit(solution)/shard_map/all_to_all | solution.py:132
  188.2 3.6 %all-to-all-start.4 = ((bf16[8,12,512]{2,1,0:T(8,128)(2,1)}), bf16[8,12,512]{2,1,0:T(8,128)(2,1)S(1)}, u32[]{:S(2)}, u32[]{:S(2)}) async-start(bf16[8,12,512]{2,1,0:T(8,128)(2,1)} %reshape.96), calls=%async_computation.4 | async-start | bytes 262144 | tf_op jit(solution)/shard_map/all_to_all | solution.py:132
  191.8 6.5 %all-to-all-done.4 = bf16[8,12,512]{2,1,0:T(8,128)(2,1)S(1)} async-done(((bf16[8,12,512]{2,1,0:T(8,128)(2,1)}), bf16[8,12,512]{2,1,0:T(8,128)(2,1)S(1)}, u32[]{:S(2)}, u32[]{:S(2)}) %all-to-all-start.4) | async-done | bytes 98336 | tf_op jit(solution)/shard_map/all_to_all | solution.py:132
  (123 shorter events, 20.1 us)
Async XLA Ops:
  1.4 21.8 %all-to-all-start = ((s32[8,6,16]{2,1,0:T(8,128)}), s32[8,6,16]{2,1,0:T(8,128)S(1)}, u32[]{:S(2)}, u32[]{:S(2)}) async-start(s32[8,6,16]{2,1,0:T(8,128)} %broadcast_in_dim.15), calls=%async_computation | async-start | bytes 65536 | tf_op jit(solution)/shard_map/all_to_all | solution.py:132
  8.8 25.4 %collective-permute-start = (bf16[128,4096]{1,0:T(8,128)(2,1)}, bf16[128,4096]{1,0:T(8,128)(2,1)S(1)}, u32[]{:S(2)}, u32[]{:S(2)}) collective-permute-start(bf16[128,4096]{1,0:T(8,128)(2,1)} %dynamic-slice_bitcast_fusion.1), channel_id=1, source_target_pairs={{0,4},{1,5},{2,6},{3,7},{4,0},{5,1},{6,2},{7,3},{8,12},{9,13},{10,... | collective-permute-start | bytes 3145736 | tf_op jit(solution)/shard_map/ppermute | solution.py:141
  10.9 6.9 %copy-start.15 = (bf16[4096]{0:T(1024)(128)(2,1)S(1)}, bf16[4096]{0:T(1024)(128)(2,1)}, u32[]{:S(2)}) copy-start(bf16[4096]{0:T(1024)(128)(2,1)} %param.22) | copy-start | bytes 24580
  12.4 11.2 %copy-start.24 = (bf16[96,96]{1,0:T(8,128)(2,1)S(1)}, bf16[96,96]{1,0:T(8,128)(2,1)}, u32[]{:S(2)}) copy-start(bf16[96,96]{1,0:T(8,128)(2,1)} %constant.115) | copy-start | bytes 55300
  12.5 27.3 %copy-start.21 = (f32[96,24]{0,1:T(8,128)S(1)}, f32[96,24]{0,1:T(8,128)}, u32[]{:S(2)}) copy-start(f32[96,24]{0,1:T(8,128)} %constant.93) | copy-start | bytes 27652
  13.4 19.9 %collective-permute-start.1 = (bf16[2,192,1024]{2,1,0:T(8,128)(2,1)}, bf16[2,192,1024]{2,1,0:T(8,128)(2,1)S(1)}, u32[]{:S(2)}, u32[]{:S(2)}) collective-permute-start(bf16[2,192,1024]{2,1,0:T(8,128)(2,1)} %pad_maximum_fusion.1), channel_id=1, source_target_pairs={{0,1},{1,2},{2,3},{3,0},{4,5},{5,6},{6,7},{7,4},{8,9},{9,10},{10,1... | collective-permute-start | bytes 2359304 | tf_op jit(solution)/shard_map/ppermute | solution.py:137
  15.8 18.4 %collective-permute-start.2 = (bf16[2,192,1024]{2,1,0:T(8,128)(2,1)}, bf16[2,192,1024]{2,1,0:T(8,128)(2,1)S(1)}, u32[]{:S(2)}, u32[]{:S(2)}) collective-permute-start(bf16[2,192,1024]{2,1,0:T(8,128)(2,1)} %pad_maximum_fusion.2), channel_id=1, source_target_pairs={{0,3},{1,0},{2,1},{3,2},{4,7},{5,4},{6,5},{7,6},{8,11},{9,8},{10,9... | collective-permute-start | bytes 2359304 | tf_op jit(solution)/shard_map/ppermute | solution.py:137
  33.3 14.4 %copy-start.7 = (bf16[2,192,1024]{2,1,0:T(8,128)(2,1)}, bf16[2,192,1024]{2,1,0:T(8,128)(2,1)S(1)}, u32[]{:S(2)}) copy-start(bf16[2,192,1024]{2,1,0:T(8,128)(2,1)S(1)} %collective-permute-done.1.w_below) | copy-start | bytes 2359300
  34.2 13.5 %copy-start.10 = (bf16[2,192,1024]{2,1,0:T(8,128)(2,1)}, bf16[2,192,1024]{2,1,0:T(8,128)(2,1)S(1)}, u32[]{:S(2)}) copy-start(bf16[2,192,1024]{2,1,0:T(8,128)(2,1)S(1)} %collective-permute-done.2.w_above) | copy-start | bytes 2359300
  34.2 13.5 %copy-start.3 = (bf16[128,4096]{1,0:T(8,128)(2,1)}, bf16[128,4096]{1,0:T(8,128)(2,1)S(1)}, u32[]{:S(2)}) copy-start(bf16[128,4096]{1,0:T(8,128)(2,1)S(1)} %collective-permute-done.lent_gate_low) | copy-start | bytes 3145732
  34.9 11.5 %all-to-all-start.1 = ((bf16[8,12,512]{2,1,0:T(8,128)(2,1)}), bf16[8,12,512]{2,1,0:T(8,128)(2,1)S(1)}, u32[]{:S(2)}, u32[]{:S(2)}) async-start(bf16[8,12,512]{2,1,0:T(8,128)(2,1)} %bitcast.8), calls=%async_computation.1 | async-start | bytes 262144 | tf_op jit(solution)/shard_map/all_to_all | solution.py:132
  47.7 15.7 %copy-start = (bf16[2,192,4096]{2,1,0:T(8,128)(2,1)S(1)}, bf16[2,192,4096]{2,1,0:T(8,128)(2,1)}, u32[]{:S(2)}) copy-start(bf16[2,192,4096]{2,1,0:T(8,128)(2,1)} %own_gate.3) | copy-start | bytes 9437188
  47.7 37.0 %all-to-all-start.2 = ((bf16[32,24,512]{2,1,0:T(8,128)(2,1)}), bf16[32,24,512]{2,1,0:T(8,128)(2,1)}, u32[]{:S(2)}, u32[]{:S(2)}) async-start(bf16[32,24,512]{2,1,0:T(8,128)(2,1)} %bitcast.54), calls=%async_computation.2 | async-start | bytes 1572864 | tf_op jit(solution)/shard_map/all_to_all | solution.py:132
  62.3 22.4 %collective-permute-start.3 = (bf16[2,192,1024]{2,1,0:T(8,128)(2,1)S(1)}, bf16[2,192,1024]{2,1,0:T(8,128)(2,1)}, u32[]{:S(2)}, u32[]{:S(2)}) collective-permute-start(bf16[2,192,1024]{2,1,0:T(8,128)(2,1)S(1)} %pad_maximum_fusion.3), channel_id=1, source_target_pairs={{0,2},{1,3},{2,0},{3,1},{4,6},{5,7},{6,4},{7,5},{8,10},{9,11},{10,... | collective-permute-start | bytes 2359304 | tf_op jit(solution)/shard_map/ppermute | solution.py:137
  63.4 20.4 %collective-permute-start.4 = (bf16[64,4096]{1,0:T(8,128)(2,1)S(1)}, bf16[64,4096]{1,0:T(8,128)(2,1)S(1)}, u32[]{:S(2)}, u32[]{:S(2)}) collective-permute-start(bf16[64,4096]{1,0:T(8,128)(2,1)S(1)} %dynamic-slice_bitcast_fusion.2), channel_id=1, source_target_pairs={{0,4},{1,5},{2,6},{3,7},{4,0},{5,1},{6,2},{7,3},{8,12},{9,13},{10,... | collective-permute-start | bytes 1572872 | tf_op jit(solution)/shard_map/ppermute | solution.py:141
  65.7 52.0 %collective-permute-start.9 = (bf16[192,4096]{1,0:T(8,128)(2,1)}, bf16[192,4096]{1,0:T(8,128)(2,1)}, u32[]{:S(2)}, u32[]{:S(2)}) collective-permute-start(bf16[192,4096]{1,0:T(8,128)(2,1)} %dynamic-slice_bitcast_fusion), channel_id=1, source_target_pairs={{0,4},{1,5},{2,6},{3,7},{4,0},{5,1},{6,2},{7,3},{8,12},{9,13},{10,... | collective-permute-start | bytes 4718600 | tf_op jit(solution)/shard_map/ppermute | solution.py:141
  87.2 30.5 %copy-start.2 = (bf16[2,192,4096]{2,1,0:T(8,128)(2,1)S(1)}, bf16[2,192,4096]{2,1,0:T(8,128)(2,1)}, u32[]{:S(2)}) copy-start(bf16[2,192,4096]{2,1,0:T(8,128)(2,1)} %own_up.3) | copy-start | bytes 9437188
  87.2 30.5 %copy-start.4 = (bf16[128,4096]{1,0:T(8,128)(2,1)S(1)}, bf16[128,4096]{1,0:T(8,128)(2,1)}, u32[]{:S(2)}) copy-start(bf16[128,4096]{1,0:T(8,128)(2,1)} %copy-done.3) | copy-start | bytes 3145732
  87.2 30.5 %copy-start.6 = (bf16[64,4096]{1,0:T(8,128)(2,1)S(1)}, bf16[64,4096]{1,0:T(8,128)(2,1)}, u32[]{:S(2)}) copy-start(bf16[64,4096]{1,0:T(8,128)(2,1)} %copy-done.5) | copy-start | bytes 1572868
  87.2 20.6 %collective-permute-start.5 = (bf16[384,1024]{1,0:T(8,128)(2,1)S(1)}, bf16[384,1024]{1,0:T(8,128)(2,1)S(1)}, u32[]{:S(2)}, u32[]{:S(2)}) collective-permute-start(bf16[384,1024]{1,0:T(8,128)(2,1)S(1)} %bitcast.49), channel_id=1, source_target_pairs={{0,1},{1,2},{2,3},{3,0},{4,5},{5,6},{6,7},{7,4},{8,9},{9,10},{10,1... | collective-permute-start | bytes 2359304 | tf_op jit(solution)/shard_map/ppermute | solution.py:137
  88.2 19.7 %collective-permute-start.7 = (bf16[384,1024]{1,0:T(8,128)(2,1)S(1)}, bf16[384,1024]{1,0:T(8,128)(2,1)S(1)}, u32[]{:S(2)}, u32[]{:S(2)}) collective-permute-start(bf16[384,1024]{1,0:T(8,128)(2,1)S(1)} %bitcast.50), channel_id=1, source_target_pairs={{0,3},{1,0},{2,1},{3,2},{4,7},{5,4},{6,5},{7,6},{8,11},{9,8},{10,9... | collective-permute-start | bytes 2359304 | tf_op jit(solution)/shard_map/ppermute | solution.py:137
  91.7 59.4 %collective-permute-start.14 = (bf16[768,1024]{1,0:T(8,128)(2,1)S(1)}, bf16[768,1024]{1,0:T(8,128)(2,1)S(1)}, u32[]{:S(2)}, u32[]{:S(2)}) collective-permute-start(bf16[768,1024]{1,0:T(8,128)(2,1)S(1)} %pad_maximum_fusion), channel_id=1, source_target_pairs={{0,4},{1,5},{2,6},{3,7},{4,0},{5,1},{6,2},{7,3},{8,12},{9,13},{10,... | collective-permute-start | bytes 4718600 | tf_op jit(solution)/shard_map/ppermute | solution.py:141
  107.8 15.1 %collective-permute-start.6 = (bf16[192,1024]{1,0:T(8,128)(2,1)S(1)}, bf16[192,1024]{1,0:T(8,128)(2,1)S(1)}, u32[]{:S(2)}, u32[]{:S(2)}) collective-permute-start(bf16[192,1024]{1,0:T(8,128)(2,1)S(1)} %slice.38), channel_id=1, source_target_pairs={{0,1},{1,2},{2,3},{3,0},{4,5},{5,6},{6,7},{7,4},{8,9},{9,10},{10,1... | collective-permute-start | bytes 1179656 | tf_op jit(solution)/shard_map/ppermute | solution.py:137
  108.0 15.0 %collective-permute-start.8 = (bf16[192,1024]{1,0:T(8,128)(2,1)S(1)}, bf16[192,1024]{1,0:T(8,128)(2,1)S(1)}, u32[]{:S(2)}, u32[]{:S(2)}) collective-permute-start(bf16[192,1024]{1,0:T(8,128)(2,1)S(1)} %slice.39), channel_id=1, source_target_pairs={{0,3},{1,0},{2,1},{3,2},{4,7},{5,4},{6,5},{7,6},{8,11},{9,8},{10,9... | collective-permute-start | bytes 1179656 | tf_op jit(solution)/shard_map/ppermute | solution.py:137
  122.9 16.2 %copy-start.20 = (bf16[1,192,1024]{2,1,0:T(8,128)(2,1)S(1)}, bf16[1,192,1024]{2,1,0:T(8,128)(2,1)}, u32[]{:S(2)}) copy-start(bf16[1,192,1024]{2,1,0:T(8,128)(2,1)} %get-tuple-element.37) | copy-start | bytes 1179652
  123.0 28.2 %copy-start.9 = (bf16[2,192,1024]{2,1,0:T(8,128)(2,1)S(1)}, bf16[2,192,1024]{2,1,0:T(8,128)(2,1)}, u32[]{:S(2)}) copy-start(bf16[2,192,1024]{2,1,0:T(8,128)(2,1)} %copy-done.7) | copy-start | bytes 2359300
  123.0 28.2 %copy-start.12 = (bf16[2,192,1024]{2,1,0:T(8,128)(2,1)S(1)}, bf16[2,192,1024]{2,1,0:T(8,128)(2,1)}, u32[]{:S(2)}) copy-start(bf16[2,192,1024]{2,1,0:T(8,128)(2,1)} %copy-done.10) | copy-start | bytes 2359300
  125.8 10.0 %collective-permute-start.10 = (bf16[384,384]{1,0:T(8,128)(2,1)S(1)}, bf16[384,384]{1,0:T(8,128)(2,1)S(1)}, u32[]{:S(2)}, u32[]{:S(2)}) collective-permute-start(bf16[384,384]{1,0:T(8,128)(2,1)S(1)} %expand_far.1.own), channel_id=1, source_target_pairs={{0,1},{1,2},{2,3},{3,0},{4,5},{5,6},{6,7},{7,4},{8,9},{9,10},{10,1... | collective-permute-start | bytes 884744 | tf_op jit(solution)/shard_map/ppermute | solution.py:137
  126.8 9.1 %collective-permute-start.11 = (bf16[384,384]{1,0:T(8,128)(2,1)S(1)}, bf16[384,384]{1,0:T(8,128)(2,1)S(1)}, u32[]{:S(2)}, u32[]{:S(2)}) collective-permute-start(bf16[384,384]{1,0:T(8,128)(2,1)S(1)} %expand_far.1.own), channel_id=1, source_target_pairs={{0,3},{1,0},{2,1},{3,2},{4,7},{5,4},{6,5},{7,6},{8,11},{9,8},{10,9... | collective-permute-start | bytes 884744 | tf_op jit(solution)/shard_map/ppermute | solution.py:137
  135.8 15.3 %collective-permute-start.12 = (bf16[192,384]{1,0:T(8,128)(2,1)S(1)}, bf16[192,384]{1,0:T(8,128)(2,1)S(1)}, u32[]{:S(2)}, u32[]{:S(2)}) collective-permute-start(bf16[192,384]{1,0:T(8,128)(2,1)S(1)} %slice.40), channel_id=1, source_target_pairs={{0,1},{1,2},{2,3},{3,0},{4,5},{5,6},{6,7},{7,4},{8,9},{9,10},{10,1... | collective-permute-start | bytes 442376 | tf_op jit(solution)/shard_map/ppermute | solution.py:137
  135.9 15.2 %collective-permute-start.13 = (bf16[192,384]{1,0:T(8,128)(2,1)S(1)}, bf16[192,384]{1,0:T(8,128)(2,1)S(1)}, u32[]{:S(2)}, u32[]{:S(2)}) collective-permute-start(bf16[192,384]{1,0:T(8,128)(2,1)S(1)} %slice.41), channel_id=1, source_target_pairs={{0,3},{1,0},{2,1},{3,2},{4,7},{5,4},{6,5},{7,6},{8,11},{9,8},{10,9... | collective-permute-start | bytes 442376 | tf_op jit(solution)/shard_map/ppermute | solution.py:137
  188.2 10.2 %all-to-all-start.4 = ((bf16[8,12,512]{2,1,0:T(8,128)(2,1)}), bf16[8,12,512]{2,1,0:T(8,128)(2,1)S(1)}, u32[]{:S(2)}, u32[]{:S(2)}) async-start(bf16[8,12,512]{2,1,0:T(8,128)(2,1)} %reshape.96), calls=%async_computation.4 | async-start | bytes 262144 | tf_op jit(solution)/shard_map/all_to_all | solution.py:132
  (14 other events, 71.8 us)

commit v6 on v5

--- a/solution.py
+++ b/solution.py
@@ -349,7 +349,7 @@
     routing = jnp.broadcast_to(routing[:, None], (N_EXP, 2, LOCAL, 2 * TOPK))
     routing = routing.reshape(KEYS, 2 * TOPK)
 
-    early = 2 * UNITS // 3
+    early = 3 * UNITS // 4
     lent_gate_low = across(lax.dynamic_slice(gate_weight, (1 - side, 0, 0), (1, early, D))[0])
 
     def quarter(weight, step):
@@ -370,25 +370,25 @@
     normed = jnp.broadcast_to(
         normed.reshape(1, 4, 2 * LOCAL, HALF), (2, 4, 2 * LOCAL, HALF)
     ).reshape(N_EXP, 2 * LOCAL, HALF)
-    normed, lent_gate_low, kept_near = lax.optimization_barrier((normed, lent_gate_low, kept_near))
+    normed, lent_gate_low, kept_near, gate_late, up_late = lax.optimization_barrier(
+        (normed, lent_gate_low, kept_near, gate_weight, up_weight)
+    )
     tokens = exchange(normed, "exp").reshape(KEYS, HALF)
     table, combine = routing_tables(routing[:, :TOPK], routing[:, TOPK:], side, groups)
     outbound = lax.dot_general(
         table, tokens, (((0,), (0,)), ((), ())), preferred_element_type=jnp.float32
     ).astype(jnp.bfloat16)
 
-    outbound, gate_late, up_late, down_late = lax.optimization_barrier(
-        (outbound, gate_weight, up_weight, down_weight)
+    lent_gate_high = across(
+        lax.dynamic_slice(gate_late, (1 - side, early, 0), (1, UNITS - early, D))[0]
+    )
+    lent_up = across(lax.dynamic_index_in_dim(up_late, 1 - side, 0, keepdims=False))
+    outbound, lent_gate_high, down_late = lax.optimization_barrier(
+        (outbound, lent_gate_high, down_weight)
     )
     inbound = exchange(outbound.reshape(groups, WIRE, HALF), "rep")
     kept_far = shift(quarter(down_late, 2), 2)
-    lent_gate_high = across(
-        lax.dynamic_slice(gate_late, (1 - side, early, 0), (1, UNITS - early, D))[0]
-    )
-    lent_up = across(lax.dynamic_index_in_dim(up_late, 1 - side, 0, keepdims=False))
-    inbound, kept_far, lent_gate_high = lax.optimization_barrier(
-        (inbound, kept_far, lent_gate_high)
-    )
+    inbound, kept_far, lent_up = lax.optimization_barrier((inbound, kept_far, lent_up))
     kept = [quarter(down_late, 0), *kept_near, kept_far]
     lent_down = across(jnp.concatenate([block[1] for block in kept]))
     slotted = inbound.reshape(groups, 2, PLACES, HALF).transpose(0, 2, 1, 3).reshape(rows, BLK)

time: 200 us -> 203 us (1.015)
  waiting for transfers between devices: 79.1 us -> 68 us
  local copies, waits for them, and re-layouts: 19.6 us -> 24.2 us
  starting transfers between devices: 48.7 us -> 52 us
  blocking collectives: 31.6 us -> 34.7 us
    ppermute x4, waiting for transfers between devices: 34.1 us -> 8.35 us  [across(): return lax.ppermute(array, 'exp', [(e, e ^ 4) for e in range(N_EXP)])]
    ppermute x11, waiting for transfers between devices: 32 us -> 50.8 us  [shift(): return lax.ppermute(array, 'exp', pairs)]
    all_to_all x4, waiting for transfers between devices: 13.1 us -> 8.84 us  [exchange(): return lax.all_to_all(array, axis, split_axis=0, concat_axis=0, tiled=True)]
    all_to_all x1, blocking collectives: 31.6 us -> 34.7 us  [exchange(): return lax.all_to_all(array, axis, split_axis=0, concat_axis=0, tiled=True)]
    ppermute x11, starting transfers between devices: 17.8 us -> 20 us  [shift(): return lax.ppermute(array, 'exp', pairs)]
  transfers between devices with their start and end apart: 19 -> 19, of which waited for: 9 -> 13; matrix products, arithmetic and copies ran while one was open for 8% -> 11% of each run, Pallas kernels for 5% -> 5%
where the time goes in v6:
time: 203 us; the launch traced here: 202 us
  waiting for transfers between devices  68 us (33%)
  starting transfers between devices  52 us (26%)
  blocking collectives  34.7 us (17%)
  local copies, waits for them, and re-layouts  24.2 us (12%)
  Pallas kernels  14.4 us (7%)
  other arithmetic  5.29 us (3%)
  matrix products  2.9 us (1%)
    ppermute x11, waiting for transfers between devices, shift(): return lax.ppermute(array, 'exp', pairs)  50.8 us
    all_to_all x1, blocking collectives, exchange(): return lax.all_to_all(array, axis, split_axis=0, concat_axis=0, tiled=True)  34.7 us
    all_to_all x4, starting transfers between devices, exchange(): return lax.all_to_all(array, axis, split_axis=0, concat_axis=0, tiled=True)  26.9 us
    ppermute x11, starting transfers between devices, shift(): return lax.ppermute(array, 'exp', pairs)  20 us
    all_to_all x4, waiting for transfers between devices, exchange(): return lax.all_to_all(array, axis, split_axis=0, concat_axis=0, tiled=True)  8.84 us
    ppermute x4, waiting for transfers between devices, across(): return lax.ppermute(array, 'exp', [(e, e ^ 4) for e in range(N_EXP)])  8.35 us
    pallas_call x2, Pallas kernels, call(): pl.pallas_call(kernel, out_shape=out_shape, grid_spec=pltpu.PrefetchScala...  8.13 us
    ppermute x4, starting transfers between devices, across(): return lax.ppermute(array, 'exp', [(e, e ^ 4) for e in range(N_EXP)])  5.1 us
  transfers between devices with their start and end apart: 19, of which 13 were waited for; matrix products, arithmetic and copies ran while one was open for 11% of the time, Pallas kernels for 5%

profile of v6, /device:TPU:4, one launch (start us, length us, event | category | flops | bytes accessed | tf_op | source)
XLA Modules:
  0.0 202.0 jit_solution(3563377700848884756)
XLA Ops:
  1.4 5.1 %all-to-all-start = ((s32[8,6,16]{2,1,0:T(8,128)}), s32[8,6,16]{2,1,0:T(8,128)S(1)}, u32[]{:S(2)}, u32[]{:S(2)}) async-start(s32[8,6,16]{2,1,0:T(8,128)} %broadcast_in_dim.15), calls=%async_computation | async-start | bytes 65536 | tf_op jit(solution)/shard_map/all_to_all | solution.py:132
  6.5 2.4 %dynamic-slice_bitcast_fusion.1 = bf16[144,4096]{1,0:T(8,128)(2,1)} fusion(bf16[2,192,4096]{2,1,0:T(8,128)(2,1)} %own_gate.3, s32[]{:T(128)S(6)} %select_n.66), kind=kLoop, calls=%fused_computation.3 | loop fusion | bytes 2359300 | tf_op jit(solution)/shard_map/squeeze | solution.py:353
  8.9 2.0 %collective-permute-start = (bf16[144,4096]{1,0:T(8,128)(2,1)}, bf16[144,4096]{1,0:T(8,128)(2,1)}, u32[]{:S(2)}, u32[]{:S(2)}) collective-permute-start(bf16[144,4096]{1,0:T(8,128)(2,1)} %dynamic-slice_bitcast_fusion.1), channel_id=1, source_target_pairs={{0,4},{1,5},{2,6},{3,7},{4,0},{5,1},{6,2},{7,3},{8,12},{9,13},{10,... | collective-permute-start | bytes 3538952 | tf_op jit(solution)/shard_map/ppermute | solution.py:141
  15.9 1.8 collective-permute-start.2
  20.4 2.8 %attend.1 = (f32[6,32,128]{2,1,0:T(8,128)S(1)}, bf16[6,32,128]{2,1,0:T(8,128)(2,1)S(1)}) custom-call(s32[2]{0:T(128)S(1)} %copy-done.7, bf16[6,32,128]{2,1,0:T(8,128)(2,1)S(1)} %reshape.83.query, bf16[2,1024,256]{2,1,0:T(8,128)(2,1)S(1)} %copy-done.2, bf16[2,1024,256]{2,1,0:T(8,128)(2,1)S(1)} %copy-done.3, bf16[2,8,256]{2,1,0:T(8,128)(2,1)S(1)} %pad.7.fresh_keys, ...), custom_call_target="tpu_custom_call" | custom-call | flops 100663296 | bytes 2342912 | tf_op jit(solution)/shard_map/attend/pallas_call | solution.py:90
  25.8 7.7 %collective-permute-done.1.w_below = bf16[2,192,1024]{2,1,0:T(8,128)(2,1)} collective-permute-done((bf16[2,192,1024]{2,1,0:T(8,128)(2,1)}, bf16[2,192,1024]{2,1,0:T(8,128)(2,1)}, u32[]{:S(2)}, u32[]{:S(2)}) %collective-permute-start.1) | collective-permute-done | bytes 786464 | tf_op jit(solution)/shard_map/ppermute | solution.py:137
  34.4 2.3 %collective-permute-done.lent_gate_low = bf16[144,4096]{1,0:T(8,128)(2,1)} collective-permute-done((bf16[144,4096]{1,0:T(8,128)(2,1)}, bf16[144,4096]{1,0:T(8,128)(2,1)}, u32[]{:S(2)}, u32[]{:S(2)}) %collective-permute-start) | collective-permute-done | bytes 1179680 | tf_op jit(solution)/shard_map/ppermute | solution.py:141
  37.4 5.4 %all-to-all-start.1 = ((bf16[8,12,512]{2,1,0:T(8,128)(2,1)}), bf16[8,12,512]{2,1,0:T(8,128)(2,1)}, u32[]{:S(2)}, u32[]{:S(2)}) async-start(bf16[8,12,512]{2,1,0:T(8,128)(2,1)} %bitcast.8), calls=%async_computation.1 | async-start | bytes 262144 | tf_op jit(solution)/shard_map/all_to_all | solution.py:132
  43.6 2.0 collective-permute-start.3
  45.6 2.7 %dynamic-slice_bitcast_fusion = bf16[192,4096]{1,0:T(8,128)(2,1)} fusion(bf16[2,192,4096]{2,1,0:T(8,128)(2,1)} %own_up.3, s32[]{:T(128)S(6)} %select_n.66), kind=kLoop, calls=%fused_computation.1 | loop fusion | bytes 3145732 | tf_op jit(solution)/shard_map/jit(dynamic_index_in_dim)/squeeze | solution.py:385
  51.4 2.2 %convolution_convert_fusion = bf16[768,512]{1,0:T(8,128)(2,1)} fusion(bf16[96,768]{0,1:T(8,128)(2,1)} %bitcast.58, bf16[96,512]{1,0:T(8,128)(2,1)} %reshape.90), kind=kOutput, calls=%fused_computation.2 | convolution fusion | flops 75890688 | bytes 1032192 | tf_op jit(solution)/shard_map/dot_general | solution.py:378
  53.7 2.8 %collective-permute-done.3.lent_gate_high = bf16[48,4096]{1,0:T(8,128)(2,1)S(1)} collective-permute-done((bf16[48,4096]{1,0:T(8,128)(2,1)}, bf16[48,4096]{1,0:T(8,128)(2,1)S(1)}, u32[]{:S(2)}, u32[]{:S(2)}) %collective-permute-start.3) | collective-permute-done | bytes 393248 | tf_op jit(solution)/shard_map/ppermute | solution.py:141
  56.4 11.6 %all-to-all-start.2 = ((bf16[32,24,512]{2,1,0:T(8,128)(2,1)}), bf16[32,24,512]{2,1,0:T(8,128)(2,1)}, u32[]{:S(2)}, u32[]{:S(2)}) async-start(bf16[32,24,512]{2,1,0:T(8,128)(2,1)} %bitcast.54), calls=%async_computation.2 | async-start | bytes 1572864 | tf_op jit(solution)/shard_map/all_to_all | solution.py:132
  68.1 2.5 %constant_dynamic-slice_fusion.1 = (bf16[1,192,1024]{2,1,0:T(8,128)(2,1)}, bf16[1,192,1024]{2,1,0:T(8,128)(2,1)}, bf16[1,192,1024]{2,1,0:T(8,128)(2,1)S(1)}, bf16[1,192,1024]{2,1,0:T(8,128)(2,1)S(1)}) fusion(bf16[2,192,4096]{2,1,0:T(8,128)(2,1)} %param.27, s32[]{:T(128)S(6)} %select_n.67, s32[]{:T(128)S(6)} %select_n.75, s32[]{:T(128)S(6)} %select_n.66, ...), kind=kLoop, calls=%fused_computation.34 | loop fusion | bytes 3145744 | tf_op jit(solution)/shard_map/dynamic_slice | solution.py:359
  70.7 3.1 %collective-permute-start.4 = (bf16[2,192,1024]{2,1,0:T(8,128)(2,1)S(1)}, bf16[2,192,1024]{2,1,0:T(8,128)(2,1)}, u32[]{:S(2)}, u32[]{:S(2)}) collective-permute-start(bf16[2,192,1024]{2,1,0:T(8,128)(2,1)S(1)} %pad_maximum_fusion.3), channel_id=1, source_target_pairs={{0,2},{1,3},{2,0},{3,1},{4,6},{5,7},{6,4},{7,5},{8,10},{9,11},{10,... | collective-permute-start | bytes 2359304 | tf_op jit(solution)/shard_map/ppermute | solution.py:137
  73.8 2.1 %slice_bitcast_fusion.1 = (bf16[192,1024]{1,0:T(8,128)(2,1)}, bf16[192,1024]{1,0:T(8,128)(2,1)}) fusion(bf16[2,192,1024]{2,1,0:T(8,128)(2,1)} %collective-permute-done.2.w_above, bf16[2,192,1024]{2,1,0:T(8,128)(2,1)} %collective-permute-done.1.w_below), kind=kLoop, calls=%fused_computation.15 | loop fusion | bytes 1572864 | tf_op jit(solution)/shard_map/squeeze | solution.py:393
  75.8 16.2 %collective-permute-done.4.w_far = bf16[2,192,1024]{2,1,0:T(8,128)(2,1)} collective-permute-done((bf16[2,192,1024]{2,1,0:T(8,128)(2,1)S(1)}, bf16[2,192,1024]{2,1,0:T(8,128)(2,1)}, u32[]{:S(2)}, u32[]{:S(2)}) %collective-permute-start.4) | collective-permute-done | bytes 786464 | tf_op jit(solution)/shard_map/ppermute | solution.py:137
  92.0 3.3 %collective-permute-done.5.lent_up = bf16[192,4096]{1,0:T(8,128)(2,1)} collective-permute-done((bf16[192,4096]{1,0:T(8,128)(2,1)}, bf16[192,4096]{1,0:T(8,128)(2,1)}, u32[]{:S(2)}, u32[]{:S(2)}) %collective-permute-start.5) | collective-permute-done | bytes 1572896 | tf_op jit(solution)/shard_map/ppermute | solution.py:141
  100.0 1.8 collective-permute-start.8
  104.1 15.3 %collective-permute-done.6.below_rows = bf16[384,1024]{1,0:T(8,128)(2,1)S(1)} collective-permute-done((bf16[384,1024]{1,0:T(8,128)(2,1)S(1)}, bf16[384,1024]{1,0:T(8,128)(2,1)S(1)}, u32[]{:S(2)}, u32[]{:S(2)}) %collective-permute-start.6) | collective-permute-done | bytes 786464 | tf_op jit(solution)/shard_map/ppermute | solution.py:137
  119.7 3.2 %collective-permute-start.9 = (bf16[192,1024]{1,0:T(8,128)(2,1)S(1)}, bf16[192,1024]{1,0:T(8,128)(2,1)S(1)}, u32[]{:S(2)}, u32[]{:S(2)}) collective-permute-start(bf16[192,1024]{1,0:T(8,128)(2,1)S(1)} %slice.39), channel_id=1, source_target_pairs={{0,3},{1,0},{2,1},{3,2},{4,7},{5,4},{6,5},{7,6},{8,11},{9,8},{10,9... | collective-permute-start | bytes 1179656 | tf_op jit(solution)/shard_map/ppermute | solution.py:137
  123.1 5.3 %expand_near.1 = (f32[384,384]{1,0:T(8,128)S(1)}, f32[384,384]{1,0:T(8,128)S(1)}) custom-call(s32[2]{0:T(128)S(1)} %pad_add_fusion.1.where, bf16[384,1024]{1,0:T(8,128)(2,1)S(1)} %bitcast.51, bf16[384,1024]{1,0:T(8,128)(2,1)S(1)} %collective-permute-done.6.below_rows, bf16[384,1024]{1,0:T(8,128)(2,1)S(1)} %collective-permute-done.8.above_rows, ...), custom_call_target="tpu_custom_call" | custom-call | flops 1811939328 | bytes 8257536 | tf_op jit(solution)/shard_map/expand_near/pallas_call | solution.py:269
  128.3 2.6 %collective-permute-done.7.far_low = bf16[192,1024]{1,0:T(8,128)(2,1)S(1)} collective-permute-done((bf16[192,1024]{1,0:T(8,128)(2,1)S(1)}, bf16[192,1024]{1,0:T(8,128)(2,1)S(1)}, u32[]{:S(2)}, u32[]{:S(2)}) %collective-permute-start.7) | collective-permute-done | bytes 393248 | tf_op jit(solution)/shard_map/ppermute | solution.py:137
  131.0 2.9 %expand_far.1.own = bf16[384,384]{1,0:T(8,128)(2,1)S(1)} custom-call(s32[2]{0:T(128)S(1)} %pad_add_fusion.1.where, bf16[192,1024]{1,0:T(8,128)(2,1)S(1)} %collective-permute-done.7.far_low, bf16[192,1024]{1,0:T(8,128)(2,1)S(1)} %collective-permute-done.9.far_high, f32[384,384]{1,0:T(8,128)S(1)} %get-tuple-element.32.gate_total, ...), custom_call_target="tpu_custom_call" | custom-call | flops 603979776 | bytes 3538944 | tf_op jit(solution)/shard_map/expand_far/pallas_call | solution.py:269
  134.5 2.8 %collective-permute-start.11 = (bf16[384,384]{1,0:T(8,128)(2,1)S(1)}, bf16[384,384]{1,0:T(8,128)(2,1)S(1)}, u32[]{:S(2)}, u32[]{:S(2)}) collective-permute-start(bf16[384,384]{1,0:T(8,128)(2,1)S(1)} %expand_far.1.own), channel_id=1, source_target_pairs={{0,3},{1,0},{2,1},{3,2},{4,7},{5,4},{6,5},{7,6},{8,11},{9,8},{10,9... | collective-permute-start | bytes 884744 | tf_op jit(solution)/shard_map/ppermute | solution.py:137
  137.3 5.2 %collective-permute-done.10.below = bf16[384,384]{1,0:T(8,128)(2,1)S(1)} collective-permute-done((bf16[384,384]{1,0:T(8,128)(2,1)S(1)}, bf16[384,384]{1,0:T(8,128)(2,1)S(1)}, u32[]{:S(2)}, u32[]{:S(2)}) %collective-permute-start.10) | collective-permute-done | bytes 294944 | tf_op jit(solution)/shard_map/ppermute | solution.py:137
  142.6 3.3 %collective-permute-start.13 = (bf16[192,384]{1,0:T(8,128)(2,1)S(1)}, bf16[192,384]{1,0:T(8,128)(2,1)S(1)}, u32[]{:S(2)}, u32[]{:S(2)}) collective-permute-start(bf16[192,384]{1,0:T(8,128)(2,1)S(1)} %slice.41), channel_id=1, source_target_pairs={{0,3},{1,0},{2,1},{3,2},{4,7},{5,4},{6,5},{7,6},{8,11},{9,8},{10,9... | collective-permute-start | bytes 442376 | tf_op jit(solution)/shard_map/ppermute | solution.py:137
  146.0 2.9 %collective-permute-done.12.far_low = bf16[192,384]{1,0:T(8,128)(2,1)S(1)} collective-permute-done((bf16[192,384]{1,0:T(8,128)(2,1)S(1)}, bf16[192,384]{1,0:T(8,128)(2,1)S(1)}, u32[]{:S(2)}, u32[]{:S(2)}) %collective-permute-start.12) | collective-permute-done | bytes 147488 | tf_op jit(solution)/shard_map/ppermute | solution.py:137
  148.9 3.4 %contract.1 = bf16[384,1024]{1,0:T(8,128)(2,1)S(1)} custom-call(bf16[384,384]{1,0:T(8,128)(2,1)S(1)} %expand_far.1.own, bf16[384,384]{1,0:T(8,128)(2,1)S(1)} %collective-permute-done.10.below, bf16[384,384]{1,0:T(8,128)(2,1)S(1)} %collective-permute-done.11.above, bf16[192,384]{1,0:T(8,128)(2,1)S(1)} %collective-permute-done.12.far_low, ...), custom_call_target="tpu_custom_call" | custom-call | flops 1207959552 | bytes 5111808 | tf_op jit(solution)/shard_map/contract/pallas_call | solution.py:314
  153.6 34.7 %all_to_all.25 = bf16[32,24,512]{2,1,0:T(8,128)(2,1)S(1)} all-to-all(bf16[32,24,512]{2,1,0:T(8,128)(2,1)S(1)} %copy.79), channel_id=1, replica_groups=mesh['rep'=32,'exp'=8] {'rep'}, dimensions={0} | all-to-all | bytes 1572864 | tf_op jit(solution)/shard_map/all_to_all | solution.py:132
  189.5 4.8 %all-to-all-start.4 = ((bf16[8,12,512]{2,1,0:T(8,128)(2,1)}), bf16[8,12,512]{2,1,0:T(8,128)(2,1)S(1)}, u32[]{:S(2)}, u32[]{:S(2)}) async-start(bf16[8,12,512]{2,1,0:T(8,128)(2,1)} %reshape.96), calls=%async_computation.4 | async-start | bytes 262144 | tf_op jit(solution)/shard_map/all_to_all | solution.py:132
  194.4 6.5 %all-to-all-done.4 = bf16[8,12,512]{2,1,0:T(8,128)(2,1)S(1)} async-done(((bf16[8,12,512]{2,1,0:T(8,128)(2,1)}), bf16[8,12,512]{2,1,0:T(8,128)(2,1)S(1)}, u32[]{:S(2)}, u32[]{:S(2)}) %all-to-all-start.4) | async-done | bytes 98336 | tf_op jit(solution)/shard_map/all_to_all | solution.py:132
  (109 shorter events, 28.8 us)
Async XLA Ops:
  1.4 22.5 %all-to-all-start = ((s32[8,6,16]{2,1,0:T(8,128)}), s32[8,6,16]{2,1,0:T(8,128)S(1)}, u32[]{:S(2)}, u32[]{:S(2)}) async-start(s32[8,6,16]{2,1,0:T(8,128)} %broadcast_in_dim.15), calls=%async_computation | async-start | bytes 65536 | tf_op jit(solution)/shard_map/all_to_all | solution.py:132
  8.9 27.7 %collective-permute-start = (bf16[144,4096]{1,0:T(8,128)(2,1)}, bf16[144,4096]{1,0:T(8,128)(2,1)}, u32[]{:S(2)}, u32[]{:S(2)}) collective-permute-start(bf16[144,4096]{1,0:T(8,128)(2,1)} %dynamic-slice_bitcast_fusion.1), channel_id=1, source_target_pairs={{0,4},{1,5},{2,6},{3,7},{4,0},{5,1},{6,2},{7,3},{8,12},{9,13},{10,... | collective-permute-start | bytes 3538952 | tf_op jit(solution)/shard_map/ppermute | solution.py:141
  11.0 6.8 %copy-start.18 = (bf16[3,2,256]{2,1,0:T(2,128)(2,1)S(1)}, bf16[3,2,256]{2,1,0:T(2,128)(2,1)}, u32[]{:S(2)}) copy-start(bf16[3,2,256]{2,1,0:T(2,128)(2,1)} %param.19) | copy-start | bytes 9220
  11.0 6.8 %copy-start.19 = (bf16[3,2,256]{2,1,0:T(2,128)(2,1)S(1)}, bf16[3,2,256]{2,1,0:T(2,128)(2,1)}, u32[]{:S(2)}) copy-start(bf16[3,2,256]{2,1,0:T(2,128)(2,1)} %param.20) | copy-start | bytes 9220
  11.0 6.9 %copy-start.16 = (bf16[3,2,4096]{2,1,0:T(2,128)(2,1)S(1)}, bf16[3,2,4096]{2,1,0:T(2,128)(2,1)}, u32[]{:S(2)}) copy-start(bf16[3,2,4096]{2,1,0:T(2,128)(2,1)} %param.15) | copy-start | bytes 147460
  11.0 6.9 %copy-start.6 = (bf16[4096]{0:T(1024)(128)(2,1)S(1)}, bf16[4096]{0:T(1024)(128)(2,1)}, u32[]{:S(2)}) copy-start(bf16[4096]{0:T(1024)(128)(2,1)} %param.22) | copy-start | bytes 24580
  11.0 6.9 %copy-start.7 = (s32[2]{0:T(128)S(1)}, s32[2]{0:T(128)}, u32[]{:S(2)}) copy-start(s32[2]{0:T(128)} %lengths.1) | copy-start | bytes 28
  12.5 12.4 %copy-start.17 = (bf16[96,96]{1,0:T(8,128)(2,1)S(1)}, bf16[96,96]{1,0:T(8,128)(2,1)}, u32[]{:S(2)}) copy-start(bf16[96,96]{1,0:T(8,128)(2,1)} %constant.115) | copy-start | bytes 55300
  12.6 12.5 %copy-start.13 = (f32[96,24]{0,1:T(8,128)S(1)}, f32[96,24]{0,1:T(8,128)}, u32[]{:S(2)}) copy-start(f32[96,24]{0,1:T(8,128)} %constant.93) | copy-start | bytes 27652
  13.5 29.3 %copy-start = (bf16[2,192,4096]{2,1,0:T(8,128)(2,1)S(1)}, bf16[2,192,4096]{2,1,0:T(8,128)(2,1)}, u32[]{:S(2)}) copy-start(bf16[2,192,4096]{2,1,0:T(8,128)(2,1)} %own_gate.3) | copy-start | bytes 9437188
  13.5 20.0 %collective-permute-start.1 = (bf16[2,192,1024]{2,1,0:T(8,128)(2,1)}, bf16[2,192,1024]{2,1,0:T(8,128)(2,1)}, u32[]{:S(2)}, u32[]{:S(2)}) collective-permute-start(bf16[2,192,1024]{2,1,0:T(8,128)(2,1)} %pad_maximum_fusion.1), channel_id=1, source_target_pairs={{0,1},{1,2},{2,3},{3,0},{4,5},{5,6},{6,7},{7,4},{8,9},{9,10},{10,1... | collective-permute-start | bytes 2359304 | tf_op jit(solution)/shard_map/ppermute | solution.py:137
  15.9 18.5 %collective-permute-start.2 = (bf16[2,192,1024]{2,1,0:T(8,128)(2,1)}, bf16[2,192,1024]{2,1,0:T(8,128)(2,1)}, u32[]{:S(2)}, u32[]{:S(2)}) collective-permute-start(bf16[2,192,1024]{2,1,0:T(8,128)(2,1)} %pad_maximum_fusion.2), channel_id=1, source_target_pairs={{0,3},{1,0},{2,1},{3,2},{4,7},{5,4},{6,5},{7,6},{8,11},{9,8},{10,9... | collective-permute-start | bytes 2359304 | tf_op jit(solution)/shard_map/ppermute | solution.py:137
  37.4 12.5 %all-to-all-start.1 = ((bf16[8,12,512]{2,1,0:T(8,128)(2,1)}), bf16[8,12,512]{2,1,0:T(8,128)(2,1)}, u32[]{:S(2)}, u32[]{:S(2)}) async-start(bf16[8,12,512]{2,1,0:T(8,128)(2,1)} %bitcast.8), calls=%async_computation.1 | async-start | bytes 262144 | tf_op jit(solution)/shard_map/all_to_all | solution.py:132
  43.6 12.8 %collective-permute-start.3 = (bf16[48,4096]{1,0:T(8,128)(2,1)}, bf16[48,4096]{1,0:T(8,128)(2,1)S(1)}, u32[]{:S(2)}, u32[]{:S(2)}) collective-permute-start(bf16[48,4096]{1,0:T(8,128)(2,1)} %dynamic-slice_bitcast_fusion.2), channel_id=1, source_target_pairs={{0,4},{1,5},{2,6},{3,7},{4,0},{5,1},{6,2},{7,3},{8,12},{9,13},{10,... | collective-permute-start | bytes 1179656 | tf_op jit(solution)/shard_map/ppermute | solution.py:141
  48.3 47.0 %collective-permute-start.5 = (bf16[192,4096]{1,0:T(8,128)(2,1)}, bf16[192,4096]{1,0:T(8,128)(2,1)}, u32[]{:S(2)}, u32[]{:S(2)}) collective-permute-start(bf16[192,4096]{1,0:T(8,128)(2,1)} %dynamic-slice_bitcast_fusion), channel_id=1, source_target_pairs={{0,4},{1,5},{2,6},{3,7},{4,0},{5,1},{6,2},{7,3},{8,12},{9,13},{10,... | collective-permute-start | bytes 4718600 | tf_op jit(solution)/shard_map/ppermute | solution.py:141
  56.4 39.6 %all-to-all-start.2 = ((bf16[32,24,512]{2,1,0:T(8,128)(2,1)}), bf16[32,24,512]{2,1,0:T(8,128)(2,1)}, u32[]{:S(2)}, u32[]{:S(2)}) async-start(bf16[32,24,512]{2,1,0:T(8,128)(2,1)} %bitcast.54), calls=%async_computation.2 | async-start | bytes 1572864 | tf_op jit(solution)/shard_map/all_to_all | solution.py:132
  70.7 21.3 %collective-permute-start.4 = (bf16[2,192,1024]{2,1,0:T(8,128)(2,1)S(1)}, bf16[2,192,1024]{2,1,0:T(8,128)(2,1)}, u32[]{:S(2)}, u32[]{:S(2)}) collective-permute-start(bf16[2,192,1024]{2,1,0:T(8,128)(2,1)S(1)} %pad_maximum_fusion.3), channel_id=1, source_target_pairs={{0,2},{1,3},{2,0},{3,1},{4,6},{5,7},{6,4},{7,5},{8,10},{9,11},{10,... | collective-permute-start | bytes 2359304 | tf_op jit(solution)/shard_map/ppermute | solution.py:137
  98.5 24.6 %copy-start.1 = (bf16[2,192,4096]{2,1,0:T(8,128)(2,1)S(1)}, bf16[2,192,4096]{2,1,0:T(8,128)(2,1)}, u32[]{:S(2)}) copy-start(bf16[2,192,4096]{2,1,0:T(8,128)(2,1)} %own_up.3) | copy-start | bytes 9437188
  98.5 20.8 %collective-permute-start.6 = (bf16[384,1024]{1,0:T(8,128)(2,1)S(1)}, bf16[384,1024]{1,0:T(8,128)(2,1)S(1)}, u32[]{:S(2)}, u32[]{:S(2)}) collective-permute-start(bf16[384,1024]{1,0:T(8,128)(2,1)S(1)} %bitcast.49), channel_id=1, source_target_pairs={{0,1},{1,2},{2,3},{3,0},{4,5},{5,6},{6,7},{7,4},{8,9},{9,10},{10,1... | collective-permute-start | bytes 2359304 | tf_op jit(solution)/shard_map/ppermute | solution.py:137
  100.0 19.7 %collective-permute-start.8 = (bf16[384,1024]{1,0:T(8,128)(2,1)S(1)}, bf16[384,1024]{1,0:T(8,128)(2,1)S(1)}, u32[]{:S(2)}, u32[]{:S(2)}) collective-permute-start(bf16[384,1024]{1,0:T(8,128)(2,1)S(1)} %bitcast.50), channel_id=1, source_target_pairs={{0,3},{1,0},{2,1},{3,2},{4,7},{5,4},{6,5},{7,6},{8,11},{9,8},{10,9... | collective-permute-start | bytes 2359304 | tf_op jit(solution)/shard_map/ppermute | solution.py:137
  103.0 43.0 %collective-permute-start.14 = (bf16[768,1024]{1,0:T(8,128)(2,1)S(1)}, bf16[768,1024]{1,0:T(8,128)(2,1)S(1)}, u32[]{:S(2)}, u32[]{:S(2)}) collective-permute-start(bf16[768,1024]{1,0:T(8,128)(2,1)S(1)} %pad_maximum_fusion), channel_id=1, source_target_pairs={{0,4},{1,5},{2,6},{3,7},{4,0},{5,1},{6,2},{7,3},{8,12},{9,13},{10,... | collective-permute-start | bytes 4718600 | tf_op jit(solution)/shard_map/ppermute | solution.py:141
  119.4 11.6 %collective-permute-start.7 = (bf16[192,1024]{1,0:T(8,128)(2,1)S(1)}, bf16[192,1024]{1,0:T(8,128)(2,1)S(1)}, u32[]{:S(2)}, u32[]{:S(2)}) collective-permute-start(bf16[192,1024]{1,0:T(8,128)(2,1)S(1)} %slice.38), channel_id=1, source_target_pairs={{0,1},{1,2},{2,3},{3,0},{4,5},{5,6},{6,7},{7,4},{8,9},{9,10},{10,1... | collective-permute-start | bytes 1179656 | tf_op jit(solution)/shard_map/ppermute | solution.py:137
  119.7 11.2 %collective-permute-start.9 = (bf16[192,1024]{1,0:T(8,128)(2,1)S(1)}, bf16[192,1024]{1,0:T(8,128)(2,1)S(1)}, u32[]{:S(2)}, u32[]{:S(2)}) collective-permute-start(bf16[192,1024]{1,0:T(8,128)(2,1)S(1)} %slice.39), channel_id=1, source_target_pairs={{0,3},{1,0},{2,1},{3,2},{4,7},{5,4},{6,5},{7,6},{8,11},{9,8},{10,9... | collective-permute-start | bytes 1179656 | tf_op jit(solution)/shard_map/ppermute | solution.py:137
  131.0 14.9 %copy-start.11 = (bf16[1,192,1024]{2,1,0:T(8,128)(2,1)S(1)}, bf16[1,192,1024]{2,1,0:T(8,128)(2,1)}, u32[]{:S(2)}) copy-start(bf16[1,192,1024]{2,1,0:T(8,128)(2,1)} %get-tuple-element.39) | copy-start | bytes 1179652
  133.9 8.6 %collective-permute-start.10 = (bf16[384,384]{1,0:T(8,128)(2,1)S(1)}, bf16[384,384]{1,0:T(8,128)(2,1)S(1)}, u32[]{:S(2)}, u32[]{:S(2)}) collective-permute-start(bf16[384,384]{1,0:T(8,128)(2,1)S(1)} %expand_far.1.own), channel_id=1, source_target_pairs={{0,1},{1,2},{2,3},{3,0},{4,5},{5,6},{6,7},{7,4},{8,9},{9,10},{10,1... | collective-permute-start | bytes 884744 | tf_op jit(solution)/shard_map/ppermute | solution.py:137
  134.5 8.1 %collective-permute-start.11 = (bf16[384,384]{1,0:T(8,128)(2,1)S(1)}, bf16[384,384]{1,0:T(8,128)(2,1)S(1)}, u32[]{:S(2)}, u32[]{:S(2)}) collective-permute-start(bf16[384,384]{1,0:T(8,128)(2,1)S(1)} %expand_far.1.own), channel_id=1, source_target_pairs={{0,3},{1,0},{2,1},{3,2},{4,7},{5,4},{6,5},{7,6},{8,11},{9,8},{10,9... | collective-permute-start | bytes 884744 | tf_op jit(solution)/shard_map/ppermute | solution.py:137
  142.5 6.4 %collective-permute-start.12 = (bf16[192,384]{1,0:T(8,128)(2,1)S(1)}, bf16[192,384]{1,0:T(8,128)(2,1)S(1)}, u32[]{:S(2)}, u32[]{:S(2)}) collective-permute-start(bf16[192,384]{1,0:T(8,128)(2,1)S(1)} %slice.40), channel_id=1, source_target_pairs={{0,1},{1,2},{2,3},{3,0},{4,5},{5,6},{6,7},{7,4},{8,9},{9,10},{10,1... | collective-permute-start | bytes 442376 | tf_op jit(solution)/shard_map/ppermute | solution.py:137
  142.6 6.3 %collective-permute-start.13 = (bf16[192,384]{1,0:T(8,128)(2,1)S(1)}, bf16[192,384]{1,0:T(8,128)(2,1)S(1)}, u32[]{:S(2)}, u32[]{:S(2)}) collective-permute-start(bf16[192,384]{1,0:T(8,128)(2,1)S(1)} %slice.41), channel_id=1, source_target_pairs={{0,3},{1,0},{2,1},{3,2},{4,7},{5,4},{6,5},{7,6},{8,11},{9,8},{10,9... | collective-permute-start | bytes 442376 | tf_op jit(solution)/shard_map/ppermute | solution.py:137
  152.3 36.0 %copy-start.12 = (f32[96,32]{0,1:T(8,128)S(1)}, f32[96,32]{0,1:T(8,128)}, u32[]{:S(2)}) copy-start(f32[96,32]{0,1:T(8,128)} %get-tuple-element.37) | copy-start | bytes 36868
  152.3 36.0 %copy-start.14 = (f32[96,24]{0,1:T(8,128)S(1)}, f32[96,24]{0,1:T(8,128)}, u32[]{:S(2)}) copy-start(f32[96,24]{0,1:T(8,128)} %constant.93) | copy-start | bytes 27652
  152.9 41.4 %copy-start.5 = (f32[6,32,128]{2,1,0:T(8,128)S(1)}, f32[6,32,128]{2,1,0:T(8,128)}, u32[]{:S(2)}) copy-start(f32[6,32,128]{2,1,0:T(8,128)} %copy-done.4) | copy-start | bytes 294916
  189.5 11.4 %all-to-all-start.4 = ((bf16[8,12,512]{2,1,0:T(8,128)(2,1)}), bf16[8,12,512]{2,1,0:T(8,128)(2,1)S(1)}, u32[]{:S(2)}, u32[]{:S(2)}) async-start(bf16[8,12,512]{2,1,0:T(8,128)(2,1)} %reshape.96), calls=%async_computation.4 | async-start | bytes 262144 | tf_op jit(solution)/shard_map/all_to_all | solution.py:132
  (7 other events, 30.2 us)

commit v7 on v5

--- a/solution.py
+++ b/solution.py
@@ -194,14 +194,17 @@
     above_rows,
     own_gate,
     own_up,
-    lent_gate_low,
-    lent_gate_high,
+    gate_first,
+    gate_second,
+    gate_third,
     lent_up,
     gate_total,
     up_total,
 ):
     turn = pl.program_id(0)
-    gate_block = jnp.concatenate([own_gate[0], lent_gate_low[...], lent_gate_high[...]], axis=0)
+    gate_block = jnp.concatenate(
+        [own_gate[0], gate_first[...], gate_second[...], gate_third[...]], axis=0
+    )
     up_block = jnp.concatenate([own_up[0], lent_up[...]], axis=0)
 
     @pl.when(turn == 0)
@@ -228,12 +231,15 @@
     up_total,
     own_gate,
     own_up,
-    lent_gate_low,
-    lent_gate_high,
+    gate_first,
+    gate_second,
+    gate_third,
     lent_up,
     out,
 ):
-    gate_block = jnp.concatenate([own_gate[0], lent_gate_low[...], lent_gate_high[...]], axis=0)
+    gate_block = jnp.concatenate(
+        [own_gate[0], gate_first[...], gate_second[...], gate_third[...]], axis=0
+    )
     up_block = jnp.concatenate([own_up[0], lent_up[...]], axis=0)
     half = far_low.shape[0]
     for start, rows in ((0, far_low), (half, far_high)):
@@ -260,7 +266,7 @@
         lent = pl.BlockSpec((UNITS, BLK), lambda turn, where: (0, column(turn, where)))
         parts = [
             pl.BlockSpec((array.shape[0], BLK), lambda turn, where: (0, column(turn, where)))
-            for array in weights[2:4]
+            for array in weights[2:5]
         ]
         outs = jax.tree.leaves(out_shape)
         out_specs = jax.tree.unflatten(
@@ -297,7 +303,7 @@
 def contract_kernel(own, below, above, far_low, far_high, w_own, w_below, w_above, w_far, lent, out):
     half = far_low.shape[0]
     blocks = [
-        jnp.concatenate([kept[0], lent[turn * UNITS : (turn + 1) * UNITS]], axis=0)
+        jnp.concatenate([kept[...], lent[turn * UNITS : (turn + 1) * UNITS]], axis=0)
         for turn, kept in enumerate((w_own, w_below, w_above, w_far))
     ]
     for start, far in ((0, far_low), (half, far_high)):
@@ -349,19 +355,18 @@
     routing = jnp.broadcast_to(routing[:, None], (N_EXP, 2, LOCAL, 2 * TOPK))
     routing = routing.reshape(KEYS, 2 * TOPK)
 
-    early = 2 * UNITS // 3
-    lent_gate_low = across(lax.dynamic_slice(gate_weight, (1 - side, 0, 0), (1, early, D))[0])
-
-    def quarter(weight, step):
+    cuts = (0, UNITS // 2, 3 * UNITS // 4, UNITS)
+
+    def gate_part(weight, part):
+        size = (1, cuts[part + 1] - cuts[part], D)
+        return across(lax.dynamic_slice(weight, (1 - side, cuts[part], 0), size)[0])
+
+    def quarter(weight, expert, step):
         start = (place + step) % 4 * BLK
-        return jnp.concatenate(
-            [
-                lax.dynamic_slice(weight, (expert, 0, start), (1, UNITS, BLK))
-                for expert in (side, 1 - side)
-            ]
-        )
-
-    kept_near = [shift(quarter(down_weight, step), step) for step in (1, -1)]
+        return lax.dynamic_slice(weight, (expert, 0, start), (1, UNITS, BLK))[0]
+
+    gate_first = gate_part(gate_weight, 0)
+    lent_near = [shift(quarter(down_weight, 1 - side, step), step) for step in (1, -1)]
 
     hidden, normed = attend(
         cache_len, queries, key_cache, value_cache, new_keys, new_values, residual, norm_gain
@@ -370,30 +375,34 @@
     normed = jnp.broadcast_to(
         normed.reshape(1, 4, 2 * LOCAL, HALF), (2, 4, 2 * LOCAL, HALF)
     ).reshape(N_EXP, 2 * LOCAL, HALF)
-    normed, lent_gate_low, kept_near = lax.optimization_barrier((normed, lent_gate_low, kept_near))
+    normed, gate_first, lent_near, gate_late = lax.optimization_barrier(
+        (normed, gate_first, lent_near, gate_weight)
+    )
     tokens = exchange(normed, "exp").reshape(KEYS, HALF)
     table, combine = routing_tables(routing[:, :TOPK], routing[:, TOPK:], side, groups)
     outbound = lax.dot_general(
         table, tokens, (((0,), (0,)), ((), ())), preferred_element_type=jnp.float32
     ).astype(jnp.bfloat16)
 
-    outbound, gate_late, up_late, down_late = lax.optimization_barrier(
-        (outbound, gate_weight, up_weight, down_weight)
+    gate_second = gate_part(gate_late, 1)
+    outbound, gate_second, gate_last, up_late, down_late = lax.optimization_barrier(
+        (outbound, gate_second, gate_weight, up_weight, down_weight)
     )
     inbound = exchange(outbound.reshape(groups, WIRE, HALF), "rep")
-    kept_far = shift(quarter(down_late, 2), 2)
-    lent_gate_high = across(
-        lax.dynamic_slice(gate_late, (1 - side, early, 0), (1, UNITS - early, D))[0]
-    )
+    lent_far = shift(quarter(down_late, 1 - side, 2), 2)
+    kept = [shift(quarter(down_late, side, step), step) for step in (1, -1, 2)]
+    gate_third = gate_part(gate_last, 2)
     lent_up = across(lax.dynamic_index_in_dim(up_late, 1 - side, 0, keepdims=False))
-    inbound, kept_far, lent_gate_high = lax.optimization_barrier(
-        (inbound, kept_far, lent_gate_high)
-    )
-    kept = [quarter(down_late, 0), *kept_near, kept_far]
-    lent_down = across(jnp.concatenate([block[1] for block in kept]))
+    inbound, lent_far, kept, gate_third = lax.optimization_barrier(
+        (inbound, lent_far, kept, gate_third)
+    )
+    kept = [quarter(down_late, side, 0), *kept]
+    lent_down = across(
+        jnp.concatenate([quarter(down_late, 1 - side, 0), *lent_near, lent_far])
+    )
     slotted = inbound.reshape(groups, 2, PLACES, HALF).transpose(0, 2, 1, 3).reshape(rows, BLK)
     where = jnp.stack([side, place])
-    weights = (gate_weight, up_weight, lent_gate_low, lent_gate_high, lent_up)
+    weights = (gate_weight, up_weight, gate_first, gate_second, gate_third, lent_up)
     activation = expand(where, ring(slotted), weights)
     partial_value = contract(ring(activation), kept, lent_down)
     partial_value = partial_value.reshape(groups, PLACES, 2, HALF).transpose(0, 2, 1, 3)

time: 200 us -> 198 us (0.990)
  waiting for transfers between devices: 79.1 us -> 66.2 us
  starting transfers between devices: 48.7 us -> 53.3 us
  local copies, waits for them, and re-layouts: 19.6 us -> 23.1 us
    ppermute x4 -> x5, waiting for transfers between devices: 34.1 us -> 21.1 us  [across(): return lax.ppermute(array, 'exp', [(e, e ^ 4) for e in range(N_EXP)])]
    dynamic_slice x2 -> x0, local copies, waits for them, and re-layouts: 4.12 us -> none  [quarter(): lax.dynamic_slice(weight, (expert, 0, start), (1, UNITS, BLK))]
    ppermute x11 -> x14, waiting for transfers between devices: 32 us -> 35.8 us  [shift(): return lax.ppermute(array, 'exp', pairs)]
    all_to_all x4, waiting for transfers between devices: 13.1 us -> 9.29 us  [exchange(): return lax.all_to_all(array, axis, split_axis=0, concat_axis=0, tiled=True)]
    ppermute x11 -> x14, starting transfers between devices: 17.8 us -> 21.1 us  [shift(): return lax.ppermute(array, 'exp', pairs)]
    unnamed x58 -> x56, local copies, waits for them, and re-layouts: 3.61 us -> 6.4 us
    squeeze x4 -> x5, local copies, waits for them, and re-layouts: 4.33 us -> 6.25 us  [the longest x2 3.31 us: quarter(): return lax.dynamic_slice(weight, (expert, 0, start), (1, UNITS, BLK))[0]]
    ppermute x4 -> x5, starting transfers between devices: 5.4 us -> 6.93 us  [across(): return lax.ppermute(array, 'exp', [(e, e ^ 4) for e in range(N_EXP)])]
  transfers between devices with their start and end apart: 19 -> 23, of which waited for: 9 -> 14; matrix products, arithmetic and copies ran while one was open for 8% -> 10% of each run, Pallas kernels for 5% -> 6%
where the time goes in v7:
time: 198 us; the launch traced here: 197 us
  waiting for transfers between devices  66.2 us (33%)
  starting transfers between devices  53.3 us (27%)
  blocking collectives  32.9 us (17%)
  local copies, waits for them, and re-layouts  23.1 us (12%)
  Pallas kernels  12.8 us (6%)
  other arithmetic  5.26 us (3%)
  matrix products  2.9 us (1%)
    ppermute x14, waiting for transfers between devices, shift(): return lax.ppermute(array, 'exp', pairs)  35.8 us
    all_to_all x1, blocking collectives, exchange(): return lax.all_to_all(array, axis, split_axis=0, concat_axis=0, tiled=True)  32.9 us
    all_to_all x4, starting transfers between devices, exchange(): return lax.all_to_all(array, axis, split_axis=0, concat_axis=0, tiled=True)  25.2 us
    ppermute x14, starting transfers between devices, shift(): return lax.ppermute(array, 'exp', pairs)  21.1 us
    ppermute x5, waiting for transfers between devices, across(): return lax.ppermute(array, 'exp', [(e, e ^ 4) for e in range(N_EXP)])  21.1 us
    all_to_all x4, waiting for transfers between devices, exchange(): return lax.all_to_all(array, axis, split_axis=0, concat_axis=0, tiled=True)  9.29 us
    pallas_call x2, Pallas kernels, call(): pl.pallas_call(kernel, out_shape=out_shape, grid_spec=pltpu.PrefetchScala...  8.22 us
    ppermute x5, starting transfers between devices, across(): return lax.ppermute(array, 'exp', [(e, e ^ 4) for e in range(N_EXP)])  6.93 us
  transfers between devices with their start and end apart: 23, of which 14 were waited for; matrix products, arithmetic and copies ran while one was open for 10% of the time, Pallas kernels for 6%

profile of v7, /device:TPU:4, one launch (start us, length us, event | category | flops | bytes accessed | tf_op | source)
XLA Modules:
  0.0 196.9 jit_solution(6351698318928280659)
XLA Ops:
  1.5 5.1 %all-to-all-start = ((s32[8,6,16]{2,1,0:T(8,128)}), s32[8,6,16]{2,1,0:T(8,128)S(1)}, u32[]{:S(2)}, u32[]{:S(2)}) async-start(s32[8,6,16]{2,1,0:T(8,128)} %broadcast_in_dim.15), calls=%async_computation | async-start | bytes 65536 | tf_op jit(solution)/shard_map/all_to_all | solution.py:132
  6.6 2.2 %dynamic-slice_bitcast_fusion.10 = (bf16[192,1024]{1,0:T(8,128)(2,1)}, bf16[192,1024]{1,0:T(8,128)(2,1)}) fusion(bf16[2,192,4096]{2,1,0:T(8,128)(2,1)} %param.27, s32[]{:T(128)S(6)} %select_n.75, s32[]{:T(128)S(6)} %select_n.79, s32[]{:T(128)S(6)} %select_n.77), kind=kLoop, calls=%fused_computation.18 | loop fusion | bytes 1572876 | tf_op jit(solution)/shard_map/squeeze | solution.py:366
  8.9 3.2 %collective-permute-start.2 = (bf16[192,1024]{1,0:T(8,128)(2,1)}, bf16[192,1024]{1,0:T(8,128)(2,1)}, u32[]{:S(2)}, u32[]{:S(2)}) collective-permute-start(bf16[192,1024]{1,0:T(8,128)(2,1)} %get-tuple-element.53), channel_id=1, source_target_pairs={{0,3},{1,0},{2,1},{3,2},{4,7},{5,4},{6,5},{7,6},{8,11},{9,8},{10,9... | collective-permute-start | bytes 1179656 | tf_op jit(solution)/shard_map/ppermute | solution.py:137
  12.1 2.1 %dynamic-slice_bitcast_fusion.1 = bf16[96,4096]{1,0:T(8,128)(2,1)} fusion(bf16[2,192,4096]{2,1,0:T(8,128)(2,1)} %own_gate.3, s32[]{:T(128)S(6)} %select_n.75), kind=kLoop, calls=%fused_computation.6 | loop fusion | bytes 1572868 | tf_op jit(solution)/shard_map/squeeze | solution.py:362
  18.3 2.8 %attend.1 = (f32[6,32,128]{2,1,0:T(8,128)S(1)}, bf16[6,32,128]{2,1,0:T(8,128)(2,1)S(1)}) custom-call(s32[2]{0:T(128)S(1)} %copy-done.16, bf16[6,32,128]{2,1,0:T(8,128)(2,1)S(1)} %reshape.83.query, bf16[2,1024,256]{2,1,0:T(8,128)(2,1)S(1)} %copy-done.5, bf16[2,1024,256]{2,1,0:T(8,128)(2,1)S(1)} %copy-done.6, bf16[2,8,256]{2,1,0:T(8,128)(2,1)S(1)} %pad.7.fresh_keys, ...), custom_call_target="tpu_custom_call" | custom-call | flops 100663296 | bytes 2342912 | tf_op jit(solution)/shard_map/attend/pallas_call | solution.py:90
  23.6 9.3 %collective-permute-done.gate_first = bf16[96,4096]{1,0:T(8,128)(2,1)} collective-permute-done((bf16[96,4096]{1,0:T(8,128)(2,1)}, bf16[96,4096]{1,0:T(8,128)(2,1)}, u32[]{:S(2)}, u32[]{:S(2)}) %collective-permute-start) | collective-permute-done | bytes 786464 | tf_op jit(solution)/shard_map/ppermute | solution.py:141
  33.6 5.1 %all-to-all-start.1 = ((bf16[8,12,512]{2,1,0:T(8,128)(2,1)}), bf16[8,12,512]{2,1,0:T(8,128)(2,1)}, u32[]{:S(2)}, u32[]{:S(2)}) async-start(bf16[8,12,512]{2,1,0:T(8,128)(2,1)} %bitcast.8), calls=%async_computation.1 | async-start | bytes 262144 | tf_op jit(solution)/shard_map/all_to_all | solution.py:132
  39.5 2.0 %collective-permute-start.3 = (bf16[48,4096]{1,0:T(8,128)(2,1)}, bf16[48,4096]{1,0:T(8,128)(2,1)S(1)}, u32[]{:S(2)}, u32[]{:S(2)}) collective-permute-start(bf16[48,4096]{1,0:T(8,128)(2,1)} %dynamic-slice_bitcast_fusion.9), channel_id=1, source_target_pairs={{0,4},{1,5},{2,6},{3,7},{4,0},{5,1},{6,2},{7,3},{8,12},{9,13},{10,... | collective-permute-start | bytes 1179656 | tf_op jit(solution)/shard_map/ppermute | solution.py:141
  43.0 2.8 %all-to-all-done.1 = bf16[8,12,512]{2,1,0:T(8,128)(2,1)} async-done(((bf16[8,12,512]{2,1,0:T(8,128)(2,1)}), bf16[8,12,512]{2,1,0:T(8,128)(2,1)}, u32[]{:S(2)}, u32[]{:S(2)}) %all-to-all-start.1) | async-done | bytes 98336 | tf_op jit(solution)/shard_map/all_to_all | solution.py:132
  45.8 1.6 reshape.90
  47.4 2.2 %convolution_convert_fusion = bf16[768,512]{1,0:T(8,128)(2,1)} fusion(bf16[96,768]{0,1:T(8,128)(2,1)} %bitcast.68, bf16[96,512]{1,0:T(8,128)(2,1)} %reshape.90), kind=kOutput, calls=%fused_computation.2 | convolution fusion | flops 75890688 | bytes 1032192 | tf_op jit(solution)/shard_map/dot_general | solution.py:383
  49.6 11.6 %all-to-all-start.2 = ((bf16[32,24,512]{2,1,0:T(8,128)(2,1)}), bf16[32,24,512]{2,1,0:T(8,128)(2,1)}, u32[]{:S(2)}, u32[]{:S(2)}) async-start(bf16[32,24,512]{2,1,0:T(8,128)(2,1)} %bitcast.64), calls=%async_computation.2 | async-start | bytes 1572864 | tf_op jit(solution)/shard_map/all_to_all | solution.py:132
  62.5 2.7 %dynamic-slice_bitcast_fusion = bf16[192,4096]{1,0:T(8,128)(2,1)} fusion(bf16[2,192,4096]{2,1,0:T(8,128)(2,1)} %own_up.3, s32[]{:T(128)S(6)} %select_n.75), kind=kLoop, calls=%fused_computation.1 | loop fusion | bytes 3145732 | tf_op jit(solution)/shard_map/jit(dynamic_index_in_dim)/squeeze | solution.py:395
  67.3 2.9 %collective-permute-start.7 = (bf16[192,1024]{1,0:T(8,128)(2,1)S(1)}, bf16[192,1024]{1,0:T(8,128)(2,1)S(1)}, u32[]{:S(2)}, u32[]{:S(2)}) collective-permute-start(bf16[192,1024]{1,0:T(8,128)(2,1)S(1)} %get-tuple-element.49), channel_id=1, source_target_pairs={{0,2},{1,3},{2,0},{3,1},{4,6},{5,7},{6,4},{7,5},{8,10},{9,11},{10,... | collective-permute-start | bytes 1179656 | tf_op jit(solution)/shard_map/ppermute | solution.py:137
  72.2 8.2 %collective-permute-done.8.gate_third = bf16[48,4096]{1,0:T(8,128)(2,1)S(1)} collective-permute-done((bf16[48,4096]{1,0:T(8,128)(2,1)S(1)}, bf16[48,4096]{1,0:T(8,128)(2,1)S(1)}, u32[]{:S(2)}, u32[]{:S(2)}) %collective-permute-start.8) | collective-permute-done | bytes 393248 | tf_op jit(solution)/shard_map/ppermute | solution.py:141
  81.1 2.9 %collective-permute-start.4 = (bf16[192,1024]{1,0:T(8,128)(2,1)S(1)}, bf16[192,1024]{1,0:T(8,128)(2,1)}, u32[]{:S(2)}, u32[]{:S(2)}) collective-permute-start(bf16[192,1024]{1,0:T(8,128)(2,1)S(1)} %get-tuple-element.52), channel_id=1, source_target_pairs={{0,2},{1,3},{2,0},{3,1},{4,6},{5,7},{6,4},{7,5},{8,10},{9,11},{10,... | collective-permute-start | bytes 1179656 | tf_op jit(solution)/shard_map/ppermute | solution.py:137
  84.8 4.4 %collective-permute-done.6.w_above = bf16[192,1024]{1,0:T(8,128)(2,1)S(1)} collective-permute-done((bf16[192,1024]{1,0:T(8,128)(2,1)S(1)}, bf16[192,1024]{1,0:T(8,128)(2,1)S(1)}, u32[]{:S(2)}, u32[]{:S(2)}) %collective-permute-start.6) | collective-permute-done | bytes 393248 | tf_op jit(solution)/shard_map/ppermute | solution.py:137
  90.7 5.9 %collective-permute-done.4 = bf16[192,1024]{1,0:T(8,128)(2,1)} collective-permute-done((bf16[192,1024]{1,0:T(8,128)(2,1)S(1)}, bf16[192,1024]{1,0:T(8,128)(2,1)}, u32[]{:S(2)}, u32[]{:S(2)}) %collective-permute-start.4) | collective-permute-done | bytes 393248 | tf_op jit(solution)/shard_map/ppermute | solution.py:137
  99.0 2.4 %collective-permute-start.11 = (bf16[384,1024]{1,0:T(8,128)(2,1)S(1)}, bf16[384,1024]{1,0:T(8,128)(2,1)S(1)}, u32[]{:S(2)}, u32[]{:S(2)}) collective-permute-start(bf16[384,1024]{1,0:T(8,128)(2,1)S(1)} %bitcast.60), channel_id=1, source_target_pairs={{0,3},{1,0},{2,1},{3,2},{4,7},{5,4},{6,5},{7,6},{8,11},{9,8},{10,9... | collective-permute-start | bytes 2359304 | tf_op jit(solution)/shard_map/ppermute | solution.py:137
  104.1 13.3 %collective-permute-done.11.above_rows = bf16[384,1024]{1,0:T(8,128)(2,1)S(1)} collective-permute-done((bf16[384,1024]{1,0:T(8,128)(2,1)S(1)}, bf16[384,1024]{1,0:T(8,128)(2,1)S(1)}, u32[]{:S(2)}, u32[]{:S(2)}) %collective-permute-start.11) | collective-permute-done | bytes 786464 | tf_op jit(solution)/shard_map/ppermute | solution.py:137
  117.4 3.4 %collective-permute-start.12 = (bf16[192,1024]{1,0:T(8,128)(2,1)S(1)}, bf16[192,1024]{1,0:T(8,128)(2,1)S(1)}, u32[]{:S(2)}, u32[]{:S(2)}) collective-permute-start(bf16[192,1024]{1,0:T(8,128)(2,1)S(1)} %slice.27), channel_id=1, source_target_pairs={{0,3},{1,0},{2,1},{3,2},{4,7},{5,4},{6,5},{7,6},{8,11},{9,8},{10,9... | collective-permute-start | bytes 1179656 | tf_op jit(solution)/shard_map/ppermute | solution.py:137
  121.0 5.3 %expand_near.1 = (f32[384,384]{1,0:T(8,128)S(1)}, f32[384,384]{1,0:T(8,128)S(1)}) custom-call(s32[2]{0:T(128)S(1)} %pad_add_fusion.1.where, bf16[384,1024]{1,0:T(8,128)(2,1)S(1)} %bitcast.62, bf16[384,1024]{1,0:T(8,128)(2,1)S(1)} %collective-permute-done.9.below_rows, bf16[384,1024]{1,0:T(8,128)(2,1)S(1)} %collective-permute-done.11.above_rows, ...), custom_call_target="tpu_custom_call" | custom-call | flops 1811939328 | bytes 8257536 | tf_op jit(solution)/shard_map/expand_near/pallas_call | solution.py:275
  127.1 3.5 %collective-permute-done.10.far_low = bf16[192,1024]{1,0:T(8,128)(2,1)S(1)} collective-permute-done((bf16[192,1024]{1,0:T(8,128)(2,1)S(1)}, bf16[192,1024]{1,0:T(8,128)(2,1)S(1)}, u32[]{:S(2)}, u32[]{:S(2)}) %collective-permute-start.10) | collective-permute-done | bytes 393248 | tf_op jit(solution)/shard_map/ppermute | solution.py:137
  130.6 2.9 %expand_far.1.own = bf16[384,384]{1,0:T(8,128)(2,1)S(1)} custom-call(s32[2]{0:T(128)S(1)} %pad_add_fusion.1.where, bf16[192,1024]{1,0:T(8,128)(2,1)S(1)} %collective-permute-done.10.far_low, bf16[192,1024]{1,0:T(8,128)(2,1)S(1)} %collective-permute-done.12.far_high, f32[384,384]{1,0:T(8,128)S(1)} %get-tuple-element.37.gate_total, ...), custom_call_target="tpu_custom_call" | custom-call | flops 603979776 | bytes 3538944 | tf_op jit(solution)/shard_map/expand_far/pallas_call | solution.py:275
  133.8 1.8 collective-permute-start.14
  135.6 6.3 %collective-permute-done.15.above = bf16[384,384]{1,0:T(8,128)(2,1)S(1)} collective-permute-done((bf16[384,384]{1,0:T(8,128)(2,1)S(1)}, bf16[384,384]{1,0:T(8,128)(2,1)S(1)}, u32[]{:S(2)}, u32[]{:S(2)}) %collective-permute-start.15) | collective-permute-done | bytes 294944 | tf_op jit(solution)/shard_map/ppermute | solution.py:137
  142.3 1.8 collective-permute-start.16
  144.1 3.6 %collective-permute-done.18.lent = bf16[768,1024]{1,0:T(8,128)(2,1)S(1)} collective-permute-done((bf16[768,1024]{1,0:T(8,128)(2,1)S(1)}, bf16[768,1024]{1,0:T(8,128)(2,1)S(1)}, u32[]{:S(2)}, u32[]{:S(2)}) %collective-permute-start.18) | collective-permute-done | bytes 1572896 | tf_op jit(solution)/shard_map/ppermute | solution.py:141
  148.8 1.8 contract.1
  151.8 32.9 %all_to_all.25 = bf16[32,24,512]{2,1,0:T(8,128)(2,1)S(1)} all-to-all(bf16[32,24,512]{2,1,0:T(8,128)(2,1)S(1)} %copy.79), channel_id=1, replica_groups=mesh['rep'=32,'exp'=8] {'rep'}, dimensions={0} | all-to-all | bytes 1572864 | tf_op jit(solution)/shard_map/all_to_all | solution.py:132
  186.0 3.4 %all-to-all-start.4 = ((bf16[8,12,512]{2,1,0:T(8,128)(2,1)}), bf16[8,12,512]{2,1,0:T(8,128)(2,1)S(1)}, u32[]{:S(2)}, u32[]{:S(2)}) async-start(bf16[8,12,512]{2,1,0:T(8,128)(2,1)} %reshape.96), calls=%async_computation.4 | async-start | bytes 262144 | tf_op jit(solution)/shard_map/all_to_all | solution.py:132
  189.4 6.4 %all-to-all-done.4 = bf16[8,12,512]{2,1,0:T(8,128)(2,1)S(1)} async-done(((bf16[8,12,512]{2,1,0:T(8,128)(2,1)}), bf16[8,12,512]{2,1,0:T(8,128)(2,1)S(1)}, u32[]{:S(2)}, u32[]{:S(2)}) %all-to-all-start.4) | async-done | bytes 98336 | tf_op jit(solution)/shard_map/all_to_all | solution.py:132
  (124 shorter events, 30.5 us)
Async XLA Ops:
  1.5 20.3 %all-to-all-start = ((s32[8,6,16]{2,1,0:T(8,128)}), s32[8,6,16]{2,1,0:T(8,128)S(1)}, u32[]{:S(2)}, u32[]{:S(2)}) async-start(s32[8,6,16]{2,1,0:T(8,128)} %broadcast_in_dim.15), calls=%async_computation | async-start | bytes 65536 | tf_op jit(solution)/shard_map/all_to_all | solution.py:132
  6.6 32.1 %copy-start = (bf16[2,192,4096]{2,1,0:T(8,128)(2,1)S(1)}, bf16[2,192,4096]{2,1,0:T(8,128)(2,1)}, u32[]{:S(2)}) copy-start(bf16[2,192,4096]{2,1,0:T(8,128)(2,1)} %own_gate.3) | copy-start | bytes 9437188
  8.9 14.1 %collective-permute-start.2 = (bf16[192,1024]{1,0:T(8,128)(2,1)}, bf16[192,1024]{1,0:T(8,128)(2,1)}, u32[]{:S(2)}, u32[]{:S(2)}) collective-permute-start(bf16[192,1024]{1,0:T(8,128)(2,1)} %get-tuple-element.53), channel_id=1, source_target_pairs={{0,3},{1,0},{2,1},{3,2},{4,7},{5,4},{6,5},{7,6},{8,11},{9,8},{10,9... | collective-permute-start | bytes 1179656 | tf_op jit(solution)/shard_map/ppermute | solution.py:137
  12.1 11.5 %collective-permute-start.1 = (bf16[192,1024]{1,0:T(8,128)(2,1)}, bf16[192,1024]{1,0:T(8,128)(2,1)}, u32[]{:S(2)}, u32[]{:S(2)}) collective-permute-start(bf16[192,1024]{1,0:T(8,128)(2,1)} %get-tuple-element.54), channel_id=1, source_target_pairs={{0,1},{1,2},{2,3},{3,0},{4,5},{5,6},{6,7},{7,4},{8,9},{9,10},{10,1... | collective-permute-start | bytes 1179656 | tf_op jit(solution)/shard_map/ppermute | solution.py:137
  14.2 18.8 %collective-permute-start = (bf16[96,4096]{1,0:T(8,128)(2,1)}, bf16[96,4096]{1,0:T(8,128)(2,1)}, u32[]{:S(2)}, u32[]{:S(2)}) collective-permute-start(bf16[96,4096]{1,0:T(8,128)(2,1)} %dynamic-slice_bitcast_fusion.1), channel_id=1, source_target_pairs={{0,4},{1,5},{2,6},{3,7},{4,0},{5,1},{6,2},{7,3},{8,12},{9,13},{10,... | collective-permute-start | bytes 2359304 | tf_op jit(solution)/shard_map/ppermute | solution.py:141
  33.6 12.2 %all-to-all-start.1 = ((bf16[8,12,512]{2,1,0:T(8,128)(2,1)}), bf16[8,12,512]{2,1,0:T(8,128)(2,1)}, u32[]{:S(2)}, u32[]{:S(2)}) async-start(bf16[8,12,512]{2,1,0:T(8,128)(2,1)} %bitcast.8), calls=%async_computation.1 | async-start | bytes 262144 | tf_op jit(solution)/shard_map/all_to_all | solution.py:132
  39.5 10.1 %collective-permute-start.3 = (bf16[48,4096]{1,0:T(8,128)(2,1)}, bf16[48,4096]{1,0:T(8,128)(2,1)S(1)}, u32[]{:S(2)}, u32[]{:S(2)}) collective-permute-start(bf16[48,4096]{1,0:T(8,128)(2,1)} %dynamic-slice_bitcast_fusion.9), channel_id=1, source_target_pairs={{0,4},{1,5},{2,6},{3,7},{4,0},{5,1},{6,2},{7,3},{8,12},{9,13},{10,... | collective-permute-start | bytes 1179656 | tf_op jit(solution)/shard_map/ppermute | solution.py:141
  49.6 47.0 %all-to-all-start.2 = ((bf16[32,24,512]{2,1,0:T(8,128)(2,1)}), bf16[32,24,512]{2,1,0:T(8,128)(2,1)}, u32[]{:S(2)}, u32[]{:S(2)}) async-start(bf16[32,24,512]{2,1,0:T(8,128)(2,1)} %bitcast.64), calls=%async_computation.2 | async-start | bytes 1572864 | tf_op jit(solution)/shard_map/all_to_all | solution.py:132
  61.3 19.0 %collective-permute-start.8 = (bf16[48,4096]{1,0:T(8,128)(2,1)S(1)}, bf16[48,4096]{1,0:T(8,128)(2,1)S(1)}, u32[]{:S(2)}, u32[]{:S(2)}) collective-permute-start(bf16[48,4096]{1,0:T(8,128)(2,1)S(1)} %dynamic-slice_bitcast_fusion.4), channel_id=1, source_target_pairs={{0,4},{1,5},{2,6},{3,7},{4,0},{5,1},{6,2},{7,3},{8,12},{9,13},{10,... | collective-permute-start | bytes 1179656 | tf_op jit(solution)/shard_map/ppermute | solution.py:141
  65.3 55.8 %collective-permute-start.13 = (bf16[192,4096]{1,0:T(8,128)(2,1)}, bf16[192,4096]{1,0:T(8,128)(2,1)}, u32[]{:S(2)}, u32[]{:S(2)}) collective-permute-start(bf16[192,4096]{1,0:T(8,128)(2,1)} %dynamic-slice_bitcast_fusion), channel_id=1, source_target_pairs={{0,4},{1,5},{2,6},{3,7},{4,0},{5,1},{6,2},{7,3},{8,12},{9,13},{10,... | collective-permute-start | bytes 4718600 | tf_op jit(solution)/shard_map/ppermute | solution.py:141
  67.3 16.7 %collective-permute-start.7 = (bf16[192,1024]{1,0:T(8,128)(2,1)S(1)}, bf16[192,1024]{1,0:T(8,128)(2,1)S(1)}, u32[]{:S(2)}, u32[]{:S(2)}) collective-permute-start(bf16[192,1024]{1,0:T(8,128)(2,1)S(1)} %get-tuple-element.49), channel_id=1, source_target_pairs={{0,2},{1,3},{2,0},{3,1},{4,6},{5,7},{6,4},{7,5},{8,10},{9,11},{10,... | collective-permute-start | bytes 1179656 | tf_op jit(solution)/shard_map/ppermute | solution.py:137
  70.1 19.1 %collective-permute-start.6 = (bf16[192,1024]{1,0:T(8,128)(2,1)S(1)}, bf16[192,1024]{1,0:T(8,128)(2,1)S(1)}, u32[]{:S(2)}, u32[]{:S(2)}) collective-permute-start(bf16[192,1024]{1,0:T(8,128)(2,1)S(1)} %get-tuple-element.50), channel_id=1, source_target_pairs={{0,3},{1,0},{2,1},{3,2},{4,7},{5,4},{6,5},{7,6},{8,11},{9,8},{10,9... | collective-permute-start | bytes 1179656 | tf_op jit(solution)/shard_map/ppermute | solution.py:137
  71.3 18.6 %collective-permute-start.5 = (bf16[192,1024]{1,0:T(8,128)(2,1)S(1)}, bf16[192,1024]{1,0:T(8,128)(2,1)S(1)}, u32[]{:S(2)}, u32[]{:S(2)}) collective-permute-start(bf16[192,1024]{1,0:T(8,128)(2,1)S(1)} %get-tuple-element.51), channel_id=1, source_target_pairs={{0,1},{1,2},{2,3},{3,0},{4,5},{5,6},{6,7},{7,4},{8,9},{9,10},{10,1... | collective-permute-start | bytes 1179656 | tf_op jit(solution)/shard_map/ppermute | solution.py:137
  81.1 15.4 %collective-permute-start.4 = (bf16[192,1024]{1,0:T(8,128)(2,1)S(1)}, bf16[192,1024]{1,0:T(8,128)(2,1)}, u32[]{:S(2)}, u32[]{:S(2)}) collective-permute-start(bf16[192,1024]{1,0:T(8,128)(2,1)S(1)} %get-tuple-element.52), channel_id=1, source_target_pairs={{0,2},{1,3},{2,0},{3,1},{4,6},{5,7},{6,4},{7,5},{8,10},{9,11},{10,... | collective-permute-start | bytes 1179656 | tf_op jit(solution)/shard_map/ppermute | solution.py:137
  98.8 22.2 %copy-start.1 = (bf16[2,192,4096]{2,1,0:T(8,128)(2,1)S(1)}, bf16[2,192,4096]{2,1,0:T(8,128)(2,1)}, u32[]{:S(2)}) copy-start(bf16[2,192,4096]{2,1,0:T(8,128)(2,1)} %own_up.3) | copy-start | bytes 9437188
  98.8 22.2 %copy-start.3 = (bf16[48,4096]{1,0:T(8,128)(2,1)S(1)}, bf16[48,4096]{1,0:T(8,128)(2,1)}, u32[]{:S(2)}) copy-start(bf16[48,4096]{1,0:T(8,128)(2,1)} %copy-done.2) | copy-start | bytes 1179652
  99.0 18.4 %collective-permute-start.11 = (bf16[384,1024]{1,0:T(8,128)(2,1)S(1)}, bf16[384,1024]{1,0:T(8,128)(2,1)S(1)}, u32[]{:S(2)}, u32[]{:S(2)}) collective-permute-start(bf16[384,1024]{1,0:T(8,128)(2,1)S(1)} %bitcast.60), channel_id=1, source_target_pairs={{0,3},{1,0},{2,1},{3,2},{4,7},{5,4},{6,5},{7,6},{8,11},{9,8},{10,9... | collective-permute-start | bytes 2359304 | tf_op jit(solution)/shard_map/ppermute | solution.py:137
  101.4 19.4 %collective-permute-start.9 = (bf16[384,1024]{1,0:T(8,128)(2,1)S(1)}, bf16[384,1024]{1,0:T(8,128)(2,1)S(1)}, u32[]{:S(2)}, u32[]{:S(2)}) collective-permute-start(bf16[384,1024]{1,0:T(8,128)(2,1)S(1)} %bitcast.61), channel_id=1, source_target_pairs={{0,1},{1,2},{2,3},{3,0},{4,5},{5,6},{6,7},{7,4},{8,9},{9,10},{10,1... | collective-permute-start | bytes 2359304 | tf_op jit(solution)/shard_map/ppermute | solution.py:137
  102.8 44.9 %collective-permute-start.18 = (bf16[768,1024]{1,0:T(8,128)(2,1)S(1)}, bf16[768,1024]{1,0:T(8,128)(2,1)S(1)}, u32[]{:S(2)}, u32[]{:S(2)}) collective-permute-start(bf16[768,1024]{1,0:T(8,128)(2,1)S(1)} %pad_maximum_fusion), channel_id=1, source_target_pairs={{0,4},{1,5},{2,6},{3,7},{4,0},{5,1},{6,2},{7,3},{8,12},{9,13},{10,... | collective-permute-start | bytes 4718600 | tf_op jit(solution)/shard_map/ppermute | solution.py:141
  117.4 9.7 %collective-permute-start.12 = (bf16[192,1024]{1,0:T(8,128)(2,1)S(1)}, bf16[192,1024]{1,0:T(8,128)(2,1)S(1)}, u32[]{:S(2)}, u32[]{:S(2)}) collective-permute-start(bf16[192,1024]{1,0:T(8,128)(2,1)S(1)} %slice.27), channel_id=1, source_target_pairs={{0,3},{1,0},{2,1},{3,2},{4,7},{5,4},{6,5},{7,6},{8,11},{9,8},{10,9... | collective-permute-start | bytes 1179656 | tf_op jit(solution)/shard_map/ppermute | solution.py:137
  120.8 9.8 %collective-permute-start.10 = (bf16[192,1024]{1,0:T(8,128)(2,1)S(1)}, bf16[192,1024]{1,0:T(8,128)(2,1)S(1)}, u32[]{:S(2)}, u32[]{:S(2)}) collective-permute-start(bf16[192,1024]{1,0:T(8,128)(2,1)S(1)} %slice.26), channel_id=1, source_target_pairs={{0,1},{1,2},{2,3},{3,0},{4,5},{5,6},{6,7},{7,4},{8,9},{9,10},{10,1... | collective-permute-start | bytes 1179656 | tf_op jit(solution)/shard_map/ppermute | solution.py:137
  130.6 18.1 %copy-start.8 = (bf16[192,1024]{1,0:T(8,128)(2,1)S(1)}, bf16[192,1024]{1,0:T(8,128)(2,1)}, u32[]{:S(2)}) copy-start(bf16[192,1024]{1,0:T(8,128)(2,1)} %copy-done.7) | copy-start | bytes 1179652
  130.6 18.1 %copy-start.10 = (bf16[192,1024]{1,0:T(8,128)(2,1)S(1)}, bf16[192,1024]{1,0:T(8,128)(2,1)}, u32[]{:S(2)}) copy-start(bf16[192,1024]{1,0:T(8,128)(2,1)} %copy-done.9) | copy-start | bytes 1179652
  130.6 18.1 %copy-start.12 = (bf16[192,1024]{1,0:T(8,128)(2,1)S(1)}, bf16[192,1024]{1,0:T(8,128)(2,1)}, u32[]{:S(2)}) copy-start(bf16[192,1024]{1,0:T(8,128)(2,1)} %copy-done.11) | copy-start | bytes 1179652
  133.5 8.4 %collective-permute-start.15 = (bf16[384,384]{1,0:T(8,128)(2,1)S(1)}, bf16[384,384]{1,0:T(8,128)(2,1)S(1)}, u32[]{:S(2)}, u32[]{:S(2)}) collective-permute-start(bf16[384,384]{1,0:T(8,128)(2,1)S(1)} %expand_far.1.own), channel_id=1, source_target_pairs={{0,3},{1,0},{2,1},{3,2},{4,7},{5,4},{6,5},{7,6},{8,11},{9,8},{10,9... | collective-permute-start | bytes 884744 | tf_op jit(solution)/shard_map/ppermute | solution.py:137
  133.8 8.5 %collective-permute-start.14 = (bf16[384,384]{1,0:T(8,128)(2,1)S(1)}, bf16[384,384]{1,0:T(8,128)(2,1)S(1)}, u32[]{:S(2)}, u32[]{:S(2)}) collective-permute-start(bf16[384,384]{1,0:T(8,128)(2,1)S(1)} %expand_far.1.own), channel_id=1, source_target_pairs={{0,1},{1,2},{2,3},{3,0},{4,5},{5,6},{6,7},{7,4},{8,9},{9,10},{10,1... | collective-permute-start | bytes 884744 | tf_op jit(solution)/shard_map/ppermute | solution.py:137
  141.9 5.8 %collective-permute-start.17 = (bf16[192,384]{1,0:T(8,128)(2,1)S(1)}, bf16[192,384]{1,0:T(8,128)(2,1)S(1)}, u32[]{:S(2)}, u32[]{:S(2)}) collective-permute-start(bf16[192,384]{1,0:T(8,128)(2,1)S(1)} %slice.29), channel_id=1, source_target_pairs={{0,3},{1,0},{2,1},{3,2},{4,7},{5,4},{6,5},{7,6},{8,11},{9,8},{10,9... | collective-permute-start | bytes 442376 | tf_op jit(solution)/shard_map/ppermute | solution.py:137
  142.3 6.4 %collective-permute-start.16 = (bf16[192,384]{1,0:T(8,128)(2,1)S(1)}, bf16[192,384]{1,0:T(8,128)(2,1)S(1)}, u32[]{:S(2)}, u32[]{:S(2)}) collective-permute-start(bf16[192,384]{1,0:T(8,128)(2,1)S(1)} %slice.28), channel_id=1, source_target_pairs={{0,1},{1,2},{2,3},{3,0},{4,5},{5,6},{6,7},{7,4},{8,9},{9,10},{10,1... | collective-permute-start | bytes 442376 | tf_op jit(solution)/shard_map/ppermute | solution.py:137
  150.5 34.2 %copy-start.19 = (f32[96,32]{0,1:T(8,128)S(1)}, f32[96,32]{0,1:T(8,128)}, u32[]{:S(2)}) copy-start(f32[96,32]{0,1:T(8,128)} %get-tuple-element.45) | copy-start | bytes 36868
  150.6 34.2 %copy-start.20 = (f32[96,24]{0,1:T(8,128)S(1)}, f32[96,24]{0,1:T(8,128)}, u32[]{:S(2)}) copy-start(f32[96,24]{0,1:T(8,128)} %constant.103) | copy-start | bytes 27652
  151.1 38.2 %copy-start.14 = (f32[6,32,128]{2,1,0:T(8,128)S(1)}, f32[6,32,128]{2,1,0:T(8,128)}, u32[]{:S(2)}) copy-start(f32[6,32,128]{2,1,0:T(8,128)} %copy-done.13) | copy-start | bytes 294916
  186.0 9.9 %all-to-all-start.4 = ((bf16[8,12,512]{2,1,0:T(8,128)(2,1)}), bf16[8,12,512]{2,1,0:T(8,128)(2,1)S(1)}, u32[]{:S(2)}, u32[]{:S(2)}) async-start(bf16[8,12,512]{2,1,0:T(8,128)(2,1)} %reshape.96), calls=%async_computation.4 | async-start | bytes 262144 | tf_op jit(solution)/shard_map/all_to_all | solution.py:132
  (17 other events, 144.5 us)

commit v8 on v7

--- a/solution.py
+++ b/solution.py
@@ -355,7 +355,7 @@
     routing = jnp.broadcast_to(routing[:, None], (N_EXP, 2, LOCAL, 2 * TOPK))
     routing = routing.reshape(KEYS, 2 * TOPK)
 
-    cuts = (0, UNITS // 2, 3 * UNITS // 4, UNITS)
+    cuts = (0, UNITS // 3, 2 * UNITS // 3, UNITS)
 
     def gate_part(weight, part):
         size = (1, cuts[part + 1] - cuts[part], D)
@@ -375,8 +375,8 @@
     normed = jnp.broadcast_to(
         normed.reshape(1, 4, 2 * LOCAL, HALF), (2, 4, 2 * LOCAL, HALF)
     ).reshape(N_EXP, 2 * LOCAL, HALF)
-    normed, gate_first, lent_near, gate_late = lax.optimization_barrier(
-        (normed, gate_first, lent_near, gate_weight)
+    normed, gate_first, lent_near, gate_late, down_next = lax.optimization_barrier(
+        (normed, gate_first, lent_near, gate_weight, down_weight)
     )
     tokens = exchange(normed, "exp").reshape(KEYS, HALF)
     table, combine = routing_tables(routing[:, :TOPK], routing[:, TOPK:], side, groups)
@@ -385,17 +385,15 @@
     ).astype(jnp.bfloat16)
 
     gate_second = gate_part(gate_late, 1)
-    outbound, gate_second, gate_last, up_late, down_late = lax.optimization_barrier(
-        (outbound, gate_second, gate_weight, up_weight, down_weight)
+    lent_far = shift(quarter(down_next, 1 - side, 2), 2)
+    outbound, gate_second, lent_far, gate_last, up_late, down_late = lax.optimization_barrier(
+        (outbound, gate_second, lent_far, gate_weight, up_weight, down_weight)
     )
     inbound = exchange(outbound.reshape(groups, WIRE, HALF), "rep")
-    lent_far = shift(quarter(down_late, 1 - side, 2), 2)
     kept = [shift(quarter(down_late, side, step), step) for step in (1, -1, 2)]
     gate_third = gate_part(gate_last, 2)
     lent_up = across(lax.dynamic_index_in_dim(up_late, 1 - side, 0, keepdims=False))
-    inbound, lent_far, kept, gate_third = lax.optimization_barrier(
-        (inbound, lent_far, kept, gate_third)
-    )
+    inbound, kept, gate_third = lax.optimization_barrier((inbound, kept, gate_third))
     kept = [quarter(down_late, side, 0), *kept]
     lent_down = across(
         jnp.concatenate([quarter(down_late, 1 - side, 0), *lent_near, lent_far])

time: 198 us -> 199 us (level)
  local copies, waits for them, and re-layouts: 23.1 us -> 28.3 us
  waiting for transfers between devices: 66.2 us -> 62.9 us
    ppermute x5, waiting for transfers between devices: 21.1 us -> 12.6 us  [across(): return lax.ppermute(array, 'exp', [(e, e ^ 4) for e in range(N_EXP)])]
    ppermute x14, waiting for transfers between devices: 35.8 us -> 43.8 us  [shift(): return lax.ppermute(array, 'exp', pairs)]
    unnamed x56 -> x48, local copies, waits for them, and re-layouts: 6.4 us -> 9.2 us
    all_to_all x4, waiting for transfers between devices: 9.29 us -> 6.52 us  [exchange(): return lax.all_to_all(array, axis, split_axis=0, concat_axis=0, tiled=True)]
    squeeze x2 -> x3, local copies, waits for them, and re-layouts: 3.31 us -> 4.79 us  [quarter(): return lax.dynamic_slice(weight, (expert, 0, start), (1, UNITS, BLK))[0]]
  transfers between devices with their start and end apart: 23 -> 23, of which waited for: 14 -> 10; matrix products, arithmetic and copies ran while one was open for 10% -> 11% of each run, Pallas kernels for 6% -> 6%
where the time goes in v8:
time: 199 us; the launch traced here: 198 us
  waiting for transfers between devices  62.9 us (32%)
  starting transfers between devices  53.9 us (27%)
  blocking collectives  32.6 us (16%)
  local copies, waits for them, and re-layouts  28.3 us (14%)
  Pallas kernels  12.8 us (6%)
  other arithmetic  3.81 us (2%)
  matrix products  2.76 us (1%)
    ppermute x14, waiting for transfers between devices, shift(): return lax.ppermute(array, 'exp', pairs)  43.8 us
    all_to_all x1, blocking collectives, exchange(): return lax.all_to_all(array, axis, split_axis=0, concat_axis=0, tiled=True)  32.6 us
    all_to_all x4, starting transfers between devices, exchange(): return lax.all_to_all(array, axis, split_axis=0, concat_axis=0, tiled=True)  26 us
    ppermute x14, starting transfers between devices, shift(): return lax.ppermute(array, 'exp', pairs)  21.1 us
    ppermute x5, waiting for transfers between devices, across(): return lax.ppermute(array, 'exp', [(e, e ^ 4) for e in range(N_EXP)])  12.6 us
    unnamed x48, local copies, waits for them, and re-layouts  9.2 us
    pallas_call x2, Pallas kernels, call(): pl.pallas_call(kernel, out_shape=out_shape, grid_spec=pltpu.PrefetchScala...  8.22 us
    ppermute x5, starting transfers between devices, across(): return lax.ppermute(array, 'exp', [(e, e ^ 4) for e in range(N_EXP)])  6.75 us
  transfers between devices with their start and end apart: 23, of which 10 were waited for; matrix products, arithmetic and copies ran while one was open for 11% of the time, Pallas kernels for 6%

profile of v8, /device:TPU:4, one launch (start us, length us, event | category | flops | bytes accessed | tf_op | source)
XLA Modules:
  0.0 197.5 jit_solution(4262190021395890287)
XLA Ops:
  1.4 5.1 %all-to-all-start = ((s32[8,6,16]{2,1,0:T(8,128)}), s32[8,6,16]{2,1,0:T(8,128)S(1)}, u32[]{:S(2)}, u32[]{:S(2)}) async-start(s32[8,6,16]{2,1,0:T(8,128)} %broadcast_in_dim.15), calls=%async_computation | async-start | bytes 65536 | tf_op jit(solution)/shard_map/all_to_all | solution.py:132
  6.5 2.0 %dynamic-slice_bitcast_fusion.3 = bf16[64,4096]{1,0:T(8,128)(2,1)} fusion(bf16[2,192,4096]{2,1,0:T(8,128)(2,1)} %own_gate.3, s32[]{:T(128)S(6)} %select_n.75), kind=kLoop, calls=%fused_computation.8 | loop fusion | bytes 1048580 | tf_op jit(solution)/shard_map/squeeze | solution.py:362
  8.5 2.0 %collective-permute-start = (bf16[64,4096]{1,0:T(8,128)(2,1)}, bf16[64,4096]{1,0:T(8,128)(2,1)}, u32[]{:S(2)}, u32[]{:S(2)}) collective-permute-start(bf16[64,4096]{1,0:T(8,128)(2,1)} %dynamic-slice_bitcast_fusion.3), channel_id=1, source_target_pairs={{0,4},{1,5},{2,6},{3,7},{4,0},{5,1},{6,2},{7,3},{8,12},{9,13},{10,... | collective-permute-start | bytes 1572872 | tf_op jit(solution)/shard_map/ppermute | solution.py:141
  10.6 2.1 %dynamic-slice_bitcast_fusion.10 = (bf16[192,1024]{1,0:T(8,128)(2,1)}, bf16[192,1024]{1,0:T(8,128)(2,1)}) fusion(bf16[2,192,4096]{2,1,0:T(8,128)(2,1)} %param.27, s32[]{:T(128)S(6)} %select_n.75, s32[]{:T(128)S(6)} %select_n.79, s32[]{:T(128)S(6)} %select_n.77), kind=kLoop, calls=%fused_computation.18 | loop fusion | bytes 1572876 | tf_op jit(solution)/shard_map/squeeze | solution.py:366
  12.6 2.7 %collective-permute-start.2 = (bf16[192,1024]{1,0:T(8,128)(2,1)}, bf16[192,1024]{1,0:T(8,128)(2,1)}, u32[]{:S(2)}, u32[]{:S(2)}) collective-permute-start(bf16[192,1024]{1,0:T(8,128)(2,1)} %get-tuple-element.54), channel_id=1, source_target_pairs={{0,3},{1,0},{2,1},{3,2},{4,7},{5,4},{6,5},{7,6},{8,11},{9,8},{10,9... | collective-permute-start | bytes 1179656 | tf_op jit(solution)/shard_map/ppermute | solution.py:137
  22.2 2.8 %attend.1 = (f32[6,32,128]{2,1,0:T(8,128)S(1)}, bf16[6,32,128]{2,1,0:T(8,128)(2,1)S(1)}) custom-call(s32[2]{0:T(128)S(1)} %copy-done.15, bf16[6,32,128]{2,1,0:T(8,128)(2,1)S(1)} %reshape.83.query, bf16[2,1024,256]{2,1,0:T(8,128)(2,1)S(1)} %copy-done.4, bf16[2,1024,256]{2,1,0:T(8,128)(2,1)S(1)} %copy-done.5, bf16[2,8,256]{2,1,0:T(8,128)(2,1)S(1)} %pad.7.fresh_keys, ...), custom_call_target="tpu_custom_call" | custom-call | flops 100663296 | bytes 2342912 | tf_op jit(solution)/shard_map/attend/pallas_call | solution.py:90
  27.6 4.5 %all-to-all-start.1 = ((bf16[8,12,512]{2,1,0:T(8,128)(2,1)}), bf16[8,12,512]{2,1,0:T(8,128)(2,1)S(1)}, u32[]{:S(2)}, u32[]{:S(2)}) async-start(bf16[8,12,512]{2,1,0:T(8,128)(2,1)} %bitcast.8), calls=%async_computation.1 | async-start | bytes 262144 | tf_op jit(solution)/shard_map/all_to_all | solution.py:132
  32.9 2.0 %collective-permute-start.3 = (bf16[64,4096]{1,0:T(8,128)(2,1)}, bf16[64,4096]{1,0:T(8,128)(2,1)}, u32[]{:S(2)}, u32[]{:S(2)}) collective-permute-start(bf16[64,4096]{1,0:T(8,128)(2,1)} %dynamic-slice_bitcast_fusion.2), channel_id=1, source_target_pairs={{0,4},{1,5},{2,6},{3,7},{4,0},{5,1},{6,2},{7,3},{8,12},{9,13},{10,... | collective-permute-start | bytes 1572872 | tf_op jit(solution)/shard_map/ppermute | solution.py:141
  35.0 1.8 dynamic-slice_bitcast_fusion.9
  36.7 3.0 %collective-permute-start.4 = (bf16[192,1024]{1,0:T(8,128)(2,1)}, bf16[192,1024]{1,0:T(8,128)(2,1)}, u32[]{:S(2)}, u32[]{:S(2)}) collective-permute-start(bf16[192,1024]{1,0:T(8,128)(2,1)} %dynamic-slice_bitcast_fusion.9), channel_id=1, source_target_pairs={{0,2},{1,3},{2,0},{3,1},{4,6},{5,7},{6,4},{7,5},{8,10},{9,11},{10,... | collective-permute-start | bytes 1179656 | tf_op jit(solution)/shard_map/ppermute | solution.py:137
  40.4 2.1 %convolution_convert_fusion = bf16[768,512]{1,0:T(8,128)(2,1)} fusion(bf16[96,768]{0,1:T(8,128)(2,1)S(1)} %bitcast.68, bf16[96,512]{1,0:T(8,128)(2,1)} %reshape.90), kind=kOutput, calls=%fused_computation.2 | convolution fusion | flops 75890688 | bytes 1032192 | tf_op jit(solution)/shard_map/dot_general | solution.py:383
  42.5 5.0 %collective-permute-done.4 = bf16[192,1024]{1,0:T(8,128)(2,1)} collective-permute-done((bf16[192,1024]{1,0:T(8,128)(2,1)}, bf16[192,1024]{1,0:T(8,128)(2,1)}, u32[]{:S(2)}, u32[]{:S(2)}) %collective-permute-start.4) | collective-permute-done | bytes 393248 | tf_op jit(solution)/shard_map/ppermute | solution.py:137
  47.5 11.6 %all-to-all-start.2 = ((bf16[32,24,512]{2,1,0:T(8,128)(2,1)}), bf16[32,24,512]{2,1,0:T(8,128)(2,1)}, u32[]{:S(2)}, u32[]{:S(2)}) async-start(bf16[32,24,512]{2,1,0:T(8,128)(2,1)} %bitcast.64), calls=%async_computation.2 | async-start | bytes 1572864 | tf_op jit(solution)/shard_map/all_to_all | solution.py:132
  59.9 3.0 %dynamic-slice_bitcast_fusion = bf16[192,4096]{1,0:T(8,128)(2,1)} fusion(bf16[2,192,4096]{2,1,0:T(8,128)(2,1)} %own_up.3, s32[]{:T(128)S(6)} %select_n.75), kind=kLoop, calls=%fused_computation.1 | loop fusion | bytes 3145732 | tf_op jit(solution)/shard_map/jit(dynamic_index_in_dim)/squeeze | solution.py:395
  65.1 2.6 %collective-permute-start.7 = (bf16[192,1024]{1,0:T(8,128)(2,1)S(1)}, bf16[192,1024]{1,0:T(8,128)(2,1)S(1)}, u32[]{:S(2)}, u32[]{:S(2)}) collective-permute-start(bf16[192,1024]{1,0:T(8,128)(2,1)S(1)} %get-tuple-element.51), channel_id=1, source_target_pairs={{0,2},{1,3},{2,0},{3,1},{4,6},{5,7},{6,4},{7,5},{8,10},{9,11},{10,... | collective-permute-start | bytes 1179656 | tf_op jit(solution)/shard_map/ppermute | solution.py:137
  69.7 8.9 %collective-permute-done.7.w_far = bf16[192,1024]{1,0:T(8,128)(2,1)S(1)} collective-permute-done((bf16[192,1024]{1,0:T(8,128)(2,1)S(1)}, bf16[192,1024]{1,0:T(8,128)(2,1)S(1)}, u32[]{:S(2)}, u32[]{:S(2)}) %collective-permute-start.7) | collective-permute-done | bytes 393248 | tf_op jit(solution)/shard_map/ppermute | solution.py:137
  79.4 5.9 %collective-permute-done.6.w_above = bf16[192,1024]{1,0:T(8,128)(2,1)S(1)} collective-permute-done((bf16[192,1024]{1,0:T(8,128)(2,1)S(1)}, bf16[192,1024]{1,0:T(8,128)(2,1)S(1)}, u32[]{:S(2)}, u32[]{:S(2)}) %collective-permute-start.6) | collective-permute-done | bytes 393248 | tf_op jit(solution)/shard_map/ppermute | solution.py:137
  90.1 2.7 %collective-permute-start.11 = (bf16[384,1024]{1,0:T(8,128)(2,1)S(1)}, bf16[384,1024]{1,0:T(8,128)(2,1)S(1)}, u32[]{:S(2)}, u32[]{:S(2)}) collective-permute-start(bf16[384,1024]{1,0:T(8,128)(2,1)S(1)} %bitcast.60), channel_id=1, source_target_pairs={{0,3},{1,0},{2,1},{3,2},{4,7},{5,4},{6,5},{7,6},{8,11},{9,8},{10,9... | collective-permute-start | bytes 2359304 | tf_op jit(solution)/shard_map/ppermute | solution.py:137
  95.0 14.8 %collective-permute-done.11.above_rows = bf16[384,1024]{1,0:T(8,128)(2,1)S(1)} collective-permute-done((bf16[384,1024]{1,0:T(8,128)(2,1)S(1)}, bf16[384,1024]{1,0:T(8,128)(2,1)S(1)}, u32[]{:S(2)}, u32[]{:S(2)}) %collective-permute-start.11) | collective-permute-done | bytes 786464 | tf_op jit(solution)/shard_map/ppermute | solution.py:137
  109.8 3.8 %collective-permute-start.12 = (bf16[192,1024]{1,0:T(8,128)(2,1)S(1)}, bf16[192,1024]{1,0:T(8,128)(2,1)S(1)}, u32[]{:S(2)}, u32[]{:S(2)}) collective-permute-start(bf16[192,1024]{1,0:T(8,128)(2,1)S(1)} %slice.27), channel_id=1, source_target_pairs={{0,3},{1,0},{2,1},{3,2},{4,7},{5,4},{6,5},{7,6},{8,11},{9,8},{10,9... | collective-permute-start | bytes 1179656 | tf_op jit(solution)/shard_map/ppermute | solution.py:137
  113.8 1.5 collective-permute-done.13.lent_up
  115.3 5.3 %expand_near.1 = (f32[384,384]{1,0:T(8,128)S(1)}, f32[384,384]{1,0:T(8,128)S(1)}) custom-call(s32[2]{0:T(128)S(1)} %pad_add_fusion.1.where, bf16[384,1024]{1,0:T(8,128)(2,1)S(1)} %bitcast.62, bf16[384,1024]{1,0:T(8,128)(2,1)S(1)} %collective-permute-done.9.below_rows, bf16[384,1024]{1,0:T(8,128)(2,1)S(1)} %collective-permute-done.11.above_rows, ...), custom_call_target="tpu_custom_call" | custom-call | flops 1811939328 | bytes 8257536 | tf_op jit(solution)/shard_map/expand_near/pallas_call | solution.py:275
  121.3 3.5 %collective-permute-done.10.far_low = bf16[192,1024]{1,0:T(8,128)(2,1)S(1)} collective-permute-done((bf16[192,1024]{1,0:T(8,128)(2,1)S(1)}, bf16[192,1024]{1,0:T(8,128)(2,1)S(1)}, u32[]{:S(2)}, u32[]{:S(2)}) %collective-permute-start.10) | collective-permute-done | bytes 393248 | tf_op jit(solution)/shard_map/ppermute | solution.py:137
  124.8 2.9 %expand_far.1.own = bf16[384,384]{1,0:T(8,128)(2,1)S(1)} custom-call(s32[2]{0:T(128)S(1)} %pad_add_fusion.1.where, bf16[192,1024]{1,0:T(8,128)(2,1)S(1)} %collective-permute-done.10.far_low, bf16[192,1024]{1,0:T(8,128)(2,1)S(1)} %collective-permute-done.12.far_high, f32[384,384]{1,0:T(8,128)S(1)} %get-tuple-element.39.gate_total, ...), custom_call_target="tpu_custom_call" | custom-call | flops 603979776 | bytes 3538944 | tf_op jit(solution)/shard_map/expand_far/pallas_call | solution.py:275
  128.0 1.8 collective-permute-start.14
  129.8 5.0 %collective-permute-done.15.above = bf16[384,384]{1,0:T(8,128)(2,1)S(1)} collective-permute-done((bf16[384,384]{1,0:T(8,128)(2,1)S(1)}, bf16[384,384]{1,0:T(8,128)(2,1)S(1)}, u32[]{:S(2)}, u32[]{:S(2)}) %collective-permute-start.15) | collective-permute-done | bytes 294944 | tf_op jit(solution)/shard_map/ppermute | solution.py:137
  134.9 1.6 collective-permute-start.17
  137.1 11.0 %collective-permute-done.18.lent = bf16[768,1024]{1,0:T(8,128)(2,1)S(1)} collective-permute-done((bf16[768,1024]{1,0:T(8,128)(2,1)S(1)}, bf16[768,1024]{1,0:T(8,128)(2,1)S(1)}, u32[]{:S(2)}, u32[]{:S(2)}) %collective-permute-start.18) | collective-permute-done | bytes 1572896 | tf_op jit(solution)/shard_map/ppermute | solution.py:141
  148.1 1.8 contract.1
  151.2 32.6 %all_to_all.25 = bf16[32,24,512]{2,1,0:T(8,128)(2,1)S(1)} all-to-all(bf16[32,24,512]{2,1,0:T(8,128)(2,1)S(1)} %copy.79), channel_id=1, replica_groups=mesh['rep'=32,'exp'=8] {'rep'}, dimensions={0} | all-to-all | bytes 1572864 | tf_op jit(solution)/shard_map/all_to_all | solution.py:132
  185.1 4.8 %all-to-all-start.4 = ((bf16[8,12,512]{2,1,0:T(8,128)(2,1)}), bf16[8,12,512]{2,1,0:T(8,128)(2,1)S(1)}, u32[]{:S(2)}, u32[]{:S(2)}) async-start(bf16[8,12,512]{2,1,0:T(8,128)(2,1)} %reshape.96), calls=%async_computation.4 | async-start | bytes 262144 | tf_op jit(solution)/shard_map/all_to_all | solution.py:132
  189.9 6.5 %all-to-all-done.4 = bf16[8,12,512]{2,1,0:T(8,128)(2,1)S(1)} async-done(((bf16[8,12,512]{2,1,0:T(8,128)(2,1)}), bf16[8,12,512]{2,1,0:T(8,128)(2,1)S(1)}, u32[]{:S(2)}, u32[]{:S(2)}) %all-to-all-start.4) | async-done | bytes 98336 | tf_op jit(solution)/shard_map/all_to_all | solution.py:132
  (117 shorter events, 30.3 us)
Async XLA Ops:
  0.0 26.8 %copy-start.21 = (bf16[96,96]{1,0:T(8,128)(2,1)S(1)}, bf16[96,96]{1,0:T(8,128)(2,1)}, u32[]{:S(2)}) copy-start(bf16[96,96]{1,0:T(8,128)(2,1)} %constant.117) | copy-start | bytes 55300
  1.4 24.3 %all-to-all-start = ((s32[8,6,16]{2,1,0:T(8,128)}), s32[8,6,16]{2,1,0:T(8,128)S(1)}, u32[]{:S(2)}, u32[]{:S(2)}) async-start(s32[8,6,16]{2,1,0:T(8,128)} %broadcast_in_dim.15), calls=%async_computation | async-start | bytes 65536 | tf_op jit(solution)/shard_map/all_to_all | solution.py:132
  6.5 25.6 %copy-start = (bf16[2,192,4096]{2,1,0:T(8,128)(2,1)S(1)}, bf16[2,192,4096]{2,1,0:T(8,128)(2,1)}, u32[]{:S(2)}) copy-start(bf16[2,192,4096]{2,1,0:T(8,128)(2,1)} %own_gate.3) | copy-start | bytes 9437188
  8.5 18.4 %collective-permute-start = (bf16[64,4096]{1,0:T(8,128)(2,1)}, bf16[64,4096]{1,0:T(8,128)(2,1)}, u32[]{:S(2)}, u32[]{:S(2)}) collective-permute-start(bf16[64,4096]{1,0:T(8,128)(2,1)} %dynamic-slice_bitcast_fusion.3), channel_id=1, source_target_pairs={{0,4},{1,5},{2,6},{3,7},{4,0},{5,1},{6,2},{7,3},{8,12},{9,13},{10,... | collective-permute-start | bytes 1572872 | tf_op jit(solution)/shard_map/ppermute | solution.py:141
  12.6 14.3 %collective-permute-start.2 = (bf16[192,1024]{1,0:T(8,128)(2,1)}, bf16[192,1024]{1,0:T(8,128)(2,1)}, u32[]{:S(2)}, u32[]{:S(2)}) collective-permute-start(bf16[192,1024]{1,0:T(8,128)(2,1)} %get-tuple-element.54), channel_id=1, source_target_pairs={{0,3},{1,0},{2,1},{3,2},{4,7},{5,4},{6,5},{7,6},{8,11},{9,8},{10,9... | collective-permute-start | bytes 1179656 | tf_op jit(solution)/shard_map/ppermute | solution.py:137
  15.3 11.6 %collective-permute-start.1 = (bf16[192,1024]{1,0:T(8,128)(2,1)}, bf16[192,1024]{1,0:T(8,128)(2,1)}, u32[]{:S(2)}, u32[]{:S(2)}) collective-permute-start(bf16[192,1024]{1,0:T(8,128)(2,1)} %get-tuple-element.55), channel_id=1, source_target_pairs={{0,1},{1,2},{2,3},{3,0},{4,5},{5,6},{6,7},{7,4},{8,9},{9,10},{10,1... | collective-permute-start | bytes 1179656 | tf_op jit(solution)/shard_map/ppermute | solution.py:137
  27.6 12.2 %all-to-all-start.1 = ((bf16[8,12,512]{2,1,0:T(8,128)(2,1)}), bf16[8,12,512]{2,1,0:T(8,128)(2,1)S(1)}, u32[]{:S(2)}, u32[]{:S(2)}) async-start(bf16[8,12,512]{2,1,0:T(8,128)(2,1)} %bitcast.8), calls=%async_computation.1 | async-start | bytes 262144 | tf_op jit(solution)/shard_map/all_to_all | solution.py:132
  32.9 14.6 %collective-permute-start.3 = (bf16[64,4096]{1,0:T(8,128)(2,1)}, bf16[64,4096]{1,0:T(8,128)(2,1)}, u32[]{:S(2)}, u32[]{:S(2)}) collective-permute-start(bf16[64,4096]{1,0:T(8,128)(2,1)} %dynamic-slice_bitcast_fusion.2), channel_id=1, source_target_pairs={{0,4},{1,5},{2,6},{3,7},{4,0},{5,1},{6,2},{7,3},{8,12},{9,13},{10,... | collective-permute-start | bytes 1572872 | tf_op jit(solution)/shard_map/ppermute | solution.py:141
  36.7 10.8 %collective-permute-start.4 = (bf16[192,1024]{1,0:T(8,128)(2,1)}, bf16[192,1024]{1,0:T(8,128)(2,1)}, u32[]{:S(2)}, u32[]{:S(2)}) collective-permute-start(bf16[192,1024]{1,0:T(8,128)(2,1)} %dynamic-slice_bitcast_fusion.9), channel_id=1, source_target_pairs={{0,2},{1,3},{2,0},{3,1},{4,6},{5,7},{6,4},{7,5},{8,10},{9,11},{10,... | collective-permute-start | bytes 1179656 | tf_op jit(solution)/shard_map/ppermute | solution.py:137
  47.5 40.1 %all-to-all-start.2 = ((bf16[32,24,512]{2,1,0:T(8,128)(2,1)}), bf16[32,24,512]{2,1,0:T(8,128)(2,1)}, u32[]{:S(2)}, u32[]{:S(2)}) async-start(bf16[32,24,512]{2,1,0:T(8,128)(2,1)} %bitcast.64), calls=%async_computation.2 | async-start | bytes 1572864 | tf_op jit(solution)/shard_map/all_to_all | solution.py:132
  59.3 27.6 %collective-permute-start.8 = (bf16[64,4096]{1,0:T(8,128)(2,1)S(1)}, bf16[64,4096]{1,0:T(8,128)(2,1)S(1)}, u32[]{:S(2)}, u32[]{:S(2)}) collective-permute-start(bf16[64,4096]{1,0:T(8,128)(2,1)S(1)} %dynamic-slice_bitcast_fusion.1), channel_id=1, source_target_pairs={{0,4},{1,5},{2,6},{3,7},{4,0},{5,1},{6,2},{7,3},{8,12},{9,13},{10,... | collective-permute-start | bytes 1572872 | tf_op jit(solution)/shard_map/ppermute | solution.py:141
  62.9 52.4 %collective-permute-start.13 = (bf16[192,4096]{1,0:T(8,128)(2,1)}, bf16[192,4096]{1,0:T(8,128)(2,1)}, u32[]{:S(2)}, u32[]{:S(2)}) collective-permute-start(bf16[192,4096]{1,0:T(8,128)(2,1)} %dynamic-slice_bitcast_fusion), channel_id=1, source_target_pairs={{0,4},{1,5},{2,6},{3,7},{4,0},{5,1},{6,2},{7,3},{8,12},{9,13},{10,... | collective-permute-start | bytes 4718600 | tf_op jit(solution)/shard_map/ppermute | solution.py:141
  65.1 13.6 %collective-permute-start.7 = (bf16[192,1024]{1,0:T(8,128)(2,1)S(1)}, bf16[192,1024]{1,0:T(8,128)(2,1)S(1)}, u32[]{:S(2)}, u32[]{:S(2)}) collective-permute-start(bf16[192,1024]{1,0:T(8,128)(2,1)S(1)} %get-tuple-element.51), channel_id=1, source_target_pairs={{0,2},{1,3},{2,0},{3,1},{4,6},{5,7},{6,4},{7,5},{8,10},{9,11},{10,... | collective-permute-start | bytes 1179656 | tf_op jit(solution)/shard_map/ppermute | solution.py:137
  67.7 17.6 %collective-permute-start.6 = (bf16[192,1024]{1,0:T(8,128)(2,1)S(1)}, bf16[192,1024]{1,0:T(8,128)(2,1)S(1)}, u32[]{:S(2)}, u32[]{:S(2)}) collective-permute-start(bf16[192,1024]{1,0:T(8,128)(2,1)S(1)} %get-tuple-element.52), channel_id=1, source_target_pairs={{0,3},{1,0},{2,1},{3,2},{4,7},{5,4},{6,5},{7,6},{8,11},{9,8},{10,9... | collective-permute-start | bytes 1179656 | tf_op jit(solution)/shard_map/ppermute | solution.py:137
  68.8 17.2 %collective-permute-start.5 = (bf16[192,1024]{1,0:T(8,128)(2,1)S(1)}, bf16[192,1024]{1,0:T(8,128)(2,1)S(1)}, u32[]{:S(2)}, u32[]{:S(2)}) collective-permute-start(bf16[192,1024]{1,0:T(8,128)(2,1)S(1)} %get-tuple-element.53), channel_id=1, source_target_pairs={{0,1},{1,2},{2,3},{3,0},{4,5},{5,6},{6,7},{7,4},{8,9},{9,10},{10,1... | collective-permute-start | bytes 1179656 | tf_op jit(solution)/shard_map/ppermute | solution.py:137
  89.9 25.4 %copy-start.1 = (bf16[2,192,4096]{2,1,0:T(8,128)(2,1)S(1)}, bf16[2,192,4096]{2,1,0:T(8,128)(2,1)}, u32[]{:S(2)}) copy-start(bf16[2,192,4096]{2,1,0:T(8,128)(2,1)} %own_up.3) | copy-start | bytes 9437188
  89.9 25.4 %copy-start.3 = (bf16[64,4096]{1,0:T(8,128)(2,1)S(1)}, bf16[64,4096]{1,0:T(8,128)(2,1)}, u32[]{:S(2)}) copy-start(bf16[64,4096]{1,0:T(8,128)(2,1)} %copy-done.2) | copy-start | bytes 1572868
  90.1 19.7 %collective-permute-start.11 = (bf16[384,1024]{1,0:T(8,128)(2,1)S(1)}, bf16[384,1024]{1,0:T(8,128)(2,1)S(1)}, u32[]{:S(2)}, u32[]{:S(2)}) collective-permute-start(bf16[384,1024]{1,0:T(8,128)(2,1)S(1)} %bitcast.60), channel_id=1, source_target_pairs={{0,3},{1,0},{2,1},{3,2},{4,7},{5,4},{6,5},{7,6},{8,11},{9,8},{10,9... | collective-permute-start | bytes 2359304 | tf_op jit(solution)/shard_map/ppermute | solution.py:137
  92.8 20.8 %collective-permute-start.9 = (bf16[384,1024]{1,0:T(8,128)(2,1)S(1)}, bf16[384,1024]{1,0:T(8,128)(2,1)S(1)}, u32[]{:S(2)}, u32[]{:S(2)}) collective-permute-start(bf16[384,1024]{1,0:T(8,128)(2,1)S(1)} %bitcast.61), channel_id=1, source_target_pairs={{0,1},{1,2},{2,3},{3,0},{4,5},{5,6},{6,7},{7,4},{8,9},{9,10},{10,1... | collective-permute-start | bytes 2359304 | tf_op jit(solution)/shard_map/ppermute | solution.py:137
  94.1 54.0 %collective-permute-start.18 = (bf16[768,1024]{1,0:T(8,128)(2,1)S(1)}, bf16[768,1024]{1,0:T(8,128)(2,1)S(1)}, u32[]{:S(2)}, u32[]{:S(2)}) collective-permute-start(bf16[768,1024]{1,0:T(8,128)(2,1)S(1)} %pad_maximum_fusion), channel_id=1, source_target_pairs={{0,4},{1,5},{2,6},{3,7},{4,0},{5,1},{6,2},{7,3},{8,12},{9,13},{10,... | collective-permute-start | bytes 4718600 | tf_op jit(solution)/shard_map/ppermute | solution.py:141
  109.8 11.5 %collective-permute-start.12 = (bf16[192,1024]{1,0:T(8,128)(2,1)S(1)}, bf16[192,1024]{1,0:T(8,128)(2,1)S(1)}, u32[]{:S(2)}, u32[]{:S(2)}) collective-permute-start(bf16[192,1024]{1,0:T(8,128)(2,1)S(1)} %slice.27), channel_id=1, source_target_pairs={{0,3},{1,0},{2,1},{3,2},{4,7},{5,4},{6,5},{7,6},{8,11},{9,8},{10,9... | collective-permute-start | bytes 1179656 | tf_op jit(solution)/shard_map/ppermute | solution.py:137
  113.6 11.2 %collective-permute-start.10 = (bf16[192,1024]{1,0:T(8,128)(2,1)S(1)}, bf16[192,1024]{1,0:T(8,128)(2,1)S(1)}, u32[]{:S(2)}, u32[]{:S(2)}) collective-permute-start(bf16[192,1024]{1,0:T(8,128)(2,1)S(1)} %slice.26), channel_id=1, source_target_pairs={{0,1},{1,2},{2,3},{3,0},{4,5},{5,6},{6,7},{7,4},{8,9},{9,10},{10,1... | collective-permute-start | bytes 1179656 | tf_op jit(solution)/shard_map/ppermute | solution.py:137
  124.8 23.3 %copy-start.9 = (bf16[192,1024]{1,0:T(8,128)(2,1)S(1)}, bf16[192,1024]{1,0:T(8,128)(2,1)}, u32[]{:S(2)}) copy-start(bf16[192,1024]{1,0:T(8,128)(2,1)} %copy-done.8) | copy-start | bytes 1179652
  124.8 23.3 %copy-start.11 = (bf16[192,1024]{1,0:T(8,128)(2,1)S(1)}, bf16[192,1024]{1,0:T(8,128)(2,1)}, u32[]{:S(2)}) copy-start(bf16[192,1024]{1,0:T(8,128)(2,1)} %copy-done.10) | copy-start | bytes 1179652
  127.7 7.2 %collective-permute-start.15 = (bf16[384,384]{1,0:T(8,128)(2,1)S(1)}, bf16[384,384]{1,0:T(8,128)(2,1)S(1)}, u32[]{:S(2)}, u32[]{:S(2)}) collective-permute-start(bf16[384,384]{1,0:T(8,128)(2,1)S(1)} %expand_far.1.own), channel_id=1, source_target_pairs={{0,3},{1,0},{2,1},{3,2},{4,7},{5,4},{6,5},{7,6},{8,11},{9,8},{10,9... | collective-permute-start | bytes 884744 | tf_op jit(solution)/shard_map/ppermute | solution.py:137
  128.0 8.5 %collective-permute-start.14 = (bf16[384,384]{1,0:T(8,128)(2,1)S(1)}, bf16[384,384]{1,0:T(8,128)(2,1)S(1)}, u32[]{:S(2)}, u32[]{:S(2)}) collective-permute-start(bf16[384,384]{1,0:T(8,128)(2,1)S(1)} %expand_far.1.own), channel_id=1, source_target_pairs={{0,1},{1,2},{2,3},{3,0},{4,5},{5,6},{6,7},{7,4},{8,9},{9,10},{10,1... | collective-permute-start | bytes 884744 | tf_op jit(solution)/shard_map/ppermute | solution.py:137
  134.9 13.2 %collective-permute-start.17 = (bf16[192,384]{1,0:T(8,128)(2,1)S(1)}, bf16[192,384]{1,0:T(8,128)(2,1)S(1)}, u32[]{:S(2)}, u32[]{:S(2)}) collective-permute-start(bf16[192,384]{1,0:T(8,128)(2,1)S(1)} %slice.29), channel_id=1, source_target_pairs={{0,3},{1,0},{2,1},{3,2},{4,7},{5,4},{6,5},{7,6},{8,11},{9,8},{10,9... | collective-permute-start | bytes 442376 | tf_op jit(solution)/shard_map/ppermute | solution.py:137
  136.5 11.7 %collective-permute-start.16 = (bf16[192,384]{1,0:T(8,128)(2,1)S(1)}, bf16[192,384]{1,0:T(8,128)(2,1)S(1)}, u32[]{:S(2)}, u32[]{:S(2)}) collective-permute-start(bf16[192,384]{1,0:T(8,128)(2,1)S(1)} %slice.28), channel_id=1, source_target_pairs={{0,1},{1,2},{2,3},{3,0},{4,5},{5,6},{6,7},{7,4},{8,9},{9,10},{10,1... | collective-permute-start | bytes 442376 | tf_op jit(solution)/shard_map/ppermute | solution.py:137
  149.9 33.9 %copy-start.18 = (f32[96,32]{0,1:T(8,128)S(1)}, f32[96,32]{0,1:T(8,128)}, u32[]{:S(2)}) copy-start(f32[96,32]{0,1:T(8,128)} %get-tuple-element.47) | copy-start | bytes 36868
  150.0 33.9 %copy-start.20 = (f32[96,24]{0,1:T(8,128)S(1)}, f32[96,24]{0,1:T(8,128)}, u32[]{:S(2)}) copy-start(f32[96,24]{0,1:T(8,128)} %constant.103) | copy-start | bytes 27652
  150.5 39.3 %copy-start.13 = (f32[6,32,128]{2,1,0:T(8,128)S(1)}, f32[6,32,128]{2,1,0:T(8,128)}, u32[]{:S(2)}) copy-start(f32[6,32,128]{2,1,0:T(8,128)} %copy-done.12) | copy-start | bytes 294916
  185.1 11.4 %all-to-all-start.4 = ((bf16[8,12,512]{2,1,0:T(8,128)(2,1)}), bf16[8,12,512]{2,1,0:T(8,128)(2,1)S(1)}, u32[]{:S(2)}, u32[]{:S(2)}) async-start(bf16[8,12,512]{2,1,0:T(8,128)(2,1)} %reshape.96), calls=%async_computation.4 | async-start | bytes 262144 | tf_op jit(solution)/shard_map/all_to_all | solution.py:132
  (13 other events, 58.5 us)

commit v9 on v8

--- a/solution.py
+++ b/solution.py
@@ -375,8 +375,8 @@
     normed = jnp.broadcast_to(
         normed.reshape(1, 4, 2 * LOCAL, HALF), (2, 4, 2 * LOCAL, HALF)
     ).reshape(N_EXP, 2 * LOCAL, HALF)
-    normed, gate_first, lent_near, gate_late, down_next = lax.optimization_barrier(
-        (normed, gate_first, lent_near, gate_weight, down_weight)
+    normed, gate_first, lent_near, up_next = lax.optimization_barrier(
+        (normed, gate_first, lent_near, up_weight)
     )
     tokens = exchange(normed, "exp").reshape(KEYS, HALF)
     table, combine = routing_tables(routing[:, :TOPK], routing[:, TOPK:], side, groups)
@@ -384,16 +384,15 @@
         table, tokens, (((0,), (0,)), ((), ())), preferred_element_type=jnp.float32
     ).astype(jnp.bfloat16)
 
-    gate_second = gate_part(gate_late, 1)
-    lent_far = shift(quarter(down_next, 1 - side, 2), 2)
-    outbound, gate_second, lent_far, gate_last, up_late, down_late = lax.optimization_barrier(
-        (outbound, gate_second, lent_far, gate_weight, up_weight, down_weight)
-    )
+    lent_up = across(lax.dynamic_index_in_dim(up_next, 1 - side, 0, keepdims=False))
+    outbound, gate_last, down_late = lax.optimization_barrier((outbound, gate_weight, down_weight))
     inbound = exchange(outbound.reshape(groups, WIRE, HALF), "rep")
     kept = [shift(quarter(down_late, side, step), step) for step in (1, -1, 2)]
-    gate_third = gate_part(gate_last, 2)
-    lent_up = across(lax.dynamic_index_in_dim(up_late, 1 - side, 0, keepdims=False))
-    inbound, kept, gate_third = lax.optimization_barrier((inbound, kept, gate_third))
+    gate_second, gate_third = gate_part(gate_last, 1), gate_part(gate_last, 2)
+    lent_far = shift(quarter(down_late, 1 - side, 2), 2)
+    inbound, kept, lent_far, gate_second, gate_third, lent_up = lax.optimization_barrier(
+        (inbound, kept, lent_far, gate_second, gate_third, lent_up)
+    )
     kept = [quarter(down_late, side, 0), *kept]
     lent_down = across(
         jnp.concatenate([quarter(down_late, 1 - side, 0), *lent_near, lent_far])

time: 199 us -> 202 us (1.015)
  starting transfers between devices: 53.9 us -> 56.9 us
  local copies, waits for them, and re-layouts: 28.3 us -> 25.9 us
  blocking collectives: 32.6 us -> 34.7 us
    all_to_all x4, waiting for transfers between devices: 6.52 us -> 10.2 us  [exchange(): return lax.all_to_all(array, axis, split_axis=0, concat_axis=0, tiled=True)]
    ppermute x14, starting transfers between devices: 21.1 us -> 23.5 us  [shift(): return lax.ppermute(array, 'exp', pairs)]
    all_to_all x1, blocking collectives: 32.6 us -> 34.7 us  [exchange(): return lax.all_to_all(array, axis, split_axis=0, concat_axis=0, tiled=True)]
    unnamed x48 -> x56, local copies, waits for them, and re-layouts: 9.2 us -> 10 us
    squeeze x3 -> x2, local copies, waits for them, and re-layouts: 4.79 us -> 4.83 us  [quarter(): return lax.dynamic_slice(weight, (expert, 0, start), (1, UNITS, BLK))[0]]
  transfers between devices with their start and end apart: 23 -> 23, of which waited for: 10 -> 11; matrix products, arithmetic and copies ran while one was open for 11% -> 7% of each run, Pallas kernels for 6% -> 5%
where the time goes in v9:
time: 202 us; the launch traced here: 201 us
  waiting for transfers between devices  64.7 us (32%)
  starting transfers between devices  56.9 us (28%)
  blocking collectives  34.7 us (17%)
  local copies, waits for them, and re-layouts  25.9 us (13%)
  Pallas kernels  12.8 us (6%)
  other arithmetic  3.72 us (2%)
    ppermute x14, waiting for transfers between devices, shift(): return lax.ppermute(array, 'exp', pairs)  43.9 us
    all_to_all x1, blocking collectives, exchange(): return lax.all_to_all(array, axis, split_axis=0, concat_axis=0, tiled=True)  34.7 us
    all_to_all x4, starting transfers between devices, exchange(): return lax.all_to_all(array, axis, split_axis=0, concat_axis=0, tiled=True)  26.6 us
    ppermute x14, starting transfers between devices, shift(): return lax.ppermute(array, 'exp', pairs)  23.5 us
    ppermute x5, waiting for transfers between devices, across(): return lax.ppermute(array, 'exp', [(e, e ^ 4) for e in range(N_EXP)])  10.6 us
    all_to_all x4, waiting for transfers between devices, exchange(): return lax.all_to_all(array, axis, split_axis=0, concat_axis=0, tiled=True)  10.2 us
    unnamed x56, local copies, waits for them, and re-layouts  10 us
    pallas_call x2, Pallas kernels, call(): pl.pallas_call(kernel, out_shape=out_shape, grid_spec=pltpu.PrefetchScala...  8.14 us
  transfers between devices with their start and end apart: 23, of which 11 were waited for; matrix products, arithmetic and copies ran while one was open for 7% of the time, Pallas kernels for 5%

profile of v9, /device:TPU:4, one launch (start us, length us, event | category | flops | bytes accessed | tf_op | source)
XLA Modules:
  0.0 201.1 jit_solution(12477808161481571834)
XLA Ops:
  0.0 2.2 %dynamic-slice_bitcast_fusion.10 = (bf16[192,1024]{1,0:T(8,128)(2,1)}, bf16[192,1024]{1,0:T(8,128)(2,1)}) fusion(bf16[2,192,4096]{2,1,0:T(8,128)(2,1)} %param.27, s32[]{:T(128)S(6)} %select_n.75, s32[]{:T(128)S(6)} %select_n.79, s32[]{:T(128)S(6)} %select_n.77), kind=kLoop, calls=%fused_computation.18 | loop fusion | bytes 1572876 | tf_op jit(solution)/shard_map/squeeze | solution.py:366
  2.2 1.6 collective-permute-start.1
  3.8 1.7 collective-permute-start.2
  5.5 1.9 dynamic-slice_bitcast_fusion.3
  9.9 3.5 %all-to-all-start = ((s32[8,6,16]{2,1,0:T(8,128)}), s32[8,6,16]{2,1,0:T(8,128)S(1)}, u32[]{:S(2)}, u32[]{:S(2)}) async-start(s32[8,6,16]{2,1,0:T(8,128)} %broadcast_in_dim.15), calls=%async_computation | async-start | bytes 65536 | tf_op jit(solution)/shard_map/all_to_all | solution.py:132
  20.4 2.8 %attend.1 = (f32[6,32,128]{2,1,0:T(8,128)S(1)}, bf16[6,32,128]{2,1,0:T(8,128)(2,1)S(1)}) custom-call(s32[2]{0:T(128)S(1)} %copy-done.18, bf16[6,32,128]{2,1,0:T(8,128)(2,1)S(1)} %reshape.83.query, bf16[2,1024,256]{2,1,0:T(8,128)(2,1)S(1)} %copy-done.7, bf16[2,1024,256]{2,1,0:T(8,128)(2,1)S(1)} %copy-done.8, bf16[2,8,256]{2,1,0:T(8,128)(2,1)S(1)} %pad.7.fresh_keys, ...), custom_call_target="tpu_custom_call" | custom-call | flops 100663296 | bytes 2342912 | tf_op jit(solution)/shard_map/attend/pallas_call | solution.py:90
  25.8 5.7 %all-to-all-start.1 = ((bf16[8,12,512]{2,1,0:T(8,128)(2,1)}), bf16[8,12,512]{2,1,0:T(8,128)(2,1)S(1)}, u32[]{:S(2)}, u32[]{:S(2)}) async-start(bf16[8,12,512]{2,1,0:T(8,128)(2,1)} %bitcast.69), calls=%async_computation.1 | async-start | bytes 262144 | tf_op jit(solution)/shard_map/all_to_all | solution.py:132
  32.8 2.0 %collective-permute-start.9 = (bf16[192,4096]{1,0:T(8,128)(2,1)}, bf16[192,4096]{1,0:T(8,128)(2,1)}, u32[]{:S(2)}, u32[]{:S(2)}) collective-permute-start(bf16[192,4096]{1,0:T(8,128)(2,1)} %dynamic-slice_bitcast_fusion), channel_id=1, source_target_pairs={{0,4},{1,5},{2,6},{3,7},{4,0},{5,1},{6,2},{7,3},{8,12},{9,13},{10,... | collective-permute-start | bytes 4718600 | tf_op jit(solution)/shard_map/ppermute | solution.py:141
  34.8 3.7 %all-to-all-done.1 = bf16[8,12,512]{2,1,0:T(8,128)(2,1)S(1)} async-done(((bf16[8,12,512]{2,1,0:T(8,128)(2,1)}), bf16[8,12,512]{2,1,0:T(8,128)(2,1)S(1)}, u32[]{:S(2)}, u32[]{:S(2)}) %all-to-all-start.1) | async-done | bytes 98336 | tf_op jit(solution)/shard_map/all_to_all | solution.py:132
  39.8 11.9 %all-to-all-start.2 = ((bf16[32,24,512]{2,1,0:T(8,128)(2,1)}), bf16[32,24,512]{2,1,0:T(8,128)(2,1)}, u32[]{:S(2)}, u32[]{:S(2)}) async-start(bf16[32,24,512]{2,1,0:T(8,128)(2,1)} %bitcast.64), calls=%async_computation.2 | async-start | bytes 1572864 | tf_op jit(solution)/shard_map/all_to_all | solution.py:132
  51.7 2.6 %dynamic-slice_bitcast_fusion.4 = (bf16[192,1024]{1,0:T(8,128)(2,1)}, bf16[192,1024]{1,0:T(8,128)(2,1)S(1)}, bf16[192,1024]{1,0:T(8,128)(2,1)S(1)}, bf16[192,102...) fusion(bf16[2,192,4096]{2,1,0:T(8,128)(2,1)} %param.27, s32[]{:T(128)S(6)} %select_n.75, ...), kind=kLoop, calls=%fused_computation.12 | loop fusion | bytes 4718616 | tf_op jit(solution)/shard_map/squeeze | solution.py:366
  54.9 2.7 %collective-permute-start.4 = (bf16[192,1024]{1,0:T(8,128)(2,1)S(1)}, bf16[192,1024]{1,0:T(8,128)(2,1)S(1)}, u32[]{:S(2)}, u32[]{:S(2)}) collective-permute-start(bf16[192,1024]{1,0:T(8,128)(2,1)S(1)} %get-tuple-element.51), channel_id=1, source_target_pairs={{0,3},{1,0},{2,1},{3,2},{4,7},{5,4},{6,5},{7,6},{8,11},{9,8},{10,9... | collective-permute-start | bytes 1179656 | tf_op jit(solution)/shard_map/ppermute | solution.py:137
  59.8 6.9 %collective-permute-done.3.w_below = bf16[192,1024]{1,0:T(8,128)(2,1)S(1)} collective-permute-done((bf16[192,1024]{1,0:T(8,128)(2,1)S(1)}, bf16[192,1024]{1,0:T(8,128)(2,1)S(1)}, u32[]{:S(2)}, u32[]{:S(2)}) %collective-permute-start.3) | collective-permute-done | bytes 393248 | tf_op jit(solution)/shard_map/ppermute | solution.py:137
  68.3 3.5 %collective-permute-start.6 = (bf16[192,1024]{1,0:T(8,128)(2,1)S(1)}, bf16[192,1024]{1,0:T(8,128)(2,1)S(1)}, u32[]{:S(2)}, u32[]{:S(2)}) collective-permute-start(bf16[192,1024]{1,0:T(8,128)(2,1)S(1)} %get-tuple-element.49), channel_id=1, source_target_pairs={{0,2},{1,3},{2,0},{3,1},{4,6},{5,7},{6,4},{7,5},{8,10},{9,11},{10,... | collective-permute-start | bytes 1179656 | tf_op jit(solution)/shard_map/ppermute | solution.py:137
  71.8 9.2 %collective-permute-done.5.w_far = bf16[192,1024]{1,0:T(8,128)(2,1)S(1)} collective-permute-done((bf16[192,1024]{1,0:T(8,128)(2,1)S(1)}, bf16[192,1024]{1,0:T(8,128)(2,1)S(1)}, u32[]{:S(2)}, u32[]{:S(2)}) %collective-permute-start.5) | collective-permute-done | bytes 393248 | tf_op jit(solution)/shard_map/ppermute | solution.py:137
  81.8 6.0 %collective-permute-done.6 = bf16[192,1024]{1,0:T(8,128)(2,1)S(1)} collective-permute-done((bf16[192,1024]{1,0:T(8,128)(2,1)S(1)}, bf16[192,1024]{1,0:T(8,128)(2,1)S(1)}, u32[]{:S(2)}, u32[]{:S(2)}) %collective-permute-start.6) | collective-permute-done | bytes 393248 | tf_op jit(solution)/shard_map/ppermute | solution.py:137
  87.8 2.4 %collective-permute-done.7.gate_second = bf16[64,4096]{1,0:T(8,128)(2,1)S(1)} collective-permute-done((bf16[64,4096]{1,0:T(8,128)(2,1)S(1)}, bf16[64,4096]{1,0:T(8,128)(2,1)S(1)}, u32[]{:S(2)}, u32[]{:S(2)}) %collective-permute-start.7) | collective-permute-done | bytes 524320 | tf_op jit(solution)/shard_map/ppermute | solution.py:141
  91.0 8.2 %collective-permute-done.8.gate_third = bf16[64,4096]{1,0:T(8,128)(2,1)S(1)} collective-permute-done((bf16[64,4096]{1,0:T(8,128)(2,1)S(1)}, bf16[64,4096]{1,0:T(8,128)(2,1)S(1)}, u32[]{:S(2)}, u32[]{:S(2)}) %collective-permute-start.8) | collective-permute-done | bytes 524320 | tf_op jit(solution)/shard_map/ppermute | solution.py:141
  102.4 1.8 collective-permute-start.10
  107.0 1.5 collective-permute-start.18
  108.6 12.5 %collective-permute-done.10.below_rows = bf16[384,1024]{1,0:T(8,128)(2,1)S(1)} collective-permute-done((bf16[384,1024]{1,0:T(8,128)(2,1)S(1)}, bf16[384,1024]{1,0:T(8,128)(2,1)S(1)}, u32[]{:S(2)}, u32[]{:S(2)}) %collective-permute-start.10) | collective-permute-done | bytes 786464 | tf_op jit(solution)/shard_map/ppermute | solution.py:137
  121.9 2.7 %collective-permute-start.13 = (bf16[192,1024]{1,0:T(8,128)(2,1)S(1)}, bf16[192,1024]{1,0:T(8,128)(2,1)S(1)}, u32[]{:S(2)}, u32[]{:S(2)}) collective-permute-start(bf16[192,1024]{1,0:T(8,128)(2,1)S(1)} %slice.27), channel_id=1, source_target_pairs={{0,3},{1,0},{2,1},{3,2},{4,7},{5,4},{6,5},{7,6},{8,11},{9,8},{10,9... | collective-permute-start | bytes 1179656 | tf_op jit(solution)/shard_map/ppermute | solution.py:137
  124.6 5.3 %expand_near.1 = (f32[384,384]{1,0:T(8,128)S(1)}, f32[384,384]{1,0:T(8,128)S(1)}) custom-call(s32[2]{0:T(128)S(1)} %pad_add_fusion.1.where, bf16[384,1024]{1,0:T(8,128)(2,1)S(1)} %bitcast.62, bf16[384,1024]{1,0:T(8,128)(2,1)S(1)} %collective-permute-done.10.below_rows, bf16[384,1024]{1,0:T(8,128)(2,1)S(1)} %collective-permute-done.12.above_rows, ...), custom_call_target="tpu_custom_call" | custom-call | flops 1811939328 | bytes 8257536 | tf_op jit(solution)/shard_map/expand_near/pallas_call | solution.py:275
  130.4 2.9 %expand_far.1.own = bf16[384,384]{1,0:T(8,128)(2,1)S(1)} custom-call(s32[2]{0:T(128)S(1)} %pad_add_fusion.1.where, bf16[192,1024]{1,0:T(8,128)(2,1)S(1)} %collective-permute-done.11.far_low, bf16[192,1024]{1,0:T(8,128)(2,1)S(1)} %collective-permute-done.13.far_high, f32[384,384]{1,0:T(8,128)S(1)} %get-tuple-element.37.gate_total, ...), custom_call_target="tpu_custom_call" | custom-call | flops 603979776 | bytes 3538944 | tf_op jit(solution)/shard_map/expand_far/pallas_call | solution.py:275
  134.3 2.4 %collective-permute-start.15 = (bf16[384,384]{1,0:T(8,128)(2,1)S(1)}, bf16[384,384]{1,0:T(8,128)(2,1)S(1)}, u32[]{:S(2)}, u32[]{:S(2)}) collective-permute-start(bf16[384,384]{1,0:T(8,128)(2,1)S(1)} %expand_far.1.own), channel_id=1, source_target_pairs={{0,3},{1,0},{2,1},{3,2},{4,7},{5,4},{6,5},{7,6},{8,11},{9,8},{10,9... | collective-permute-start | bytes 884744 | tf_op jit(solution)/shard_map/ppermute | solution.py:137
  136.6 5.8 %collective-permute-done.14.below = bf16[384,384]{1,0:T(8,128)(2,1)S(1)} collective-permute-done((bf16[384,384]{1,0:T(8,128)(2,1)S(1)}, bf16[384,384]{1,0:T(8,128)(2,1)S(1)}, u32[]{:S(2)}, u32[]{:S(2)}) %collective-permute-start.14) | collective-permute-done | bytes 294944 | tf_op jit(solution)/shard_map/ppermute | solution.py:137
  142.7 3.3 %collective-permute-start.17 = (bf16[192,384]{1,0:T(8,128)(2,1)S(1)}, bf16[192,384]{1,0:T(8,128)(2,1)S(1)}, u32[]{:S(2)}, u32[]{:S(2)}) collective-permute-start(bf16[192,384]{1,0:T(8,128)(2,1)S(1)} %slice.29), channel_id=1, source_target_pairs={{0,3},{1,0},{2,1},{3,2},{4,7},{5,4},{6,5},{7,6},{8,11},{9,8},{10,9... | collective-permute-start | bytes 442376 | tf_op jit(solution)/shard_map/ppermute | solution.py:137
  145.9 2.9 %collective-permute-done.16.far_low = bf16[192,384]{1,0:T(8,128)(2,1)S(1)} collective-permute-done((bf16[192,384]{1,0:T(8,128)(2,1)S(1)}, bf16[192,384]{1,0:T(8,128)(2,1)S(1)}, u32[]{:S(2)}, u32[]{:S(2)}) %collective-permute-start.16) | collective-permute-done | bytes 147488 | tf_op jit(solution)/shard_map/ppermute | solution.py:137
  148.9 1.8 contract.1
  152.0 34.7 %all_to_all.25 = bf16[32,24,512]{2,1,0:T(8,128)(2,1)S(1)} all-to-all(bf16[32,24,512]{2,1,0:T(8,128)(2,1)S(1)} %copy.79), channel_id=1, replica_groups=mesh['rep'=32,'exp'=8] {'rep'}, dimensions={0} | all-to-all | bytes 1572864 | tf_op jit(solution)/shard_map/all_to_all | solution.py:132
  188.0 5.4 %all-to-all-start.4 = ((bf16[8,12,512]{2,1,0:T(8,128)(2,1)}), bf16[8,12,512]{2,1,0:T(8,128)(2,1)S(1)}, u32[]{:S(2)}, u32[]{:S(2)}) async-start(bf16[8,12,512]{2,1,0:T(8,128)(2,1)} %reshape.96), calls=%async_computation.4 | async-start | bytes 262144 | tf_op jit(solution)/shard_map/all_to_all | solution.py:132
  193.5 6.5 %all-to-all-done.4 = bf16[8,12,512]{2,1,0:T(8,128)(2,1)S(1)} async-done(((bf16[8,12,512]{2,1,0:T(8,128)(2,1)}), bf16[8,12,512]{2,1,0:T(8,128)(2,1)S(1)}, u32[]{:S(2)}, u32[]{:S(2)}) %all-to-all-start.4) | async-done | bytes 98336 | tf_op jit(solution)/shard_map/all_to_all | solution.py:132
  (123 shorter events, 32.6 us)
Async XLA Ops:
  0.0 25.0 %copy-start.25 = (bf16[96,96]{1,0:T(8,128)(2,1)S(1)}, bf16[96,96]{1,0:T(8,128)(2,1)}, u32[]{:S(2)}) copy-start(bf16[96,96]{1,0:T(8,128)(2,1)} %constant.117) | copy-start | bytes 55300
  0.0 25.1 %copy-start.23 = (f32[96,24]{0,1:T(8,128)S(1)}, f32[96,24]{0,1:T(8,128)}, u32[]{:S(2)}) copy-start(f32[96,24]{0,1:T(8,128)} %constant.103) | copy-start | bytes 27652
  0.0 31.5 %copy-start.1 = (bf16[2,192,4096]{2,1,0:T(8,128)(2,1)S(1)}, bf16[2,192,4096]{2,1,0:T(8,128)(2,1)}, u32[]{:S(2)}) copy-start(bf16[2,192,4096]{2,1,0:T(8,128)(2,1)} %own_up.3) | copy-start | bytes 9437188
  2.2 22.9 %collective-permute-start.1 = (bf16[192,1024]{1,0:T(8,128)(2,1)}, bf16[192,1024]{1,0:T(8,128)(2,1)}, u32[]{:S(2)}, u32[]{:S(2)}) collective-permute-start(bf16[192,1024]{1,0:T(8,128)(2,1)} %get-tuple-element.56), channel_id=1, source_target_pairs={{0,1},{1,2},{2,3},{3,0},{4,5},{5,6},{6,7},{7,4},{8,9},{9,10},{10,1... | collective-permute-start | bytes 1179656 | tf_op jit(solution)/shard_map/ppermute | solution.py:137
  3.8 21.4 %collective-permute-start.2 = (bf16[192,1024]{1,0:T(8,128)(2,1)}, bf16[192,1024]{1,0:T(8,128)(2,1)}, u32[]{:S(2)}, u32[]{:S(2)}) collective-permute-start(bf16[192,1024]{1,0:T(8,128)(2,1)} %get-tuple-element.55), channel_id=1, source_target_pairs={{0,3},{1,0},{2,1},{3,2},{4,7},{5,4},{6,5},{7,6},{8,11},{9,8},{10,9... | collective-permute-start | bytes 1179656 | tf_op jit(solution)/shard_map/ppermute | solution.py:137
  7.3 17.8 %collective-permute-start = (bf16[64,4096]{1,0:T(8,128)(2,1)}, bf16[64,4096]{1,0:T(8,128)(2,1)}, u32[]{:S(2)}, u32[]{:S(2)}) collective-permute-start(bf16[64,4096]{1,0:T(8,128)(2,1)} %dynamic-slice_bitcast_fusion.3), channel_id=1, source_target_pairs={{0,4},{1,5},{2,6},{3,7},{4,0},{5,1},{6,2},{7,3},{8,12},{9,13},{10,... | collective-permute-start | bytes 1572872 | tf_op jit(solution)/shard_map/ppermute | solution.py:141
  9.9 14.0 %all-to-all-start = ((s32[8,6,16]{2,1,0:T(8,128)}), s32[8,6,16]{2,1,0:T(8,128)S(1)}, u32[]{:S(2)}, u32[]{:S(2)}) async-start(s32[8,6,16]{2,1,0:T(8,128)} %broadcast_in_dim.15), calls=%async_computation | async-start | bytes 65536 | tf_op jit(solution)/shard_map/all_to_all | solution.py:132
  25.8 12.7 %all-to-all-start.1 = ((bf16[8,12,512]{2,1,0:T(8,128)(2,1)}), bf16[8,12,512]{2,1,0:T(8,128)(2,1)S(1)}, u32[]{:S(2)}, u32[]{:S(2)}) async-start(bf16[8,12,512]{2,1,0:T(8,128)(2,1)} %bitcast.69), calls=%async_computation.1 | async-start | bytes 262144 | tf_op jit(solution)/shard_map/all_to_all | solution.py:132
  32.8 67.2 %collective-permute-start.9 = (bf16[192,4096]{1,0:T(8,128)(2,1)}, bf16[192,4096]{1,0:T(8,128)(2,1)}, u32[]{:S(2)}, u32[]{:S(2)}) collective-permute-start(bf16[192,4096]{1,0:T(8,128)(2,1)} %dynamic-slice_bitcast_fusion), channel_id=1, source_target_pairs={{0,4},{1,5},{2,6},{3,7},{4,0},{5,1},{6,2},{7,3},{8,12},{9,13},{10,... | collective-permute-start | bytes 4718600 | tf_op jit(solution)/shard_map/ppermute | solution.py:141
  39.8 60.2 %all-to-all-start.2 = ((bf16[32,24,512]{2,1,0:T(8,128)(2,1)}), bf16[32,24,512]{2,1,0:T(8,128)(2,1)}, u32[]{:S(2)}, u32[]{:S(2)}) async-start(bf16[32,24,512]{2,1,0:T(8,128)(2,1)} %bitcast.64), calls=%async_computation.2 | async-start | bytes 1572864 | tf_op jit(solution)/shard_map/all_to_all | solution.py:132
  54.4 12.4 %collective-permute-start.3 = (bf16[192,1024]{1,0:T(8,128)(2,1)S(1)}, bf16[192,1024]{1,0:T(8,128)(2,1)S(1)}, u32[]{:S(2)}, u32[]{:S(2)}) collective-permute-start(bf16[192,1024]{1,0:T(8,128)(2,1)S(1)} %get-tuple-element.52), channel_id=1, source_target_pairs={{0,1},{1,2},{2,3},{3,0},{4,5},{5,6},{6,7},{7,4},{8,9},{9,10},{10,1... | collective-permute-start | bytes 1179656 | tf_op jit(solution)/shard_map/ppermute | solution.py:137
  54.9 12.6 %collective-permute-start.4 = (bf16[192,1024]{1,0:T(8,128)(2,1)S(1)}, bf16[192,1024]{1,0:T(8,128)(2,1)S(1)}, u32[]{:S(2)}, u32[]{:S(2)}) collective-permute-start(bf16[192,1024]{1,0:T(8,128)(2,1)S(1)} %get-tuple-element.51), channel_id=1, source_target_pairs={{0,3},{1,0},{2,1},{3,2},{4,7},{5,4},{6,5},{7,6},{8,11},{9,8},{10,9... | collective-permute-start | bytes 1179656 | tf_op jit(solution)/shard_map/ppermute | solution.py:137
  57.7 32.5 %collective-permute-start.7 = (bf16[64,4096]{1,0:T(8,128)(2,1)S(1)}, bf16[64,4096]{1,0:T(8,128)(2,1)S(1)}, u32[]{:S(2)}, u32[]{:S(2)}) collective-permute-start(bf16[64,4096]{1,0:T(8,128)(2,1)S(1)} %get-tuple-element.54), channel_id=1, source_target_pairs={{0,4},{1,5},{2,6},{3,7},{4,0},{5,1},{6,2},{7,3},{8,12},{9,13},{10,... | collective-permute-start | bytes 1572872 | tf_op jit(solution)/shard_map/ppermute | solution.py:141
  58.3 40.9 %collective-permute-start.8 = (bf16[64,4096]{1,0:T(8,128)(2,1)S(1)}, bf16[64,4096]{1,0:T(8,128)(2,1)S(1)}, u32[]{:S(2)}, u32[]{:S(2)}) collective-permute-start(bf16[64,4096]{1,0:T(8,128)(2,1)S(1)} %get-tuple-element.53), channel_id=1, source_target_pairs={{0,4},{1,5},{2,6},{3,7},{4,0},{5,1},{6,2},{7,3},{8,12},{9,13},{10,... | collective-permute-start | bytes 1572872 | tf_op jit(solution)/shard_map/ppermute | solution.py:141
  67.5 13.6 %collective-permute-start.5 = (bf16[192,1024]{1,0:T(8,128)(2,1)S(1)}, bf16[192,1024]{1,0:T(8,128)(2,1)S(1)}, u32[]{:S(2)}, u32[]{:S(2)}) collective-permute-start(bf16[192,1024]{1,0:T(8,128)(2,1)S(1)} %get-tuple-element.50), channel_id=1, source_target_pairs={{0,2},{1,3},{2,0},{3,1},{4,6},{5,7},{6,4},{7,5},{8,10},{9,11},{10,... | collective-permute-start | bytes 1179656 | tf_op jit(solution)/shard_map/ppermute | solution.py:137
  68.3 19.4 %collective-permute-start.6 = (bf16[192,1024]{1,0:T(8,128)(2,1)S(1)}, bf16[192,1024]{1,0:T(8,128)(2,1)S(1)}, u32[]{:S(2)}, u32[]{:S(2)}) collective-permute-start(bf16[192,1024]{1,0:T(8,128)(2,1)S(1)} %get-tuple-element.49), channel_id=1, source_target_pairs={{0,2},{1,3},{2,0},{3,1},{4,6},{5,7},{6,4},{7,5},{8,10},{9,11},{10,... | collective-permute-start | bytes 1179656 | tf_op jit(solution)/shard_map/ppermute | solution.py:137
  102.3 22.3 %copy-start.2 = (bf16[2,192,4096]{2,1,0:T(8,128)(2,1)S(1)}, bf16[2,192,4096]{2,1,0:T(8,128)(2,1)}, u32[]{:S(2)}) copy-start(bf16[2,192,4096]{2,1,0:T(8,128)(2,1)} %own_up.3) | copy-start | bytes 9437188
  102.3 22.3 %copy-start.4 = (bf16[64,4096]{1,0:T(8,128)(2,1)S(1)}, bf16[64,4096]{1,0:T(8,128)(2,1)}, u32[]{:S(2)}) copy-start(bf16[64,4096]{1,0:T(8,128)(2,1)} %copy-done.3) | copy-start | bytes 1572868
  102.3 22.3 %copy-start.6 = (bf16[64,4096]{1,0:T(8,128)(2,1)S(1)}, bf16[64,4096]{1,0:T(8,128)(2,1)}, u32[]{:S(2)}) copy-start(bf16[64,4096]{1,0:T(8,128)(2,1)} %copy-done.5) | copy-start | bytes 1572868
  102.4 18.6 %collective-permute-start.10 = (bf16[384,1024]{1,0:T(8,128)(2,1)S(1)}, bf16[384,1024]{1,0:T(8,128)(2,1)S(1)}, u32[]{:S(2)}, u32[]{:S(2)}) collective-permute-start(bf16[384,1024]{1,0:T(8,128)(2,1)S(1)} %bitcast.60), channel_id=1, source_target_pairs={{0,1},{1,2},{2,3},{3,0},{4,5},{5,6},{6,7},{7,4},{8,9},{9,10},{10,1... | collective-permute-start | bytes 2359304 | tf_op jit(solution)/shard_map/ppermute | solution.py:137
  104.2 17.6 %collective-permute-start.12 = (bf16[384,1024]{1,0:T(8,128)(2,1)S(1)}, bf16[384,1024]{1,0:T(8,128)(2,1)S(1)}, u32[]{:S(2)}, u32[]{:S(2)}) collective-permute-start(bf16[384,1024]{1,0:T(8,128)(2,1)S(1)} %bitcast.61), channel_id=1, source_target_pairs={{0,3},{1,0},{2,1},{3,2},{4,7},{5,4},{6,5},{7,6},{8,11},{9,8},{10,9... | collective-permute-start | bytes 2359304 | tf_op jit(solution)/shard_map/ppermute | solution.py:137
  107.0 38.9 %collective-permute-start.18 = (bf16[768,1024]{1,0:T(8,128)(2,1)S(1)}, bf16[768,1024]{1,0:T(8,128)(2,1)S(1)}, u32[]{:S(2)}, u32[]{:S(2)}) collective-permute-start(bf16[768,1024]{1,0:T(8,128)(2,1)S(1)} %pad_maximum_fusion), channel_id=1, source_target_pairs={{0,4},{1,5},{2,6},{3,7},{4,0},{5,1},{6,2},{7,3},{8,12},{9,13},{10,... | collective-permute-start | bytes 4718600 | tf_op jit(solution)/shard_map/ppermute | solution.py:141
  121.1 9.3 %collective-permute-start.11 = (bf16[192,1024]{1,0:T(8,128)(2,1)S(1)}, bf16[192,1024]{1,0:T(8,128)(2,1)S(1)}, u32[]{:S(2)}, u32[]{:S(2)}) collective-permute-start(bf16[192,1024]{1,0:T(8,128)(2,1)S(1)} %slice.26), channel_id=1, source_target_pairs={{0,1},{1,2},{2,3},{3,0},{4,5},{5,6},{6,7},{7,4},{8,9},{9,10},{10,1... | collective-permute-start | bytes 1179656 | tf_op jit(solution)/shard_map/ppermute | solution.py:137
  121.9 8.5 %collective-permute-start.13 = (bf16[192,1024]{1,0:T(8,128)(2,1)S(1)}, bf16[192,1024]{1,0:T(8,128)(2,1)S(1)}, u32[]{:S(2)}, u32[]{:S(2)}) collective-permute-start(bf16[192,1024]{1,0:T(8,128)(2,1)S(1)} %slice.27), channel_id=1, source_target_pairs={{0,3},{1,0},{2,1},{3,2},{4,7},{5,4},{6,5},{7,6},{8,11},{9,8},{10,9... | collective-permute-start | bytes 1179656 | tf_op jit(solution)/shard_map/ppermute | solution.py:137
  133.3 9.1 %collective-permute-start.14 = (bf16[384,384]{1,0:T(8,128)(2,1)S(1)}, bf16[384,384]{1,0:T(8,128)(2,1)S(1)}, u32[]{:S(2)}, u32[]{:S(2)}) collective-permute-start(bf16[384,384]{1,0:T(8,128)(2,1)S(1)} %expand_far.1.own), channel_id=1, source_target_pairs={{0,1},{1,2},{2,3},{3,0},{4,5},{5,6},{6,7},{7,4},{8,9},{9,10},{10,1... | collective-permute-start | bytes 884744 | tf_op jit(solution)/shard_map/ppermute | solution.py:137
  134.3 8.4 %collective-permute-start.15 = (bf16[384,384]{1,0:T(8,128)(2,1)S(1)}, bf16[384,384]{1,0:T(8,128)(2,1)S(1)}, u32[]{:S(2)}, u32[]{:S(2)}) collective-permute-start(bf16[384,384]{1,0:T(8,128)(2,1)S(1)} %expand_far.1.own), channel_id=1, source_target_pairs={{0,3},{1,0},{2,1},{3,2},{4,7},{5,4},{6,5},{7,6},{8,11},{9,8},{10,9... | collective-permute-start | bytes 884744 | tf_op jit(solution)/shard_map/ppermute | solution.py:137
  142.4 6.4 %collective-permute-start.16 = (bf16[192,384]{1,0:T(8,128)(2,1)S(1)}, bf16[192,384]{1,0:T(8,128)(2,1)S(1)}, u32[]{:S(2)}, u32[]{:S(2)}) collective-permute-start(bf16[192,384]{1,0:T(8,128)(2,1)S(1)} %slice.28), channel_id=1, source_target_pairs={{0,1},{1,2},{2,3},{3,0},{4,5},{5,6},{6,7},{7,4},{8,9},{9,10},{10,1... | collective-permute-start | bytes 442376 | tf_op jit(solution)/shard_map/ppermute | solution.py:137
  142.7 6.2 %collective-permute-start.17 = (bf16[192,384]{1,0:T(8,128)(2,1)S(1)}, bf16[192,384]{1,0:T(8,128)(2,1)S(1)}, u32[]{:S(2)}, u32[]{:S(2)}) collective-permute-start(bf16[192,384]{1,0:T(8,128)(2,1)S(1)} %slice.29), channel_id=1, source_target_pairs={{0,3},{1,0},{2,1},{3,2},{4,7},{5,4},{6,5},{7,6},{8,11},{9,8},{10,9... | collective-permute-start | bytes 442376 | tf_op jit(solution)/shard_map/ppermute | solution.py:137
  150.7 36.0 %copy-start.22 = (f32[96,32]{0,1:T(8,128)S(1)}, f32[96,32]{0,1:T(8,128)}, u32[]{:S(2)}) copy-start(f32[96,32]{0,1:T(8,128)} %get-tuple-element.45) | copy-start | bytes 36868
  150.7 36.0 %copy-start.24 = (f32[96,24]{0,1:T(8,128)S(1)}, f32[96,24]{0,1:T(8,128)}, u32[]{:S(2)}) copy-start(f32[96,24]{0,1:T(8,128)} %constant.103) | copy-start | bytes 27652
  151.3 42.1 %copy-start.16 = (f32[6,32,128]{2,1,0:T(8,128)S(1)}, f32[6,32,128]{2,1,0:T(8,128)}, u32[]{:S(2)}) copy-start(f32[6,32,128]{2,1,0:T(8,128)} %copy-done.15) | copy-start | bytes 294916
  188.0 12.0 %all-to-all-start.4 = ((bf16[8,12,512]{2,1,0:T(8,128)(2,1)}), bf16[8,12,512]{2,1,0:T(8,128)(2,1)S(1)}, u32[]{:S(2)}, u32[]{:S(2)}) async-start(bf16[8,12,512]{2,1,0:T(8,128)(2,1)} %reshape.96), calls=%async_computation.4 | async-start | bytes 262144 | tf_op jit(solution)/shard_map/all_to_all | solution.py:132
  (17 other events, 104.6 us)

commit v10 on v8

--- a/solution.py
+++ b/solution.py
@@ -355,7 +355,7 @@
     routing = jnp.broadcast_to(routing[:, None], (N_EXP, 2, LOCAL, 2 * TOPK))
     routing = routing.reshape(KEYS, 2 * TOPK)
 
-    cuts = (0, UNITS // 3, 2 * UNITS // 3, UNITS)
+    cuts = (0, 5 * UNITS // 12, 3 * UNITS // 4, UNITS)
 
     def gate_part(weight, part):
         size = (1, cuts[part + 1] - cuts[part], D)

time: 199 us -> 195 us (0.980)
  local copies, waits for them, and re-layouts: 28.3 us -> 24.7 us
    ppermute x5, waiting for transfers between devices: 12.6 us -> 17.5 us  [across(): return lax.ppermute(array, 'exp', [(e, e ^ 4) for e in range(N_EXP)])]
    ppermute x14, waiting for transfers between devices: 43.8 us -> 39.2 us  [shift(): return lax.ppermute(array, 'exp', pairs)]
    unnamed x48 -> x50, local copies, waits for them, and re-layouts: 9.2 us -> 7.05 us
  transfers between devices with their start and end apart: 23 -> 23, of which waited for: 10 -> 11; matrix products, arithmetic and copies ran while one was open for 11% -> 10% of each run, Pallas kernels for 6% -> 6%
where the time goes in v10:
time: 195 us; the launch traced here: 194 us
  waiting for transfers between devices  63.2 us (32%)
  starting transfers between devices  53.3 us (27%)
  blocking collectives  32.7 us (17%)
  local copies, waits for them, and re-layouts  24.7 us (13%)
  Pallas kernels  12.9 us (7%)
  other arithmetic  3.86 us (2%)
  matrix products  2.76 us (1%)
    ppermute x14, waiting for transfers between devices, shift(): return lax.ppermute(array, 'exp', pairs)  39.2 us
    all_to_all x1, blocking collectives, exchange(): return lax.all_to_all(array, axis, split_axis=0, concat_axis=0, tiled=True)  32.7 us
    all_to_all x4, starting transfers between devices, exchange(): return lax.all_to_all(array, axis, split_axis=0, concat_axis=0, tiled=True)  25.3 us
    ppermute x14, starting transfers between devices, shift(): return lax.ppermute(array, 'exp', pairs)  21.1 us
    ppermute x5, waiting for transfers between devices, across(): return lax.ppermute(array, 'exp', [(e, e ^ 4) for e in range(N_EXP)])  17.5 us
    pallas_call x2, Pallas kernels, call(): pl.pallas_call(kernel, out_shape=out_shape, grid_spec=pltpu.PrefetchScala...  8.25 us
    unnamed x50, local copies, waits for them, and re-layouts  7.05 us
    ppermute x5, starting transfers between devices, across(): return lax.ppermute(array, 'exp', [(e, e ^ 4) for e in range(N_EXP)])  6.82 us
  transfers between devices with their start and end apart: 23, of which 11 were waited for; matrix products, arithmetic and copies ran while one was open for 10% of the time, Pallas kernels for 6%

profile of v10, /device:TPU:4, one launch (start us, length us, event | category | flops | bytes accessed | tf_op | source)
XLA Modules:
  0.0 193.9 jit_solution(14969159639730683615)
XLA Ops:
  1.5 5.1 %all-to-all-start = ((s32[8,6,16]{2,1,0:T(8,128)}), s32[8,6,16]{2,1,0:T(8,128)S(1)}, u32[]{:S(2)}, u32[]{:S(2)}) async-start(s32[8,6,16]{2,1,0:T(8,128)} %broadcast_in_dim.15), calls=%async_computation | async-start | bytes 65536 | tf_op jit(solution)/shard_map/all_to_all | solution.py:132
  6.6 2.1 %dynamic-slice_bitcast_fusion.1 = bf16[80,4096]{1,0:T(8,128)(2,1)} fusion(bf16[2,192,4096]{2,1,0:T(8,128)(2,1)} %own_gate.3, s32[]{:T(128)S(6)} %select_n.75), kind=kLoop, calls=%fused_computation.6 | loop fusion | bytes 1310724 | tf_op jit(solution)/shard_map/squeeze | solution.py:362
  8.7 2.0 %collective-permute-start = (bf16[80,4096]{1,0:T(8,128)(2,1)}, bf16[80,4096]{1,0:T(8,128)(2,1)}, u32[]{:S(2)}, u32[]{:S(2)}) collective-permute-start(bf16[80,4096]{1,0:T(8,128)(2,1)} %dynamic-slice_bitcast_fusion.1), channel_id=1, source_target_pairs={{0,4},{1,5},{2,6},{3,7},{4,0},{5,1},{6,2},{7,3},{8,12},{9,13},{10,... | collective-permute-start | bytes 1966088 | tf_op jit(solution)/shard_map/ppermute | solution.py:141
  10.7 2.1 %dynamic-slice_bitcast_fusion.10 = (bf16[192,1024]{1,0:T(8,128)(2,1)}, bf16[192,1024]{1,0:T(8,128)(2,1)}) fusion(bf16[2,192,4096]{2,1,0:T(8,128)(2,1)} %param.27, s32[]{:T(128)S(6)} %select_n.75, s32[]{:T(128)S(6)} %select_n.79, s32[]{:T(128)S(6)} %select_n.77), kind=kLoop, calls=%fused_computation.18 | loop fusion | bytes 1572876 | tf_op jit(solution)/shard_map/squeeze | solution.py:366
  12.8 2.7 %collective-permute-start.2 = (bf16[192,1024]{1,0:T(8,128)(2,1)}, bf16[192,1024]{1,0:T(8,128)(2,1)}, u32[]{:S(2)}, u32[]{:S(2)}) collective-permute-start(bf16[192,1024]{1,0:T(8,128)(2,1)} %get-tuple-element.54), channel_id=1, source_target_pairs={{0,3},{1,0},{2,1},{3,2},{4,7},{5,4},{6,5},{7,6},{8,11},{9,8},{10,9... | collective-permute-start | bytes 1179656 | tf_op jit(solution)/shard_map/ppermute | solution.py:137
  19.5 2.8 %attend.1 = (f32[6,32,128]{2,1,0:T(8,128)S(1)}, bf16[6,32,128]{2,1,0:T(8,128)(2,1)S(1)}) custom-call(s32[2]{0:T(128)S(1)} %copy-done.14, bf16[6,32,128]{2,1,0:T(8,128)(2,1)S(1)} %reshape.83.query, bf16[2,1024,256]{2,1,0:T(8,128)(2,1)S(1)} %copy-done.3, bf16[2,1024,256]{2,1,0:T(8,128)(2,1)S(1)} %copy-done.4, bf16[2,8,256]{2,1,0:T(8,128)(2,1)S(1)} %pad.7.fresh_keys, ...), custom_call_target="tpu_custom_call" | custom-call | flops 100663296 | bytes 2342912 | tf_op jit(solution)/shard_map/attend/pallas_call | solution.py:90
  24.2 2.6 %collective-permute-done.1 = bf16[192,1024]{1,0:T(8,128)(2,1)} collective-permute-done((bf16[192,1024]{1,0:T(8,128)(2,1)}, bf16[192,1024]{1,0:T(8,128)(2,1)}, u32[]{:S(2)}, u32[]{:S(2)}) %collective-permute-start.1) | collective-permute-done | bytes 393248 | tf_op jit(solution)/shard_map/ppermute | solution.py:137
  27.5 3.9 %all-to-all-start.1 = ((bf16[8,12,512]{2,1,0:T(8,128)(2,1)}), bf16[8,12,512]{2,1,0:T(8,128)(2,1)S(1)}, u32[]{:S(2)}, u32[]{:S(2)}) async-start(bf16[8,12,512]{2,1,0:T(8,128)(2,1)} %bitcast.8), calls=%async_computation.1 | async-start | bytes 262144 | tf_op jit(solution)/shard_map/all_to_all | solution.py:132
  32.2 2.0 %collective-permute-start.3 = (bf16[64,4096]{1,0:T(8,128)(2,1)}, bf16[64,4096]{1,0:T(8,128)(2,1)}, u32[]{:S(2)}, u32[]{:S(2)}) collective-permute-start(bf16[64,4096]{1,0:T(8,128)(2,1)} %dynamic-slice_bitcast_fusion.2), channel_id=1, source_target_pairs={{0,4},{1,5},{2,6},{3,7},{4,0},{5,1},{6,2},{7,3},{8,12},{9,13},{10,... | collective-permute-start | bytes 1572872 | tf_op jit(solution)/shard_map/ppermute | solution.py:141
  34.2 1.8 dynamic-slice_bitcast_fusion.9
  36.0 3.0 %collective-permute-start.4 = (bf16[192,1024]{1,0:T(8,128)(2,1)}, bf16[192,1024]{1,0:T(8,128)(2,1)}, u32[]{:S(2)}, u32[]{:S(2)}) collective-permute-start(bf16[192,1024]{1,0:T(8,128)(2,1)} %dynamic-slice_bitcast_fusion.9), channel_id=1, source_target_pairs={{0,2},{1,3},{2,0},{3,1},{4,6},{5,7},{6,4},{7,5},{8,10},{9,11},{10,... | collective-permute-start | bytes 1179656 | tf_op jit(solution)/shard_map/ppermute | solution.py:137
  39.7 2.1 %convolution_convert_fusion = bf16[768,512]{1,0:T(8,128)(2,1)} fusion(bf16[96,768]{0,1:T(8,128)(2,1)S(1)} %bitcast.68, bf16[96,512]{1,0:T(8,128)(2,1)} %reshape.90), kind=kOutput, calls=%fused_computation.2 | convolution fusion | flops 75890688 | bytes 1032192 | tf_op jit(solution)/shard_map/dot_general | solution.py:383
  41.8 4.9 %collective-permute-done.4 = bf16[192,1024]{1,0:T(8,128)(2,1)} collective-permute-done((bf16[192,1024]{1,0:T(8,128)(2,1)}, bf16[192,1024]{1,0:T(8,128)(2,1)}, u32[]{:S(2)}, u32[]{:S(2)}) %collective-permute-start.4) | collective-permute-done | bytes 393248 | tf_op jit(solution)/shard_map/ppermute | solution.py:137
  46.7 11.6 %all-to-all-start.2 = ((bf16[32,24,512]{2,1,0:T(8,128)(2,1)}), bf16[32,24,512]{2,1,0:T(8,128)(2,1)}, u32[]{:S(2)}, u32[]{:S(2)}) async-start(bf16[32,24,512]{2,1,0:T(8,128)(2,1)} %bitcast.64), calls=%async_computation.2 | async-start | bytes 1572864 | tf_op jit(solution)/shard_map/all_to_all | solution.py:132
  59.1 2.9 %dynamic-slice_bitcast_fusion = bf16[192,4096]{1,0:T(8,128)(2,1)} fusion(bf16[2,192,4096]{2,1,0:T(8,128)(2,1)} %own_up.3, s32[]{:T(128)S(6)} %select_n.75), kind=kLoop, calls=%fused_computation.1 | loop fusion | bytes 3145732 | tf_op jit(solution)/shard_map/jit(dynamic_index_in_dim)/squeeze | solution.py:395
  64.3 2.6 %collective-permute-start.7 = (bf16[192,1024]{1,0:T(8,128)(2,1)S(1)}, bf16[192,1024]{1,0:T(8,128)(2,1)S(1)}, u32[]{:S(2)}, u32[]{:S(2)}) collective-permute-start(bf16[192,1024]{1,0:T(8,128)(2,1)S(1)} %get-tuple-element.51), channel_id=1, source_target_pairs={{0,2},{1,3},{2,0},{3,1},{4,6},{5,7},{6,4},{7,5},{8,10},{9,11},{10,... | collective-permute-start | bytes 1179656 | tf_op jit(solution)/shard_map/ppermute | solution.py:137
  69.0 8.6 %collective-permute-done.8.gate_third = bf16[48,4096]{1,0:T(8,128)(2,1)S(1)} collective-permute-done((bf16[48,4096]{1,0:T(8,128)(2,1)S(1)}, bf16[48,4096]{1,0:T(8,128)(2,1)S(1)}, u32[]{:S(2)}, u32[]{:S(2)}) %collective-permute-start.8) | collective-permute-done | bytes 393248 | tf_op jit(solution)/shard_map/ppermute | solution.py:141
  78.7 5.9 %collective-permute-done.6.w_above = bf16[192,1024]{1,0:T(8,128)(2,1)S(1)} collective-permute-done((bf16[192,1024]{1,0:T(8,128)(2,1)S(1)}, bf16[192,1024]{1,0:T(8,128)(2,1)S(1)}, u32[]{:S(2)}, u32[]{:S(2)}) %collective-permute-start.6) | collective-permute-done | bytes 393248 | tf_op jit(solution)/shard_map/ppermute | solution.py:137
  88.5 2.7 %collective-permute-start.11 = (bf16[384,1024]{1,0:T(8,128)(2,1)S(1)}, bf16[384,1024]{1,0:T(8,128)(2,1)S(1)}, u32[]{:S(2)}, u32[]{:S(2)}) collective-permute-start(bf16[384,1024]{1,0:T(8,128)(2,1)S(1)} %bitcast.60), channel_id=1, source_target_pairs={{0,3},{1,0},{2,1},{3,2},{4,7},{5,4},{6,5},{7,6},{8,11},{9,8},{10,9... | collective-permute-start | bytes 2359304 | tf_op jit(solution)/shard_map/ppermute | solution.py:137
  93.5 14.8 %collective-permute-done.11.above_rows = bf16[384,1024]{1,0:T(8,128)(2,1)S(1)} collective-permute-done((bf16[384,1024]{1,0:T(8,128)(2,1)S(1)}, bf16[384,1024]{1,0:T(8,128)(2,1)S(1)}, u32[]{:S(2)}, u32[]{:S(2)}) %collective-permute-start.11) | collective-permute-done | bytes 786464 | tf_op jit(solution)/shard_map/ppermute | solution.py:137
  108.2 3.8 %collective-permute-start.12 = (bf16[192,1024]{1,0:T(8,128)(2,1)S(1)}, bf16[192,1024]{1,0:T(8,128)(2,1)S(1)}, u32[]{:S(2)}, u32[]{:S(2)}) collective-permute-start(bf16[192,1024]{1,0:T(8,128)(2,1)S(1)} %slice.27), channel_id=1, source_target_pairs={{0,3},{1,0},{2,1},{3,2},{4,7},{5,4},{6,5},{7,6},{8,11},{9,8},{10,9... | collective-permute-start | bytes 1179656 | tf_op jit(solution)/shard_map/ppermute | solution.py:137
  112.2 5.3 %expand_near.1 = (f32[384,384]{1,0:T(8,128)S(1)}, f32[384,384]{1,0:T(8,128)S(1)}) custom-call(s32[2]{0:T(128)S(1)} %pad_add_fusion.1.where, bf16[384,1024]{1,0:T(8,128)(2,1)S(1)} %bitcast.62, bf16[384,1024]{1,0:T(8,128)(2,1)S(1)} %collective-permute-done.9.below_rows, bf16[384,1024]{1,0:T(8,128)(2,1)S(1)} %collective-permute-done.11.above_rows, ...), custom_call_target="tpu_custom_call" | custom-call | flops 1811939328 | bytes 8257536 | tf_op jit(solution)/shard_map/expand_near/pallas_call | solution.py:275
  117.6 2.2 %collective-permute-done.12.far_high = bf16[192,1024]{1,0:T(8,128)(2,1)S(1)} collective-permute-done((bf16[192,1024]{1,0:T(8,128)(2,1)S(1)}, bf16[192,1024]{1,0:T(8,128)(2,1)S(1)}, u32[]{:S(2)}, u32[]{:S(2)}) %collective-permute-start.12) | collective-permute-done | bytes 393248 | tf_op jit(solution)/shard_map/ppermute | solution.py:137
  119.7 3.5 %collective-permute-done.10.far_low = bf16[192,1024]{1,0:T(8,128)(2,1)S(1)} collective-permute-done((bf16[192,1024]{1,0:T(8,128)(2,1)S(1)}, bf16[192,1024]{1,0:T(8,128)(2,1)S(1)}, u32[]{:S(2)}, u32[]{:S(2)}) %collective-permute-start.10) | collective-permute-done | bytes 393248 | tf_op jit(solution)/shard_map/ppermute | solution.py:137
  123.3 2.9 %expand_far.1.own = bf16[384,384]{1,0:T(8,128)(2,1)S(1)} custom-call(s32[2]{0:T(128)S(1)} %pad_add_fusion.1.where, bf16[192,1024]{1,0:T(8,128)(2,1)S(1)} %collective-permute-done.10.far_low, bf16[192,1024]{1,0:T(8,128)(2,1)S(1)} %collective-permute-done.12.far_high, f32[384,384]{1,0:T(8,128)S(1)} %get-tuple-element.39.gate_total, ...), custom_call_target="tpu_custom_call" | custom-call | flops 603979776 | bytes 3538944 | tf_op jit(solution)/shard_map/expand_far/pallas_call | solution.py:275
  126.4 1.8 collective-permute-start.14
  128.3 5.1 %collective-permute-done.15.above = bf16[384,384]{1,0:T(8,128)(2,1)S(1)} collective-permute-done((bf16[384,384]{1,0:T(8,128)(2,1)S(1)}, bf16[384,384]{1,0:T(8,128)(2,1)S(1)}, u32[]{:S(2)}, u32[]{:S(2)}) %collective-permute-start.15) | collective-permute-done | bytes 294944 | tf_op jit(solution)/shard_map/ppermute | solution.py:137
  135.6 8.9 %collective-permute-done.18.lent = bf16[768,1024]{1,0:T(8,128)(2,1)S(1)} collective-permute-done((bf16[768,1024]{1,0:T(8,128)(2,1)S(1)}, bf16[768,1024]{1,0:T(8,128)(2,1)S(1)}, u32[]{:S(2)}, u32[]{:S(2)}) %collective-permute-start.18) | collective-permute-done | bytes 1572896 | tf_op jit(solution)/shard_map/ppermute | solution.py:141
  144.5 1.8 contract.1
  147.6 32.7 %all_to_all.25 = bf16[32,24,512]{2,1,0:T(8,128)(2,1)S(1)} all-to-all(bf16[32,24,512]{2,1,0:T(8,128)(2,1)S(1)} %copy.79), channel_id=1, replica_groups=mesh['rep'=32,'exp'=8] {'rep'}, dimensions={0} | all-to-all | bytes 1572864 | tf_op jit(solution)/shard_map/all_to_all | solution.py:132
  181.5 4.7 %all-to-all-start.4 = ((bf16[8,12,512]{2,1,0:T(8,128)(2,1)}), bf16[8,12,512]{2,1,0:T(8,128)(2,1)S(1)}, u32[]{:S(2)}, u32[]{:S(2)}) async-start(bf16[8,12,512]{2,1,0:T(8,128)(2,1)} %reshape.96), calls=%async_computation.4 | async-start | bytes 262144 | tf_op jit(solution)/shard_map/all_to_all | solution.py:132
  186.3 6.5 %all-to-all-done.4 = bf16[8,12,512]{2,1,0:T(8,128)(2,1)S(1)} async-done(((bf16[8,12,512]{2,1,0:T(8,128)(2,1)}), bf16[8,12,512]{2,1,0:T(8,128)(2,1)S(1)}, u32[]{:S(2)}, u32[]{:S(2)}) %all-to-all-start.4) | async-done | bytes 98336 | tf_op jit(solution)/shard_map/all_to_all | solution.py:132
  (119 shorter events, 28.1 us)
Async XLA Ops:
  1.5 21.6 %all-to-all-start = ((s32[8,6,16]{2,1,0:T(8,128)}), s32[8,6,16]{2,1,0:T(8,128)S(1)}, u32[]{:S(2)}, u32[]{:S(2)}) async-start(s32[8,6,16]{2,1,0:T(8,128)} %broadcast_in_dim.15), calls=%async_computation | async-start | bytes 65536 | tf_op jit(solution)/shard_map/all_to_all | solution.py:132
  6.6 24.7 %copy-start = (bf16[2,192,4096]{2,1,0:T(8,128)(2,1)S(1)}, bf16[2,192,4096]{2,1,0:T(8,128)(2,1)}, u32[]{:S(2)}) copy-start(bf16[2,192,4096]{2,1,0:T(8,128)(2,1)} %own_gate.3) | copy-start | bytes 9437188
  8.7 18.0 %collective-permute-start = (bf16[80,4096]{1,0:T(8,128)(2,1)}, bf16[80,4096]{1,0:T(8,128)(2,1)}, u32[]{:S(2)}, u32[]{:S(2)}) collective-permute-start(bf16[80,4096]{1,0:T(8,128)(2,1)} %dynamic-slice_bitcast_fusion.1), channel_id=1, source_target_pairs={{0,4},{1,5},{2,6},{3,7},{4,0},{5,1},{6,2},{7,3},{8,12},{9,13},{10,... | collective-permute-start | bytes 1966088 | tf_op jit(solution)/shard_map/ppermute | solution.py:141
  12.8 26.1 %copy-start.18 = (f32[96,24]{0,1:T(8,128)S(1)}, f32[96,24]{0,1:T(8,128)}, u32[]{:S(2)}) copy-start(f32[96,24]{0,1:T(8,128)} %constant.103) | copy-start | bytes 27652
  12.8 11.4 %collective-permute-start.2 = (bf16[192,1024]{1,0:T(8,128)(2,1)}, bf16[192,1024]{1,0:T(8,128)(2,1)}, u32[]{:S(2)}, u32[]{:S(2)}) collective-permute-start(bf16[192,1024]{1,0:T(8,128)(2,1)} %get-tuple-element.54), channel_id=1, source_target_pairs={{0,3},{1,0},{2,1},{3,2},{4,7},{5,4},{6,5},{7,6},{8,11},{9,8},{10,9... | collective-permute-start | bytes 1179656 | tf_op jit(solution)/shard_map/ppermute | solution.py:137
  15.5 11.3 %collective-permute-start.1 = (bf16[192,1024]{1,0:T(8,128)(2,1)}, bf16[192,1024]{1,0:T(8,128)(2,1)}, u32[]{:S(2)}, u32[]{:S(2)}) collective-permute-start(bf16[192,1024]{1,0:T(8,128)(2,1)} %get-tuple-element.55), channel_id=1, source_target_pairs={{0,1},{1,2},{2,3},{3,0},{4,5},{5,6},{6,7},{7,4},{8,9},{9,10},{10,1... | collective-permute-start | bytes 1179656 | tf_op jit(solution)/shard_map/ppermute | solution.py:137
  27.5 11.5 %all-to-all-start.1 = ((bf16[8,12,512]{2,1,0:T(8,128)(2,1)}), bf16[8,12,512]{2,1,0:T(8,128)(2,1)S(1)}, u32[]{:S(2)}, u32[]{:S(2)}) async-start(bf16[8,12,512]{2,1,0:T(8,128)(2,1)} %bitcast.8), calls=%async_computation.1 | async-start | bytes 262144 | tf_op jit(solution)/shard_map/all_to_all | solution.py:132
  32.2 14.5 %collective-permute-start.3 = (bf16[64,4096]{1,0:T(8,128)(2,1)}, bf16[64,4096]{1,0:T(8,128)(2,1)}, u32[]{:S(2)}, u32[]{:S(2)}) collective-permute-start(bf16[64,4096]{1,0:T(8,128)(2,1)} %dynamic-slice_bitcast_fusion.2), channel_id=1, source_target_pairs={{0,4},{1,5},{2,6},{3,7},{4,0},{5,1},{6,2},{7,3},{8,12},{9,13},{10,... | collective-permute-start | bytes 1572872 | tf_op jit(solution)/shard_map/ppermute | solution.py:141
  36.0 10.7 %collective-permute-start.4 = (bf16[192,1024]{1,0:T(8,128)(2,1)}, bf16[192,1024]{1,0:T(8,128)(2,1)}, u32[]{:S(2)}, u32[]{:S(2)}) collective-permute-start(bf16[192,1024]{1,0:T(8,128)(2,1)} %dynamic-slice_bitcast_fusion.9), channel_id=1, source_target_pairs={{0,2},{1,3},{2,0},{3,1},{4,6},{5,7},{6,4},{7,5},{8,10},{9,11},{10,... | collective-permute-start | bytes 1179656 | tf_op jit(solution)/shard_map/ppermute | solution.py:137
  46.7 39.5 %all-to-all-start.2 = ((bf16[32,24,512]{2,1,0:T(8,128)(2,1)}), bf16[32,24,512]{2,1,0:T(8,128)(2,1)}, u32[]{:S(2)}, u32[]{:S(2)}) async-start(bf16[32,24,512]{2,1,0:T(8,128)(2,1)} %bitcast.64), calls=%async_computation.2 | async-start | bytes 1572864 | tf_op jit(solution)/shard_map/all_to_all | solution.py:132
  58.4 19.2 %collective-permute-start.8 = (bf16[48,4096]{1,0:T(8,128)(2,1)S(1)}, bf16[48,4096]{1,0:T(8,128)(2,1)S(1)}, u32[]{:S(2)}, u32[]{:S(2)}) collective-permute-start(bf16[48,4096]{1,0:T(8,128)(2,1)S(1)} %dynamic-slice_bitcast_fusion.5), channel_id=1, source_target_pairs={{0,4},{1,5},{2,6},{3,7},{4,0},{5,1},{6,2},{7,3},{8,12},{9,13},{10,... | collective-permute-start | bytes 1179656 | tf_op jit(solution)/shard_map/ppermute | solution.py:141
  62.0 50.2 %collective-permute-start.13 = (bf16[192,4096]{1,0:T(8,128)(2,1)}, bf16[192,4096]{1,0:T(8,128)(2,1)}, u32[]{:S(2)}, u32[]{:S(2)}) collective-permute-start(bf16[192,4096]{1,0:T(8,128)(2,1)} %dynamic-slice_bitcast_fusion), channel_id=1, source_target_pairs={{0,4},{1,5},{2,6},{3,7},{4,0},{5,1},{6,2},{7,3},{8,12},{9,13},{10,... | collective-permute-start | bytes 4718600 | tf_op jit(solution)/shard_map/ppermute | solution.py:141
  64.3 13.6 %collective-permute-start.7 = (bf16[192,1024]{1,0:T(8,128)(2,1)S(1)}, bf16[192,1024]{1,0:T(8,128)(2,1)S(1)}, u32[]{:S(2)}, u32[]{:S(2)}) collective-permute-start(bf16[192,1024]{1,0:T(8,128)(2,1)S(1)} %get-tuple-element.51), channel_id=1, source_target_pairs={{0,2},{1,3},{2,0},{3,1},{4,6},{5,7},{6,4},{7,5},{8,10},{9,11},{10,... | collective-permute-start | bytes 1179656 | tf_op jit(solution)/shard_map/ppermute | solution.py:137
  67.0 17.6 %collective-permute-start.6 = (bf16[192,1024]{1,0:T(8,128)(2,1)S(1)}, bf16[192,1024]{1,0:T(8,128)(2,1)S(1)}, u32[]{:S(2)}, u32[]{:S(2)}) collective-permute-start(bf16[192,1024]{1,0:T(8,128)(2,1)S(1)} %get-tuple-element.52), channel_id=1, source_target_pairs={{0,3},{1,0},{2,1},{3,2},{4,7},{5,4},{6,5},{7,6},{8,11},{9,8},{10,9... | collective-permute-start | bytes 1179656 | tf_op jit(solution)/shard_map/ppermute | solution.py:137
  68.1 17.2 %collective-permute-start.5 = (bf16[192,1024]{1,0:T(8,128)(2,1)S(1)}, bf16[192,1024]{1,0:T(8,128)(2,1)S(1)}, u32[]{:S(2)}, u32[]{:S(2)}) collective-permute-start(bf16[192,1024]{1,0:T(8,128)(2,1)S(1)} %get-tuple-element.53), channel_id=1, source_target_pairs={{0,1},{1,2},{2,3},{3,0},{4,5},{5,6},{6,7},{7,4},{8,9},{9,10},{10,1... | collective-permute-start | bytes 1179656 | tf_op jit(solution)/shard_map/ppermute | solution.py:137
  88.4 23.8 %copy-start.1 = (bf16[2,192,4096]{2,1,0:T(8,128)(2,1)S(1)}, bf16[2,192,4096]{2,1,0:T(8,128)(2,1)}, u32[]{:S(2)}) copy-start(bf16[2,192,4096]{2,1,0:T(8,128)(2,1)} %own_up.3) | copy-start | bytes 9437188
  88.5 19.7 %collective-permute-start.11 = (bf16[384,1024]{1,0:T(8,128)(2,1)S(1)}, bf16[384,1024]{1,0:T(8,128)(2,1)S(1)}, u32[]{:S(2)}, u32[]{:S(2)}) collective-permute-start(bf16[384,1024]{1,0:T(8,128)(2,1)S(1)} %bitcast.60), channel_id=1, source_target_pairs={{0,3},{1,0},{2,1},{3,2},{4,7},{5,4},{6,5},{7,6},{8,11},{9,8},{10,9... | collective-permute-start | bytes 2359304 | tf_op jit(solution)/shard_map/ppermute | solution.py:137
  91.2 20.8 %collective-permute-start.9 = (bf16[384,1024]{1,0:T(8,128)(2,1)S(1)}, bf16[384,1024]{1,0:T(8,128)(2,1)S(1)}, u32[]{:S(2)}, u32[]{:S(2)}) collective-permute-start(bf16[384,1024]{1,0:T(8,128)(2,1)S(1)} %bitcast.61), channel_id=1, source_target_pairs={{0,1},{1,2},{2,3},{3,0},{4,5},{5,6},{6,7},{7,4},{8,9},{9,10},{10,1... | collective-permute-start | bytes 2359304 | tf_op jit(solution)/shard_map/ppermute | solution.py:137
  92.6 51.8 %collective-permute-start.18 = (bf16[768,1024]{1,0:T(8,128)(2,1)S(1)}, bf16[768,1024]{1,0:T(8,128)(2,1)S(1)}, u32[]{:S(2)}, u32[]{:S(2)}) collective-permute-start(bf16[768,1024]{1,0:T(8,128)(2,1)S(1)} %pad_maximum_fusion), channel_id=1, source_target_pairs={{0,4},{1,5},{2,6},{3,7},{4,0},{5,1},{6,2},{7,3},{8,12},{9,13},{10,... | collective-permute-start | bytes 4718600 | tf_op jit(solution)/shard_map/ppermute | solution.py:141
  108.2 11.5 %collective-permute-start.12 = (bf16[192,1024]{1,0:T(8,128)(2,1)S(1)}, bf16[192,1024]{1,0:T(8,128)(2,1)S(1)}, u32[]{:S(2)}, u32[]{:S(2)}) collective-permute-start(bf16[192,1024]{1,0:T(8,128)(2,1)S(1)} %slice.27), channel_id=1, source_target_pairs={{0,3},{1,0},{2,1},{3,2},{4,7},{5,4},{6,5},{7,6},{8,11},{9,8},{10,9... | collective-permute-start | bytes 1179656 | tf_op jit(solution)/shard_map/ppermute | solution.py:137
  112.1 11.2 %collective-permute-start.10 = (bf16[192,1024]{1,0:T(8,128)(2,1)S(1)}, bf16[192,1024]{1,0:T(8,128)(2,1)S(1)}, u32[]{:S(2)}, u32[]{:S(2)}) collective-permute-start(bf16[192,1024]{1,0:T(8,128)(2,1)S(1)} %slice.26), channel_id=1, source_target_pairs={{0,1},{1,2},{2,3},{3,0},{4,5},{5,6},{6,7},{7,4},{8,9},{9,10},{10,1... | collective-permute-start | bytes 1179656 | tf_op jit(solution)/shard_map/ppermute | solution.py:137
  123.3 21.2 %copy-start.6 = (bf16[192,1024]{1,0:T(8,128)(2,1)S(1)}, bf16[192,1024]{1,0:T(8,128)(2,1)}, u32[]{:S(2)}) copy-start(bf16[192,1024]{1,0:T(8,128)(2,1)} %copy-done.5) | copy-start | bytes 1179652
  123.3 21.2 %copy-start.8 = (bf16[192,1024]{1,0:T(8,128)(2,1)S(1)}, bf16[192,1024]{1,0:T(8,128)(2,1)}, u32[]{:S(2)}) copy-start(bf16[192,1024]{1,0:T(8,128)(2,1)} %copy-done.7) | copy-start | bytes 1179652
  123.3 21.2 %copy-start.10 = (bf16[192,1024]{1,0:T(8,128)(2,1)S(1)}, bf16[192,1024]{1,0:T(8,128)(2,1)}, u32[]{:S(2)}) copy-start(bf16[192,1024]{1,0:T(8,128)(2,1)} %copy-done.9) | copy-start | bytes 1179652
  126.2 7.2 %collective-permute-start.15 = (bf16[384,384]{1,0:T(8,128)(2,1)S(1)}, bf16[384,384]{1,0:T(8,128)(2,1)S(1)}, u32[]{:S(2)}, u32[]{:S(2)}) collective-permute-start(bf16[384,384]{1,0:T(8,128)(2,1)S(1)} %expand_far.1.own), channel_id=1, source_target_pairs={{0,3},{1,0},{2,1},{3,2},{4,7},{5,4},{6,5},{7,6},{8,11},{9,8},{10,9... | collective-permute-start | bytes 884744 | tf_op jit(solution)/shard_map/ppermute | solution.py:137
  126.4 8.5 %collective-permute-start.14 = (bf16[384,384]{1,0:T(8,128)(2,1)S(1)}, bf16[384,384]{1,0:T(8,128)(2,1)S(1)}, u32[]{:S(2)}, u32[]{:S(2)}) collective-permute-start(bf16[384,384]{1,0:T(8,128)(2,1)S(1)} %expand_far.1.own), channel_id=1, source_target_pairs={{0,1},{1,2},{2,3},{3,0},{4,5},{5,6},{6,7},{7,4},{8,9},{9,10},{10,1... | collective-permute-start | bytes 884744 | tf_op jit(solution)/shard_map/ppermute | solution.py:137
  133.4 11.1 %collective-permute-start.17 = (bf16[192,384]{1,0:T(8,128)(2,1)S(1)}, bf16[192,384]{1,0:T(8,128)(2,1)S(1)}, u32[]{:S(2)}, u32[]{:S(2)}) collective-permute-start(bf16[192,384]{1,0:T(8,128)(2,1)S(1)} %slice.29), channel_id=1, source_target_pairs={{0,3},{1,0},{2,1},{3,2},{4,7},{5,4},{6,5},{7,6},{8,11},{9,8},{10,9... | collective-permute-start | bytes 442376 | tf_op jit(solution)/shard_map/ppermute | solution.py:137
  134.9 9.5 %collective-permute-start.16 = (bf16[192,384]{1,0:T(8,128)(2,1)S(1)}, bf16[192,384]{1,0:T(8,128)(2,1)S(1)}, u32[]{:S(2)}, u32[]{:S(2)}) collective-permute-start(bf16[192,384]{1,0:T(8,128)(2,1)S(1)} %slice.28), channel_id=1, source_target_pairs={{0,1},{1,2},{2,3},{3,0},{4,5},{5,6},{6,7},{7,4},{8,9},{9,10},{10,1... | collective-permute-start | bytes 442376 | tf_op jit(solution)/shard_map/ppermute | solution.py:137
  146.3 34.0 %copy-start.17 = (f32[96,32]{0,1:T(8,128)S(1)}, f32[96,32]{0,1:T(8,128)}, u32[]{:S(2)}) copy-start(f32[96,32]{0,1:T(8,128)} %get-tuple-element.47) | copy-start | bytes 36868
  146.3 34.0 %copy-start.19 = (f32[96,24]{0,1:T(8,128)S(1)}, f32[96,24]{0,1:T(8,128)}, u32[]{:S(2)}) copy-start(f32[96,24]{0,1:T(8,128)} %constant.103) | copy-start | bytes 27652
  146.9 39.3 %copy-start.12 = (f32[6,32,128]{2,1,0:T(8,128)S(1)}, f32[6,32,128]{2,1,0:T(8,128)}, u32[]{:S(2)}) copy-start(f32[6,32,128]{2,1,0:T(8,128)} %copy-done.11) | copy-start | bytes 294916
  181.5 11.3 %all-to-all-start.4 = ((bf16[8,12,512]{2,1,0:T(8,128)(2,1)}), bf16[8,12,512]{2,1,0:T(8,128)(2,1)S(1)}, u32[]{:S(2)}, u32[]{:S(2)}) async-start(bf16[8,12,512]{2,1,0:T(8,128)(2,1)} %reshape.96), calls=%async_computation.4 | async-start | bytes 262144 | tf_op jit(solution)/shard_map/all_to_all | solution.py:132
  (14 other events, 122.0 us)
